TPU v7x, 32 devices: a whole 2x2x4 slice. The times are simulated.
32 devices in a mesh: seg: 2 (over y), samp: 4 (over x, core), var: 4 (over z).
Axes of the slice: x: 2, y: 2, z: 4, core: 2. Of those that a mesh axis runs over, the one named last changes fastest.
Arguments:
- dosage: bfloat16 [8192, 4096], P('samp', ('seg', 'var')), parts along dimension 1
- observed: int32 [8, 8192], P(('seg', 'var'), 'samp'), parts along dimension 0, may hold values from 0 to 1, as said below
- band_reach: int32 [8], P(('seg', 'var')), parts along dimension 0, may hold values from 0 to 2
Outputs:
- ld_blocks: float32 [8, 512, 3, 512], P(('seg', 'var'), 'samp'), parts along dimension 0
There are 2 independent parts, one for each index of `seg`. A program takes and returns all parts, laid end to end along the dimension named above; each array names one. Nothing has to cross between parts.
Inputs may be any that keep to these rules, and one draw needn't show every extreme that they name: observed is 0 or 1 for each variant block of each individual; every block is observed for at least one individual.
All inputs are finite; a program needn't handle non-finite values.
Results may differ from a plain program's by a relative error of at most 0.0011.
Values may be sent and summed in bfloat16 or wider, within the bound.
No kernel may reach another device: no remote copies, remote signals or barrier semaphores. Data moves between devices by JAX's collectives and lax.ppermute only.
A program may use at most 64 MiB of HBM per device.

v0:
```python
import jax
import jax.numpy as jnp
from jax import lax
from jax.sharding import PartitionSpec as P

BAND = 3


EPSILON = 1e-05


def from_behind(shard, axis, by):
    peers = lax.axis_size(axis)
    pairs = [(i, i + by) for i in range(peers) if 0 <= i + by < peers]
    return lax.ppermute(shard, axis, pairs)


def fetch_partners(values, flags):
    received = []
    for offset in range(1, BAND):
        received.append(from_behind((values, flags), "var", -offset))
    return received


def finish_moments(totals, first_sum, second_sum):
    centre = first_sum / totals
    spread_inverse = 1.0 / jnp.sqrt(second_sum / totals - centre * centre + EPSILON)
    return (centre, spread_inverse)


def standardize(values, weights, centre, spread_inverse):
    return (
        weights[:, None] * (values.astype(jnp.float32) - centre[None, :]) * spread_inverse[None, :]
    ).astype(jnp.bfloat16)


def per_device(dosage, observed, band_reach):
    block_width = dosage.shape[1]
    weights = observed[0].astype(jnp.float32)
    weights_half = observed[0].astype(jnp.bfloat16)
    first_sum = jnp.dot(weights_half[None, :], dosage, preferred_element_type=jnp.float32)[0]
    second_sum = jnp.sum(weights[:, None] * jnp.square(dosage.astype(jnp.float32)), axis=0)
    own_total = jnp.sum(weights)
    received = fetch_partners(dosage, weights_half)
    partner_weights = [entry[1].astype(jnp.float32) for entry in received]
    intersection_local = jnp.stack(
        [own_total] + [jnp.sum(weights * other) for other in partner_weights]
    )
    totals, first_sum, second_sum, intersections = lax.psum(
        (own_total, first_sum, second_sum, intersection_local), "samp"
    )
    centre, spread_inverse = finish_moments(totals, first_sum, second_sum)
    standard = standardize(dosage, weights, centre, spread_inverse)
    partner_standard = []
    for offset in range(1, BAND):
        far_centre, far_inverse = from_behind((centre, spread_inverse), "var", -offset)
        partner_standard.append(
            standardize(
                received[offset - 1][0], partner_weights[offset - 1], far_centre, far_inverse
            )
        )
    stacked = jnp.concatenate([standard] + partner_standard, axis=1)
    shared = lax.psum_scatter(
        lax.dot_general(
            standard, stacked, (((0,), (0,)), ((), ())), preferred_element_type=jnp.float32
        ),
        "samp",
        scatter_dimension=0,
        tiled=True,
    )
    shared = shared.reshape(1, shared.shape[0], BAND, block_width)
    divisor = jnp.maximum(intersections, 1.0)
    keep = jnp.arange(BAND, dtype=jnp.int32) <= band_reach[0]
    return jnp.where(
        keep[None, None, :, None], shared / divisor[None, None, :, None], jnp.float32(0.0)
    )


def solution(mesh):
    return jax.shard_map(
        per_device,
        mesh=mesh,
        in_specs=(P("samp", ("seg", "var")), P(("seg", "var"), "samp"), P(("seg", "var"))),
        out_specs=P(("seg", "var"), "samp", None, None),
        check_vma=False,
    )
```

profile of v0, /device:TPU:0, one launch (start us, length us, event | category | flops | bytes accessed | tf_op | source)
XLA Modules:
  0.0 207.9 jit_solution(12277508751332168561)
XLA Ops:
  6.5 1.4 collective-permute-start.5
  8.0 0.7 convert_reduce_fusion
  8.7 1.3 collective-permute-start
  10.0 1.3 collective-permute-start.4
  11.3 1.3 collective-permute-start.1
  12.6 0.7 convert_element_type.40
  13.3 2.2 %fusion.10 = f32[512]{0:T(512)S(1)} fusion(bf16[2048,512]{1,0:T(8,128)(2,1)} %param.3, f32[2048]{0:T(1024)S(1)} %bitcast.14), kind=kLoop, calls=%fused_computation.12 | loop fusion | flops 4193792 | bytes 2107392 | tf_op jit(solution)/shard_map/reduce_sum | solution.py:42
  15.5 2.0 fusion.11
  17.4 0.6 convert_reduce_fusion.1
  18.1 0.0 collective-permute-done
  18.1 85.8 %collective-permute-done.4 = bf16[2048]{0:T(1024)(128)(2,1)S(1)} collective-permute-done((bf16[2048]{0:T(1024)(128)(2,1)S(1)}, bf16[2048]{0:T(1024)(128)(2,1)S(1)}, u32[]{:S(2)}, u32[]{:S(2)}) %collective-permute-start.4) | collective-permute-done | bytes 4128 | tf_op jit(solution)/shard_map/ppermute | solution.py:15
  103.9 0.6 multiply_reduce_fusion.1
  104.5 1.9 pad_maximum_fusion
  106.5 6.6 %all-reduce = (f32[512]{0:T(512)S(1)}, f32[]{:T(128)}, f32[512]{0:T(512)S(1)}, f32[3]{0:T(128)S(1)}) all-reduce(f32[512]{0:T(512)S(1)} %fusion.10, f32[]{:T(128)} %convert_reduce_fusion.1, f32[512]{0:T(512)S(1)} %bitcast.17, f32[3]{0:T(128)S(1)} %pad_maximum_fusion), channel_id=1, replica_groups=mesh['seg'=2,'samp'=4,'var'=4] {'samp'}, use_global_device_ids=true, to_apply=%region_4.0 | all-reduce | flops 1028 | bytes 8224 | tf_op jit(solution)/shard_map/psum | solution.py:49
  113.1 0.7 broadcast_divide_fusion
  113.8 1.3 collective-permute-start.6
  115.1 1.3 collective-permute-start.2
  116.4 1.3 collective-permute-start.7
  117.7 0.6 fusion.8
  118.3 29.8 %collective-permute-done.6 = f32[512]{0:T(512)S(1)} collective-permute-done((f32[512]{0:T(512)S(1)}, f32[512]{0:T(512)S(1)}, u32[]{:S(2)}, u32[]{:S(2)}) %collective-permute-start.6) | collective-permute-done | bytes 2080 | tf_op jit(solution)/shard_map/ppermute | solution.py:15
  148.2 1.3 collective-permute-start.3
  149.5 0.0 collective-permute-done.5
  149.5 2.2 %multiply_convert_fusion = bf16[2048,512]{1,0:T(8,128)(2,1)S(1)} fusion(bf16[2048,512]{1,0:T(8,128)(2,1)} %collective-permute-done.5, f32[512]{0:T(512)S(1)} %collective-permute-done.7, f32[512]{0:T(512)S(1)} %collective-permute-done.6, f32[2048]{0:T(1024)S(1)} %convert_element_type.48), kind=kLoop, calls=%fused_computation.13 | loop fusion | flops 5242880 | bytes 4206592 | tf_op jit(solution)/shard_map/convert_element_type | solution.py:34
  151.7 0.0 collective-permute-done.2
  151.7 1.9 collective-permute-done.3
  153.6 2.2 %multiply_convert_fusion.1 = bf16[2048,512]{1,0:T(8,128)(2,1)S(1)} fusion(bf16[2048,512]{1,0:T(8,128)(2,1)} %collective-permute-done.1, f32[512]{0:T(512)S(1)} %collective-permute-done.3, f32[512]{0:T(512)S(1)} %collective-permute-done.2, f32[2048]{0:T(1024)S(1)} %convert_element_type.45), kind=kLoop, calls=%fused_computation.14 | loop fusion | flops 5242880 | bytes 4206592 | tf_op jit(solution)/shard_map/convert_element_type | solution.py:34
  155.9 5.4 %fusion = f32[512,1536]{1,0:T(8,128)} fusion(bf16[2048,512]{1,0:T(8,128)(2,1)S(1)} %fusion.8, bf16[2048,512]{1,0:T(8,128)(2,1)S(1)} %multiply_convert_fusion, bf16[2048,512]{1,0:T(8,128)(2,1)S(1)} %multiply_convert_fusion.1), kind=kOutput, calls=%fused_computation | convolution fusion | flops 3240099840 | bytes 9437184 | tf_op jit(solution)/shard_map/dot_general | solution.py:64
  161.3 0.0 reduce-scatter.2.cloned.1.call-update
  162.0 36.4 %reduce-scatter.2.cloned.1.call-done = f32[128,1536]{1,0:T(8,128)} async-done(((f32[512,1536]{1,0:T(8,128)}), f32[128,1536]{1,0:T(8,128)}) %reduce-scatter.2.cloned.1.call-update) | async-done | bytes 786448 | tf_op jit(solution)/shard_map/reduce_scatter | solution.py:63
  198.4 1.4 copy.5
  199.8 0.1 divide_select_fusion
  199.9 1.1 copy.6
  (11 shorter events, 0.0 us)
Async XLA Ops:
  6.5 111.1 %copy-start = (bf16[2048,512]{1,0:T(8,128)(2,1)S(1)}, bf16[2048,512]{1,0:T(8,128)(2,1)}, u32[]{:S(2)}) copy-start(bf16[2048,512]{1,0:T(8,128)(2,1)} %param.3) | copy-start | bytes 6291460
  6.5 10.9 %copy-start.1 = (s32[1,2048]{1,0:T(1,128)S(1)}, s32[1,2048]{1,0:T(1,128)}, u32[]{:S(2)}) copy-start(s32[1,2048]{1,0:T(1,128)} %param.4) | copy-start | bytes 24580
  6.5 191.8 %reduce-scatter.2.cloned.1.call-start = ((), (), s32[]{:S(2)}) async-start(), calls=%async_computation.1 | async-start | bytes 3932160 | tf_op jit(solution)/shard_map/reduce_scatter | solution.py:63
  6.5 142.9 %collective-permute-start.5 = (bf16[2048,512]{1,0:T(8,128)(2,1)}, bf16[2048,512]{1,0:T(8,128)(2,1)}, u32[]{:S(2)}, u32[]{:S(2)}) collective-permute-start(bf16[2048,512]{1,0:T(8,128)(2,1)} %param.3), channel_id=1, source_target_pairs={{2,0},{3,1},{6,4},{7,5},{10,8},{11,9},{14,12},{15,13},{18,16},{19,... | collective-permute-start | bytes 6291464 | tf_op jit(solution)/shard_map/ppermute | solution.py:15
  8.7 9.4 %collective-permute-start = (bf16[2048]{0:T(1024)(128)(2,1)S(1)}, bf16[2048]{0:T(1024)(128)(2,1)S(1)}, u32[]{:S(2)}, u32[]{:S(2)}) collective-permute-start(bf16[2048]{0:T(1024)(128)(2,1)S(1)} %convert_reduce_fusion), channel_id=1, source_target_pairs={{1,0},{2,1},{3,2},{5,4},{6,5},{7,6},{9,8},{10,9},{11,10},{13,12},{... | collective-permute-start | bytes 12296 | tf_op jit(solution)/shard_map/ppermute | solution.py:15
  10.0 93.9 %collective-permute-start.4 = (bf16[2048]{0:T(1024)(128)(2,1)S(1)}, bf16[2048]{0:T(1024)(128)(2,1)S(1)}, u32[]{:S(2)}, u32[]{:S(2)}) collective-permute-start(bf16[2048]{0:T(1024)(128)(2,1)S(1)} %convert_reduce_fusion), channel_id=1, source_target_pairs={{2,0},{3,1},{6,4},{7,5},{10,8},{11,9},{14,12},{15,13},{18,16},{19,... | collective-permute-start | bytes 12296 | tf_op jit(solution)/shard_map/ppermute | solution.py:15
  11.3 142.3 %collective-permute-start.1 = (bf16[2048,512]{1,0:T(8,128)(2,1)}, bf16[2048,512]{1,0:T(8,128)(2,1)}, u32[]{:S(2)}, u32[]{:S(2)}) collective-permute-start(bf16[2048,512]{1,0:T(8,128)(2,1)} %param.3), channel_id=1, source_target_pairs={{1,0},{2,1},{3,2},{5,4},{6,5},{7,6},{9,8},{10,9},{11,10},{13,12},{... | collective-permute-start | bytes 6291464 | tf_op jit(solution)/shard_map/ppermute | solution.py:15
  113.8 34.4 %collective-permute-start.6 = (f32[512]{0:T(512)S(1)}, f32[512]{0:T(512)S(1)}, u32[]{:S(2)}, u32[]{:S(2)}) collective-permute-start(f32[512]{0:T(512)S(1)} %get-tuple-element.11), channel_id=1, source_target_pairs={{2,0},{3,1},{6,4},{7,5},{10,8},{11,9},{14,12},{15,13},{18,16},{19,... | collective-permute-start | bytes 6152 | tf_op jit(solution)/shard_map/ppermute | solution.py:15
  115.1 36.6 %collective-permute-start.2 = (f32[512]{0:T(512)S(1)}, f32[512]{0:T(512)S(1)}, u32[]{:S(2)}, u32[]{:S(2)}) collective-permute-start(f32[512]{0:T(512)S(1)} %get-tuple-element.11), channel_id=1, source_target_pairs={{1,0},{2,1},{3,2},{5,4},{6,5},{7,6},{9,8},{10,9},{11,10},{13,12},{... | collective-permute-start | bytes 6152 | tf_op jit(solution)/shard_map/ppermute | solution.py:15
  116.4 33.1 %collective-permute-start.7 = (f32[512]{0:T(512)S(1)}, f32[512]{0:T(512)S(1)}, u32[]{:S(2)}, u32[]{:S(2)}) collective-permute-start(f32[512]{0:T(512)S(1)} %get-tuple-element.12), channel_id=1, source_target_pairs={{2,0},{3,1},{6,4},{7,5},{10,8},{11,9},{14,12},{15,13},{18,16},{19,... | collective-permute-start | bytes 6152 | tf_op jit(solution)/shard_map/ppermute | solution.py:15
  148.2 5.5 %collective-permute-start.3 = (f32[512]{0:T(512)S(1)}, f32[512]{0:T(512)S(1)}, u32[]{:S(2)}, u32[]{:S(2)}) collective-permute-start(f32[512]{0:T(512)S(1)} %get-tuple-element.12), channel_id=1, source_target_pairs={{1,0},{2,1},{3,2},{5,4},{6,5},{7,6},{9,8},{10,9},{11,10},{13,12},{... | collective-permute-start | bytes 6152 | tf_op jit(solution)/shard_map/ppermute | solution.py:15
Sparse Core Ops, SparseCore 0:
  161.4 36.9 reduce-scatter.1
where the time goes:
time: 208 us
  waiting for transfers between devices  154 us (74%)
  between operations  14.2 us (7%)
  other arithmetic  12.7 us (6%)
  starting transfers between devices  10.4 us (5%)
  matrix products  7.37 us (4%)
  blocking collectives  6.64 us (3%)
  local copies, waits for them, and re-layouts  2.55 us (1%)
    ppermute x8, waiting for transfers between devices, from_behind(): return lax.ppermute(shard, axis, pairs)  118 us
    reduce_scatter x1, waiting for transfers between devices, per_device(): lax.psum_scatter(lax.dot_general(standard, stacked, (((0,), (0,)), ((), (...  36.4 us
    ppermute x8, starting transfers between devices, from_behind(): return lax.ppermute(shard, axis, pairs)  10.4 us
    psum x1, blocking collectives, per_device(): lax.psum((own_total, first_sum, second_sum, intersection_local), 'samp')  6.64 us
    dot_general x1, matrix products, per_device(): lax.dot_general(standard, stacked, (((0,), (0,)), ((), ())), preferred_el...  5.39 us
    convert_element_type x3, other arithmetic, standardize(): return (weights[:, None] * (values.astype(jnp.float32) - centre[None, :])...  5.09 us
  transfers between devices with their start and end apart: 9, of which 4 were waited for; matrix products, arithmetic and copies ran while one was open for 6% of the time, Pallas kernels for 0%

commit v1 on v0

v1 whole, which is shorter than its diff:
```python
import jax
import jax.numpy as jnp
from jax import lax
from jax.sharding import PartitionSpec as P

BAND = 3


EPSILON = 1e-05


def from_above(shard, axis):
    peers = lax.axis_size(axis)
    return lax.ppermute(shard, axis, [(i, i - 1) for i in range(1, peers)])


def from_below(shard, axis):
    peers = lax.axis_size(axis)
    return lax.ppermute(shard, axis, [(i, i + 1) for i in range(peers - 2)])


def swap(shard, axis, bit):
    peers = lax.axis_size(axis)
    return lax.ppermute(shard, axis, [(i, i ^ bit) for i in range(peers)])


def sum_all(value, axis):
    bit = 1
    while bit < lax.axis_size(axis):
        value = value + swap(value, axis, bit)
        bit *= 2
    return value


def sum_rows(partial, axis):
    peers = lax.axis_size(axis)
    place = lax.axis_index(axis)
    rows, columns = partial.shape
    bit = 1
    partial = partial.reshape(peers, rows // peers, columns)
    while bit < peers:
        pairs = partial.reshape(partial.shape[0] // 2, 2, *partial.shape[1:])
        high = (place & bit) != 0
        keep = jnp.where(high, pairs[:, 1], pairs[:, 0])
        give = jnp.where(high, pairs[:, 0], pairs[:, 1])
        partial = keep + swap(give, axis, bit)
        bit *= 2
    return partial[0]


def finish_moments(totals, first_sum, second_sum):
    centre = first_sum / totals
    spread_inverse = 1.0 / jnp.sqrt(second_sum / totals - centre * centre + EPSILON)
    return (centre, spread_inverse)


def standardize(values, weights, centre, spread_inverse):
    return (
        weights[:, None] * (values.astype(jnp.float32) - centre[None, :]) * spread_inverse[None, :]
    ).astype(jnp.bfloat16)


def cross(left, right):
    return lax.dot_general(
        left, right, (((0,), (0,)), ((), ())), preferred_element_type=jnp.float32
    )


def per_device(dosage, observed, band_reach):
    width = dosage.shape[1]
    flags = observed[0].astype(jnp.bfloat16)
    above_flags = from_above(flags, "var")
    below_flags = from_below(flags, "var")
    above = from_above(dosage, "var")
    below = from_below(dosage, "var")
    weights = observed[0].astype(jnp.float32)
    above_weights = above_flags.astype(jnp.float32)
    below_weights = below_flags.astype(jnp.float32)
    first_sum = jnp.dot(flags[None, :], dosage, preferred_element_type=jnp.float32)
    second_sum = jnp.sum(weights[:, None] * jnp.square(dosage.astype(jnp.float32)), axis=0)
    counts = jnp.stack(
        [jnp.sum(weights), jnp.sum(weights * above_weights), jnp.sum(below_weights * above_weights)]
    )
    sums = jnp.concatenate(
        [first_sum, second_sum[None, :], jnp.broadcast_to(counts[:, None], (3, width))], axis=0
    )
    sums = sum_all(sums, "samp")
    totals = sums[2]
    shares = jnp.maximum(sums[2:5], 1.0)
    centre, spread_inverse = finish_moments(totals, sums[0], sums[1])
    moments = jnp.stack([centre, spread_inverse])
    above_moments = from_above(moments, "var")
    below_moments = from_below(moments, "var")
    own = standardize(dosage, weights, centre, spread_inverse)
    same = sum_rows(cross(own, own), "samp") / shares[0]
    above_standard = standardize(above, above_weights, above_moments[0], above_moments[1])
    below_standard = standardize(below, below_weights, below_moments[0], below_moments[1])
    far = sum_rows(cross(below_standard, above_standard), "samp") / shares[2]
    far = from_above(far, "var")
    near = sum_rows(cross(own, above_standard), "samp") / shares[1]
    result = jnp.stack([same, near, far], axis=1)
    keep = jnp.arange(BAND, dtype=jnp.int32) <= band_reach[0]
    return jnp.where(keep[None, :, None], result, jnp.float32(0.0))[None]


def solution(mesh):
    return jax.shard_map(
        per_device,
        mesh=mesh,
        in_specs=(P("samp", ("seg", "var")), P(("seg", "var"), "samp"), P(("seg", "var"))),
        out_specs=P(("seg", "var"), "samp", None, None),
        check_vma=False,
    )
```

time: 208 us -> 103 us (0.50)
  waiting for transfers between devices: 154 us -> 55.8 us
  starting transfers between devices: 10.4 us -> 26.5 us
  between operations: 14.2 us -> 0.89 us
  blocking collectives: 6.64 us -> 0 us
  other arithmetic: 12.7 us -> 7.72 us
  matrix products: 7.37 us -> 11.5 us
  local copies, waits for them, and re-layouts: 2.55 us -> 0.02 us
    ppermute x8 -> x15, waiting for transfers between devices: 118 us -> 55.8 us  [the longest x3 30.4 us: from_below(): return lax.ppermute(shard, axis, [(i, i + 1) for i in range(peers - 2)])]
    reduce_scatter x1 -> x0, waiting for transfers between devices: 36.4 us -> none  [per_device(): lax.psum_scatter(lax.dot_general(standard, stacked, (((0,), (0,)), ((), (...]
    ppermute x8 -> x15, starting transfers between devices: 10.4 us -> 26.5 us  [the longest x3 15.4 us: from_below(): return lax.ppermute(shard, axis, [(i, i + 1) for i in range(peers - 2)])]
    psum x1 -> x0, blocking collectives: 6.64 us -> none  [per_device(): lax.psum((own_total, first_sum, second_sum, intersection_local), 'samp')]
    convert_element_type x6 -> x3, other arithmetic: 5.83 us -> 0.88 us  [the longest x1 0.88 us: per_device(): flags = observed[0].astype(jnp.bfloat16)]
    dot_general x2 -> x4, matrix products: 7.37 us -> 11.5 us  [the longest x3 9.56 us: cross(): lax.dot_general(left, right, (((0,), (0,)), ((), ())), preferred_element_...]
  transfers between devices with their start and end apart: 9 -> 15, of which waited for: 4 -> 6; matrix products, arithmetic and copies ran while one was open for 6% -> 10% of each run, Pallas kernels for 0% -> 0%
where the time goes in v1:
time: 103 us; the launch traced here: 102 us
  waiting for transfers between devices  55.8 us (54%)
  starting transfers between devices  26.5 us (26%)
  matrix products  11.5 us (11%)
  other arithmetic  7.72 us (7%)
    ppermute x3, waiting for transfers between devices, from_below(): return lax.ppermute(shard, axis, [(i, i + 1) for i in range(peers - 2)])  30.4 us
    ppermute x8, waiting for transfers between devices, swap(): return lax.ppermute(shard, axis, [(i, i ^ bit) for i in range(peers)])  16.2 us
    ppermute x3, starting transfers between devices, from_below(): return lax.ppermute(shard, axis, [(i, i + 1) for i in range(peers - 2)])  15.4 us
    dot_general x3, matrix products, cross(): lax.dot_general(left, right, (((0,), (0,)), ((), ())), preferred_element_...  9.56 us
    ppermute x4, waiting for transfers between devices, from_above(): return lax.ppermute(shard, axis, [(i, i - 1) for i in range(1, peers)])  9.16 us
    ppermute x8, starting transfers between devices, swap(): return lax.ppermute(shard, axis, [(i, i ^ bit) for i in range(peers)])  5.92 us
    ppermute x4, starting transfers between devices, from_above(): return lax.ppermute(shard, axis, [(i, i - 1) for i in range(1, peers)])  5.15 us
  transfers between devices with their start and end apart: 15, of which 6 were waited for; matrix products, arithmetic and copies ran while one was open for 10% of the time, Pallas kernels for 0%

profile of v1, /device:TPU:0, one launch (start us, length us, event | category | flops | bytes accessed | tf_op | source)
XLA Modules:
  0.0 102.5 jit_solution(14783872917755156644)
XLA Ops:
  0.0 0.9 convert_reduce_fusion
  0.9 1.3 %collective-permute-start = (bf16[2048]{0:T(1024)(128)(2,1)S(1)}, bf16[2048]{0:T(1024)(128)(2,1)S(1)}, u32[]{:S(2)}, u32[]{:S(2)}) collective-permute-start(bf16[2048]{0:T(1024)(128)(2,1)S(1)} %convert_reduce_fusion), channel_id=1, source_target_pairs={{1,0},{2,1},{3,2},{5,4},{6,5},{7,6},{9,8},{10,9},{11,10},{13,12},{... | collective-permute-start | bytes 12296 | tf_op jit(solution)/shard_map/ppermute | solution.py:14
  2.2 5.6 %collective-permute-start.1 = (bf16[2048]{0:T(1024)(128)(2,1)S(1)}, bf16[2048]{0:T(1024)(128)(2,1)S(1)}, u32[]{:S(2)}, u32[]{:S(2)}) collective-permute-start(bf16[2048]{0:T(1024)(128)(2,1)S(1)} %convert_reduce_fusion), channel_id=1, source_target_pairs={{0,1},{1,2},{4,5},{5,6},{8,9},{9,10},{12,13},{13,14},{16,17},{17,1... | collective-permute-start | bytes 12296 | tf_op jit(solution)/shard_map/ppermute | solution.py:19
  7.8 0.7 convert_element_type.40
  8.5 2.0 %fusion.18 = f32[1,512]{1,0:T(1,128)S(1)} fusion(bf16[2048,512]{1,0:T(8,128)(2,1)} %param.3, s32[1,2048]{1,0:T(1,128)} %param.4), kind=kOutput, calls=%fused_computation.44 | convolution fusion | flops 2099200 | bytes 2107392 | tf_op jit(solution)/shard_map/dot_general | solution.py:79
  10.5 0.6 fusion.1
  11.1 0.7 convert_reduce_fusion.1
  11.8 0.6 multiply_reduce_fusion.1
  12.4 2.0 %pad_maximum_fusion.1 = f32[5]{0:T(128)S(1)} fusion(f32[1]{0:T(128)} %bitcast.6, f32[1]{0:T(128)} %bitcast.5, f32[1]{0:T(128)} %bitcast.4), kind=kLoop, calls=%fused_computation.55 | loop fusion | flops 10 | bytes 32 | tf_op jit(solution)/shard_map/stack | solution.py:81
  14.4 5.3 %collective-permute-start.10 = (bf16[2048,512]{1,0:T(8,128)(2,1)S(1)}, bf16[2048,512]{1,0:T(8,128)(2,1)}, u32[]{:S(2)}, u32[]{:S(2)}) collective-permute-start(bf16[2048,512]{1,0:T(8,128)(2,1)S(1)} %copy-done), channel_id=1, source_target_pairs={{0,1},{1,2},{4,5},{5,6},{8,9},{9,10},{12,13},{13,14},{16,17},{17,1... | collective-permute-start | bytes 6291464 | tf_op jit(solution)/shard_map/ppermute | solution.py:19
  19.7 1.3 %collective-permute-start.6 = (bf16[2048,512]{1,0:T(8,128)(2,1)S(1)}, bf16[2048,512]{1,0:T(8,128)(2,1)}, u32[]{:S(2)}, u32[]{:S(2)}) collective-permute-start(bf16[2048,512]{1,0:T(8,128)(2,1)S(1)} %copy-done), channel_id=1, source_target_pairs={{1,0},{2,1},{3,2},{5,4},{6,5},{7,6},{9,8},{10,9},{11,10},{13,12},{... | collective-permute-start | bytes 6291464 | tf_op jit(solution)/shard_map/ppermute | solution.py:14
  21.7 1.5 %collective-permute-start.3 = (f32[5,512]{1,0:T(8,128)S(1)}, f32[5,512]{1,0:T(8,128)S(1)}, u32[]{:S(2)}, u32[]{:S(2)}) collective-permute-start(f32[5,512]{1,0:T(8,128)S(1)} %fusion.22), channel_id=1, source_target_pairs={{0,8},{4,12},{8,0},{12,4},{1,9},{5,13},{9,1},{13,5},{2,10},{6,14},... | collective-permute-start | bytes 30728 | tf_op jit(solution)/shard_map/ppermute | solution.py:24
  23.2 2.2 %collective-permute-done.3 = f32[5,512]{1,0:T(8,128)S(1)} collective-permute-done((f32[5,512]{1,0:T(8,128)S(1)}, f32[5,512]{1,0:T(8,128)S(1)}, u32[]{:S(2)}, u32[]{:S(2)}) %collective-permute-start.3) | collective-permute-done | bytes 10272 | tf_op jit(solution)/shard_map/ppermute | solution.py:24
  25.6 4.5 %collective-permute-start.11 = (f32[2,512]{1,0:T(2,128)S(1)}, f32[2,512]{1,0:T(2,128)S(1)}, u32[]{:S(2)}, u32[]{:S(2)}) collective-permute-start(f32[2,512]{1,0:T(2,128)S(1)} %pad_maximum_fusion), channel_id=1, source_target_pairs={{0,1},{1,2},{4,5},{5,6},{8,9},{9,10},{12,13},{13,14},{16,17},{17,1... | collective-permute-start | bytes 12296 | tf_op jit(solution)/shard_map/ppermute | solution.py:19
  30.1 1.3 %collective-permute-start.7 = (f32[2,512]{1,0:T(2,128)S(1)}, f32[2,512]{1,0:T(2,128)S(1)}, u32[]{:S(2)}, u32[]{:S(2)}) collective-permute-start(f32[2,512]{1,0:T(2,128)S(1)} %pad_maximum_fusion), channel_id=1, source_target_pairs={{1,0},{2,1},{3,2},{5,4},{6,5},{7,6},{9,8},{10,9},{11,10},{13,12},{... | collective-permute-start | bytes 12296 | tf_op jit(solution)/shard_map/ppermute | solution.py:14
  31.4 1.9 %fusion.14 = f32[512,512]{1,0:T(8,128)S(1)} fusion(bf16[2048,512]{1,0:T(8,128)(2,1)S(1)} %copy-done, f32[512]{0:T(512)S(1)} %bitcast.134, f32[512]{0:T(512)S(1)} %bitcast.136, f32[2048]{0:T(1024)S(1)} %bitcast.126), kind=kOutput, calls=%fused_computation.30 | convolution fusion | flops 1078984704 | bytes 3158016 | tf_op jit(solution)/shard_map/dot_general | solution.py:64
  33.5 30.4 %collective-permute-done.11 = f32[2,512]{1,0:T(2,128)S(1)} collective-permute-done((f32[2,512]{1,0:T(2,128)S(1)}, f32[2,512]{1,0:T(2,128)S(1)}, u32[]{:S(2)}, u32[]{:S(2)}) %collective-permute-start.11) | collective-permute-done | bytes 4128 | tf_op jit(solution)/shard_map/ppermute | solution.py:19
  64.0 5.5 %collective-permute-done.7 = f32[2,512]{1,0:T(2,128)S(1)} collective-permute-done((f32[2,512]{1,0:T(2,128)S(1)}, f32[2,512]{1,0:T(2,128)S(1)}, u32[]{:S(2)}, u32[]{:S(2)}) %collective-permute-start.7) | collective-permute-done | bytes 4128 | tf_op jit(solution)/shard_map/ppermute | solution.py:14
  69.5 0.1 fusion.11
  69.7 4.1 %fusion.5 = f32[512,512]{1,0:T(8,128)S(1)} fusion(bf16[2048,512]{1,0:T(8,128)(2,1)} %collective-permute-done.10, f32[512]{0:T(512)S(1)} %bitcast.143, f32[512]{0:T(512)S(1)} %bitcast.142, f32[2048]{0:T(1024)S(1)} %convert_element_type.45, bf16[2048,512]{1,0:T(8,128)(2,1)} %collective-permute-done.6, f32[512]{0:T(512)S(1)} %bitcast.140, ...), kind=kOutput, calls=%fused_computation.9 | convolution fusion | flops 1084227584 | bytes 5267456 | tf_op jit(solution)/shard_map/dot_general | solution.py:64
  74.0 3.5 %fusion.12 = f32[512,512]{1,0:T(8,128)S(1)} fusion(bf16[2048,512]{1,0:T(8,128)(2,1)} %collective-permute-done.6, f32[512]{0:T(512)S(1)} %bitcast.141, f32[512]{0:T(512)S(1)} %bitcast.139, f32[2048]{0:T(1024)S(1)} %convert_element_type.44, bf16[2048,512]{1,0:T(8,128)(2,1)S(1)} %copy-done, f32[512]{0:T(512)S(1)} %bitcast.135, f32[512]{0:T(512)S(1)} %bitcast.137, ...), kind=kOutput, calls=%fused_computation.29 | convolution fusion | flops 1084227584 | bytes 5267456 | tf_op jit(solution)/shard_map/dot_general | solution.py:64
  77.6 0.6 collective-permute-start.8
  78.2 1.6 %collective-permute-start.5 = (f32[1,128,512]{2,1,0:T(8,128)S(1)}, f32[1,128,512]{2,1,0:T(8,128)S(1)}, u32[]{:S(2)}, u32[]{:S(2)}) collective-permute-start(f32[1,128,512]{2,1,0:T(8,128)S(1)} %select_bitcast_fusion.5), channel_id=1, source_target_pairs={{0,8},{4,12},{8,0},{12,4},{1,9},{5,13},{9,1},{13,5},{2,10},{6,14},... | collective-permute-start | bytes 786440 | tf_op jit(solution)/shard_map/ppermute | solution.py:24
  79.8 0.1 fusion.9
  79.9 0.6 collective-permute-start.13
  80.6 0.1 fusion.10
  80.8 1.6 %collective-permute-start.9 = (f32[1,128,512]{2,1,0:T(8,128)S(1)}, f32[1,128,512]{2,1,0:T(8,128)S(1)}, u32[]{:S(2)}, u32[]{:S(2)}) collective-permute-start(f32[1,128,512]{2,1,0:T(8,128)S(1)} %select_bitcast_fusion.4), channel_id=1, source_target_pairs={{0,8},{4,12},{8,0},{12,4},{1,9},{5,13},{9,1},{13,5},{2,10},{6,14},... | collective-permute-start | bytes 786440 | tf_op jit(solution)/shard_map/ppermute | solution.py:24
  82.3 10.8 %collective-permute-done.13 = f32[1,128,512]{2,1,0:T(8,128)S(1)} collective-permute-done((f32[1,128,512]{2,1,0:T(8,128)S(1)}, f32[1,128,512]{2,1,0:T(8,128)S(1)}, u32[]{:S(2)}, u32[]{:S(2)}) %collective-permute-start.13) | collective-permute-done | bytes 262176 | tf_op jit(solution)/shard_map/ppermute | solution.py:24
  93.1 1.3 %collective-permute-start.14 = (f32[128,512]{1,0:T(8,128)S(1)}, f32[128,512]{1,0:T(8,128)S(1)}, u32[]{:S(2)}, u32[]{:S(2)}) collective-permute-start(f32[128,512]{1,0:T(8,128)S(1)} %bitcast_divide_fusion), channel_id=1, source_target_pairs={{1,0},{2,1},{3,2},{5,4},{6,5},{7,6},{9,8},{10,9},{11,10},{13,12},{... | collective-permute-start | bytes 786440 | tf_op jit(solution)/shard_map/ppermute | solution.py:14
  94.5 3.2 %collective-permute-done.9 = f32[1,128,512]{2,1,0:T(8,128)S(1)} collective-permute-done((f32[1,128,512]{2,1,0:T(8,128)S(1)}, f32[1,128,512]{2,1,0:T(8,128)S(1)}, u32[]{:S(2)}, u32[]{:S(2)}) %collective-permute-start.9) | collective-permute-done | bytes 262176 | tf_op jit(solution)/shard_map/ppermute | solution.py:24
  97.8 3.6 %collective-permute-done.14 = f32[128,512]{1,0:T(8,128)S(1)} collective-permute-done((f32[128,512]{1,0:T(8,128)S(1)}, f32[128,512]{1,0:T(8,128)S(1)}, u32[]{:S(2)}, u32[]{:S(2)}) %collective-permute-start.14) | collective-permute-done | bytes 262176 | tf_op jit(solution)/shard_map/ppermute | solution.py:14
  101.4 1.0 %maximum_select_fusion = f32[1,128,3,512]{3,1,2,0:T(8,128)} fusion(f32[1,128,1,512]{3,1,2,0:T(8,128)S(1)} %bitcast.123, f32[1,128,1,512]{3,1,2,0:T(8,128)S(1)} %fusion.16, f32[1,128,1,512]{3,1,2,0:T(8,128)S(1)} %fusion.17, pred[3]{0:T(512)(128)(4,1)S(1)} %iota_compare_fusion), kind=kLoop, calls=%fused_computation.13 | loop fusion | flops 589824 | bytes 1572867 | tf_op jit(solution)/shard_map/jit(_where)/select_n | solution.py:103
  (37 shorter events, 1.0 us)
Async XLA Ops:
  0.0 10.5 %copy-start = (bf16[2048,512]{1,0:T(8,128)(2,1)S(1)}, bf16[2048,512]{1,0:T(8,128)(2,1)}, u32[]{:S(2)}) copy-start(bf16[2048,512]{1,0:T(8,128)(2,1)} %param.3) | copy-start | bytes 6291460
  0.9 10.9 %collective-permute-start = (bf16[2048]{0:T(1024)(128)(2,1)S(1)}, bf16[2048]{0:T(1024)(128)(2,1)S(1)}, u32[]{:S(2)}, u32[]{:S(2)}) collective-permute-start(bf16[2048]{0:T(1024)(128)(2,1)S(1)} %convert_reduce_fusion), channel_id=1, source_target_pairs={{1,0},{2,1},{3,2},{5,4},{6,5},{7,6},{9,8},{10,9},{11,10},{13,12},{... | collective-permute-start | bytes 12296 | tf_op jit(solution)/shard_map/ppermute | solution.py:14
  2.2 9.6 %collective-permute-start.1 = (bf16[2048]{0:T(1024)(128)(2,1)S(1)}, bf16[2048]{0:T(1024)(128)(2,1)S(1)}, u32[]{:S(2)}, u32[]{:S(2)}) collective-permute-start(bf16[2048]{0:T(1024)(128)(2,1)S(1)} %convert_reduce_fusion), channel_id=1, source_target_pairs={{0,1},{1,2},{4,5},{5,6},{8,9},{9,10},{12,13},{13,14},{16,17},{17,1... | collective-permute-start | bytes 12296 | tf_op jit(solution)/shard_map/ppermute | solution.py:19
  8.5 2.6 %copy-start.1 = (s32[1,2048]{1,0:T(1,128)S(1)}, s32[1,2048]{1,0:T(1,128)}, u32[]{:S(2)}) copy-start(s32[1,2048]{1,0:T(1,128)} %param.4) | copy-start | bytes 24580
  14.4 7.2 %collective-permute-start.2 = (f32[5,512]{1,0:T(8,128)S(1)}, f32[5,512]{1,0:T(8,128)S(1)}, u32[]{:S(2)}, u32[]{:S(2)}) collective-permute-start(f32[5,512]{1,0:T(8,128)S(1)} %maximum_maximum_fusion), channel_id=1, source_target_pairs={{0,4},{4,0},{8,12},{12,8},{1,5},{5,1},{9,13},{13,9},{2,6},{6,2},{1... | collective-permute-start | bytes 30728 | tf_op jit(solution)/shard_map/ppermute | solution.py:24
  14.4 55.2 %collective-permute-start.10 = (bf16[2048,512]{1,0:T(8,128)(2,1)S(1)}, bf16[2048,512]{1,0:T(8,128)(2,1)}, u32[]{:S(2)}, u32[]{:S(2)}) collective-permute-start(bf16[2048,512]{1,0:T(8,128)(2,1)S(1)} %copy-done), channel_id=1, source_target_pairs={{0,1},{1,2},{4,5},{5,6},{8,9},{9,10},{12,13},{13,14},{16,17},{17,1... | collective-permute-start | bytes 6291464 | tf_op jit(solution)/shard_map/ppermute | solution.py:19
  19.7 50.0 %collective-permute-start.6 = (bf16[2048,512]{1,0:T(8,128)(2,1)S(1)}, bf16[2048,512]{1,0:T(8,128)(2,1)}, u32[]{:S(2)}, u32[]{:S(2)}) collective-permute-start(bf16[2048,512]{1,0:T(8,128)(2,1)S(1)} %copy-done), channel_id=1, source_target_pairs={{1,0},{2,1},{3,2},{5,4},{6,5},{7,6},{9,8},{10,9},{11,10},{13,12},{... | collective-permute-start | bytes 6291464 | tf_op jit(solution)/shard_map/ppermute | solution.py:14
  21.7 3.7 %collective-permute-start.3 = (f32[5,512]{1,0:T(8,128)S(1)}, f32[5,512]{1,0:T(8,128)S(1)}, u32[]{:S(2)}, u32[]{:S(2)}) collective-permute-start(f32[5,512]{1,0:T(8,128)S(1)} %fusion.22), channel_id=1, source_target_pairs={{0,8},{4,12},{8,0},{12,4},{1,9},{5,13},{9,1},{13,5},{2,10},{6,14},... | collective-permute-start | bytes 30728 | tf_op jit(solution)/shard_map/ppermute | solution.py:24
  25.6 38.4 %collective-permute-start.11 = (f32[2,512]{1,0:T(2,128)S(1)}, f32[2,512]{1,0:T(2,128)S(1)}, u32[]{:S(2)}, u32[]{:S(2)}) collective-permute-start(f32[2,512]{1,0:T(2,128)S(1)} %pad_maximum_fusion), channel_id=1, source_target_pairs={{0,1},{1,2},{4,5},{5,6},{8,9},{9,10},{12,13},{13,14},{16,17},{17,1... | collective-permute-start | bytes 12296 | tf_op jit(solution)/shard_map/ppermute | solution.py:19
  30.1 39.3 %collective-permute-start.7 = (f32[2,512]{1,0:T(2,128)S(1)}, f32[2,512]{1,0:T(2,128)S(1)}, u32[]{:S(2)}, u32[]{:S(2)}) collective-permute-start(f32[2,512]{1,0:T(2,128)S(1)} %pad_maximum_fusion), channel_id=1, source_target_pairs={{1,0},{2,1},{3,2},{5,4},{6,5},{7,6},{9,8},{10,9},{11,10},{13,12},{... | collective-permute-start | bytes 12296 | tf_op jit(solution)/shard_map/ppermute | solution.py:14
  33.4 36.1 %collective-permute-start.4 = (f32[2,128,512]{2,1,0:T(8,128)S(1)}, f32[2,128,512]{2,1,0:T(8,128)S(1)}, u32[]{:S(2)}, u32[]{:S(2)}) collective-permute-start(f32[2,128,512]{2,1,0:T(8,128)S(1)} %select_bitcast_fusion.2), channel_id=1, source_target_pairs={{0,4},{4,0},{8,12},{12,8},{1,5},{5,1},{9,13},{13,9},{2,6},{6,2},{1... | collective-permute-start | bytes 1572872 | tf_op jit(solution)/shard_map/ppermute | solution.py:24
  73.9 5.9 %collective-permute-start.12 = (f32[2,128,512]{2,1,0:T(8,128)S(1)}, f32[2,128,512]{2,1,0:T(8,128)S(1)}, u32[]{:S(2)}, u32[]{:S(2)}) collective-permute-start(f32[2,128,512]{2,1,0:T(8,128)S(1)} %select_bitcast_fusion), channel_id=1, source_target_pairs={{0,4},{4,0},{8,12},{12,8},{1,5},{5,1},{9,13},{13,9},{2,6},{6,2},{1... | collective-permute-start | bytes 1572872 | tf_op jit(solution)/shard_map/ppermute | solution.py:24
  77.6 3.0 %collective-permute-start.8 = (f32[2,128,512]{2,1,0:T(8,128)S(1)}, f32[2,128,512]{2,1,0:T(8,128)S(1)}, u32[]{:S(2)}, u32[]{:S(2)}) collective-permute-start(f32[2,128,512]{2,1,0:T(8,128)S(1)} %select_bitcast_fusion.1), channel_id=1, source_target_pairs={{0,4},{4,0},{8,12},{12,8},{1,5},{5,1},{9,13},{13,9},{2,6},{6,2},{1... | collective-permute-start | bytes 1572872 | tf_op jit(solution)/shard_map/ppermute | solution.py:24
  78.2 16.2 %collective-permute-start.5 = (f32[1,128,512]{2,1,0:T(8,128)S(1)}, f32[1,128,512]{2,1,0:T(8,128)S(1)}, u32[]{:S(2)}, u32[]{:S(2)}) collective-permute-start(f32[1,128,512]{2,1,0:T(8,128)S(1)} %select_bitcast_fusion.5), channel_id=1, source_target_pairs={{0,8},{4,12},{8,0},{12,4},{1,9},{5,13},{9,1},{13,5},{2,10},{6,14},... | collective-permute-start | bytes 786440 | tf_op jit(solution)/shard_map/ppermute | solution.py:24
  79.9 13.1 %collective-permute-start.13 = (f32[1,128,512]{2,1,0:T(8,128)S(1)}, f32[1,128,512]{2,1,0:T(8,128)S(1)}, u32[]{:S(2)}, u32[]{:S(2)}) collective-permute-start(f32[1,128,512]{2,1,0:T(8,128)S(1)} %select_bitcast_fusion.3), channel_id=1, source_target_pairs={{0,8},{4,12},{8,0},{12,4},{1,9},{5,13},{9,1},{13,5},{2,10},{6,14},... | collective-permute-start | bytes 786440 | tf_op jit(solution)/shard_map/ppermute | solution.py:24
  80.8 17.0 %collective-permute-start.9 = (f32[1,128,512]{2,1,0:T(8,128)S(1)}, f32[1,128,512]{2,1,0:T(8,128)S(1)}, u32[]{:S(2)}, u32[]{:S(2)}) collective-permute-start(f32[1,128,512]{2,1,0:T(8,128)S(1)} %select_bitcast_fusion.4), channel_id=1, source_target_pairs={{0,8},{4,12},{8,0},{12,4},{1,9},{5,13},{9,1},{13,5},{2,10},{6,14},... | collective-permute-start | bytes 786440 | tf_op jit(solution)/shard_map/ppermute | solution.py:24
  93.1 8.3 %collective-permute-start.14 = (f32[128,512]{1,0:T(8,128)S(1)}, f32[128,512]{1,0:T(8,128)S(1)}, u32[]{:S(2)}, u32[]{:S(2)}) collective-permute-start(f32[128,512]{1,0:T(8,128)S(1)} %bitcast_divide_fusion), channel_id=1, source_target_pairs={{1,0},{2,1},{3,2},{5,4},{6,5},{7,6},{9,8},{10,9},{11,10},{13,12},{... | collective-permute-start | bytes 786440 | tf_op jit(solution)/shard_map/ppermute | solution.py:14

commit v2 on v1

v2 whole, which is shorter than its diff:
```python
import jax
import jax.numpy as jnp
import numpy as np
from jax import lax
from jax.experimental import pallas as pl
from jax.experimental.pallas import tpu as pltpu
from jax.sharding import PartitionSpec as P

BAND = 3


EPSILON = 1e-05

HOLE = float("nan")


def from_above(shard, axis):
    peers = lax.axis_size(axis)
    return lax.ppermute(shard, axis, [(i, i - 1) for i in range(1, peers)])


def from_below(shard, axis):
    peers = lax.axis_size(axis)
    return lax.ppermute(shard, axis, [(i, i + 1) for i in range(peers - 2)])


def swap(shard, axis, bit):
    peers = lax.axis_size(axis)
    return lax.ppermute(shard, axis, [(i, i ^ bit) for i in range(peers)])


def bits_of(peers):
    return [1 << k for k in range(peers.bit_length() - 1)]


def sum_all(value, axis):
    for bit in bits_of(lax.axis_size(axis)):
        value = value + swap(value, axis, bit)
    return value


def sum_rows(partial, axis):
    place = lax.axis_index(axis)
    for bit in bits_of(lax.axis_size(axis)):
        pairs = partial.reshape(partial.shape[0] // 2, 2, *partial.shape[1:])
        high = (place & bit) != 0
        keep = jnp.where(high, pairs[:, 1], pairs[:, 0])
        give = jnp.where(high, pairs[:, 0], pairs[:, 1])
        partial = keep + swap(give, axis, bit)
    return partial[0]


def local(kernel, outs, *args):
    spec = pl.BlockSpec(memory_space=pltpu.VMEM)
    size = sum(int(np.prod(a.shape)) * a.dtype.itemsize for a in (*args, *outs))
    return pl.pallas_call(
        kernel,
        out_shape=tuple(jax.ShapeDtypeStruct(o.shape, o.dtype) for o in outs),
        in_specs=[spec] * len(args),
        out_specs=tuple([spec] * len(outs)),
        cost_estimate=pl.CostEstimate(flops=2 * size, bytes_accessed=size, transcendentals=0),
    )(*args)


def like(shape, dtype):
    return jax.ShapeDtypeStruct(shape, dtype)


def pick(values, order_ref):
    shape = (values.shape[1], order_ref.shape[1])
    chosen = lax.broadcasted_iota(jnp.int32, shape, 0) == order_ref[...]
    return jnp.dot(
        values,
        jnp.where(chosen, 1.0, 0.0).astype(jnp.bfloat16),
        preferred_element_type=jnp.float32,
    )


def head_kernel(dosage_ref, observed_ref, order_ref, down_ref, up_ref):
    lanes = down_ref.shape[1]
    samples = dosage_ref.shape[0]
    flags = observed_ref[...].astype(jnp.float32)
    present = jnp.transpose(jnp.broadcast_to(flags, (lanes, samples))) > 0.5
    down = dosage_ref[:, :lanes].astype(jnp.float32)
    down_ref[...] = jnp.where(present, down, HOLE).astype(jnp.bfloat16)
    up = pick(dosage_ref[...], order_ref)
    up_ref[...] = jnp.where(present, up, HOLE).astype(jnp.bfloat16)


def moments_kernel(dosage_ref, observed_ref, sums_ref):
    flags = observed_ref[...].astype(jnp.float32)
    rows = jnp.broadcast_to(flags, (8, flags.shape[1])).astype(jnp.bfloat16)
    values = dosage_ref[...]
    exact = values.astype(jnp.float32)
    square = exact * exact
    high = square.astype(jnp.bfloat16)
    low = (square - high.astype(jnp.float32)).astype(jnp.bfloat16)

    def total(part):
        return jnp.dot(rows, part, preferred_element_type=jnp.float32)[:1]

    sums_ref[0:1, :] = total(values)
    sums_ref[1:2, :] = total(high) + total(low)
    count = jnp.sum(flags, axis=1, keepdims=True)
    sums_ref[2:3, :] = jnp.broadcast_to(count, (1, sums_ref.shape[1]))
    sums_ref[3:8, :] = jnp.zeros((5, sums_ref.shape[1]), jnp.float32)


def finish_moments(totals, first_sum, second_sum):
    centre = first_sum / totals
    spread_inverse = 1.0 / jnp.sqrt(second_sum / totals - centre * centre + EPSILON)
    return (centre, spread_inverse)


def own_kernel(dosage_ref, down_ref, sums_ref, order_ref, moments_ref, own_ref, *cut_refs):
    lanes = down_ref.shape[1]
    width = own_ref.shape[1]
    centre, inverse = finish_moments(sums_ref[2:3, :], sums_ref[0:1, :], sums_ref[1:2, :])
    moments_ref[0:1, :] = centre
    moments_ref[1:2, :] = inverse
    moments_ref[2:8, :] = jnp.zeros((6, width), jnp.float32)
    down = down_ref[...].astype(jnp.float32)
    present = down == down
    parts = []
    for low in range(0, width, lanes):
        spread = dosage_ref[:, low : low + lanes].astype(jnp.float32)
        spread = (spread - centre[:, low : low + lanes]) * inverse[:, low : low + lanes]
        parts.append(jnp.where(present, spread, 0.0).astype(jnp.bfloat16))
        own_ref[:, low : low + lanes] = parts[-1]
    half = len(cut_refs) // 2
    low = lanes
    for ref in cut_refs[:half]:
        ref[...] = own_ref[:, low : low + ref.shape[1]]
        low += ref.shape[1]
    up = pick(own_ref[...], order_ref).astype(jnp.bfloat16)
    low = 0
    for ref in cut_refs[half:]:
        ref[...] = up[:, low : low + ref.shape[1]]
        low += ref.shape[1]


def first_kernel(
    own_ref, above_ref, below_ref, above_m_ref, below_m_ref, shares_ref, above_out, below_out
):
    def split(ref):
        values = ref[...].astype(jnp.float32)
        return values, values == values

    def standardize(values, present, moments):
        spread = (values - moments[0:1, :]) * moments[1:2, :]
        return jnp.where(present, spread, 0.0).astype(jnp.bfloat16)

    _, own_present = split(own_ref)
    above, above_present = split(above_ref)
    below, below_present = split(below_ref)
    above_out[...] = standardize(above, above_present, above_m_ref)
    below_out[...] = standardize(below, below_present, below_m_ref)
    above_one = jnp.where(above_present, 1.0, 0.0)
    shares_ref[0:1, :] = jnp.sum(jnp.where(own_present, above_one, 0.0), axis=0, keepdims=True)
    shares_ref[1:2, :] = jnp.sum(jnp.where(below_present, above_one, 0.0), axis=0, keepdims=True)
    shares_ref[2:8, :] = jnp.zeros((6, shares_ref.shape[1]), jnp.float32)


def cross(left, right):
    return lax.dot_general(
        left, right, (((0,), (0,)), ((), ())), preferred_element_type=jnp.float32
    )


def per_device(dosage, observed, band_reach):
    samples, width = dosage.shape
    peers = lax.axis_size("samp")
    rows = width // peers
    row_edges = (0, rows // 4, 3 * rows // 4, rows)
    edges = tuple(edge * peers for edge in row_edges)
    order = np.concatenate(
        [
            (np.arange(peers)[:, None] * rows + np.arange(low, high)[None, :]).ravel()
            for low, high in zip(row_edges[:-1], row_edges[1:])
        ]
    ).astype(np.int32)[None, :]
    first, split, tail = edges[1], row_edges[2], rows - row_edges[2]
    quarters = width // first
    half = jnp.bfloat16
    down_a, up_a = local(
        head_kernel,
        [like((samples, first), half)] * 2,
        dosage,
        observed,
        jnp.asarray(order[:, :first]),
    )
    above_a = from_above(down_a, "var")
    below_a = from_below(up_a, "var")
    (sums,) = local(moments_kernel, [like((8, width), jnp.float32)], dosage, observed)
    sums = sum_all(sums, "samp")
    cuts = [like((samples, edges[2] - edges[1]), half), like((samples, edges[3] - edges[2]), half)]
    moments, own, down_b, down_c, up_b, up_c = local(
        own_kernel,
        [like((8, width), jnp.float32), like((samples, width), half)] + cuts * 2,
        dosage,
        down_a,
        sums,
        jnp.asarray(order[:, first:]),
    )
    above_m = from_above(moments[:, :first], "var")
    below_m = moments.reshape(8, peers, rows)[:, :, : row_edges[1]].reshape(8, first)
    below_m = from_below(below_m, "var")
    above_b = from_above(down_b, "var")
    below_b = from_below(up_b, "var")
    above_c = from_above(down_c, "var")
    below_c = from_below(up_c, "var")
    same = sum_rows(cross(own, own).reshape(peers, rows, width), "samp")
    shares, above_a, below_a = local(
        first_kernel,
        [like((8, first), jnp.float32)] + [like((samples, first), half)] * 2,
        down_a,
        above_a,
        below_a,
        above_m,
        below_m,
    )
    shares = jnp.maximum(sum_all(shares, "samp"), 1.0)
    above_1 = jnp.concatenate([above_a, above_b], axis=1)
    below_1 = jnp.concatenate([below_a, below_b], axis=1)
    near = cross(own, above_1).reshape(peers, rows, edges[2])
    far = cross(below_1, above_1)
    far = [
        far[edges[k] : edges[k + 1]].reshape(peers, row_edges[k + 1] - row_edges[k], edges[2])
        for k in range(2)
    ]
    one = sum_rows(jnp.concatenate([near] + far, axis=1), "samp")
    near_1 = one[:rows]
    far_1 = from_above(one[rows:] / shares[1:2, :1], "var")
    far = cross(below_1, above_c)
    far = [
        far[edges[k] : edges[k + 1]].reshape(peers, row_edges[k + 1] - row_edges[k], first)
        for k in range(2)
    ]
    last = cross(below_c, jnp.concatenate([above_1, above_c], axis=1))
    last = last.reshape(peers, tail, width)
    last = [last[:, :, k * first : (k + 1) * first] for k in range(quarters)]
    two = sum_rows(jnp.concatenate(far + last, axis=1), "samp")
    far_2 = from_above(two / shares[1:2, :1], "var")
    near_2 = sum_rows(cross(own, above_c).reshape(peers, rows, first), "samp")
    near = jnp.concatenate([near_1, near_2], axis=1) / shares[0:1, :1]
    far_2 = jnp.concatenate(
        [
            jnp.concatenate([far_1, far_2[:split]], axis=1),
            jnp.concatenate(
                [far_2[split + k * tail : split + (k + 1) * tail] for k in range(quarters)],
                axis=1,
            ),
        ],
        axis=0,
    )
    result = jnp.stack([same / jnp.maximum(sums[2:3], 1.0), near, far_2], axis=1)
    keep = jnp.arange(BAND, dtype=jnp.int32) <= band_reach[0]
    return jnp.where(keep[None, :, None], result, jnp.float32(0.0))[None]


def solution(mesh):
    return jax.shard_map(
        per_device,
        mesh=mesh,
        in_specs=(P("samp", ("seg", "var")), P(("seg", "var"), "samp"), P(("seg", "var"))),
        out_specs=P(("seg", "var"), "samp", None, None),
        check_vma=False,
    )
```

time: 103 us -> 114 us (1.11)
  waiting for transfers between devices: 55.8 us -> 32.8 us
  Pallas kernels: 0 us -> 14.8 us
  starting transfers between devices: 26.5 us -> 38 us
  local copies, waits for them, and re-layouts: 0.02 us -> 8.72 us
  other arithmetic: 7.72 us -> 6.49 us
    ppermute x3 -> x4, waiting for transfers between devices: 30.4 us -> 0.01 us  [from_below(): return lax.ppermute(shard, axis, [(i, i + 1) for i in range(peers - 2)])]
    pallas_call x0 -> x4, Pallas kernels: none -> 14.8 us  [local(): pl.pallas_call(kernel, out_shape=tuple((jax.ShapeDtypeStruct(o.shape, o.d...]
    ppermute x4 -> x6, waiting for transfers between devices: 9.16 us -> 21.6 us  [from_above(): return lax.ppermute(shard, axis, [(i, i - 1) for i in range(1, peers)])]
    ppermute x8 -> x12, waiting for transfers between devices: 16.2 us -> 11.1 us  [swap(): return lax.ppermute(shard, axis, [(i, i ^ bit) for i in range(peers)])]
    ppermute x3 -> x4, starting transfers between devices: 15.4 us -> 20 us  [from_below(): return lax.ppermute(shard, axis, [(i, i + 1) for i in range(peers - 2)])]
    ppermute x8 -> x12, starting transfers between devices: 5.92 us -> 10.2 us  [swap(): return lax.ppermute(shard, axis, [(i, i ^ bit) for i in range(peers)])]
    unnamed x4 -> x26, local copies, waits for them, and re-layouts: 0.01 us -> 3.93 us
    ppermute x4 -> x6, starting transfers between devices: 5.15 us -> 7.85 us  [from_above(): return lax.ppermute(shard, axis, [(i, i - 1) for i in range(1, peers)])]
  transfers between devices with their start and end apart: 15 -> 22, of which waited for: 6 -> 9; matrix products, arithmetic and copies ran while one was open for 10% -> 21% of each run, Pallas kernels for 0% -> 10%
where the time goes in v2:
time: 114 us; the launch traced here: 113 us
  starting transfers between devices  38 us (33%)
  waiting for transfers between devices  32.8 us (29%)
  Pallas kernels  14.8 us (13%)
  matrix products  11.5 us (10%)
  local copies, waits for them, and re-layouts  8.72 us (8%)
  other arithmetic  6.49 us (6%)
  between operations  1.15 us (1%)
    ppermute x6, waiting for transfers between devices, from_above(): return lax.ppermute(shard, axis, [(i, i - 1) for i in range(1, peers)])  21.6 us
    ppermute x4, starting transfers between devices, from_below(): return lax.ppermute(shard, axis, [(i, i + 1) for i in range(peers - 2)])  20 us
    pallas_call x4, Pallas kernels, local(): pl.pallas_call(kernel, out_shape=tuple((jax.ShapeDtypeStruct(o.shape, o.d...  14.8 us
    dot_general x6, matrix products, cross(): lax.dot_general(left, right, (((0,), (0,)), ((), ())), preferred_element_...  11.5 us
    ppermute x12, waiting for transfers between devices, swap(): return lax.ppermute(shard, axis, [(i, i ^ bit) for i in range(peers)])  11.1 us
    ppermute x12, starting transfers between devices, swap(): return lax.ppermute(shard, axis, [(i, i ^ bit) for i in range(peers)])  10.2 us
    ppermute x6, starting transfers between devices, from_above(): return lax.ppermute(shard, axis, [(i, i - 1) for i in range(1, peers)])  7.85 us
    unnamed x26, local copies, waits for them, and re-layouts  3.93 us
  transfers between devices with their start and end apart: 22, of which 9 were waited for; matrix products, arithmetic and copies ran while one was open for 21% of the time, Pallas kernels for 10%

profile of v2, /device:TPU:0, one launch (start us, length us, event | category | flops | bytes accessed | tf_op | source)
XLA Modules:
  0.0 113.4 jit_solution(11279003858364536885)
XLA Ops:
  0.0 3.3 %shard_map.56 = f32[8,512]{1,0:T(8,128)} custom-call(bf16[2048,512]{1,0:T(8,128)(2,1)} %dosage_ref.5, s32[1,2048]{1,0:T(1,128)} %observed_ref.3), custom_call_target="tpu_custom_call" | custom-call | flops 4243456 | bytes 2121728 | tf_op jit(solution)/shard_map/pallas_call | solution.py:56
  3.8 3.2 %shard_map.55 = (bf16[2048,128]{1,0:T(8,128)(2,1)}, bf16[2048,128]{1,0:T(8,128)(2,1)}) custom-call(bf16[2048,512]{1,0:T(8,128)(2,1)} %dosage_ref.5, s32[1,2048]{1,0:T(1,128)} %observed_ref.3, s32[1,128]{1,0:T(1,128)} %constant.20.clone.order_ref), custom_call_target="tpu_custom_call" | custom-call | flops 6308864 | bytes 3154432 | tf_op jit(solution)/shard_map/pallas_call | solution.py:56
  7.0 1.3 %collective-permute-start.4 = (bf16[2048,128]{1,0:T(8,128)(2,1)}, bf16[2048,128]{1,0:T(8,128)(2,1)S(1)}, u32[]{:S(2)}, u32[]{:S(2)}) collective-permute-start(bf16[2048,128]{1,0:T(8,128)(2,1)} %get-tuple-element.16.down_ref.own_ref), channel_id=1, source_target_pairs={{1,0},{2,1},{3,2},{5,4},{6,5},{7,6},{9,8},{10,9},{11,10},{13,12},{... | collective-permute-start | bytes 1572872 | tf_op jit(solution)/shard_map/ppermute | solution.py:19
  8.3 6.0 %collective-permute-start.5 = (bf16[2048,128]{1,0:T(8,128)(2,1)}, bf16[2048,128]{1,0:T(8,128)(2,1)}, u32[]{:S(2)}, u32[]{:S(2)}) collective-permute-start(bf16[2048,128]{1,0:T(8,128)(2,1)} %get-tuple-element.18), channel_id=1, source_target_pairs={{0,1},{1,2},{4,5},{5,6},{8,9},{9,10},{12,13},{13,14},{16,17},{17,1... | collective-permute-start | bytes 1572872 | tf_op jit(solution)/shard_map/ppermute | solution.py:24
  14.9 2.0 %collective-permute-start.1 = (f32[8,512]{1,0:T(8,128)S(1)}, f32[8,512]{1,0:T(8,128)S(1)}, u32[]{:S(2)}, u32[]{:S(2)}) collective-permute-start(f32[8,512]{1,0:T(8,128)S(1)} %add.36), channel_id=1, source_target_pairs={{0,8},{4,12},{8,0},{12,4},{1,9},{5,13},{9,1},{13,5},{2,10},{6,14},... | collective-permute-start | bytes 49160 | tf_op jit(solution)/shard_map/ppermute | solution.py:29
  16.9 1.8 %collective-permute-done.1 = f32[8,512]{1,0:T(8,128)S(1)} collective-permute-done((f32[8,512]{1,0:T(8,128)S(1)}, f32[8,512]{1,0:T(8,128)S(1)}, u32[]{:S(2)}, u32[]{:S(2)}) %collective-permute-start.1) | collective-permute-done | bytes 16416 | tf_op jit(solution)/shard_map/ppermute | solution.py:29
  19.3 5.5 %shard_map.57 = (f32[8,512]{1,0:T(8,128)}, bf16[2048,512]{1,0:T(8,128)(2,1)}, bf16[2048,256]{1,0:T(8,128)(2,1)}, bf16[2048,128]{1,0:T(8,128)(2,1)}, bf16[2048,25...) custom-call(bf16[2048,512]{1,0:T(8,128)(2,1)} %dosage_ref.5, bf16[2048,128]{1,0:T(8,128)(2,1)} %get-tuple-element.16.down_ref.own_ref, ...), custom_call_target="tpu_custom_call" | custom-call | flops 15797248 | bytes 7898624 | tf_op jit(solution)/shard_map/pallas_call | solution.py:56
  25.5 1.3 %collective-permute-start.6 = (f32[8,128]{1,0:T(8,128)S(1)}, f32[8,128]{1,0:T(8,128)S(1)}, u32[]{:S(2)}, u32[]{:S(2)}) collective-permute-start(f32[8,128]{1,0:T(8,128)S(1)} %slice.132), channel_id=1, source_target_pairs={{1,0},{2,1},{3,2},{5,4},{6,5},{7,6},{9,8},{10,9},{11,10},{13,12},{... | collective-permute-start | bytes 12296 | tf_op jit(solution)/shard_map/ppermute | solution.py:19
  27.6 4.5 %collective-permute-start.7 = (f32[8,128]{1,0:T(8,128)S(1)}, f32[8,128]{1,0:T(8,128)S(1)}, u32[]{:S(2)}, u32[]{:S(2)}) collective-permute-start(f32[8,128]{1,0:T(8,128)S(1)} %reshape.378), channel_id=1, source_target_pairs={{0,1},{1,2},{4,5},{5,6},{8,9},{9,10},{12,13},{13,14},{16,17},{17,1... | collective-permute-start | bytes 12296 | tf_op jit(solution)/shard_map/ppermute | solution.py:24
  32.2 4.1 %collective-permute-start.9 = (bf16[2048,256]{1,0:T(8,128)(2,1)}, bf16[2048,256]{1,0:T(8,128)(2,1)}, u32[]{:S(2)}, u32[]{:S(2)}) collective-permute-start(bf16[2048,256]{1,0:T(8,128)(2,1)} %get-tuple-element.23), channel_id=1, source_target_pairs={{0,1},{1,2},{4,5},{5,6},{8,9},{9,10},{12,13},{13,14},{16,17},{17,1... | collective-permute-start | bytes 3145736 | tf_op jit(solution)/shard_map/ppermute | solution.py:24
  36.3 3.5 %fusion.20 = f32[512,512]{1,0:T(8,128)S(1)} fusion(bf16[2048,512]{1,0:T(8,128)(2,1)} %get-tuple-element.17), kind=kOutput, calls=%fused_computation.64 | convolution fusion | flops 1073741824 | bytes 3145728 | tf_op jit(solution)/shard_map/dot_general | solution.py:165
  41.4 1.3 %collective-permute-start.12 = (bf16[2048,128]{1,0:T(8,128)(2,1)}, bf16[2048,128]{1,0:T(8,128)(2,1)}, u32[]{:S(2)}, u32[]{:S(2)}) collective-permute-start(bf16[2048,128]{1,0:T(8,128)(2,1)} %get-tuple-element.24), channel_id=1, source_target_pairs={{1,0},{2,1},{3,2},{5,4},{6,5},{7,6},{9,8},{10,9},{11,10},{13,12},{... | collective-permute-start | bytes 1572872 | tf_op jit(solution)/shard_map/ppermute | solution.py:19
  42.7 5.4 %collective-permute-start.18 = (bf16[2048,128]{1,0:T(8,128)(2,1)}, bf16[2048,128]{1,0:T(8,128)(2,1)}, u32[]{:S(2)}, u32[]{:S(2)}) collective-permute-start(bf16[2048,128]{1,0:T(8,128)(2,1)} %get-tuple-element.26), channel_id=1, source_target_pairs={{0,1},{1,2},{4,5},{5,6},{8,9},{9,10},{12,13},{13,14},{16,17},{17,1... | collective-permute-start | bytes 1572872 | tf_op jit(solution)/shard_map/ppermute | solution.py:24
  48.9 1.4 %collective-permute-start.8 = (bf16[2048,256]{1,0:T(8,128)(2,1)}, bf16[2048,256]{1,0:T(8,128)(2,1)}, u32[]{:S(2)}, u32[]{:S(2)}) collective-permute-start(bf16[2048,256]{1,0:T(8,128)(2,1)} %get-tuple-element.21), channel_id=1, source_target_pairs={{1,0},{2,1},{3,2},{5,4},{6,5},{7,6},{9,8},{10,9},{11,10},{13,12},{... | collective-permute-start | bytes 3145736 | tf_op jit(solution)/shard_map/ppermute | solution.py:19
  50.4 2.8 %shard_map.58 = (f32[8,128]{1,0:T(8,128)}, bf16[2048,128]{1,0:T(8,128)(2,1)}, bf16[2048,128]{1,0:T(8,128)(2,1)}) custom-call(bf16[2048,128]{1,0:T(8,128)(2,1)} %get-tuple-element.16.down_ref.own_ref, bf16[2048,128]{1,0:T(8,128)(2,1)} %copy-done.3, bf16[2048,128]{1,0:T(8,128)(2,1)} %collective-permute-done.5.below_ref, f32[8,128]{1,0:T(8,128)} %copy-done.7, ...), custom_call_target="tpu_custom_call" | custom-call | flops 5267456 | bytes 2633728 | tf_op jit(solution)/shard_map/pallas_call | solution.py:56
  55.2 1.5 %collective-permute-start.16 = (f32[8,128]{1,0:T(8,128)S(1)}, f32[8,128]{1,0:T(8,128)S(1)}, u32[]{:S(2)}, u32[]{:S(2)}) collective-permute-start(f32[8,128]{1,0:T(8,128)S(1)} %add.44), channel_id=1, source_target_pairs={{0,8},{4,12},{8,0},{12,4},{1,9},{5,13},{9,1},{13,5},{2,10},{6,14},... | collective-permute-start | bytes 12296 | tf_op jit(solution)/shard_map/ppermute | solution.py:29
  59.4 1.8 %fusion.23 = f32[512,128]{1,0:T(8,128)S(1)} fusion(bf16[2048,512]{1,0:T(8,128)(2,1)S(1)} %copy-done, bf16[2048,128]{1,0:T(8,128)(2,1)} %collective-permute-done.12), kind=kOutput, calls=%fused_computation.67 | convolution fusion | flops 268435456 | bytes 2883584 | tf_op jit(solution)/shard_map/dot_general | solution.py:165
  61.9 1.6 %collective-permute-start.3 = (f32[1,128,512]{2,1,0:T(8,128)S(1)}, f32[1,128,512]{2,1,0:T(8,128)S(1)}, u32[]{:S(2)}, u32[]{:S(2)}) collective-permute-start(f32[1,128,512]{2,1,0:T(8,128)S(1)} %select_bitcast_fusion.3), channel_id=1, source_target_pairs={{0,8},{4,12},{8,0},{12,4},{1,9},{5,13},{9,1},{13,5},{2,10},{6,14},... | collective-permute-start | bytes 786440 | tf_op jit(solution)/shard_map/ppermute | solution.py:29
  64.4 1.3 %constant_dynamic-update-slice_fusion.2 = bf16[2048,384]{1,0:T(8,128)(2,1)S(1)} fusion(bf16[2048,384]{1,0:T(8,128)(2,1)S(1)} %constant_dynamic-update-slice_fusion.3, bf16[2048,256]{1,0:T(8,128)(2,1)} %collective-permute-done.9), kind=kLoop, calls=%fused_computation.49 | loop fusion | bytes 2097152 | tf_op jit(solution)/shard_map/concatenate | solution.py:224
  65.6 12.6 %collective-permute-done.8 = bf16[2048,256]{1,0:T(8,128)(2,1)} collective-permute-done((bf16[2048,256]{1,0:T(8,128)(2,1)}, bf16[2048,256]{1,0:T(8,128)(2,1)}, u32[]{:S(2)}, u32[]{:S(2)}) %collective-permute-start.8) | collective-permute-done | bytes 1048608 | tf_op jit(solution)/shard_map/ppermute | solution.py:19
  78.2 1.3 %constant_dynamic-update-slice_fusion = bf16[2048,384]{1,0:T(8,128)(2,1)S(1)} fusion(bf16[2048,384]{1,0:T(8,128)(2,1)S(1)} %constant_dynamic-update-slice_fusion.1, bf16[2048,256]{1,0:T(8,128)(2,1)} %collective-permute-done.8), kind=kLoop, calls=%fused_computation.47 | loop fusion | bytes 2097152 | tf_op jit(solution)/shard_map/concatenate | solution.py:223
  80.5 1.9 %fusion.24 = f32[384,128]{1,0:T(8,128)S(1)} fusion(bf16[2048,384]{1,0:T(8,128)(2,1)S(1)} %constant_dynamic-update-slice_fusion.2, bf16[2048,128]{1,0:T(8,128)(2,1)} %collective-permute-done.12), kind=kOutput, calls=%fused_computation.68 | convolution fusion | flops 201326592 | bytes 2293760 | tf_op jit(solution)/shard_map/dot_general | solution.py:165
  82.5 1.3 %fusion.21 = f32[512,384]{1,0:T(8,128)S(1)} fusion(bf16[2048,512]{1,0:T(8,128)(2,1)S(1)} %copy-done, bf16[2048,384]{1,0:T(8,128)(2,1)S(1)} %constant_dynamic-update-slice_fusion), kind=kOutput, calls=%fused_computation.65 | convolution fusion | flops 805306368 | bytes 4456448 | tf_op jit(solution)/shard_map/dot_general | solution.py:165
  83.8 2.1 %fusion = f32[128,512]{1,0:T(8,128)S(1)} fusion(bf16[2048,128]{1,0:T(8,128)(2,1)} %collective-permute-done.18, bf16[2048,128]{1,0:T(8,128)(2,1)} %collective-permute-done.12, bf16[2048,256]{1,0:T(8,128)(2,1)} %collective-permute-done.8, bf16[2048,128]{1,0:T(8,128)(2,1)S(1)} %copy-done.4), kind=kOutput, calls=%fused_computation | convolution fusion | flops 274726912 | bytes 2883584 | tf_op jit(solution)/shard_map/dot_general | solution.py:165
  87.6 1.5 %collective-permute-start.20 = (f32[1,224,128]{2,1,0:T(8,128)S(1)}, f32[1,224,128]{2,1,0:T(8,128)S(1)}, u32[]{:S(2)}, u32[]{:S(2)}) collective-permute-start(f32[1,224,128]{2,1,0:T(8,128)S(1)} %select_bitcast_fusion.6), channel_id=1, source_target_pairs={{0,8},{4,12},{8,0},{12,4},{1,9},{5,13},{9,1},{13,5},{2,10},{6,14},... | collective-permute-start | bytes 344072 | tf_op jit(solution)/shard_map/ppermute | solution.py:29
  89.2 3.7 %collective-permute-done.20 = f32[1,224,128]{2,1,0:T(8,128)S(1)} collective-permute-done((f32[1,224,128]{2,1,0:T(8,128)S(1)}, f32[1,224,128]{2,1,0:T(8,128)S(1)}, u32[]{:S(2)}, u32[]{:S(2)}) %collective-permute-start.20) | collective-permute-done | bytes 114720 | tf_op jit(solution)/shard_map/ppermute | solution.py:29
  93.5 1.3 %collective-permute-start.21 = (f32[224,128]{1,0:T(8,128)S(1)}, f32[224,128]{1,0:T(8,128)S(1)}, u32[]{:S(2)}, u32[]{:S(2)}) collective-permute-start(f32[224,128]{1,0:T(8,128)S(1)} %fusion.14), channel_id=1, source_target_pairs={{1,0},{2,1},{3,2},{5,4},{6,5},{7,6},{9,8},{10,9},{11,10},{13,12},{... | collective-permute-start | bytes 344072 | tf_op jit(solution)/shard_map/ppermute | solution.py:19
  94.9 1.5 %collective-permute-start.11 = (f32[1,224,384]{2,1,0:T(8,128)S(1)}, f32[1,224,384]{2,1,0:T(8,128)S(1)}, u32[]{:S(2)}, u32[]{:S(2)}) collective-permute-start(f32[1,224,384]{2,1,0:T(8,128)S(1)} %select_bitcast_fusion.2), channel_id=1, source_target_pairs={{0,8},{4,12},{8,0},{12,4},{1,9},{5,13},{9,1},{13,5},{2,10},{6,14},... | collective-permute-start | bytes 1032200 | tf_op jit(solution)/shard_map/ppermute | solution.py:29
  96.6 3.6 %collective-permute-done.21 = f32[224,128]{1,0:T(8,128)S(1)} collective-permute-done((f32[224,128]{1,0:T(8,128)S(1)}, f32[224,128]{1,0:T(8,128)S(1)}, u32[]{:S(2)}, u32[]{:S(2)}) %collective-permute-start.21) | collective-permute-done | bytes 114720 | tf_op jit(solution)/shard_map/ppermute | solution.py:19
  100.2 4.1 %collective-permute-done.11 = f32[1,224,384]{2,1,0:T(8,128)S(1)} collective-permute-done((f32[1,224,384]{2,1,0:T(8,128)S(1)}, f32[1,224,384]{2,1,0:T(8,128)S(1)}, u32[]{:S(2)}, u32[]{:S(2)}) %collective-permute-start.11) | collective-permute-done | bytes 344096 | tf_op jit(solution)/shard_map/ppermute | solution.py:29
  104.9 1.3 %collective-permute-start.17 = (f32[96,384]{1,0:T(8,128)S(1)}, f32[96,384]{1,0:T(8,128)S(1)}, u32[]{:S(2)}, u32[]{:S(2)}) collective-permute-start(f32[96,384]{1,0:T(8,128)S(1)} %fusion.11), channel_id=1, source_target_pairs={{1,0},{2,1},{3,2},{5,4},{6,5},{7,6},{9,8},{10,9},{11,10},{13,12},{... | collective-permute-start | bytes 442376 | tf_op jit(solution)/shard_map/ppermute | solution.py:19
  106.9 5.4 %collective-permute-done.17 = f32[96,384]{1,0:T(8,128)S(1)} collective-permute-done((f32[96,384]{1,0:T(8,128)S(1)}, f32[96,384]{1,0:T(8,128)S(1)}, u32[]{:S(2)}, u32[]{:S(2)}) %collective-permute-start.17) | collective-permute-done | bytes 147488 | tf_op jit(solution)/shard_map/ppermute | solution.py:19
  (92 shorter events, 17.2 us)
Async XLA Ops:
  3.3 11.6 %copy-start.6 = (f32[8,512]{1,0:T(8,128)S(1)}, f32[8,512]{1,0:T(8,128)}, u32[]{:S(2)}) copy-start(f32[8,512]{1,0:T(8,128)} %shard_map.56) | copy-start | bytes 49156
  3.3 11.6 %collective-permute-start = (f32[8,512]{1,0:T(8,128)}, f32[8,512]{1,0:T(8,128)S(1)}, u32[]{:S(2)}, u32[]{:S(2)}) collective-permute-start(f32[8,512]{1,0:T(8,128)} %shard_map.56), channel_id=1, source_target_pairs={{0,4},{4,0},{8,12},{12,8},{1,5},{5,1},{9,13},{13,9},{2,6},{6,2},{1... | collective-permute-start | bytes 49160 | tf_op jit(solution)/shard_map/ppermute | solution.py:29
  7.0 41.1 %collective-permute-start.4 = (bf16[2048,128]{1,0:T(8,128)(2,1)}, bf16[2048,128]{1,0:T(8,128)(2,1)S(1)}, u32[]{:S(2)}, u32[]{:S(2)}) collective-permute-start(bf16[2048,128]{1,0:T(8,128)(2,1)} %get-tuple-element.16.down_ref.own_ref), channel_id=1, source_target_pairs={{1,0},{2,1},{3,2},{5,4},{6,5},{7,6},{9,8},{10,9},{11,10},{13,12},{... | collective-permute-start | bytes 1572872 | tf_op jit(solution)/shard_map/ppermute | solution.py:19
  8.3 42.1 %collective-permute-start.5 = (bf16[2048,128]{1,0:T(8,128)(2,1)}, bf16[2048,128]{1,0:T(8,128)(2,1)}, u32[]{:S(2)}, u32[]{:S(2)}) collective-permute-start(bf16[2048,128]{1,0:T(8,128)(2,1)} %get-tuple-element.18), channel_id=1, source_target_pairs={{0,1},{1,2},{4,5},{5,6},{8,9},{9,10},{12,13},{13,14},{16,17},{17,1... | collective-permute-start | bytes 1572872 | tf_op jit(solution)/shard_map/ppermute | solution.py:24
  14.9 3.8 %collective-permute-start.1 = (f32[8,512]{1,0:T(8,128)S(1)}, f32[8,512]{1,0:T(8,128)S(1)}, u32[]{:S(2)}, u32[]{:S(2)}) collective-permute-start(f32[8,512]{1,0:T(8,128)S(1)} %add.36), channel_id=1, source_target_pairs={{0,8},{4,12},{8,0},{12,4},{1,9},{5,13},{9,1},{13,5},{2,10},{6,14},... | collective-permute-start | bytes 49160 | tf_op jit(solution)/shard_map/ppermute | solution.py:29
  25.5 15.8 %collective-permute-start.6 = (f32[8,128]{1,0:T(8,128)S(1)}, f32[8,128]{1,0:T(8,128)S(1)}, u32[]{:S(2)}, u32[]{:S(2)}) collective-permute-start(f32[8,128]{1,0:T(8,128)S(1)} %slice.132), channel_id=1, source_target_pairs={{1,0},{2,1},{3,2},{5,4},{6,5},{7,6},{9,8},{10,9},{11,10},{13,12},{... | collective-permute-start | bytes 12296 | tf_op jit(solution)/shard_map/ppermute | solution.py:19
  27.6 15.0 %collective-permute-start.7 = (f32[8,128]{1,0:T(8,128)S(1)}, f32[8,128]{1,0:T(8,128)S(1)}, u32[]{:S(2)}, u32[]{:S(2)}) collective-permute-start(f32[8,128]{1,0:T(8,128)S(1)} %reshape.378), channel_id=1, source_target_pairs={{0,1},{1,2},{4,5},{5,6},{8,9},{9,10},{12,13},{13,14},{16,17},{17,1... | collective-permute-start | bytes 12296 | tf_op jit(solution)/shard_map/ppermute | solution.py:24
  32.2 32.2 %collective-permute-start.9 = (bf16[2048,256]{1,0:T(8,128)(2,1)}, bf16[2048,256]{1,0:T(8,128)(2,1)}, u32[]{:S(2)}, u32[]{:S(2)}) collective-permute-start(bf16[2048,256]{1,0:T(8,128)(2,1)} %get-tuple-element.23), channel_id=1, source_target_pairs={{0,1},{1,2},{4,5},{5,6},{8,9},{9,10},{12,13},{13,14},{16,17},{17,1... | collective-permute-start | bytes 3145736 | tf_op jit(solution)/shard_map/ppermute | solution.py:24
  41.4 9.0 %copy-start.7 = (f32[8,128]{1,0:T(8,128)}, f32[8,128]{1,0:T(8,128)S(1)}, u32[]{:S(2)}) copy-start(f32[8,128]{1,0:T(8,128)S(1)} %collective-permute-done.6.above_m_ref) | copy-start | bytes 12292
  41.4 18.0 %collective-permute-start.12 = (bf16[2048,128]{1,0:T(8,128)(2,1)}, bf16[2048,128]{1,0:T(8,128)(2,1)}, u32[]{:S(2)}, u32[]{:S(2)}) collective-permute-start(bf16[2048,128]{1,0:T(8,128)(2,1)} %get-tuple-element.24), channel_id=1, source_target_pairs={{1,0},{2,1},{3,2},{5,4},{6,5},{7,6},{9,8},{10,9},{11,10},{13,12},{... | collective-permute-start | bytes 1572872 | tf_op jit(solution)/shard_map/ppermute | solution.py:19
  42.7 7.7 %copy-start.8 = (f32[8,128]{1,0:T(8,128)}, f32[8,128]{1,0:T(8,128)S(1)}, u32[]{:S(2)}) copy-start(f32[8,128]{1,0:T(8,128)S(1)} %collective-permute-done.7.below_m_ref) | copy-start | bytes 12292
  42.7 41.1 %collective-permute-start.18 = (bf16[2048,128]{1,0:T(8,128)(2,1)}, bf16[2048,128]{1,0:T(8,128)(2,1)}, u32[]{:S(2)}, u32[]{:S(2)}) collective-permute-start(bf16[2048,128]{1,0:T(8,128)(2,1)} %get-tuple-element.26), channel_id=1, source_target_pairs={{0,1},{1,2},{4,5},{5,6},{8,9},{9,10},{12,13},{13,14},{16,17},{17,1... | collective-permute-start | bytes 1572872 | tf_op jit(solution)/shard_map/ppermute | solution.py:24
  48.9 10.5 %copy-start = (bf16[2048,512]{1,0:T(8,128)(2,1)S(1)}, bf16[2048,512]{1,0:T(8,128)(2,1)}, u32[]{:S(2)}) copy-start(bf16[2048,512]{1,0:T(8,128)(2,1)} %get-tuple-element.17) | copy-start | bytes 6291460
  48.9 29.3 %collective-permute-start.8 = (bf16[2048,256]{1,0:T(8,128)(2,1)}, bf16[2048,256]{1,0:T(8,128)(2,1)}, u32[]{:S(2)}, u32[]{:S(2)}) collective-permute-start(bf16[2048,256]{1,0:T(8,128)(2,1)} %get-tuple-element.21), channel_id=1, source_target_pairs={{1,0},{2,1},{3,2},{5,4},{6,5},{7,6},{9,8},{10,9},{11,10},{13,12},{... | collective-permute-start | bytes 3145736 | tf_op jit(solution)/shard_map/ppermute | solution.py:19
  53.1 5.7 %copy-start.5 = (f32[2,128,512]{2,1,0:T(8,128)S(1)}, f32[2,128,512]{2,1,0:T(8,128)}, u32[]{:S(2)}) copy-start(f32[2,128,512]{2,1,0:T(8,128)} %select_bitcast_fusion.1) | copy-start | bytes 1572868
  53.1 1.4 %collective-permute-start.15 = (f32[8,128]{1,0:T(8,128)}, f32[8,128]{1,0:T(8,128)S(1)}, u32[]{:S(2)}, u32[]{:S(2)}) collective-permute-start(f32[8,128]{1,0:T(8,128)} %get-tuple-element.25), channel_id=1, source_target_pairs={{0,4},{4,0},{8,12},{12,8},{1,5},{5,1},{9,13},{13,9},{2,6},{6,2},{1... | collective-permute-start | bytes 12296 | tf_op jit(solution)/shard_map/ppermute | solution.py:29
  55.2 3.6 %collective-permute-start.16 = (f32[8,128]{1,0:T(8,128)S(1)}, f32[8,128]{1,0:T(8,128)S(1)}, u32[]{:S(2)}, u32[]{:S(2)}) collective-permute-start(f32[8,128]{1,0:T(8,128)S(1)} %add.44), channel_id=1, source_target_pairs={{0,8},{4,12},{8,0},{12,4},{1,9},{5,13},{9,1},{13,5},{2,10},{6,14},... | collective-permute-start | bytes 12296 | tf_op jit(solution)/shard_map/ppermute | solution.py:29
  58.8 3.0 %collective-permute-start.2 = (f32[2,128,512]{2,1,0:T(8,128)S(1)}, f32[2,128,512]{2,1,0:T(8,128)S(1)}, u32[]{:S(2)}, u32[]{:S(2)}) collective-permute-start(f32[2,128,512]{2,1,0:T(8,128)S(1)} %copy-done.5), channel_id=1, source_target_pairs={{0,4},{4,0},{8,12},{12,8},{1,5},{5,1},{9,13},{13,9},{2,6},{6,2},{1... | collective-permute-start | bytes 1572872 | tf_op jit(solution)/shard_map/ppermute | solution.py:29
  61.2 2.3 %collective-permute-start.13 = (f32[2,128,128]{2,1,0:T(8,128)S(1)}, f32[2,128,128]{2,1,0:T(8,128)S(1)}, u32[]{:S(2)}, u32[]{:S(2)}) collective-permute-start(f32[2,128,128]{2,1,0:T(8,128)S(1)} %select_bitcast_fusion.5), channel_id=1, source_target_pairs={{0,4},{4,0},{8,12},{12,8},{1,5},{5,1},{9,13},{13,9},{2,6},{6,2},{1... | collective-permute-start | bytes 393224 | tf_op jit(solution)/shard_map/ppermute | solution.py:29
  61.9 34.5 %collective-permute-start.3 = (f32[1,128,512]{2,1,0:T(8,128)S(1)}, f32[1,128,512]{2,1,0:T(8,128)S(1)}, u32[]{:S(2)}, u32[]{:S(2)}) collective-permute-start(f32[1,128,512]{2,1,0:T(8,128)S(1)} %select_bitcast_fusion.3), channel_id=1, source_target_pairs={{0,8},{4,12},{8,0},{12,4},{1,9},{5,13},{9,1},{13,5},{2,10},{6,14},... | collective-permute-start | bytes 786440 | tf_op jit(solution)/shard_map/ppermute | solution.py:29
  63.6 25.6 %collective-permute-start.14 = (f32[1,128,128]{2,1,0:T(8,128)S(1)}, f32[1,128,128]{2,1,0:T(8,128)S(1)}, u32[]{:S(2)}, u32[]{:S(2)}) collective-permute-start(f32[1,128,128]{2,1,0:T(8,128)S(1)} %select_bitcast_fusion.7), channel_id=1, source_target_pairs={{0,8},{4,12},{8,0},{12,4},{1,9},{5,13},{9,1},{13,5},{2,10},{6,14},... | collective-permute-start | bytes 196616 | tf_op jit(solution)/shard_map/ppermute | solution.py:29
  80.5 1.9 %copy-start.1 = (f32[384,384]{1,0:T(8,128)}, f32[384,384]{1,0:T(8,128)S(1)}, u32[]{:S(2)}) copy-start(f32[384,384]{1,0:T(8,128)S(1)} %fusion.22) | copy-start | bytes 1769476
  82.4 1.3 %copy-start.2 = (f32[384,128]{1,0:T(8,128)}, f32[384,128]{1,0:T(8,128)S(1)}, u32[]{:S(2)}) copy-start(f32[384,128]{1,0:T(8,128)S(1)} %fusion.24) | copy-start | bytes 589828
  82.4 1.3 %copy-start.4 = (bf16[2048,128]{1,0:T(8,128)(2,1)S(1)}, bf16[2048,128]{1,0:T(8,128)(2,1)}, u32[]{:S(2)}) copy-start(bf16[2048,128]{1,0:T(8,128)(2,1)} %get-tuple-element.20) | copy-start | bytes 1572868
  83.8 2.1 %slice-start.2 = ((f32[384,128]{1,0:T(8,128)}), f32[256,128]{1,0:T(8,128)S(1)}, s32[]{:S(2)}) async-start(f32[384,128]{1,0:T(8,128)} %copy-done.2), calls=%async_computation.2 | async-start | bytes 262144 | tf_op jit(solution)/shard_map/slice | solution.py:236
  85.9 1.0 slice-start.1
  86.0 1.6 %collective-permute-start.19 = (f32[2,224,128]{2,1,0:T(8,128)S(1)}, f32[2,224,128]{2,1,0:T(8,128)S(1)}, u32[]{:S(2)}, u32[]{:S(2)}) collective-permute-start(f32[2,224,128]{2,1,0:T(8,128)S(1)} %select_bitcast_fusion.4), channel_id=1, source_target_pairs={{0,4},{4,0},{8,12},{12,8},{1,5},{5,1},{9,13},{13,9},{2,6},{6,2},{1... | collective-permute-start | bytes 688136 | tf_op jit(solution)/shard_map/ppermute | solution.py:29
  87.1 7.7 %collective-permute-start.10 = (f32[2,224,384]{2,1,0:T(8,128)S(1)}, f32[2,224,384]{2,1,0:T(8,128)S(1)}, u32[]{:S(2)}, u32[]{:S(2)}) collective-permute-start(f32[2,224,384]{2,1,0:T(8,128)S(1)} %select_bitcast_fusion), channel_id=1, source_target_pairs={{0,4},{4,0},{8,12},{12,8},{1,5},{5,1},{9,13},{13,9},{2,6},{6,2},{1... | collective-permute-start | bytes 2064392 | tf_op jit(solution)/shard_map/ppermute | solution.py:29
  87.6 5.3 %collective-permute-start.20 = (f32[1,224,128]{2,1,0:T(8,128)S(1)}, f32[1,224,128]{2,1,0:T(8,128)S(1)}, u32[]{:S(2)}, u32[]{:S(2)}) collective-permute-start(f32[1,224,128]{2,1,0:T(8,128)S(1)} %select_bitcast_fusion.6), channel_id=1, source_target_pairs={{0,8},{4,12},{8,0},{12,4},{1,9},{5,13},{9,1},{13,5},{2,10},{6,14},... | collective-permute-start | bytes 344072 | tf_op jit(solution)/shard_map/ppermute | solution.py:29
  93.5 6.7 %collective-permute-start.21 = (f32[224,128]{1,0:T(8,128)S(1)}, f32[224,128]{1,0:T(8,128)S(1)}, u32[]{:S(2)}, u32[]{:S(2)}) collective-permute-start(f32[224,128]{1,0:T(8,128)S(1)} %fusion.14), channel_id=1, source_target_pairs={{1,0},{2,1},{3,2},{5,4},{6,5},{7,6},{9,8},{10,9},{11,10},{13,12},{... | collective-permute-start | bytes 344072 | tf_op jit(solution)/shard_map/ppermute | solution.py:19
  94.9 9.3 %collective-permute-start.11 = (f32[1,224,384]{2,1,0:T(8,128)S(1)}, f32[1,224,384]{2,1,0:T(8,128)S(1)}, u32[]{:S(2)}, u32[]{:S(2)}) collective-permute-start(f32[1,224,384]{2,1,0:T(8,128)S(1)} %select_bitcast_fusion.2), channel_id=1, source_target_pairs={{0,8},{4,12},{8,0},{12,4},{1,9},{5,13},{9,1},{13,5},{2,10},{6,14},... | collective-permute-start | bytes 1032200 | tf_op jit(solution)/shard_map/ppermute | solution.py:29
  104.9 7.4 %collective-permute-start.17 = (f32[96,384]{1,0:T(8,128)S(1)}, f32[96,384]{1,0:T(8,128)S(1)}, u32[]{:S(2)}, u32[]{:S(2)}) collective-permute-start(f32[96,384]{1,0:T(8,128)S(1)} %fusion.11), channel_id=1, source_target_pairs={{1,0},{2,1},{3,2},{5,4},{6,5},{7,6},{9,8},{10,9},{11,10},{13,12},{... | collective-permute-start | bytes 442376 | tf_op jit(solution)/shard_map/ppermute | solution.py:19
  (2 other events, 1.8 us)

commit v3 on v1

v3 whole, which is shorter than its diff:
```python
import jax
import jax.numpy as jnp
import numpy as np
from jax import lax
from jax.experimental import pallas as pl
from jax.sharding import PartitionSpec as P

BAND = 3


EPSILON = 1e-05

HOLE = float("nan")


def from_above(shard, axis):
    peers = lax.axis_size(axis)
    return lax.ppermute(shard, axis, [(i, i - 1) for i in range(1, peers)])


def from_below(shard, axis):
    peers = lax.axis_size(axis)
    return lax.ppermute(shard, axis, [(i, i + 1) for i in range(peers - 2)])


def swap(shard, axis, bit):
    peers = lax.axis_size(axis)
    return lax.ppermute(shard, axis, [(i, i ^ bit) for i in range(peers)])


def bits_of(peers):
    return [1 << k for k in range(peers.bit_length() - 1)]


def sum_all(value, axis):
    for bit in bits_of(lax.axis_size(axis)):
        value = value + swap(value, axis, bit)
    return value


def sum_rows(partial, axis):
    place = lax.axis_index(axis)
    for bit in bits_of(lax.axis_size(axis)):
        pairs = partial.reshape(partial.shape[0] // 2, 2, *partial.shape[1:])
        high = (place & bit) != 0
        keep = jnp.where(high, pairs[:, 1], pairs[:, 0])
        give = jnp.where(high, pairs[:, 0], pairs[:, 1])
        partial = keep + swap(give, axis, bit)
    return partial[0]


def like(shape, dtype):
    return jax.ShapeDtypeStruct(shape, dtype)


def head_kernel(dosage_ref, observed_ref, order_ref, down_1, down_2, up_1, up_2, sums_ref):
    samples, width = dosage_ref.shape
    lanes = 128

    @pl.when(pl.program_id(0) == 0)
    def _():
        sums_ref[...] = jnp.zeros_like(sums_ref)

    flags = observed_ref[...].astype(jnp.float32)
    present = jnp.transpose(jnp.broadcast_to(flags, (lanes, samples))) > 0.5
    count = jnp.sum(jnp.where(present, 1.0, 0.0), axis=0, keepdims=True)
    chosen = lax.broadcasted_iota(jnp.int32, (width, width), 0) == order_ref[...]
    up = jnp.dot(
        dosage_ref[...],
        jnp.where(chosen, 1.0, 0.0).astype(jnp.bfloat16),
        preferred_element_type=jnp.float32,
    )
    edge = down_1.shape[1]
    for low in range(0, width, lanes):
        part = slice(low, low + lanes)
        down = dosage_ref[:, part].astype(jnp.float32)
        kept = jnp.where(present, down, 0.0)
        sums_ref[0:1, part] += jnp.sum(kept, axis=0, keepdims=True)
        sums_ref[1:2, part] += jnp.sum(kept * kept, axis=0, keepdims=True)
        sums_ref[2:3, part] += count
        down = jnp.where(present, down, HOLE).astype(jnp.bfloat16)
        coded = jnp.where(present, up[:, part], HOLE).astype(jnp.bfloat16)
        if low < edge:
            down_1[:, part] = down
            up_1[:, part] = coded
        else:
            down_2[:, low - edge : low - edge + lanes] = down
            up_2[:, low - edge : low - edge + lanes] = coded


def head(dosage, observed, order, edge):
    samples, width = dosage.shape
    block = 256 if samples % 256 == 0 else samples
    cuts = [edge, width - edge] * 2
    return pl.pallas_call(
        head_kernel,
        grid=(samples // block,),
        out_shape=tuple(like((samples, cut), jnp.bfloat16) for cut in cuts)
        + (like((8, width), jnp.float32),),
        in_specs=[
            pl.BlockSpec((block, width), lambda i: (i, 0)),
            pl.BlockSpec((1, block), lambda i: (0, i)),
            pl.BlockSpec((1, width), lambda i: (0, 0)),
        ],
        out_specs=tuple(pl.BlockSpec((block, cut), lambda i: (i, 0)) for cut in cuts)
        + (pl.BlockSpec((8, width), lambda i: (0, 0)),),
        name="head",
    )(dosage, observed, order)


def finish_moments(sums):
    centre = sums[0:1] / sums[2:3]
    spread_inverse = 1.0 / jnp.sqrt(sums[1:2] / sums[2:3] - centre * centre + EPSILON)
    return jnp.concatenate([centre, spread_inverse], axis=0)


def standardize(values, present, moments):
    spread = (values.astype(jnp.float32) - moments[0:1]) * moments[1:2]
    return lax.optimization_barrier(jnp.where(present, spread, 0.0).astype(jnp.bfloat16))


def cross(left, right):
    return lax.dot_general(
        left, right, (((0,), (0,)), ((), ())), preferred_element_type=jnp.float32
    )


def per_device(dosage, observed, band_reach):
    _, width = dosage.shape
    peers = lax.axis_size("samp")
    rows = width // peers
    kept = 3 * rows // 4
    tail = rows - kept
    edge, rest = kept * peers, tail * peers
    owners = np.arange(peers)[:, None] * rows
    order = np.concatenate(
        [
            (owners + np.arange(0, kept)[None, :]).ravel(),
            (owners + np.arange(kept, rows)[None, :]).ravel(),
        ]
    ).astype(np.int32)[None, :]
    pieces = width // rest
    down_1, down_2, up_1, up_2, sums = head(dosage, observed, jnp.asarray(order), edge)
    above_1 = from_above(down_1, "var")
    below_1 = from_below(up_1, "var")
    sums = sum_all(sums, "samp")
    moments = finish_moments(sums)
    above_m = from_above(moments, "var")
    below_m = from_below(moments, "var")
    above_2 = from_above(down_2, "var")
    below_2 = from_below(up_2, "var")
    own = standardize(dosage, (observed[0] != 0)[:, None], moments)
    same = sum_rows(cross(own, own).reshape(peers, rows, width), "samp")
    below_m = below_m.reshape(2, peers, rows)
    below_m1 = below_m[:, :, :kept].reshape(2, edge)
    below_m2 = below_m[:, :, kept:].reshape(2, rest)
    own_present = jnp.logical_not(jnp.isnan(down_1))
    above_present = jnp.logical_not(jnp.isnan(above_1))
    below_present = jnp.logical_not(jnp.isnan(below_1))
    above_1 = standardize(above_1, above_present, above_m[:, :edge])
    below_1 = standardize(below_1, below_present, below_m1)
    shares = [
        jnp.sum(jnp.where(other & above_present, 1.0, 0.0), axis=0, keepdims=True)
        for other in (own_present, below_present)
    ]
    shares = jnp.concatenate(shares + [jnp.zeros((6, edge), jnp.float32)], axis=0)
    near = cross(own, above_1).reshape(peers, rows, edge)
    far = cross(below_1, above_1).reshape(peers, kept, edge)
    shares = jnp.broadcast_to(shares[None], (peers, 8, edge))
    one = sum_rows(jnp.concatenate([near, far, shares], axis=1), "samp")
    shares = jnp.maximum(one[rows + kept :], 1.0)
    near_1 = one[:rows] / shares[0:1]
    far_1 = one[rows : rows + kept] / shares[1:2]
    far_1 = from_above(far_1, "var")
    above_2 = standardize(above_2, jnp.logical_not(jnp.isnan(above_2)), above_m[:, edge:])
    below_2 = standardize(below_2, jnp.logical_not(jnp.isnan(below_2)), below_m2)
    far = cross(below_1, above_2).reshape(peers, kept, rest)
    last = [cross(below_2, above_1), cross(below_2, above_2)]
    last = [part.reshape(peers, tail, part.shape[1]) for part in last]
    last = [last[0][:, :, k * rest : (k + 1) * rest] for k in range(pieces - 1)] + [last[1]]
    two = sum_rows(jnp.concatenate([far] + last, axis=1), "samp") / shares[1:2, :rest]
    far_2 = from_above(two, "var")
    near_2 = sum_rows(cross(own, above_2).reshape(peers, rows, rest), "samp")
    near_2 = near_2 / shares[0:1, :rest]
    near = jnp.concatenate([near_1, near_2], axis=1)
    low = [far_2[kept + k * tail : kept + (k + 1) * tail] for k in range(pieces)]
    far = jnp.concatenate(
        [
            jnp.concatenate([far_1, far_2[:kept]], axis=1),
            jnp.concatenate(low, axis=1),
        ],
        axis=0,
    )
    result = jnp.stack([same / jnp.maximum(sums[2:3], 1.0), near, far], axis=1)
    keep = jnp.arange(BAND, dtype=jnp.int32) <= band_reach[0]
    return jnp.where(keep[None, :, None], result, jnp.float32(0.0))[None]


def solution(mesh):
    return jax.shard_map(
        per_device,
        mesh=mesh,
        in_specs=(P("samp", ("seg", "var")), P(("seg", "var"), "samp"), P(("seg", "var"))),
        out_specs=P(("seg", "var"), "samp", None, None),
        check_vma=False,
    )
```

time: 103 us -> 117 us (1.14)
  other arithmetic: 7.72 us -> 16.1 us
  Pallas kernels: 0 us -> 7.06 us
  matrix products: 11.5 us -> 5.7 us
  waiting for transfers between devices: 55.8 us -> 58.3 us
  starting transfers between devices: 26.5 us -> 28.1 us
    pallas_call x0 -> x1, Pallas kernels: none -> 7.06 us  [head(): pl.pallas_call(head_kernel, grid=(samples // block,), out_shape=tuple((li...]
    ppermute x3, waiting for transfers between devices: 30.4 us -> 26 us  [from_below(): return lax.ppermute(shard, axis, [(i, i + 1) for i in range(peers - 2)])]
    ppermute x8 -> x10, waiting for transfers between devices: 16.2 us -> 20.6 us  [swap(): return lax.ppermute(shard, axis, [(i, i ^ bit) for i in range(peers)])]
    reduce_sum x3 -> x1, other arithmetic: 1.88 us -> 6.2 us  [per_device(): jnp.sum(jnp.where(other & above_present, 1.0, 0.0), axis=0, keepdims=True)]
    dot_general x3 -> x7, matrix products: 9.56 us -> 5.7 us  [cross(): lax.dot_general(left, right, (((0,), (0,)), ((), ())), preferred_element_...]
    convert_element_type x4 -> x3, other arithmetic: 1.59 us -> 4.95 us  [standardize(): jnp.where(present, spread, 0.0).astype(jnp.bfloat16)]
    ppermute x4 -> x5, waiting for transfers between devices: 9.16 us -> 11.7 us  [from_above(): return lax.ppermute(shard, axis, [(i, i - 1) for i in range(1, peers)])]
    another operation x4 -> x3, other arithmetic: 2.1 us -> 0.11 us  [per_device(): result = jnp.stack([same / jnp.maximum(sums[2:3], 1.0), near, far], axis=1)]
  transfers between devices with their start and end apart: 15 -> 18, of which waited for: 6 -> 9; matrix products, arithmetic and copies ran while one was open for 10% -> 18% of each run, Pallas kernels for 0% -> 0%
where the time goes in v3:
time: 117 us
  waiting for transfers between devices  58.3 us (50%)
  starting transfers between devices  28.1 us (24%)
  other arithmetic  16.1 us (14%)
  Pallas kernels  7.06 us (6%)
  matrix products  5.7 us (5%)
    ppermute x3, waiting for transfers between devices, from_below(): return lax.ppermute(shard, axis, [(i, i + 1) for i in range(peers - 2)])  26 us
    ppermute x10, waiting for transfers between devices, swap(): return lax.ppermute(shard, axis, [(i, i ^ bit) for i in range(peers)])  20.6 us
    ppermute x3, starting transfers between devices, from_below(): return lax.ppermute(shard, axis, [(i, i + 1) for i in range(peers - 2)])  14.2 us
    ppermute x5, waiting for transfers between devices, from_above(): return lax.ppermute(shard, axis, [(i, i - 1) for i in range(1, peers)])  11.7 us
    ppermute x10, starting transfers between devices, swap(): return lax.ppermute(shard, axis, [(i, i ^ bit) for i in range(peers)])  7.45 us
    pallas_call x1, Pallas kernels, head(): pl.pallas_call(head_kernel, grid=(samples // block,), out_shape=tuple((li...  7.06 us
    ppermute x5, starting transfers between devices, from_above(): return lax.ppermute(shard, axis, [(i, i - 1) for i in range(1, peers)])  6.44 us
    reduce_sum x1, other arithmetic, per_device(): jnp.sum(jnp.where(other & above_present, 1.0, 0.0), axis=0, keepdims=True)  6.2 us
  transfers between devices with their start and end apart: 18, of which 9 were waited for; matrix products, arithmetic and copies ran while one was open for 18% of the time, Pallas kernels for 0%

profile of v3, /device:TPU:0, one launch (start us, length us, event | category | flops | bytes accessed | tf_op | source)
XLA Modules:
  0.0 116.9 jit_solution(7009018890925308539)
XLA Ops:
  0.0 7.1 %head.1 = (bf16[2048,384]{1,0:T(8,128)(2,1)}, bf16[2048,128]{1,0:T(8,128)(2,1)}, bf16[2048,384]{1,0:T(8,128)(2,1)}, bf16[2048,128]{1,0:T(8,128)(2,1)}, f32[8,512]{1,0:T(8,128)}) custom-call(bf16[2048,512]{1,0:T(8,128)(2,1)} %dosage_ref.1, s32[1,2048]{1,0:T(1,128)} %observed_ref.1, s32[1,512]{1,0:T(1,128)} %constant.8.clone.order_ref), custom_call_target="tpu_custom_call" | custom-call | tf_op jit(solution)/shard_map/head/pallas_call | solution.py:95
  7.1 1.3 %collective-permute-start.4 = (bf16[2048,384]{1,0:T(8,128)(2,1)}, bf16[2048,384]{1,0:T(8,128)(2,1)}, u32[]{:S(2)}, u32[]{:S(2)}) collective-permute-start(bf16[2048,384]{1,0:T(8,128)(2,1)} %get-tuple-element.11), channel_id=1, source_target_pairs={{1,0},{2,1},{3,2},{5,4},{6,5},{7,6},{9,8},{10,9},{11,10},{13,12},{... | collective-permute-start | bytes 4718600 | tf_op jit(solution)/shard_map/ppermute | solution.py:18
  8.4 6.8 %collective-permute-start.6 = (bf16[2048,384]{1,0:T(8,128)(2,1)}, bf16[2048,384]{1,0:T(8,128)(2,1)}, u32[]{:S(2)}, u32[]{:S(2)}) collective-permute-start(bf16[2048,384]{1,0:T(8,128)(2,1)} %get-tuple-element.12), channel_id=1, source_target_pairs={{0,1},{1,2},{4,5},{5,6},{8,9},{9,10},{12,13},{13,14},{16,17},{17,1... | collective-permute-start | bytes 4718600 | tf_op jit(solution)/shard_map/ppermute | solution.py:23
  15.1 1.3 %collective-permute-start.10 = (bf16[2048,128]{1,0:T(8,128)(2,1)}, bf16[2048,128]{1,0:T(8,128)(2,1)}, u32[]{:S(2)}, u32[]{:S(2)}) collective-permute-start(bf16[2048,128]{1,0:T(8,128)(2,1)} %get-tuple-element.13), channel_id=1, source_target_pairs={{1,0},{2,1},{3,2},{5,4},{6,5},{7,6},{9,8},{10,9},{11,10},{13,12},{... | collective-permute-start | bytes 1572872 | tf_op jit(solution)/shard_map/ppermute | solution.py:18
  16.4 5.4 %collective-permute-start.14 = (bf16[2048,128]{1,0:T(8,128)(2,1)}, bf16[2048,128]{1,0:T(8,128)(2,1)}, u32[]{:S(2)}, u32[]{:S(2)}) collective-permute-start(bf16[2048,128]{1,0:T(8,128)(2,1)} %get-tuple-element.14), channel_id=1, source_target_pairs={{0,1},{1,2},{4,5},{5,6},{8,9},{9,10},{12,13},{13,14},{16,17},{17,1... | collective-permute-start | bytes 1572872 | tf_op jit(solution)/shard_map/ppermute | solution.py:23
  23.2 1.9 %collective-permute-start.1 = (f32[8,512]{1,0:T(8,128)S(1)}, f32[8,512]{1,0:T(8,128)S(1)}, u32[]{:S(2)}, u32[]{:S(2)}) collective-permute-start(f32[8,512]{1,0:T(8,128)S(1)} %add.36), channel_id=1, source_target_pairs={{0,8},{4,12},{8,0},{12,4},{1,9},{5,13},{9,1},{13,5},{2,10},{6,14},... | collective-permute-start | bytes 49160 | tf_op jit(solution)/shard_map/ppermute | solution.py:28
  25.2 1.7 %collective-permute-done.1 = f32[8,512]{1,0:T(8,128)S(1)} collective-permute-done((f32[8,512]{1,0:T(8,128)S(1)}, f32[8,512]{1,0:T(8,128)S(1)}, u32[]{:S(2)}, u32[]{:S(2)}) %collective-permute-start.1) | collective-permute-done | bytes 16416 | tf_op jit(solution)/shard_map/ppermute | solution.py:28
  27.0 2.1 %collective-permute-start.7 = (f32[2,512]{1,0:T(2,128)S(1)}, f32[2,512]{1,0:T(2,128)S(1)}, u32[]{:S(2)}, u32[]{:S(2)}) collective-permute-start(f32[2,512]{1,0:T(2,128)S(1)} %pad_maximum_fusion.1), channel_id=1, source_target_pairs={{0,1},{1,2},{4,5},{5,6},{8,9},{9,10},{12,13},{13,14},{16,17},{17,1... | collective-permute-start | bytes 12296 | tf_op jit(solution)/shard_map/ppermute | solution.py:23
  29.0 2.0 %select_convert_fusion = bf16[2048,512]{1,0:T(8,128)(2,1)S(1)} fusion(bf16[2048,512]{1,0:T(8,128)(2,1)} %dosage_ref.1, f32[512]{0:T(512)S(1)} %bitcast.163, f32[512]{0:T(512)S(1)} %bitcast.164, pred[2048]{0:T(1024)(128)(4,1)S(1)} %compare_reduce_fusion), kind=kLoop, calls=%fused_computation | loop fusion | flops 5242880 | bytes 4200448 | tf_op jit(solution)/shard_map/convert_element_type | solution.py:119
  31.0 1.3 %fusion.13 = f32[512,512]{1,0:T(8,128)S(1)} fusion(bf16[2048,512]{1,0:T(8,128)(2,1)S(1)} %select_convert_fusion), kind=kOutput, calls=%fused_computation.73 | convolution fusion | flops 1073741824 | bytes 3145728 | tf_op jit(solution)/shard_map/dot_general | solution.py:123
  32.3 0.9 select_bitcast_fusion.1
  33.2 26.0 %collective-permute-done.7 = f32[2,512]{1,0:T(2,128)S(1)} collective-permute-done((f32[2,512]{1,0:T(2,128)S(1)}, f32[2,512]{1,0:T(2,128)S(1)}, u32[]{:S(2)}, u32[]{:S(2)}) %collective-permute-start.7) | collective-permute-done | bytes 4128 | tf_op jit(solution)/shard_map/ppermute | solution.py:23
  59.2 1.3 %collective-permute-start.5 = (f32[2,512]{1,0:T(2,128)S(1)}, f32[2,512]{1,0:T(2,128)S(1)}, u32[]{:S(2)}, u32[]{:S(2)}) collective-permute-start(f32[2,512]{1,0:T(2,128)S(1)} %pad_maximum_fusion.1), channel_id=1, source_target_pairs={{1,0},{2,1},{3,2},{5,4},{6,5},{7,6},{9,8},{10,9},{11,10},{13,12},{... | collective-permute-start | bytes 12296 | tf_op jit(solution)/shard_map/ppermute | solution.py:18
  60.5 4.6 %collective-permute-done.5 = f32[2,512]{1,0:T(2,128)S(1)} collective-permute-done((f32[2,512]{1,0:T(2,128)S(1)}, f32[2,512]{1,0:T(2,128)S(1)}, u32[]{:S(2)}, u32[]{:S(2)}) %collective-permute-start.5) | collective-permute-done | bytes 4128 | tf_op jit(solution)/shard_map/ppermute | solution.py:18
  65.6 1.4 %select_convert_fusion.4 = bf16[2048,128]{1,0:T(8,128)(2,1)S(1)} fusion(bf16[2048,128]{1,0:T(8,128)(2,1)} %collective-permute-done.10, f32[128]{0:T(128)S(1)} %get-tuple-element.40, f32[128]{0:T(128)S(1)} %get-tuple-element.39), kind=kLoop, calls=%fused_computation.7 | loop fusion | flops 1572864 | bytes 1049600 | tf_op jit(solution)/shard_map/convert_element_type | solution.py:119
  67.0 1.6 %select_convert_fusion.3 = bf16[2048,128]{1,0:T(8,128)(2,1)S(1)} fusion(bf16[2048,128]{1,0:T(8,128)(2,1)} %collective-permute-done.14, f32[128]{0:T(128)S(1)} %mul.66, f32[128]{0:T(128)S(1)} %sub.66), kind=kLoop, calls=%fused_computation.6 | loop fusion | flops 1572864 | bytes 1049600 | tf_op jit(solution)/shard_map/convert_element_type | solution.py:119
  68.6 0.7 fusion.16
  70.3 1.3 %fusion.1 = f32[1,2,128,512]{3,2,1,0:T(8,128)S(1)} fusion(f32[2,128,512]{2,1,0:T(8,128)} %collective-permute-done.2, f32[2,2,128,512]{3,2,1,0:T(8,128)S(1)} %bitcast.152, pred[]{:T(512)S(6)} %ne.41), kind=kLoop, calls=%fused_computation.15 | loop fusion | flops 262144 | bytes 2097153 | tf_op jit(solution)/shard_map/reshape | solution.py:44
  71.7 1.7 %collective-permute-start.3 = (f32[1,128,512]{2,1,0:T(8,128)S(1)}, f32[1,128,512]{2,1,0:T(8,128)S(1)}, u32[]{:S(2)}, u32[]{:S(2)}) collective-permute-start(f32[1,128,512]{2,1,0:T(8,128)S(1)} %select_bitcast_fusion.3), channel_id=1, source_target_pairs={{0,8},{4,12},{8,0},{12,4},{1,9},{5,13},{9,1},{13,5},{2,10},{6,14},... | collective-permute-start | bytes 786440 | tf_op jit(solution)/shard_map/ppermute | solution.py:28
  73.9 6.8 %collective-permute-done.3 = f32[1,128,512]{2,1,0:T(8,128)S(1)} collective-permute-done((f32[1,128,512]{2,1,0:T(8,128)S(1)}, f32[1,128,512]{2,1,0:T(8,128)S(1)}, u32[]{:S(2)}, u32[]{:S(2)}) %collective-permute-start.3) | collective-permute-done | bytes 262176 | tf_op jit(solution)/shard_map/ppermute | solution.py:28
  80.8 6.2 %select_reduce_fusion.1 = (f32[384]{0:T(512)S(1)}, f32[384]{0:T(512)S(1)}, bf16[2048,384]{1,0:T(8,128)(2,1)S(1)}, bf16[2048,384]{1,0:T(8,128)(2,1)S(1)}) fusion(bf16[2048,384]{1,0:T(8,128)(2,1)S(1)} %copy-done, bf16[2048,384]{1,0:T(8,128)(2,1)} %collective-permute-done.4, bf16[2048,384]{1,0:T(8,128)(2,1)} %collective-permute-done.6, f32[384]{0:T(512)S(1)} %mul.60, ...), kind=kLoop, calls=%fused_computation.2 | loop fusion | flops 19660032 | bytes 7873536 | tf_op jit(solution)/shard_map/reduce_sum | solution.py:163
  87.5 1.3 %fusion.14 = f32[512,384]{1,0:T(8,128)S(1)} fusion(bf16[2048,512]{1,0:T(8,128)(2,1)S(1)} %select_convert_fusion, bf16[2048,384]{1,0:T(8,128)(2,1)S(1)} %get-tuple-element.24), kind=kOutput, calls=%fused_computation.74 | convolution fusion | flops 805306368 | bytes 4456448 | tf_op jit(solution)/shard_map/dot_general | solution.py:123
  89.3 1.0 fusion.15
  91.4 1.5 %collective-permute-done.8 = f32[2,232,384]{2,1,0:T(8,128)S(1)} collective-permute-done((f32[2,232,384]{2,1,0:T(8,128)S(1)}, f32[2,232,384]{2,1,0:T(8,128)S(1)}, u32[]{:S(2)}, u32[]{:S(2)}) %collective-permute-start.8) | collective-permute-done | bytes 712736 | tf_op jit(solution)/shard_map/ppermute | solution.py:28
  93.0 1.7 %collective-permute-start.9 = (f32[1,232,384]{2,1,0:T(8,128)S(1)}, f32[1,232,384]{2,1,0:T(8,128)S(1)}, u32[]{:S(2)}, u32[]{:S(2)}) collective-permute-start(f32[1,232,384]{2,1,0:T(8,128)S(1)} %select_bitcast_fusion.2), channel_id=1, source_target_pairs={{0,8},{4,12},{8,0},{12,4},{1,9},{5,13},{9,1},{13,5},{2,10},{6,14},... | collective-permute-start | bytes 1069064 | tf_op jit(solution)/shard_map/ppermute | solution.py:28
  95.3 9.0 %collective-permute-done.9 = f32[1,232,384]{2,1,0:T(8,128)S(1)} collective-permute-done((f32[1,232,384]{2,1,0:T(8,128)S(1)}, f32[1,232,384]{2,1,0:T(8,128)S(1)}, u32[]{:S(2)}, u32[]{:S(2)}) %collective-permute-start.9) | collective-permute-done | bytes 356384 | tf_op jit(solution)/shard_map/ppermute | solution.py:28
  104.4 1.5 %collective-permute-done.16 = f32[1,224,128]{2,1,0:T(8,128)S(1)} collective-permute-done((f32[1,224,128]{2,1,0:T(8,128)S(1)}, f32[1,224,128]{2,1,0:T(8,128)S(1)}, u32[]{:S(2)}, u32[]{:S(2)}) %collective-permute-start.16) | collective-permute-done | bytes 114720 | tf_op jit(solution)/shard_map/ppermute | solution.py:28
  106.0 1.3 %collective-permute-start.17 = (f32[224,128]{1,0:T(8,128)S(1)}, f32[224,128]{1,0:T(8,128)S(1)}, u32[]{:S(2)}, u32[]{:S(2)}) collective-permute-start(f32[224,128]{1,0:T(8,128)S(1)} %bitcast_divide_fusion.1), channel_id=1, source_target_pairs={{1,0},{2,1},{3,2},{5,4},{6,5},{7,6},{9,8},{10,9},{11,10},{13,12},{... | collective-permute-start | bytes 344072 | tf_op jit(solution)/shard_map/ppermute | solution.py:18
  107.3 1.3 %collective-permute-start.13 = (f32[96,384]{1,0:T(8,128)S(1)}, f32[96,384]{1,0:T(8,128)S(1)}, u32[]{:S(2)}, u32[]{:S(2)}) collective-permute-start(f32[96,384]{1,0:T(8,128)S(1)} %fusion.5), channel_id=1, source_target_pairs={{1,0},{2,1},{3,2},{5,4},{6,5},{7,6},{9,8},{10,9},{11,10},{13,12},{... | collective-permute-start | bytes 442376 | tf_op jit(solution)/shard_map/ppermute | solution.py:18
  108.7 4.6 %collective-permute-done.17 = f32[224,128]{1,0:T(8,128)S(1)} collective-permute-done((f32[224,128]{1,0:T(8,128)S(1)}, f32[224,128]{1,0:T(8,128)S(1)}, u32[]{:S(2)}, u32[]{:S(2)}) %collective-permute-start.17) | collective-permute-done | bytes 114720 | tf_op jit(solution)/shard_map/ppermute | solution.py:18
  113.3 2.5 %collective-permute-done.13 = f32[96,384]{1,0:T(8,128)S(1)} collective-permute-done((f32[96,384]{1,0:T(8,128)S(1)}, f32[96,384]{1,0:T(8,128)S(1)}, u32[]{:S(2)}, u32[]{:S(2)}) %collective-permute-start.13) | collective-permute-done | bytes 147488 | tf_op jit(solution)/shard_map/ppermute | solution.py:18
  115.8 1.0 maximum_select_fusion
  (74 shorter events, 5.8 us)
Async XLA Ops:
  0.0 21.8 %copy-start.1 = (s32[1,2048]{1,0:T(1,128)S(1)}, s32[1,2048]{1,0:T(1,128)}, u32[]{:S(2)}) copy-start(s32[1,2048]{1,0:T(1,128)} %observed_ref.1) | copy-start | bytes 24580
  7.1 73.7 %collective-permute-start.4 = (bf16[2048,384]{1,0:T(8,128)(2,1)}, bf16[2048,384]{1,0:T(8,128)(2,1)}, u32[]{:S(2)}, u32[]{:S(2)}) collective-permute-start(bf16[2048,384]{1,0:T(8,128)(2,1)} %get-tuple-element.11), channel_id=1, source_target_pairs={{1,0},{2,1},{3,2},{5,4},{6,5},{7,6},{9,8},{10,9},{11,10},{13,12},{... | collective-permute-start | bytes 4718600 | tf_op jit(solution)/shard_map/ppermute | solution.py:18
  8.4 72.4 %collective-permute-start.6 = (bf16[2048,384]{1,0:T(8,128)(2,1)}, bf16[2048,384]{1,0:T(8,128)(2,1)}, u32[]{:S(2)}, u32[]{:S(2)}) collective-permute-start(bf16[2048,384]{1,0:T(8,128)(2,1)} %get-tuple-element.12), channel_id=1, source_target_pairs={{0,1},{1,2},{4,5},{5,6},{8,9},{9,10},{12,13},{13,14},{16,17},{17,1... | collective-permute-start | bytes 4718600 | tf_op jit(solution)/shard_map/ppermute | solution.py:23
  15.1 7.3 %collective-permute-start = (f32[8,512]{1,0:T(8,128)}, f32[8,512]{1,0:T(8,128)S(1)}, u32[]{:S(2)}, u32[]{:S(2)}) collective-permute-start(f32[8,512]{1,0:T(8,128)} %get-tuple-element.10), channel_id=1, source_target_pairs={{0,4},{4,0},{8,12},{12,8},{1,5},{5,1},{9,13},{13,9},{2,6},{6,2},{1... | collective-permute-start | bytes 49160 | tf_op jit(solution)/shard_map/ppermute | solution.py:28
  15.1 50.5 %collective-permute-start.10 = (bf16[2048,128]{1,0:T(8,128)(2,1)}, bf16[2048,128]{1,0:T(8,128)(2,1)}, u32[]{:S(2)}, u32[]{:S(2)}) collective-permute-start(bf16[2048,128]{1,0:T(8,128)(2,1)} %get-tuple-element.13), channel_id=1, source_target_pairs={{1,0},{2,1},{3,2},{5,4},{6,5},{7,6},{9,8},{10,9},{11,10},{13,12},{... | collective-permute-start | bytes 1572872 | tf_op jit(solution)/shard_map/ppermute | solution.py:18
  16.4 50.6 %collective-permute-start.14 = (bf16[2048,128]{1,0:T(8,128)(2,1)}, bf16[2048,128]{1,0:T(8,128)(2,1)}, u32[]{:S(2)}, u32[]{:S(2)}) collective-permute-start(bf16[2048,128]{1,0:T(8,128)(2,1)} %get-tuple-element.14), channel_id=1, source_target_pairs={{0,1},{1,2},{4,5},{5,6},{8,9},{9,10},{12,13},{13,14},{16,17},{17,1... | collective-permute-start | bytes 1572872 | tf_op jit(solution)/shard_map/ppermute | solution.py:23
  23.2 3.7 %collective-permute-start.1 = (f32[8,512]{1,0:T(8,128)S(1)}, f32[8,512]{1,0:T(8,128)S(1)}, u32[]{:S(2)}, u32[]{:S(2)}) collective-permute-start(f32[8,512]{1,0:T(8,128)S(1)} %add.36), channel_id=1, source_target_pairs={{0,8},{4,12},{8,0},{12,4},{1,9},{5,13},{9,1},{13,5},{2,10},{6,14},... | collective-permute-start | bytes 49160 | tf_op jit(solution)/shard_map/ppermute | solution.py:28
  27.0 32.2 %collective-permute-start.7 = (f32[2,512]{1,0:T(2,128)S(1)}, f32[2,512]{1,0:T(2,128)S(1)}, u32[]{:S(2)}, u32[]{:S(2)}) collective-permute-start(f32[2,512]{1,0:T(2,128)S(1)} %pad_maximum_fusion.1), channel_id=1, source_target_pairs={{0,1},{1,2},{4,5},{5,6},{8,9},{9,10},{12,13},{13,14},{16,17},{17,1... | collective-permute-start | bytes 12296 | tf_op jit(solution)/shard_map/ppermute | solution.py:23
  59.2 6.0 %collective-permute-start.5 = (f32[2,512]{1,0:T(2,128)S(1)}, f32[2,512]{1,0:T(2,128)S(1)}, u32[]{:S(2)}, u32[]{:S(2)}) collective-permute-start(f32[2,512]{1,0:T(2,128)S(1)} %pad_maximum_fusion.1), channel_id=1, source_target_pairs={{1,0},{2,1},{3,2},{5,4},{6,5},{7,6},{9,8},{10,9},{11,10},{13,12},{... | collective-permute-start | bytes 12296 | tf_op jit(solution)/shard_map/ppermute | solution.py:18
  65.1 5.2 %collective-permute-start.2 = (f32[2,128,512]{2,1,0:T(8,128)}, f32[2,128,512]{2,1,0:T(8,128)}, u32[]{:S(2)}, u32[]{:S(2)}) collective-permute-start(f32[2,128,512]{2,1,0:T(8,128)} %select_bitcast_fusion.1), channel_id=1, source_target_pairs={{0,4},{4,0},{8,12},{12,8},{1,5},{5,1},{9,13},{13,9},{2,6},{6,2},{1... | collective-permute-start | bytes 1572872 | tf_op jit(solution)/shard_map/ppermute | solution.py:28
  69.4 4.0 %collective-permute-start.11 = (f32[2,128,128]{2,1,0:T(8,128)S(1)}, f32[2,128,128]{2,1,0:T(8,128)S(1)}, u32[]{:S(2)}, u32[]{:S(2)}) collective-permute-start(f32[2,128,128]{2,1,0:T(8,128)S(1)} %select_bitcast_fusion.5), channel_id=1, source_target_pairs={{0,4},{4,0},{8,12},{12,8},{1,5},{5,1},{9,13},{13,9},{2,6},{6,2},{1... | collective-permute-start | bytes 393224 | tf_op jit(solution)/shard_map/ppermute | solution.py:28
  70.3 10.5 %copy-start = (bf16[2048,384]{1,0:T(8,128)(2,1)S(1)}, bf16[2048,384]{1,0:T(8,128)(2,1)}, u32[]{:S(2)}) copy-start(bf16[2048,384]{1,0:T(8,128)(2,1)} %get-tuple-element.11) | copy-start | bytes 4718596
  71.7 9.0 %collective-permute-start.3 = (f32[1,128,512]{2,1,0:T(8,128)S(1)}, f32[1,128,512]{2,1,0:T(8,128)S(1)}, u32[]{:S(2)}, u32[]{:S(2)}) collective-permute-start(f32[1,128,512]{2,1,0:T(8,128)S(1)} %select_bitcast_fusion.3), channel_id=1, source_target_pairs={{0,8},{4,12},{8,0},{12,4},{1,9},{5,13},{9,1},{13,5},{2,10},{6,14},... | collective-permute-start | bytes 786440 | tf_op jit(solution)/shard_map/ppermute | solution.py:28
  73.4 35.2 %collective-permute-start.12 = (f32[1,128,128]{2,1,0:T(8,128)S(1)}, f32[1,128,128]{2,1,0:T(8,128)S(1)}, u32[]{:S(2)}, u32[]{:S(2)}) collective-permute-start(f32[1,128,128]{2,1,0:T(8,128)S(1)} %select_bitcast_fusion.7), channel_id=1, source_target_pairs={{0,8},{4,12},{8,0},{12,4},{1,9},{5,13},{9,1},{13,5},{2,10},{6,14},... | collective-permute-start | bytes 196616 | tf_op jit(solution)/shard_map/ppermute | solution.py:28
  90.7 2.2 %collective-permute-start.8 = (f32[2,232,384]{2,1,0:T(8,128)S(1)}, f32[2,232,384]{2,1,0:T(8,128)S(1)}, u32[]{:S(2)}, u32[]{:S(2)}) collective-permute-start(f32[2,232,384]{2,1,0:T(8,128)S(1)} %select_bitcast_fusion), channel_id=1, source_target_pairs={{0,4},{4,0},{8,12},{12,8},{1,5},{5,1},{9,13},{13,9},{2,6},{6,2},{1... | collective-permute-start | bytes 2138120 | tf_op jit(solution)/shard_map/ppermute | solution.py:28
  90.8 3.9 %collective-permute-start.15 = (f32[2,224,128]{2,1,0:T(8,128)S(1)}, f32[2,224,128]{2,1,0:T(8,128)S(1)}, u32[]{:S(2)}, u32[]{:S(2)}) collective-permute-start(f32[2,224,128]{2,1,0:T(8,128)S(1)} %select_bitcast_fusion.4), channel_id=1, source_target_pairs={{0,4},{4,0},{8,12},{12,8},{1,5},{5,1},{9,13},{13,9},{2,6},{6,2},{1... | collective-permute-start | bytes 688136 | tf_op jit(solution)/shard_map/ppermute | solution.py:28
  93.0 11.3 %collective-permute-start.9 = (f32[1,232,384]{2,1,0:T(8,128)S(1)}, f32[1,232,384]{2,1,0:T(8,128)S(1)}, u32[]{:S(2)}, u32[]{:S(2)}) collective-permute-start(f32[1,232,384]{2,1,0:T(8,128)S(1)} %select_bitcast_fusion.2), channel_id=1, source_target_pairs={{0,8},{4,12},{8,0},{12,4},{1,9},{5,13},{9,1},{13,5},{2,10},{6,14},... | collective-permute-start | bytes 1069064 | tf_op jit(solution)/shard_map/ppermute | solution.py:28
  94.8 11.1 %collective-permute-start.16 = (f32[1,224,128]{2,1,0:T(8,128)S(1)}, f32[1,224,128]{2,1,0:T(8,128)S(1)}, u32[]{:S(2)}, u32[]{:S(2)}) collective-permute-start(f32[1,224,128]{2,1,0:T(8,128)S(1)} %select_bitcast_fusion.6), channel_id=1, source_target_pairs={{0,8},{4,12},{8,0},{12,4},{1,9},{5,13},{9,1},{13,5},{2,10},{6,14},... | collective-permute-start | bytes 344072 | tf_op jit(solution)/shard_map/ppermute | solution.py:28
  106.0 7.3 %collective-permute-start.17 = (f32[224,128]{1,0:T(8,128)S(1)}, f32[224,128]{1,0:T(8,128)S(1)}, u32[]{:S(2)}, u32[]{:S(2)}) collective-permute-start(f32[224,128]{1,0:T(8,128)S(1)} %bitcast_divide_fusion.1), channel_id=1, source_target_pairs={{1,0},{2,1},{3,2},{5,4},{6,5},{7,6},{9,8},{10,9},{11,10},{13,12},{... | collective-permute-start | bytes 344072 | tf_op jit(solution)/shard_map/ppermute | solution.py:18
  107.3 8.5 %collective-permute-start.13 = (f32[96,384]{1,0:T(8,128)S(1)}, f32[96,384]{1,0:T(8,128)S(1)}, u32[]{:S(2)}, u32[]{:S(2)}) collective-permute-start(f32[96,384]{1,0:T(8,128)S(1)} %fusion.5), channel_id=1, source_target_pairs={{1,0},{2,1},{3,2},{5,4},{6,5},{7,6},{9,8},{10,9},{11,10},{13,12},{... | collective-permute-start | bytes 442376 | tf_op jit(solution)/shard_map/ppermute | solution.py:18

commit v4 on v3

--- a/solution.py
+++ b/solution.py
@@ -3,6 +3,7 @@
 import numpy as np
 from jax import lax
 from jax.experimental import pallas as pl
+from jax.experimental.pallas import tpu as pltpu
 from jax.sharding import PartitionSpec as P
 
 BAND = 3
@@ -49,6 +50,17 @@
     return partial[0]
 
 
+GRANT = 20 << 20
+
+
+def block_of(samples):
+    return 512 if samples % 512 == 0 else samples
+
+
+def in_hbm(array):
+    return pltpu.with_memory_space_constraint(array, pltpu.HBM)
+
+
 def like(shape, dtype):
     return jax.ShapeDtypeStruct(shape, dtype)
 
@@ -64,12 +76,7 @@
     flags = observed_ref[...].astype(jnp.float32)
     present = jnp.transpose(jnp.broadcast_to(flags, (lanes, samples))) > 0.5
     count = jnp.sum(jnp.where(present, 1.0, 0.0), axis=0, keepdims=True)
-    chosen = lax.broadcasted_iota(jnp.int32, (width, width), 0) == order_ref[...]
-    up = jnp.dot(
-        dosage_ref[...],
-        jnp.where(chosen, 1.0, 0.0).astype(jnp.bfloat16),
-        preferred_element_type=jnp.float32,
-    )
+    up = jnp.dot(dosage_ref[...], order_ref[...], preferred_element_type=jnp.float32)
     edge = down_1.shape[1]
     for low in range(0, width, lanes):
         part = slice(low, low + lanes)
@@ -90,7 +97,7 @@
 
 def head(dosage, observed, order, edge):
     samples, width = dosage.shape
-    block = 256 if samples % 256 == 0 else samples
+    block = block_of(samples)
     cuts = [edge, width - edge] * 2
     return pl.pallas_call(
         head_kernel,
@@ -100,12 +107,13 @@
         in_specs=[
             pl.BlockSpec((block, width), lambda i: (i, 0)),
             pl.BlockSpec((1, block), lambda i: (0, i)),
-            pl.BlockSpec((1, width), lambda i: (0, 0)),
+            pl.BlockSpec((width, width), lambda i: (0, 0)),
         ],
         out_specs=tuple(pl.BlockSpec((block, cut), lambda i: (i, 0)) for cut in cuts)
         + (pl.BlockSpec((8, width), lambda i: (0, 0)),),
+        compiler_params=pltpu.CompilerParams(vmem_limit_bytes=GRANT),
         name="head",
-    )(dosage, observed, order)
+    )(in_hbm(dosage), observed, order)
 
 
 def finish_moments(sums):
@@ -116,13 +124,128 @@
 
 def standardize(values, present, moments):
     spread = (values.astype(jnp.float32) - moments[0:1]) * moments[1:2]
-    return lax.optimization_barrier(jnp.where(present, spread, 0.0).astype(jnp.bfloat16))
+    return jnp.where(present, spread, 0.0).astype(jnp.bfloat16)
+
+
+def decode(ref, moments_ref):
+    values = ref[...].astype(jnp.float32)
+    spread = (values - moments_ref[0:1, :]) * moments_ref[1:2, :]
+    return jnp.where(values == values, spread, 0.0).astype(jnp.bfloat16)
+
+
+def flags_of(ref):
+    values = ref[:, :128].astype(jnp.float32)
+    return jnp.where(values == values, 1.0, 0.0)
 
 
 def cross(left, right):
     return lax.dot_general(
         left, right, (((0,), (0,)), ((), ())), preferred_element_type=jnp.float32
     )
+
+
+def first_kernel(
+    coded_ref, above_ref, below_ref, own_ref, above_m, below_m, out_ref, above_out, below_out
+):
+    peers, _, edge = out_ref.shape
+    rows = own_ref.shape[1] // peers
+    kept = edge // peers
+
+    @pl.when(pl.program_id(0) == 0)
+    def _():
+        out_ref[...] = jnp.zeros_like(out_ref)
+
+    above = decode(above_ref, above_m)
+    below = decode(below_ref, below_m)
+    above_out[...] = above
+    below_out[...] = below
+    near = cross(own_ref[...], above)
+    far = cross(below, above)
+    above_one = flags_of(above_ref)
+    shares = [
+        jnp.sum(flags_of(ref) * above_one, axis=0, keepdims=True) for ref in (coded_ref, below_ref)
+    ]
+    for k in range(peers):
+        out_ref[k, :rows, :] += near[k * rows : (k + 1) * rows]
+        out_ref[k, rows : rows + kept, :] += far[k * kept : (k + 1) * kept]
+        for low in range(0, edge, 128):
+            out_ref[k, rows + kept : rows + kept + 1, low : low + 128] += shares[0]
+            out_ref[k, rows + kept + 1 : rows + kept + 2, low : low + 128] += shares[1]
+
+
+def first_pass(coded, above, below, own, above_m, below_m, peers):
+    samples, width = own.shape
+    edge = above.shape[1]
+    block = block_of(samples)
+    tall = (peers, width // peers + edge // peers + 8, edge)
+
+    def rows_of(cut):
+        return pl.BlockSpec((block, cut), lambda i: (i, 0))
+
+    moments = pl.BlockSpec((2, edge), lambda i: (0, 0))
+    flops = 2 * samples * edge * (width + edge)
+    return pl.pallas_call(
+        first_kernel,
+        grid=(samples // block,),
+        out_shape=(like(tall, jnp.float32),) + (like((samples, edge), jnp.bfloat16),) * 2,
+        in_specs=[rows_of(128), rows_of(edge), rows_of(edge), rows_of(width), moments, moments],
+        out_specs=(pl.BlockSpec(tall, lambda i: (0, 0, 0)), rows_of(edge), rows_of(edge)),
+        compiler_params=pltpu.CompilerParams(vmem_limit_bytes=GRANT),
+        cost_estimate=pl.CostEstimate(
+            flops=flops, bytes_accessed=12 * samples * edge, transcendentals=0
+        ),
+        name="first",
+    )(coded, above, below, own, above_m, below_m)
+
+
+def second_kernel(above_ref, below_ref, above_1, below_1, own_ref, above_m, below_m, out_ref):
+    peers, _, rest = out_ref.shape
+    width, edge = own_ref.shape[1], above_1.shape[1]
+    rows, kept, tail = width // peers, edge // peers, rest // peers
+
+    @pl.when(pl.program_id(0) == 0)
+    def _():
+        out_ref[...] = jnp.zeros_like(out_ref)
+
+    above = decode(above_ref, above_m)
+    below = decode(below_ref, below_m)
+    near = cross(own_ref[...], above)
+    far = cross(below_1[...], above)
+    last = cross(below, above_1[...])
+    corner = cross(below, above)
+    for k in range(peers):
+        out_ref[k, :rows, :] += near[k * rows : (k + 1) * rows]
+        low = rows + kept
+        out_ref[k, rows:low, :] += far[k * kept : (k + 1) * kept]
+        for left in range(0, edge, rest):
+            out_ref[k, low : low + tail, :] += last[k * tail : (k + 1) * tail, left : left + rest]
+            low += tail
+        out_ref[k, low : low + tail, :] += corner[k * tail : (k + 1) * tail]
+
+
+def second_pass(above, below, above_1, below_1, own, above_m, below_m, peers):
+    samples, width = own.shape
+    edge, rest = above_1.shape[1], above.shape[1]
+    block = block_of(samples)
+    tall = (peers, (width + edge + width) // peers, rest)
+
+    def rows_of(cut):
+        return pl.BlockSpec((block, cut), lambda i: (i, 0))
+
+    moments = pl.BlockSpec((2, rest), lambda i: (0, 0))
+    flops = 2 * samples * rest * (2 * width + edge)
+    return pl.pallas_call(
+        second_kernel,
+        grid=(samples // block,),
+        out_shape=like(tall, jnp.float32),
+        in_specs=[rows_of(rest)] * 2 + [rows_of(edge)] * 2 + [rows_of(width)] + [moments] * 2,
+        out_specs=pl.BlockSpec(tall, lambda i: (0, 0, 0)),
+        compiler_params=pltpu.CompilerParams(vmem_limit_bytes=GRANT),
+        cost_estimate=pl.CostEstimate(
+            flops=flops, bytes_accessed=2 * samples * (2 * width + edge), transcendentals=0
+        ),
+        name="second",
+    )(above, below, in_hbm(above_1), in_hbm(below_1), own, above_m, below_m)
 
 
 def per_device(dosage, observed, band_reach):
@@ -138,9 +261,10 @@
             (owners + np.arange(0, kept)[None, :]).ravel(),
             (owners + np.arange(kept, rows)[None, :]).ravel(),
         ]
-    ).astype(np.int32)[None, :]
+    )
     pieces = width // rest
-    down_1, down_2, up_1, up_2, sums = head(dosage, observed, jnp.asarray(order), edge)
+    chosen = jnp.asarray(np.arange(width)[:, None] == order[None, :], jnp.bfloat16)
+    down_1, down_2, up_1, up_2, sums = head(dosage, observed, chosen, edge)
     above_1 = from_above(down_1, "var")
     below_1 = from_below(up_1, "var")
     sums = sum_all(sums, "samp")
@@ -150,39 +274,27 @@
     above_2 = from_above(down_2, "var")
     below_2 = from_below(up_2, "var")
     own = standardize(dosage, (observed[0] != 0)[:, None], moments)
+    own = lax.optimization_barrier(own)
     same = sum_rows(cross(own, own).reshape(peers, rows, width), "samp")
     below_m = below_m.reshape(2, peers, rows)
     below_m1 = below_m[:, :, :kept].reshape(2, edge)
     below_m2 = below_m[:, :, kept:].reshape(2, rest)
-    own_present = jnp.logical_not(jnp.isnan(down_1))
-    above_present = jnp.logical_not(jnp.isnan(above_1))
-    below_present = jnp.logical_not(jnp.isnan(below_1))
-    above_1 = standardize(above_1, above_present, above_m[:, :edge])
-    below_1 = standardize(below_1, below_present, below_m1)
-    shares = [
-        jnp.sum(jnp.where(other & above_present, 1.0, 0.0), axis=0, keepdims=True)
-        for other in (own_present, below_present)
-    ]
-    shares = jnp.concatenate(shares + [jnp.zeros((6, edge), jnp.float32)], axis=0)
-    near = cross(own, above_1).reshape(peers, rows, edge)
-    far = cross(below_1, above_1).reshape(peers, kept, edge)
-    shares = jnp.broadcast_to(shares[None], (peers, 8, edge))
-    one = sum_rows(jnp.concatenate([near, far, shares], axis=1), "samp")
+    above_m1, above_m2 = above_m[:, :edge], above_m[:, edge:]
+    one, above_1, below_1 = first_pass(
+        down_1, above_1, below_1, own, above_m1, below_m1, peers
+    )
+    one = sum_rows(one, "samp")
     shares = jnp.maximum(one[rows + kept :], 1.0)
     near_1 = one[:rows] / shares[0:1]
     far_1 = one[rows : rows + kept] / shares[1:2]
     far_1 = from_above(far_1, "var")
-    above_2 = standardize(above_2, jnp.logical_not(jnp.isnan(above_2)), above_m[:, edge:])
-    below_2 = standardize(below_2, jnp.logical_not(jnp.isnan(below_2)), below_m2)
-    far = cross(below_1, above_2).reshape(peers, kept, rest)
-    last = [cross(below_2, above_1), cross(below_2, above_2)]
-    last = [part.reshape(peers, tail, part.shape[1]) for part in last]
-    last = [last[0][:, :, k * rest : (k + 1) * rest] for k in range(pieces - 1)] + [last[1]]
-    two = sum_rows(jnp.concatenate([far] + last, axis=1), "samp") / shares[1:2, :rest]
-    far_2 = from_above(two, "var")
-    near_2 = sum_rows(cross(own, above_2).reshape(peers, rows, rest), "samp")
-    near_2 = near_2 / shares[0:1, :rest]
-    near = jnp.concatenate([near_1, near_2], axis=1)
+    two = second_pass(
+        above_2, below_2, above_1, below_1, own, above_m2, below_m2, peers
+    )
+    two = sum_rows(two, "samp")
+    far_2 = two[rows:] / shares[1:2, :rest]
+    far_2 = from_above(far_2, "var")
+    near = jnp.concatenate([near_1, two[:rows] / shares[0:1, :rest]], axis=1)
     low = [far_2[kept + k * tail : kept + (k + 1) * tail] for k in range(pieces)]
     far = jnp.concatenate(
         [

time: 117 us -> 102 us (0.87)
  other arithmetic: 16.1 us -> 6.31 us
  waiting for transfers between devices: 58.3 us -> 49 us
  Pallas kernels: 7.06 us -> 14.1 us
  matrix products: 5.7 us -> 1.28 us
  local copies, waits for them, and re-layouts: 0.64 us -> 4.34 us
  starting transfers between devices: 28.1 us -> 25.3 us
    pallas_call x0 -> x2, Pallas kernels: none -> 8.97 us  [the longest x1 4.92 us: first_pass(): pl.pallas_call(first_kernel, grid=(samples // block,), out_shape=(like(ta...]
    ppermute x3, waiting for transfers between devices: 26 us -> 19.5 us  [from_below(): return lax.ppermute(shard, axis, [(i, i + 1) for i in range(peers - 2)])]
    reduce_sum x1 -> x0, other arithmetic: 6.2 us -> none  [per_device(): jnp.sum(jnp.where(other & above_present, 1.0, 0.0), axis=0, keepdims=True)]
    dot_general x7 -> x1, matrix products: 5.7 us -> 1.28 us  [cross(): lax.dot_general(left, right, (((0,), (0,)), ((), ())), preferred_element_...]
    unnamed x8 -> x10, local copies, waits for them, and re-layouts: 0.04 us -> 4.04 us
    convert_element_type x3 -> x1, other arithmetic: 4.95 us -> 1.95 us  [standardize(): return jnp.where(present, spread, 0.0).astype(jnp.bfloat16)]
    ppermute x10 -> x8, waiting for transfers between devices: 20.6 us -> 17.9 us  [swap(): return lax.ppermute(shard, axis, [(i, i ^ bit) for i in range(peers)])]
    pallas_call x1, Pallas kernels: 7.06 us -> 5.16 us  [head(): pl.pallas_call(head_kernel, grid=(samples // block,), out_shape=tuple((li...]
  transfers between devices with their start and end apart: 18 -> 16, of which waited for: 9 -> 9; matrix products, arithmetic and copies ran while one was open for 18% -> 7% of each run, Pallas kernels for 0% -> 5%
where the time goes in v4:
time: 102 us; the launch traced here: 101 us
  waiting for transfers between devices  49 us (48%)
  starting transfers between devices  25.3 us (25%)
  Pallas kernels  14.1 us (14%)
  other arithmetic  6.31 us (6%)
  local copies, waits for them, and re-layouts  4.34 us (4%)
  matrix products  1.28 us (1%)
    ppermute x3, waiting for transfers between devices, from_below(): return lax.ppermute(shard, axis, [(i, i + 1) for i in range(peers - 2)])  19.5 us
    ppermute x8, waiting for transfers between devices, swap(): return lax.ppermute(shard, axis, [(i, i ^ bit) for i in range(peers)])  17.9 us
    ppermute x3, starting transfers between devices, from_below(): return lax.ppermute(shard, axis, [(i, i + 1) for i in range(peers - 2)])  12.5 us
    ppermute x5, waiting for transfers between devices, from_above(): return lax.ppermute(shard, axis, [(i, i - 1) for i in range(1, peers)])  11.6 us
    ppermute x5, starting transfers between devices, from_above(): return lax.ppermute(shard, axis, [(i, i - 1) for i in range(1, peers)])  6.44 us
    ppermute x8, starting transfers between devices, swap(): return lax.ppermute(shard, axis, [(i, i ^ bit) for i in range(peers)])  6.39 us
    pallas_call x1, Pallas kernels, head(): pl.pallas_call(head_kernel, grid=(samples // block,), out_shape=tuple((li...  5.16 us
    pallas_call x1, Pallas kernels, first_pass(): pl.pallas_call(first_kernel, grid=(samples // block,), out_shape=(like(ta...  4.92 us
  transfers between devices with their start and end apart: 16, of which 9 were waited for; matrix products, arithmetic and copies ran while one was open for 7% of the time, Pallas kernels for 5%

profile of v4, /device:TPU:0, one launch (start us, length us, event | category | flops | bytes accessed | tf_op | source)
XLA Modules:
  0.0 101.3 jit_solution(373130999165623718)
XLA Ops:
  0.0 1.0 %copy-done.2 = bf16[512,512]{1,0:T(8,128)(2,1)S(1)} copy-done((bf16[512,512]{1,0:T(8,128)(2,1)S(1)}, bf16[512,512]{1,0:T(8,128)(2,1)}, u32[]{:S(2)}) %copy-start.2) | copy-done | bytes 524312
  1.7 5.2 %head.1 = (bf16[2048,384]{1,0:T(8,128)(2,1)}, bf16[2048,128]{1,0:T(8,128)(2,1)}, bf16[2048,384]{1,0:T(8,128)(2,1)}, bf16[2048,128]{1,0:T(8,128)(2,1)}, f32[8,512]{1,0:T(8,128)S(1)}) custom-call(bf16[2048,512]{1,0:T(8,128)(2,1)} %dosage_ref.1, s32[1,2048]{1,0:T(1,128)S(1)} %copy-done.3, bf16[512,512]{1,0:T(8,128)(2,1)S(1)} %copy-done.2), custom_call_target="tpu_custom_call" | custom-call | tf_op jit(solution)/shard_map/head/pallas_call | solution.py:102
  7.4 5.7 %collective-permute-start.5 = (bf16[2048,384]{1,0:T(8,128)(2,1)}, bf16[2048,384]{1,0:T(8,128)(2,1)}, u32[]{:S(2)}, u32[]{:S(2)}) collective-permute-start(bf16[2048,384]{1,0:T(8,128)(2,1)} %get-tuple-element.15), channel_id=1, source_target_pairs={{0,1},{1,2},{4,5},{5,6},{8,9},{9,10},{12,13},{13,14},{16,17},{17,1... | collective-permute-start | bytes 4718600 | tf_op jit(solution)/shard_map/ppermute | solution.py:24
  13.1 1.3 %collective-permute-start.4 = (bf16[2048,384]{1,0:T(8,128)(2,1)}, bf16[2048,384]{1,0:T(8,128)(2,1)}, u32[]{:S(2)}, u32[]{:S(2)}) collective-permute-start(bf16[2048,384]{1,0:T(8,128)(2,1)} %get-tuple-element.14.coded_ref), channel_id=1, source_target_pairs={{1,0},{2,1},{3,2},{5,4},{6,5},{7,6},{9,8},{10,9},{11,10},{13,12},{... | collective-permute-start | bytes 4718600 | tf_op jit(solution)/shard_map/ppermute | solution.py:19
  14.4 1.6 %collective-permute-start.1 = (f32[8,512]{1,0:T(8,128)S(1)}, f32[8,512]{1,0:T(8,128)S(1)}, u32[]{:S(2)}, u32[]{:S(2)}) collective-permute-start(f32[8,512]{1,0:T(8,128)S(1)} %add.30), channel_id=1, source_target_pairs={{0,8},{4,12},{8,0},{12,4},{1,9},{5,13},{9,1},{13,5},{2,10},{6,14},... | collective-permute-start | bytes 49160 | tf_op jit(solution)/shard_map/ppermute | solution.py:29
  16.0 2.2 %collective-permute-done.1 = f32[8,512]{1,0:T(8,128)S(1)} collective-permute-done((f32[8,512]{1,0:T(8,128)S(1)}, f32[8,512]{1,0:T(8,128)S(1)}, u32[]{:S(2)}, u32[]{:S(2)}) %collective-permute-start.1) | collective-permute-done | bytes 16416 | tf_op jit(solution)/shard_map/ppermute | solution.py:29
  18.2 2.0 %select_convert_fusion.own_ref = bf16[2048,512]{1,0:T(8,128)(2,1)S(1)} fusion(bf16[2048,512]{1,0:T(8,128)(2,1)} %dosage_ref.1, f32[512]{0:T(512)S(1)} %bitcast.124, f32[512]{0:T(512)S(1)} %bitcast.125, pred[2048]{0:T(1024)(128)(4,1)S(1)} %compare_reduce_fusion), kind=kLoop, calls=%fused_computation | loop fusion | flops 5242880 | bytes 4200448 | tf_op jit(solution)/shard_map/convert_element_type | solution.py:127
  20.2 1.3 %fusion.11 = f32[512,512]{1,0:T(8,128)S(1)} fusion(bf16[2048,512]{1,0:T(8,128)(2,1)S(1)} %select_convert_fusion.own_ref), kind=kOutput, calls=%fused_computation.50 | convolution fusion | flops 1073741824 | bytes 3145728 | tf_op jit(solution)/shard_map/dot_general | solution.py:142
  21.4 1.0 %select_bitcast_fusion.1 = f32[2,128,512]{2,1,0:T(8,128)} fusion(f32[2,2,128,512]{3,2,1,0:T(8,128)S(1)} %bitcast.121, pred[]{:T(512)S(6)} %ne.24), kind=kLoop, calls=%fused_computation.11 | loop fusion | flops 131072 | bytes 1572865 | tf_op jit(solution)/shard_map/jit(_where)/select_n | solution.py:48
  22.5 4.5 %collective-permute-start.7 = (f32[2,512]{1,0:T(2,128)S(1)}, f32[2,512]{1,0:T(2,128)S(1)}, u32[]{:S(2)}, u32[]{:S(2)}) collective-permute-start(f32[2,512]{1,0:T(2,128)S(1)} %pad_maximum_fusion), channel_id=1, source_target_pairs={{0,1},{1,2},{4,5},{5,6},{8,9},{9,10},{12,13},{13,14},{16,17},{17,1... | collective-permute-start | bytes 12296 | tf_op jit(solution)/shard_map/ppermute | solution.py:24
  27.1 1.3 %collective-permute-start.6 = (f32[2,512]{1,0:T(2,128)S(1)}, f32[2,512]{1,0:T(2,128)S(1)}, u32[]{:S(2)}, u32[]{:S(2)}) collective-permute-start(f32[2,512]{1,0:T(2,128)S(1)} %pad_maximum_fusion), channel_id=1, source_target_pairs={{1,0},{2,1},{3,2},{5,4},{6,5},{7,6},{9,8},{10,9},{11,10},{13,12},{... | collective-permute-start | bytes 12296 | tf_op jit(solution)/shard_map/ppermute | solution.py:19
  28.4 18.2 %collective-permute-done.7 = f32[2,512]{1,0:T(2,128)S(1)} collective-permute-done((f32[2,512]{1,0:T(2,128)S(1)}, f32[2,512]{1,0:T(2,128)S(1)}, u32[]{:S(2)}, u32[]{:S(2)}) %collective-permute-start.7) | collective-permute-done | bytes 4128 | tf_op jit(solution)/shard_map/ppermute | solution.py:24
  46.5 1.3 %collective-permute-start.10 = (bf16[2048,128]{1,0:T(8,128)(2,1)}, bf16[2048,128]{1,0:T(8,128)(2,1)S(1)}, u32[]{:S(2)}, u32[]{:S(2)}) collective-permute-start(bf16[2048,128]{1,0:T(8,128)(2,1)} %get-tuple-element.17), channel_id=1, source_target_pairs={{1,0},{2,1},{3,2},{5,4},{6,5},{7,6},{9,8},{10,9},{11,10},{13,12},{... | collective-permute-start | bytes 1572872 | tf_op jit(solution)/shard_map/ppermute | solution.py:19
  47.8 4.1 %collective-permute-done.6 = f32[2,512]{1,0:T(2,128)S(1)} collective-permute-done((f32[2,512]{1,0:T(2,128)S(1)}, f32[2,512]{1,0:T(2,128)S(1)}, u32[]{:S(2)}, u32[]{:S(2)}) %collective-permute-start.6) | collective-permute-done | bytes 4128 | tf_op jit(solution)/shard_map/ppermute | solution.py:19
  51.9 2.2 %collective-permute-start.11 = (bf16[2048,128]{1,0:T(8,128)(2,1)}, bf16[2048,128]{1,0:T(8,128)(2,1)S(1)}, u32[]{:S(2)}, u32[]{:S(2)}) collective-permute-start(bf16[2048,128]{1,0:T(8,128)(2,1)} %get-tuple-element.18), channel_id=1, source_target_pairs={{0,1},{1,2},{4,5},{5,6},{8,9},{9,10},{12,13},{13,14},{16,17},{17,1... | collective-permute-start | bytes 1572872 | tf_op jit(solution)/shard_map/ppermute | solution.py:24
  55.1 1.5 %fusion.1 = f32[1,2,128,512]{3,2,1,0:T(8,128)S(1)} fusion(f32[2,128,512]{2,1,0:T(8,128)} %collective-permute-done.2, f32[2,2,128,512]{3,2,1,0:T(8,128)} %bitcast.122, pred[]{:T(512)S(6)} %ne.24), kind=kLoop, calls=%fused_computation.10 | loop fusion | flops 262144 | bytes 2097153 | tf_op jit(solution)/shard_map/reshape | solution.py:45
  56.6 4.9 %first.1 = (f32[4,232,384]{2,1,0:T(8,128)S(1)}, bf16[2048,384]{1,0:T(8,128)(2,1)S(1)}, bf16[2048,384]{1,0:T(8,128)(2,1)S(1)}) custom-call(bf16[2048,384]{1,0:T(8,128)(2,1)} %get-tuple-element.14.coded_ref, bf16[2048,384]{1,0:T(8,128)(2,1)} %collective-permute-done.4.above_ref, bf16[2048,384]{1,0:T(8,128)(2,1)} %collective-permute-done.5.below_ref, ...), custom_call_target="tpu_custom_call" | custom-call | flops 1409286144 | bytes 9437184 | tf_op jit(solution)/shard_map/first/pallas_call | solution.py:187
  61.6 1.2 %copy-done = bf16[2048,384]{1,0:T(8,128)(2,1)} copy-done((bf16[2048,384]{1,0:T(8,128)(2,1)}, bf16[2048,384]{1,0:T(8,128)(2,1)S(1)}, u32[]{:S(2)}) %copy-start) | copy-done | bytes 1572888
  62.7 1.1 %copy-done.1 = bf16[2048,384]{1,0:T(8,128)(2,1)} copy-done((bf16[2048,384]{1,0:T(8,128)(2,1)}, bf16[2048,384]{1,0:T(8,128)(2,1)S(1)}, u32[]{:S(2)}) %copy-start.1) | copy-done | bytes 1572888
  63.9 1.3 %collective-permute-done.11.below_ref = bf16[2048,128]{1,0:T(8,128)(2,1)S(1)} collective-permute-done((bf16[2048,128]{1,0:T(8,128)(2,1)}, bf16[2048,128]{1,0:T(8,128)(2,1)S(1)}, u32[]{:S(2)}, u32[]{:S(2)}) %collective-permute-start.11) | collective-permute-done | bytes 524320 | tf_op jit(solution)/shard_map/ppermute | solution.py:24
  65.2 4.1 %second.1 = f32[4,352,128]{2,1,0:T(8,128)S(1)} custom-call(bf16[2048,128]{1,0:T(8,128)(2,1)S(1)} %collective-permute-done.10.above_ref, bf16[2048,128]{1,0:T(8,128)(2,1)S(1)} %collective-permute-done.11.below_ref, bf16[2048,384]{1,0:T(8,128)(2,1)} %copy-done, bf16[2048,384]{1,0:T(8,128)(2,1)} %copy-done.1, bf16[2048,512]{1,0:T(8,128)(2,1)S(1)} %select_convert_fusion.own_ref, ...), custom_call_target="tpu_custom_call" | custom-call | flops 738197504 | bytes 5767168 | tf_op jit(solution)/shard_map/second/pallas_call | solution.py:237
  70.0 1.6 %collective-permute-start.3 = (f32[1,128,512]{2,1,0:T(8,128)S(1)}, f32[1,128,512]{2,1,0:T(8,128)S(1)}, u32[]{:S(2)}, u32[]{:S(2)}) collective-permute-start(f32[1,128,512]{2,1,0:T(8,128)S(1)} %select_bitcast_fusion.4), channel_id=1, source_target_pairs={{0,8},{4,12},{8,0},{12,4},{1,9},{5,13},{9,1},{13,5},{2,10},{6,14},... | collective-permute-start | bytes 786440 | tf_op jit(solution)/shard_map/ppermute | solution.py:29
  71.7 1.0 collective-permute-start.13
  72.9 1.2 %collective-permute-start.9 = (f32[1,232,384]{2,1,0:T(8,128)S(1)}, f32[1,232,384]{2,1,0:T(8,128)S(1)}, u32[]{:S(2)}, u32[]{:S(2)}) collective-permute-start(f32[1,232,384]{2,1,0:T(8,128)S(1)} %select_bitcast_fusion.3), channel_id=1, source_target_pairs={{0,8},{4,12},{8,0},{12,4},{1,9},{5,13},{9,1},{13,5},{2,10},{6,14},... | collective-permute-start | bytes 1069064 | tf_op jit(solution)/shard_map/ppermute | solution.py:29
  74.0 5.2 %collective-permute-done.3 = f32[1,128,512]{2,1,0:T(8,128)S(1)} collective-permute-done((f32[1,128,512]{2,1,0:T(8,128)S(1)}, f32[1,128,512]{2,1,0:T(8,128)S(1)}, u32[]{:S(2)}, u32[]{:S(2)}) %collective-permute-start.3) | collective-permute-done | bytes 262176 | tf_op jit(solution)/shard_map/ppermute | solution.py:29
  79.4 3.8 %collective-permute-done.13 = f32[1,352,128]{2,1,0:T(8,128)S(1)} collective-permute-done((f32[1,352,128]{2,1,0:T(8,128)S(1)}, f32[1,352,128]{2,1,0:T(8,128)S(1)}, u32[]{:S(2)}, u32[]{:S(2)}) %collective-permute-start.13) | collective-permute-done | bytes 180256 | tf_op jit(solution)/shard_map/ppermute | solution.py:29
  83.2 6.7 %collective-permute-done.9 = f32[1,232,384]{2,1,0:T(8,128)S(1)} collective-permute-done((f32[1,232,384]{2,1,0:T(8,128)S(1)}, f32[1,232,384]{2,1,0:T(8,128)S(1)}, u32[]{:S(2)}, u32[]{:S(2)}) %collective-permute-start.9) | collective-permute-done | bytes 356384 | tf_op jit(solution)/shard_map/ppermute | solution.py:29
  90.0 1.3 %collective-permute-start.15 = (f32[224,128]{1,0:T(8,128)S(1)}, f32[224,128]{1,0:T(8,128)S(1)}, u32[]{:S(2)}, u32[]{:S(2)}) collective-permute-start(f32[224,128]{1,0:T(8,128)S(1)} %fusion.6), channel_id=1, source_target_pairs={{1,0},{2,1},{3,2},{5,4},{6,5},{7,6},{9,8},{10,9},{11,10},{13,12},{... | collective-permute-start | bytes 344072 | tf_op jit(solution)/shard_map/ppermute | solution.py:19
  91.4 1.3 %collective-permute-start.14 = (f32[96,384]{1,0:T(8,128)S(1)}, f32[96,384]{1,0:T(8,128)S(1)}, u32[]{:S(2)}, u32[]{:S(2)}) collective-permute-start(f32[96,384]{1,0:T(8,128)S(1)} %fusion.5), channel_id=1, source_target_pairs={{1,0},{2,1},{3,2},{5,4},{6,5},{7,6},{9,8},{10,9},{11,10},{13,12},{... | collective-permute-start | bytes 442376 | tf_op jit(solution)/shard_map/ppermute | solution.py:19
  92.7 5.1 %collective-permute-done.15 = f32[224,128]{1,0:T(8,128)S(1)} collective-permute-done((f32[224,128]{1,0:T(8,128)S(1)}, f32[224,128]{1,0:T(8,128)S(1)}, u32[]{:S(2)}, u32[]{:S(2)}) %collective-permute-start.15) | collective-permute-done | bytes 114720 | tf_op jit(solution)/shard_map/ppermute | solution.py:19
  97.8 2.4 %collective-permute-done.14 = f32[96,384]{1,0:T(8,128)S(1)} collective-permute-done((f32[96,384]{1,0:T(8,128)S(1)}, f32[96,384]{1,0:T(8,128)S(1)}, u32[]{:S(2)}, u32[]{:S(2)}) %collective-permute-start.14) | collective-permute-done | bytes 147488 | tf_op jit(solution)/shard_map/ppermute | solution.py:19
  100.2 1.0 %maximum_select_fusion = f32[1,128,3,512]{3,1,2,0:T(8,128)} fusion(f32[1,128,1,512]{3,1,2,0:T(8,128)S(1)} %maximum_bitcast_fusion.1, f32[1,128,1,512]{3,1,2,0:T(8,128)S(1)} %maximum_bitcast_fusion, f32[1,128,1,512]{3,1,2,0:T(8,128)S(1)} %fusion.3, pred[3]{0:T(512)(128)(4,1)S(1)} %iota_compare_fusion), kind=kLoop, calls=%fused_computation.1 | loop fusion | flops 589824 | bytes 1572867 | tf_op jit(solution)/shard_map/jit(_where)/select_n | solution.py:308
  (51 shorter events, 2.9 us)
Async XLA Ops:
  0.0 1.0 %copy-start.2 = (bf16[512,512]{1,0:T(8,128)(2,1)S(1)}, bf16[512,512]{1,0:T(8,128)(2,1)}, u32[]{:S(2)}) copy-start(bf16[512,512]{1,0:T(8,128)(2,1)} %constant.21.clone.order_ref) | copy-start | bytes 1572868
  1.0 0.7 copy-start.3
  6.9 7.5 %collective-permute-start = (f32[8,512]{1,0:T(8,128)S(1)}, f32[8,512]{1,0:T(8,128)S(1)}, u32[]{:S(2)}, u32[]{:S(2)}) collective-permute-start(f32[8,512]{1,0:T(8,128)S(1)} %get-tuple-element.13), channel_id=1, source_target_pairs={{0,4},{4,0},{8,12},{12,8},{1,5},{5,1},{9,13},{13,9},{2,6},{6,2},{1... | collective-permute-start | bytes 49160 | tf_op jit(solution)/shard_map/ppermute | solution.py:29
  7.4 49.2 %collective-permute-start.5 = (bf16[2048,384]{1,0:T(8,128)(2,1)}, bf16[2048,384]{1,0:T(8,128)(2,1)}, u32[]{:S(2)}, u32[]{:S(2)}) collective-permute-start(bf16[2048,384]{1,0:T(8,128)(2,1)} %get-tuple-element.15), channel_id=1, source_target_pairs={{0,1},{1,2},{4,5},{5,6},{8,9},{9,10},{12,13},{13,14},{16,17},{17,1... | collective-permute-start | bytes 4718600 | tf_op jit(solution)/shard_map/ppermute | solution.py:24
  13.1 43.6 %collective-permute-start.4 = (bf16[2048,384]{1,0:T(8,128)(2,1)}, bf16[2048,384]{1,0:T(8,128)(2,1)}, u32[]{:S(2)}, u32[]{:S(2)}) collective-permute-start(bf16[2048,384]{1,0:T(8,128)(2,1)} %get-tuple-element.14.coded_ref), channel_id=1, source_target_pairs={{1,0},{2,1},{3,2},{5,4},{6,5},{7,6},{9,8},{10,9},{11,10},{13,12},{... | collective-permute-start | bytes 4718600 | tf_op jit(solution)/shard_map/ppermute | solution.py:19
  14.4 3.8 %collective-permute-start.1 = (f32[8,512]{1,0:T(8,128)S(1)}, f32[8,512]{1,0:T(8,128)S(1)}, u32[]{:S(2)}, u32[]{:S(2)}) collective-permute-start(f32[8,512]{1,0:T(8,128)S(1)} %add.30), channel_id=1, source_target_pairs={{0,8},{4,12},{8,0},{12,4},{1,9},{5,13},{9,1},{13,5},{2,10},{6,14},... | collective-permute-start | bytes 49160 | tf_op jit(solution)/shard_map/ppermute | solution.py:29
  21.4 30.5 %copy-start.4 = (f32[512,512]{1,0:T(8,128)}, f32[512,512]{1,0:T(8,128)S(1)}, u32[]{:S(2)}) copy-start(f32[512,512]{1,0:T(8,128)S(1)} %fusion.11) | copy-start | bytes 3145732
  22.5 32.6 %collective-permute-start.2 = (f32[2,128,512]{2,1,0:T(8,128)}, f32[2,128,512]{2,1,0:T(8,128)}, u32[]{:S(2)}, u32[]{:S(2)}) collective-permute-start(f32[2,128,512]{2,1,0:T(8,128)} %select_bitcast_fusion.1), channel_id=1, source_target_pairs={{0,4},{4,0},{8,12},{12,8},{1,5},{5,1},{9,13},{13,9},{2,6},{6,2},{1... | collective-permute-start | bytes 1572872 | tf_op jit(solution)/shard_map/ppermute | solution.py:29
  22.5 24.0 %collective-permute-start.7 = (f32[2,512]{1,0:T(2,128)S(1)}, f32[2,512]{1,0:T(2,128)S(1)}, u32[]{:S(2)}, u32[]{:S(2)}) collective-permute-start(f32[2,512]{1,0:T(2,128)S(1)} %pad_maximum_fusion), channel_id=1, source_target_pairs={{0,1},{1,2},{4,5},{5,6},{8,9},{9,10},{12,13},{13,14},{16,17},{17,1... | collective-permute-start | bytes 12296 | tf_op jit(solution)/shard_map/ppermute | solution.py:24
  27.1 24.8 %collective-permute-start.6 = (f32[2,512]{1,0:T(2,128)S(1)}, f32[2,512]{1,0:T(2,128)S(1)}, u32[]{:S(2)}, u32[]{:S(2)}) collective-permute-start(f32[2,512]{1,0:T(2,128)S(1)} %pad_maximum_fusion), channel_id=1, source_target_pairs={{1,0},{2,1},{3,2},{5,4},{6,5},{7,6},{9,8},{10,9},{11,10},{13,12},{... | collective-permute-start | bytes 12296 | tf_op jit(solution)/shard_map/ppermute | solution.py:19
  46.5 17.3 %collective-permute-start.10 = (bf16[2048,128]{1,0:T(8,128)(2,1)}, bf16[2048,128]{1,0:T(8,128)(2,1)S(1)}, u32[]{:S(2)}, u32[]{:S(2)}) collective-permute-start(bf16[2048,128]{1,0:T(8,128)(2,1)} %get-tuple-element.17), channel_id=1, source_target_pairs={{1,0},{2,1},{3,2},{5,4},{6,5},{7,6},{9,8},{10,9},{11,10},{13,12},{... | collective-permute-start | bytes 1572872 | tf_op jit(solution)/shard_map/ppermute | solution.py:19
  51.9 13.3 %collective-permute-start.11 = (bf16[2048,128]{1,0:T(8,128)(2,1)}, bf16[2048,128]{1,0:T(8,128)(2,1)S(1)}, u32[]{:S(2)}, u32[]{:S(2)}) collective-permute-start(bf16[2048,128]{1,0:T(8,128)(2,1)} %get-tuple-element.18), channel_id=1, source_target_pairs={{0,1},{1,2},{4,5},{5,6},{8,9},{9,10},{12,13},{13,14},{16,17},{17,1... | collective-permute-start | bytes 1572872 | tf_op jit(solution)/shard_map/ppermute | solution.py:24
  61.6 1.2 %copy-start = (bf16[2048,384]{1,0:T(8,128)(2,1)}, bf16[2048,384]{1,0:T(8,128)(2,1)S(1)}, u32[]{:S(2)}) copy-start(bf16[2048,384]{1,0:T(8,128)(2,1)S(1)} %get-tuple-element.19.above_1) | copy-start | bytes 4718596
  62.7 1.1 %copy-start.1 = (bf16[2048,384]{1,0:T(8,128)(2,1)}, bf16[2048,384]{1,0:T(8,128)(2,1)S(1)}, u32[]{:S(2)}) copy-start(bf16[2048,384]{1,0:T(8,128)(2,1)S(1)} %get-tuple-element.20.below_1) | copy-start | bytes 4718596
  69.3 2.3 %collective-permute-start.12 = (f32[2,352,128]{2,1,0:T(8,128)S(1)}, f32[2,352,128]{2,1,0:T(8,128)S(1)}, u32[]{:S(2)}, u32[]{:S(2)}) collective-permute-start(f32[2,352,128]{2,1,0:T(8,128)S(1)} %select_bitcast_fusion.2), channel_id=1, source_target_pairs={{0,4},{4,0},{8,12},{12,8},{1,5},{5,1},{9,13},{13,9},{2,6},{6,2},{1... | collective-permute-start | bytes 1081352 | tf_op jit(solution)/shard_map/ppermute | solution.py:29
  69.4 3.2 %collective-permute-start.8 = (f32[2,232,384]{2,1,0:T(8,128)S(1)}, f32[2,232,384]{2,1,0:T(8,128)S(1)}, u32[]{:S(2)}, u32[]{:S(2)}) collective-permute-start(f32[2,232,384]{2,1,0:T(8,128)S(1)} %select_bitcast_fusion), channel_id=1, source_target_pairs={{0,4},{4,0},{8,12},{12,8},{1,5},{5,1},{9,13},{13,9},{2,6},{6,2},{1... | collective-permute-start | bytes 2138120 | tf_op jit(solution)/shard_map/ppermute | solution.py:29
  70.0 9.2 %collective-permute-start.3 = (f32[1,128,512]{2,1,0:T(8,128)S(1)}, f32[1,128,512]{2,1,0:T(8,128)S(1)}, u32[]{:S(2)}, u32[]{:S(2)}) collective-permute-start(f32[1,128,512]{2,1,0:T(8,128)S(1)} %select_bitcast_fusion.4), channel_id=1, source_target_pairs={{0,8},{4,12},{8,0},{12,4},{1,9},{5,13},{9,1},{13,5},{2,10},{6,14},... | collective-permute-start | bytes 786440 | tf_op jit(solution)/shard_map/ppermute | solution.py:29
  71.7 11.4 %collective-permute-start.13 = (f32[1,352,128]{2,1,0:T(8,128)S(1)}, f32[1,352,128]{2,1,0:T(8,128)S(1)}, u32[]{:S(2)}, u32[]{:S(2)}) collective-permute-start(f32[1,352,128]{2,1,0:T(8,128)S(1)} %select_bitcast_fusion.5), channel_id=1, source_target_pairs={{0,8},{4,12},{8,0},{12,4},{1,9},{5,13},{9,1},{13,5},{2,10},{6,14},... | collective-permute-start | bytes 540680 | tf_op jit(solution)/shard_map/ppermute | solution.py:29
  72.9 17.0 %collective-permute-start.9 = (f32[1,232,384]{2,1,0:T(8,128)S(1)}, f32[1,232,384]{2,1,0:T(8,128)S(1)}, u32[]{:S(2)}, u32[]{:S(2)}) collective-permute-start(f32[1,232,384]{2,1,0:T(8,128)S(1)} %select_bitcast_fusion.3), channel_id=1, source_target_pairs={{0,8},{4,12},{8,0},{12,4},{1,9},{5,13},{9,1},{13,5},{2,10},{6,14},... | collective-permute-start | bytes 1069064 | tf_op jit(solution)/shard_map/ppermute | solution.py:29
  90.0 7.8 %collective-permute-start.15 = (f32[224,128]{1,0:T(8,128)S(1)}, f32[224,128]{1,0:T(8,128)S(1)}, u32[]{:S(2)}, u32[]{:S(2)}) collective-permute-start(f32[224,128]{1,0:T(8,128)S(1)} %fusion.6), channel_id=1, source_target_pairs={{1,0},{2,1},{3,2},{5,4},{6,5},{7,6},{9,8},{10,9},{11,10},{13,12},{... | collective-permute-start | bytes 344072 | tf_op jit(solution)/shard_map/ppermute | solution.py:19
  91.4 8.9 %collective-permute-start.14 = (f32[96,384]{1,0:T(8,128)S(1)}, f32[96,384]{1,0:T(8,128)S(1)}, u32[]{:S(2)}, u32[]{:S(2)}) collective-permute-start(f32[96,384]{1,0:T(8,128)S(1)} %fusion.5), channel_id=1, source_target_pairs={{1,0},{2,1},{3,2},{5,4},{6,5},{7,6},{9,8},{10,9},{11,10},{13,12},{... | collective-permute-start | bytes 442376 | tf_op jit(solution)/shard_map/ppermute | solution.py:19

commit v5 on v4

v5 whole, which is shorter than its diff:
```python
import jax
import jax.numpy as jnp
import numpy as np
from jax import lax
from jax.experimental import pallas as pl
from jax.experimental.pallas import tpu as pltpu
from jax.sharding import PartitionSpec as P

BAND = 3


EPSILON = 1e-05


def from_above(shard, axis):
    peers = lax.axis_size(axis)
    return lax.ppermute(shard, axis, [(i, i - 1) for i in range(1, peers)])


def from_below(shard, axis):
    peers = lax.axis_size(axis)
    return lax.ppermute(shard, axis, [(i, i + 1) for i in range(peers - 2)])


def swap(shard, axis, bit):
    peers = lax.axis_size(axis)
    return lax.ppermute(shard, axis, [(i, i ^ bit) for i in range(peers)])


def bits_of(peers):
    return [1 << k for k in range(peers.bit_length() - 1)]


def sum_all(value, axis):
    for bit in bits_of(lax.axis_size(axis)):
        value = value + swap(value, axis, bit)
    return value


def sum_rows(partial, axis):
    place = lax.axis_index(axis)
    for bit in bits_of(lax.axis_size(axis)):
        pairs = partial.reshape(partial.shape[0] // 2, 2, *partial.shape[1:])
        high = (place & bit) != 0
        keep = jnp.where(high, pairs[:, 1], pairs[:, 0])
        give = jnp.where(high, pairs[:, 0], pairs[:, 1])
        partial = keep + swap(give, axis, bit)
    return partial[0]


GRANT = 20 << 20


def block_of(samples):
    return 512 if samples % 512 == 0 else samples


def in_hbm(array):
    return pltpu.with_memory_space_constraint(array, pltpu.HBM)


def like(shape, dtype):
    return jax.ShapeDtypeStruct(shape, dtype)


def mask_of(row):
    lanes = 128
    return jnp.transpose(jnp.broadcast_to(row.astype(jnp.float32), (lanes, row.shape[1]))) > 0.5


def head_kernel(dosage_ref, order_ref, up_ref, down_ref, chosen_ref):
    @pl.when(pl.program_id(0) == 0)
    def _():
        rows = lax.broadcasted_iota(jnp.int32, chosen_ref.shape, 0)
        chosen_ref[...] = jnp.where(rows == order_ref[...], 1.0, 0.0).astype(jnp.bfloat16)

    down_ref[...] = dosage_ref[:, : down_ref.shape[1]]
    up = jnp.dot(dosage_ref[...], chosen_ref[...], preferred_element_type=jnp.float32)
    up_ref[...] = up.astype(jnp.bfloat16)


def head_pass(dosage, order):
    samples, width = dosage.shape
    block, edge = block_of(samples), order.shape[1]
    return pl.pallas_call(
        head_kernel,
        grid=(samples // block,),
        out_shape=(like((samples, edge), jnp.bfloat16),) * 2,
        in_specs=[
            pl.BlockSpec((block, width), lambda i: (i, 0)),
            pl.BlockSpec((1, edge), lambda i: (0, 0)),
        ],
        out_specs=(pl.BlockSpec((block, edge), lambda i: (i, 0)),) * 2,
        scratch_shapes=[pltpu.VMEM((width, edge), jnp.bfloat16)],
        compiler_params=pltpu.CompilerParams(vmem_limit_bytes=GRANT),
        name="head",
    )(in_hbm(dosage), in_hbm(order))


def moments_kernel(dosage_ref, observed_ref, chosen_ref, down_2, up_2, sums_ref):
    width = dosage_ref.shape[1]
    lanes = 128

    @pl.when(pl.program_id(0) == 0)
    def _():
        sums_ref[...] = jnp.zeros_like(sums_ref)

    present = mask_of(observed_ref[...])
    count = jnp.sum(jnp.where(present, 1.0, 0.0), axis=0, keepdims=True)
    for low in range(0, width, lanes):
        part = slice(low, low + lanes)
        kept = jnp.where(present, dosage_ref[:, part].astype(jnp.float32), 0.0)
        sums_ref[0:1, part] += jnp.sum(kept, axis=0, keepdims=True)
        sums_ref[1:2, part] += jnp.sum(kept * kept, axis=0, keepdims=True)
        sums_ref[2:3, part] += count
    down_2[...] = dosage_ref[:, width - down_2.shape[1] :]
    up = jnp.dot(dosage_ref[...], chosen_ref[...], preferred_element_type=jnp.float32)
    up_2[...] = up.astype(jnp.bfloat16)


def moments_pass(dosage, observed, chosen):
    samples, width = dosage.shape
    block, rest = block_of(samples), chosen.shape[1]
    return pl.pallas_call(
        moments_kernel,
        grid=(samples // block,),
        out_shape=(like((samples, rest), jnp.bfloat16),) * 2 + (like((8, width), jnp.float32),),
        in_specs=[
            pl.BlockSpec((block, width), lambda i: (i, 0)),
            pl.BlockSpec((1, block), lambda i: (0, i)),
            pl.BlockSpec((width, rest), lambda i: (0, 0)),
        ],
        out_specs=(pl.BlockSpec((block, rest), lambda i: (i, 0)),) * 2
        + (pl.BlockSpec((8, width), lambda i: (0, 0)),),
        compiler_params=pltpu.CompilerParams(vmem_limit_bytes=GRANT),
        cost_estimate=pl.CostEstimate(
            flops=2 * samples * width * rest,
            bytes_accessed=2 * samples * (width + 2 * rest),
            transcendentals=0,
        ),
        name="moments",
    )(in_hbm(dosage), observed, chosen)


def finish_moments(sums):
    centre = sums[0:1] / sums[2:3]
    spread_inverse = 1.0 / jnp.sqrt(sums[1:2] / sums[2:3] - centre * centre + EPSILON)
    return jnp.concatenate([centre, spread_inverse], axis=0)


def flags_in(facts_ref, block):
    start = pl.multiple_of(pl.program_id(0) * block, block)
    return mask_of(facts_ref[2:3, pl.ds(start, block)])


def standardize(values, present, moments):
    spread = (values.astype(jnp.float32) - moments[0:1]) * moments[1:2]
    return jnp.where(present, spread, 0.0).astype(jnp.bfloat16)


def decode(ref, facts_ref, present, first):
    parts = []
    for low in range(0, ref.shape[1], present.shape[1]):
        part = slice(low, low + present.shape[1])
        place = slice(first + low, first + low + present.shape[1])
        spread = ref[:, part].astype(jnp.float32) - facts_ref[0:1, place]
        spread = spread * facts_ref[1:2, place]
        parts.append(jnp.where(present, spread, 0.0).astype(jnp.bfloat16))
    return parts[0] if len(parts) == 1 else jnp.concatenate(parts, axis=1)


def cross(left, right):
    return lax.dot_general(
        left, right, (((0,), (0,)), ((), ())), preferred_element_type=jnp.float32
    )


def first_kernel(
    observed_ref,
    above_ref,
    below_ref,
    own_ref,
    above_f,
    below_f,
    out_ref,
    above_out,
    below_out,
):
    peers, _, edge = out_ref.shape
    rows = own_ref.shape[1] // peers
    kept = edge // peers

    @pl.when(pl.program_id(0) == 0)
    def _():
        out_ref[...] = jnp.zeros_like(out_ref)

    own_present = mask_of(observed_ref[...])
    block = above_ref.shape[0]
    above_present = flags_in(above_f, block)
    below_present = flags_in(below_f, block)
    above = decode(above_ref, above_f, above_present, 0)
    below = decode(below_ref, below_f, below_present, 0)
    above_out[...] = above
    below_out[...] = below
    near = cross(own_ref[...], above)
    far = cross(below, above)
    shares = [
        jnp.sum(jnp.where(other & above_present, 1.0, 0.0), axis=0, keepdims=True)
        for other in (own_present, below_present)
    ]
    for k in range(peers):
        out_ref[k, :rows, :] += near[k * rows : (k + 1) * rows]
        out_ref[k, rows : rows + kept, :] += far[k * kept : (k + 1) * kept]
        for low in range(0, edge, 128):
            out_ref[k, rows + kept : rows + kept + 1, low : low + 128] += shares[0]
            out_ref[k, rows + kept + 1 : rows + kept + 2, low : low + 128] += shares[1]


def first_pass(observed, above, below, own, above_f, below_f, peers):
    samples, width = own.shape
    edge = above.shape[1]
    block = block_of(samples)
    tall = (peers, width // peers + edge // peers + 8, edge)

    def rows_of(cut):
        return pl.BlockSpec((block, cut), lambda i: (i, 0))

    flags = pl.BlockSpec(above_f.shape, lambda i: (0, 0))
    flops = 2 * samples * edge * (width + edge)
    return pl.pallas_call(
        first_kernel,
        grid=(samples // block,),
        out_shape=(like(tall, jnp.float32),) + (like((samples, edge), jnp.bfloat16),) * 2,
        in_specs=[pl.BlockSpec((1, block), lambda i: (0, i))]
        + [rows_of(edge), rows_of(edge), rows_of(width), flags, flags],
        out_specs=(pl.BlockSpec(tall, lambda i: (0, 0, 0)), rows_of(edge), rows_of(edge)),
        compiler_params=pltpu.CompilerParams(vmem_limit_bytes=GRANT),
        cost_estimate=pl.CostEstimate(
            flops=flops, bytes_accessed=12 * samples * edge, transcendentals=0
        ),
        name="first",
    )(observed, above, below, own, above_f, below_f)


def second_kernel(
    above_ref,
    below_ref,
    above_1,
    below_1,
    own_ref,
    above_f,
    below_f,
    out_ref,
):
    peers, _, rest = out_ref.shape
    width, edge = own_ref.shape[1], above_1.shape[1]
    rows, kept, tail = width // peers, edge // peers, rest // peers

    @pl.when(pl.program_id(0) == 0)
    def _():
        out_ref[...] = jnp.zeros_like(out_ref)

    block = above_ref.shape[0]
    above = decode(above_ref, above_f, flags_in(above_f, block), edge)
    below = decode(below_ref, below_f, flags_in(below_f, block), edge)
    near = cross(own_ref[...], above)
    far = cross(below_1[...], above)
    last = cross(below, above_1[...])
    corner = cross(below, above)
    for k in range(peers):
        out_ref[k, :rows, :] += near[k * rows : (k + 1) * rows]
        low = rows + kept
        out_ref[k, rows:low, :] += far[k * kept : (k + 1) * kept]
        for left in range(0, edge, rest):
            out_ref[k, low : low + tail, :] += last[k * tail : (k + 1) * tail, left : left + rest]
            low += tail
        out_ref[k, low : low + tail, :] += corner[k * tail : (k + 1) * tail]


def second_pass(
    above, below, above_1, below_1, own, above_f, below_f, peers
):
    samples, width = own.shape
    edge, rest = above_1.shape[1], above.shape[1]
    block = block_of(samples)
    tall = (peers, (width + edge + width) // peers, rest)

    def rows_of(cut):
        return pl.BlockSpec((block, cut), lambda i: (i, 0))

    flags = pl.BlockSpec(above_f.shape, lambda i: (0, 0))
    flops = 2 * samples * rest * (2 * width + edge)
    return pl.pallas_call(
        second_kernel,
        grid=(samples // block,),
        out_shape=like(tall, jnp.float32),
        in_specs=[rows_of(rest)] * 2 + [rows_of(edge)] * 2 + [rows_of(width)] + [flags] * 2,
        out_specs=pl.BlockSpec(tall, lambda i: (0, 0, 0)),
        compiler_params=pltpu.CompilerParams(vmem_limit_bytes=GRANT),
        cost_estimate=pl.CostEstimate(
            flops=flops, bytes_accessed=2 * samples * (2 * width + edge), transcendentals=0
        ),
        name="second",
    )(above, below, above_1, below_1, own, above_f, below_f)


def per_device(dosage, observed, band_reach):
    samples, width = dosage.shape
    peers = lax.axis_size("samp")
    rows = width // peers
    kept = 3 * rows // 4
    tail = rows - kept
    edge, rest = kept * peers, tail * peers
    owners = np.arange(peers)[:, None] * rows
    order = np.concatenate(
        [
            (owners + np.arange(0, kept)[None, :]).ravel(),
            (owners + np.arange(kept, rows)[None, :]).ravel(),
        ]
    )
    pieces = width // rest
    chosen = (np.arange(width)[:, None] == order[None, :]).astype(jnp.bfloat16)
    up_1, down_1 = head_pass(dosage, jnp.asarray(order[None, :edge], jnp.int32))
    below_1 = from_below(up_1, "var")
    above_1 = from_above(down_1, "var")
    down_2, up_2, sums = moments_pass(dosage, observed, chosen[:, edge:])
    sums = sum_all(sums, "samp")
    moments = finish_moments(sums)
    cuts = [(k * rows, k * rows + kept) for k in range(peers)]
    cuts += [(k * rows + kept, (k + 1) * rows) for k in range(peers)]
    ordered = jnp.concatenate([moments[:, low:high] for low, high in cuts], axis=1)
    above_f, below_f = [
        jnp.concatenate(
            [jnp.pad(part, ((0, 0), (0, samples - width))), observed.astype(jnp.float32)]
        )
        for part in (moments, ordered)
    ]
    below_f = from_below(below_f, "var")
    above_f = from_above(above_f, "var")
    below_2 = from_below(up_2, "var")
    above_2 = from_above(down_2, "var")
    own = standardize(dosage, (observed[0] != 0)[:, None], moments)
    own = lax.optimization_barrier(own)
    same = sum_rows(cross(own, own).reshape(peers, rows, width), "samp")
    one, above_1, below_1 = first_pass(
        observed, above_1, below_1, own, above_f, below_f, peers
    )
    one = sum_rows(one, "samp")
    shares = jnp.maximum(one[rows + kept :], 1.0)
    near_1 = one[:rows] / shares[0:1]
    far_1 = one[rows : rows + kept] / shares[1:2]
    far_1 = from_above(far_1, "var")
    two = second_pass(
        above_2, below_2, above_1, below_1, own, above_f, below_f, peers
    )
    two = sum_rows(two, "samp")
    far_2 = two[rows:] / shares[1:2, :rest]
    far_2 = from_above(far_2, "var")
    near = jnp.concatenate([near_1, two[:rows] / shares[0:1, :rest]], axis=1)
    low = [far_2[kept + k * tail : kept + (k + 1) * tail] for k in range(pieces)]
    far = jnp.concatenate(
        [
            jnp.concatenate([far_1, far_2[:kept]], axis=1),
            jnp.concatenate(low, axis=1),
        ],
        axis=0,
    )
    result = jnp.stack([same / jnp.maximum(sums[2:3], 1.0), near, far], axis=1)
    keep = jnp.arange(BAND, dtype=jnp.int32) <= band_reach[0]
    return jnp.where(keep[None, :, None], result, jnp.float32(0.0))[None]


def solution(mesh):
    return jax.shard_map(
        per_device,
        mesh=mesh,
        in_specs=(P("samp", ("seg", "var")), P(("seg", "var"), "samp"), P(("seg", "var"))),
        out_specs=P(("seg", "var"), "samp", None, None),
        check_vma=False,
    )
```

time: 102 us -> 109 us (1.069)
  waiting for transfers between devices: 49 us -> 52.2 us
  Pallas kernels: 14.1 us -> 16.8 us
  starting transfers between devices: 25.3 us -> 26.9 us
    ppermute x5, waiting for transfers between devices: 11.6 us -> 28.9 us  [from_above(): return lax.ppermute(shard, axis, [(i, i - 1) for i in range(1, peers)])]
    ppermute x3, waiting for transfers between devices: 19.5 us -> 5.87 us  [from_below(): return lax.ppermute(shard, axis, [(i, i + 1) for i in range(peers - 2)])]
    pallas_call x1 -> x2, Pallas kernels: 5.16 us -> 8.87 us  [the longest x1 4.79 us: head_pass(): pl.pallas_call(head_kernel, grid=(samples // block,), out_shape=(like((sa...]
    ppermute x3, starting transfers between devices: 12.5 us -> 13.7 us  [from_below(): return lax.ppermute(shard, axis, [(i, i + 1) for i in range(peers - 2)])]
  transfers between devices with their start and end apart: 16 -> 16, of which waited for: 9 -> 8; matrix products, arithmetic and copies ran while one was open for 7% -> 6% of each run, Pallas kernels for 5% -> 9%
where the time goes in v5:
time: 109 us; the launch traced here: 108 us
  waiting for transfers between devices  52.2 us (48%)
  starting transfers between devices  26.9 us (25%)
  Pallas kernels  16.8 us (15%)
  other arithmetic  6.32 us (6%)
  local copies, waits for them, and re-layouts  3.49 us (3%)
  matrix products  1.28 us (1%)
    ppermute x5, waiting for transfers between devices, from_above(): return lax.ppermute(shard, axis, [(i, i - 1) for i in range(1, peers)])  28.9 us
    ppermute x8, waiting for transfers between devices, swap(): return lax.ppermute(shard, axis, [(i, i ^ bit) for i in range(peers)])  17.5 us
    ppermute x3, starting transfers between devices, from_below(): return lax.ppermute(shard, axis, [(i, i + 1) for i in range(peers - 2)])  13.7 us
    ppermute x8, starting transfers between devices, swap(): return lax.ppermute(shard, axis, [(i, i ^ bit) for i in range(peers)])  6.74 us
    ppermute x5, starting transfers between devices, from_above(): return lax.ppermute(shard, axis, [(i, i - 1) for i in range(1, peers)])  6.45 us
    ppermute x3, waiting for transfers between devices, from_below(): return lax.ppermute(shard, axis, [(i, i + 1) for i in range(peers - 2)])  5.87 us
    pallas_call x1, Pallas kernels, head_pass(): pl.pallas_call(head_kernel, grid=(samples // block,), out_shape=(like((sa...  4.79 us
    pallas_call x1, Pallas kernels, first_pass(): pl.pallas_call(first_kernel, grid=(samples // block,), out_shape=(like(ta...  4.78 us
  transfers between devices with their start and end apart: 16, of which 8 were waited for; matrix products, arithmetic and copies ran while one was open for 6% of the time, Pallas kernels for 9%

profile of v5, /device:TPU:0, one launch (start us, length us, event | category | flops | bytes accessed | tf_op | source)
XLA Modules:
  0.0 107.9 jit_solution(16043124794919580144)
XLA Ops:
  0.7 0.9 copy-done.2
  1.6 4.1 %moments.1 = (bf16[2048,128]{1,0:T(8,128)(2,1)}, bf16[2048,128]{1,0:T(8,128)(2,1)S(1)}, f32[8,512]{1,0:T(8,128)S(1)}) custom-call(bf16[2048,512]{1,0:T(8,128)(2,1)} %dosage_ref.3, s32[1,2048]{1,0:T(1,128)S(1)} %copy-done, bf16[512,128]{1,0:T(8,128)(2,1)S(1)} %copy-done.2), custom_call_target="tpu_custom_call" | custom-call | flops 268435456 | bytes 3145728 | tf_op jit(solution)/shard_map/moments/pallas_call | solution.py:124
  5.7 0.8 copy-done.3
  7.0 4.8 %head.1 = (bf16[2048,384]{1,0:T(8,128)(2,1)}, bf16[2048,384]{1,0:T(8,128)(2,1)}) custom-call(bf16[2048,512]{1,0:T(8,128)(2,1)} %dosage_ref.3, s32[1,384]{1,0:T(1,128)} %constant.24.clone.order_ref), custom_call_target="tpu_custom_call" | custom-call | tf_op jit(solution)/shard_map/head/pallas_call | solution.py:85
  11.8 1.3 %collective-permute-start.4 = (bf16[2048,384]{1,0:T(8,128)(2,1)}, bf16[2048,384]{1,0:T(8,128)(2,1)}, u32[]{:S(2)}, u32[]{:S(2)}) collective-permute-start(bf16[2048,384]{1,0:T(8,128)(2,1)} %get-tuple-element.14), channel_id=1, source_target_pairs={{1,0},{2,1},{3,2},{5,4},{6,5},{7,6},{9,8},{10,9},{11,10},{13,12},{... | collective-permute-start | bytes 4718600 | tf_op jit(solution)/shard_map/ppermute | solution.py:17
  13.0 6.3 %collective-permute-start.5 = (bf16[2048,384]{1,0:T(8,128)(2,1)}, bf16[2048,384]{1,0:T(8,128)(2,1)}, u32[]{:S(2)}, u32[]{:S(2)}) collective-permute-start(bf16[2048,384]{1,0:T(8,128)(2,1)} %get-tuple-element.15), channel_id=1, source_target_pairs={{0,1},{1,2},{4,5},{5,6},{8,9},{9,10},{12,13},{13,14},{16,17},{17,1... | collective-permute-start | bytes 4718600 | tf_op jit(solution)/shard_map/ppermute | solution.py:22
  19.4 1.9 %collective-permute-start.1 = (f32[8,512]{1,0:T(8,128)S(1)}, f32[8,512]{1,0:T(8,128)S(1)}, u32[]{:S(2)}, u32[]{:S(2)}) collective-permute-start(f32[8,512]{1,0:T(8,128)S(1)} %add.34), channel_id=1, source_target_pairs={{0,8},{4,12},{8,0},{12,4},{1,9},{5,13},{9,1},{13,5},{2,10},{6,14},... | collective-permute-start | bytes 49160 | tf_op jit(solution)/shard_map/ppermute | solution.py:27
  21.3 1.8 %collective-permute-done.1 = f32[8,512]{1,0:T(8,128)S(1)} collective-permute-done((f32[8,512]{1,0:T(8,128)S(1)}, f32[8,512]{1,0:T(8,128)S(1)}, u32[]{:S(2)}, u32[]{:S(2)}) %collective-permute-start.1) | collective-permute-done | bytes 16416 | tf_op jit(solution)/shard_map/ppermute | solution.py:27
  23.1 2.0 %select_convert_fusion.own_ref = bf16[2048,512]{1,0:T(8,128)(2,1)S(1)} fusion(bf16[2048,512]{1,0:T(8,128)(2,1)} %dosage_ref.3, f32[512]{0:T(512)S(1)} %bitcast.122, f32[512]{0:T(512)S(1)} %bitcast.123, pred[2048]{0:T(1024)(128)(4,1)S(1)} %compare_reduce_fusion), kind=kLoop, calls=%fused_computation | loop fusion | flops 5242880 | bytes 4200448 | tf_op jit(solution)/shard_map/convert_element_type | solution.py:158
  25.1 1.3 %fusion.19 = f32[512,512]{1,0:T(8,128)S(1)} fusion(bf16[2048,512]{1,0:T(8,128)(2,1)S(1)} %select_convert_fusion.own_ref), kind=kOutput, calls=%fused_computation.77 | convolution fusion | flops 1073741824 | bytes 3145728 | tf_op jit(solution)/shard_map/dot_general | solution.py:173
  26.4 1.0 copy-done.4
  27.3 0.9 select_bitcast_fusion.1
  28.5 1.3 %collective-permute-start.6 = (f32[3,2048]{1,0:T(4,128)S(1)}, f32[3,2048]{1,0:T(4,128)S(1)}, u32[]{:S(2)}, u32[]{:S(2)}) collective-permute-start(f32[3,2048]{1,0:T(4,128)S(1)} %get-tuple-element.35), channel_id=1, source_target_pairs={{1,0},{2,1},{3,2},{5,4},{6,5},{7,6},{9,8},{10,9},{11,10},{13,12},{... | collective-permute-start | bytes 73736 | tf_op jit(solution)/shard_map/ppermute | solution.py:17
  29.8 1.3 %collective-permute-start.10 = (bf16[2048,128]{1,0:T(8,128)(2,1)}, bf16[2048,128]{1,0:T(8,128)(2,1)S(1)}, u32[]{:S(2)}, u32[]{:S(2)}) collective-permute-start(bf16[2048,128]{1,0:T(8,128)(2,1)} %get-tuple-element.17), channel_id=1, source_target_pairs={{1,0},{2,1},{3,2},{5,4},{6,5},{7,6},{9,8},{10,9},{11,10},{13,12},{... | collective-permute-start | bytes 1572872 | tf_op jit(solution)/shard_map/ppermute | solution.py:17
  31.1 21.3 %collective-permute-done.6.above_f = f32[3,2048]{1,0:T(4,128)S(1)} collective-permute-done((f32[3,2048]{1,0:T(4,128)S(1)}, f32[3,2048]{1,0:T(4,128)S(1)}, u32[]{:S(2)}, u32[]{:S(2)}) %collective-permute-start.6) | collective-permute-done | bytes 24608 | tf_op jit(solution)/shard_map/ppermute | solution.py:17
  52.4 3.9 %collective-permute-start.11 = (bf16[2048,128]{1,0:T(8,128)(2,1)}, bf16[2048,128]{1,0:T(8,128)(2,1)S(1)}, u32[]{:S(2)}, u32[]{:S(2)}) collective-permute-start(bf16[2048,128]{1,0:T(8,128)(2,1)} %copy-done.3), channel_id=1, source_target_pairs={{0,1},{1,2},{4,5},{5,6},{8,9},{9,10},{12,13},{13,14},{16,17},{17,1... | collective-permute-start | bytes 1572872 | tf_op jit(solution)/shard_map/ppermute | solution.py:22
  57.0 3.4 %collective-permute-start.7 = (f32[3,2048]{1,0:T(4,128)S(1)}, f32[3,2048]{1,0:T(4,128)S(1)}, u32[]{:S(2)}, u32[]{:S(2)}) collective-permute-start(f32[3,2048]{1,0:T(4,128)S(1)} %get-tuple-element.34), channel_id=1, source_target_pairs={{0,1},{1,2},{4,5},{5,6},{8,9},{9,10},{12,13},{13,14},{16,17},{17,1... | collective-permute-start | bytes 73736 | tf_op jit(solution)/shard_map/ppermute | solution.py:22
  60.5 1.5 %fusion.1 = f32[1,2,128,512]{3,2,1,0:T(8,128)S(1)} fusion(f32[2,128,512]{2,1,0:T(8,128)} %collective-permute-done.2, f32[2,2,128,512]{3,2,1,0:T(8,128)} %bitcast.121, pred[]{:T(512)S(6)} %ne.24), kind=kLoop, calls=%fused_computation.10 | loop fusion | flops 262144 | bytes 2097153 | tf_op jit(solution)/shard_map/reshape | solution.py:43
  62.0 5.9 %collective-permute-done.7.below_f = f32[3,2048]{1,0:T(4,128)S(1)} collective-permute-done((f32[3,2048]{1,0:T(4,128)S(1)}, f32[3,2048]{1,0:T(4,128)S(1)}, u32[]{:S(2)}, u32[]{:S(2)}) %collective-permute-start.7) | collective-permute-done | bytes 24608 | tf_op jit(solution)/shard_map/ppermute | solution.py:22
  67.8 4.8 %first.1 = (f32[4,232,384]{2,1,0:T(8,128)S(1)}, bf16[2048,384]{1,0:T(8,128)(2,1)S(1)}, bf16[2048,384]{1,0:T(8,128)(2,1)S(1)}) custom-call(s32[1,2048]{1,0:T(1,128)S(1)} %copy-done.1, bf16[2048,384]{1,0:T(8,128)(2,1)} %collective-permute-done.4.above_ref, bf16[2048,384]{1,0:T(8,128)(2,1)} %collective-permute-done.5.below_ref, ...), custom_call_target="tpu_custom_call" | custom-call | flops 1409286144 | bytes 9437184 | tf_op jit(solution)/shard_map/first/pallas_call | solution.py:230
  72.6 3.2 %second.1 = f32[4,352,128]{2,1,0:T(8,128)S(1)} custom-call(bf16[2048,128]{1,0:T(8,128)(2,1)S(1)} %collective-permute-done.10.above_ref, bf16[2048,128]{1,0:T(8,128)(2,1)S(1)} %collective-permute-done.11.below_ref, bf16[2048,384]{1,0:T(8,128)(2,1)S(1)} %get-tuple-element.19.above_1, bf16[2048,384]{1,0:T(8,128)(2,1)S(1)} %get-tuple-element.20.below_1, ...), custom_call_target="tpu_custom_call" | custom-call | flops 738197504 | bytes 5767168 | tf_op jit(solution)/shard_map/second/pallas_call | solution.py:293
  76.6 1.6 %collective-permute-start.3 = (f32[1,128,512]{2,1,0:T(8,128)S(1)}, f32[1,128,512]{2,1,0:T(8,128)S(1)}, u32[]{:S(2)}, u32[]{:S(2)}) collective-permute-start(f32[1,128,512]{2,1,0:T(8,128)S(1)} %select_bitcast_fusion.4), channel_id=1, source_target_pairs={{0,8},{4,12},{8,0},{12,4},{1,9},{5,13},{9,1},{13,5},{2,10},{6,14},... | collective-permute-start | bytes 786440 | tf_op jit(solution)/shard_map/ppermute | solution.py:27
  78.3 1.0 collective-permute-start.13
  79.5 1.2 %collective-permute-start.9 = (f32[1,232,384]{2,1,0:T(8,128)S(1)}, f32[1,232,384]{2,1,0:T(8,128)S(1)}, u32[]{:S(2)}, u32[]{:S(2)}) collective-permute-start(f32[1,232,384]{2,1,0:T(8,128)S(1)} %select_bitcast_fusion.3), channel_id=1, source_target_pairs={{0,8},{4,12},{8,0},{12,4},{1,9},{5,13},{9,1},{13,5},{2,10},{6,14},... | collective-permute-start | bytes 1069064 | tf_op jit(solution)/shard_map/ppermute | solution.py:27
  80.6 5.2 %collective-permute-done.3 = f32[1,128,512]{2,1,0:T(8,128)S(1)} collective-permute-done((f32[1,128,512]{2,1,0:T(8,128)S(1)}, f32[1,128,512]{2,1,0:T(8,128)S(1)}, u32[]{:S(2)}, u32[]{:S(2)}) %collective-permute-start.3) | collective-permute-done | bytes 262176 | tf_op jit(solution)/shard_map/ppermute | solution.py:27
  86.0 3.8 %collective-permute-done.13 = f32[1,352,128]{2,1,0:T(8,128)S(1)} collective-permute-done((f32[1,352,128]{2,1,0:T(8,128)S(1)}, f32[1,352,128]{2,1,0:T(8,128)S(1)}, u32[]{:S(2)}, u32[]{:S(2)}) %collective-permute-start.13) | collective-permute-done | bytes 180256 | tf_op jit(solution)/shard_map/ppermute | solution.py:27
  89.8 6.7 %collective-permute-done.9 = f32[1,232,384]{2,1,0:T(8,128)S(1)} collective-permute-done((f32[1,232,384]{2,1,0:T(8,128)S(1)}, f32[1,232,384]{2,1,0:T(8,128)S(1)}, u32[]{:S(2)}, u32[]{:S(2)}) %collective-permute-start.9) | collective-permute-done | bytes 356384 | tf_op jit(solution)/shard_map/ppermute | solution.py:27
  96.6 1.3 %collective-permute-start.15 = (f32[224,128]{1,0:T(8,128)S(1)}, f32[224,128]{1,0:T(8,128)S(1)}, u32[]{:S(2)}, u32[]{:S(2)}) collective-permute-start(f32[224,128]{1,0:T(8,128)S(1)} %fusion.6), channel_id=1, source_target_pairs={{1,0},{2,1},{3,2},{5,4},{6,5},{7,6},{9,8},{10,9},{11,10},{13,12},{... | collective-permute-start | bytes 344072 | tf_op jit(solution)/shard_map/ppermute | solution.py:17
  97.9 1.3 %collective-permute-start.14 = (f32[96,384]{1,0:T(8,128)S(1)}, f32[96,384]{1,0:T(8,128)S(1)}, u32[]{:S(2)}, u32[]{:S(2)}) collective-permute-start(f32[96,384]{1,0:T(8,128)S(1)} %fusion.5), channel_id=1, source_target_pairs={{1,0},{2,1},{3,2},{5,4},{6,5},{7,6},{9,8},{10,9},{11,10},{13,12},{... | collective-permute-start | bytes 442376 | tf_op jit(solution)/shard_map/ppermute | solution.py:17
  99.3 5.2 %collective-permute-done.15 = f32[224,128]{1,0:T(8,128)S(1)} collective-permute-done((f32[224,128]{1,0:T(8,128)S(1)}, f32[224,128]{1,0:T(8,128)S(1)}, u32[]{:S(2)}, u32[]{:S(2)}) %collective-permute-start.15) | collective-permute-done | bytes 114720 | tf_op jit(solution)/shard_map/ppermute | solution.py:17
  104.5 2.4 %collective-permute-done.14 = f32[96,384]{1,0:T(8,128)S(1)} collective-permute-done((f32[96,384]{1,0:T(8,128)S(1)}, f32[96,384]{1,0:T(8,128)S(1)}, u32[]{:S(2)}, u32[]{:S(2)}) %collective-permute-start.14) | collective-permute-done | bytes 147488 | tf_op jit(solution)/shard_map/ppermute | solution.py:17
  106.9 1.0 maximum_select_fusion
  (51 shorter events, 2.9 us)
Async XLA Ops:
  0.0 0.7 copy-start
  0.7 0.9 copy-start.2
  1.6 19.7 %copy-start.1 = (s32[1,2048]{1,0:T(1,128)S(1)}, s32[1,2048]{1,0:T(1,128)}, u32[]{:S(2)}) copy-start(s32[1,2048]{1,0:T(1,128)} %observed_ref.3) | copy-start | bytes 24580
  5.7 0.8 copy-start.3
  6.5 12.9 %collective-permute-start = (f32[8,512]{1,0:T(8,128)S(1)}, f32[8,512]{1,0:T(8,128)S(1)}, u32[]{:S(2)}, u32[]{:S(2)}) collective-permute-start(f32[8,512]{1,0:T(8,128)S(1)} %get-tuple-element.13), channel_id=1, source_target_pairs={{0,4},{4,0},{8,12},{12,8},{1,5},{5,1},{9,13},{13,9},{2,6},{6,2},{1... | collective-permute-start | bytes 49160 | tf_op jit(solution)/shard_map/ppermute | solution.py:27
  11.8 56.1 %collective-permute-start.4 = (bf16[2048,384]{1,0:T(8,128)(2,1)}, bf16[2048,384]{1,0:T(8,128)(2,1)}, u32[]{:S(2)}, u32[]{:S(2)}) collective-permute-start(bf16[2048,384]{1,0:T(8,128)(2,1)} %get-tuple-element.14), channel_id=1, source_target_pairs={{1,0},{2,1},{3,2},{5,4},{6,5},{7,6},{9,8},{10,9},{11,10},{13,12},{... | collective-permute-start | bytes 4718600 | tf_op jit(solution)/shard_map/ppermute | solution.py:17
  13.0 54.8 %collective-permute-start.5 = (bf16[2048,384]{1,0:T(8,128)(2,1)}, bf16[2048,384]{1,0:T(8,128)(2,1)}, u32[]{:S(2)}, u32[]{:S(2)}) collective-permute-start(bf16[2048,384]{1,0:T(8,128)(2,1)} %get-tuple-element.15), channel_id=1, source_target_pairs={{0,1},{1,2},{4,5},{5,6},{8,9},{9,10},{12,13},{13,14},{16,17},{17,1... | collective-permute-start | bytes 4718600 | tf_op jit(solution)/shard_map/ppermute | solution.py:22
  19.4 3.7 %collective-permute-start.1 = (f32[8,512]{1,0:T(8,128)S(1)}, f32[8,512]{1,0:T(8,128)S(1)}, u32[]{:S(2)}, u32[]{:S(2)}) collective-permute-start(f32[8,512]{1,0:T(8,128)S(1)} %add.34), channel_id=1, source_target_pairs={{0,8},{4,12},{8,0},{12,4},{1,9},{5,13},{9,1},{13,5},{2,10},{6,14},... | collective-permute-start | bytes 49160 | tf_op jit(solution)/shard_map/ppermute | solution.py:27
  26.4 1.0 copy-start.4
  28.3 28.7 %collective-permute-start.2 = (f32[2,128,512]{2,1,0:T(8,128)}, f32[2,128,512]{2,1,0:T(8,128)}, u32[]{:S(2)}, u32[]{:S(2)}) collective-permute-start(f32[2,128,512]{2,1,0:T(8,128)} %select_bitcast_fusion.1), channel_id=1, source_target_pairs={{0,4},{4,0},{8,12},{12,8},{1,5},{5,1},{9,13},{13,9},{2,6},{6,2},{1... | collective-permute-start | bytes 1572872 | tf_op jit(solution)/shard_map/ppermute | solution.py:27
  28.5 23.9 %collective-permute-start.6 = (f32[3,2048]{1,0:T(4,128)S(1)}, f32[3,2048]{1,0:T(4,128)S(1)}, u32[]{:S(2)}, u32[]{:S(2)}) collective-permute-start(f32[3,2048]{1,0:T(4,128)S(1)} %get-tuple-element.35), channel_id=1, source_target_pairs={{1,0},{2,1},{3,2},{5,4},{6,5},{7,6},{9,8},{10,9},{11,10},{13,12},{... | collective-permute-start | bytes 73736 | tf_op jit(solution)/shard_map/ppermute | solution.py:17
  29.8 42.8 %collective-permute-start.10 = (bf16[2048,128]{1,0:T(8,128)(2,1)}, bf16[2048,128]{1,0:T(8,128)(2,1)S(1)}, u32[]{:S(2)}, u32[]{:S(2)}) collective-permute-start(bf16[2048,128]{1,0:T(8,128)(2,1)} %get-tuple-element.17), channel_id=1, source_target_pairs={{1,0},{2,1},{3,2},{5,4},{6,5},{7,6},{9,8},{10,9},{11,10},{13,12},{... | collective-permute-start | bytes 1572872 | tf_op jit(solution)/shard_map/ppermute | solution.py:17
  52.4 20.3 %collective-permute-start.11 = (bf16[2048,128]{1,0:T(8,128)(2,1)}, bf16[2048,128]{1,0:T(8,128)(2,1)S(1)}, u32[]{:S(2)}, u32[]{:S(2)}) collective-permute-start(bf16[2048,128]{1,0:T(8,128)(2,1)} %copy-done.3), channel_id=1, source_target_pairs={{0,1},{1,2},{4,5},{5,6},{8,9},{9,10},{12,13},{13,14},{16,17},{17,1... | collective-permute-start | bytes 1572872 | tf_op jit(solution)/shard_map/ppermute | solution.py:22
  57.0 10.8 %collective-permute-start.7 = (f32[3,2048]{1,0:T(4,128)S(1)}, f32[3,2048]{1,0:T(4,128)S(1)}, u32[]{:S(2)}, u32[]{:S(2)}) collective-permute-start(f32[3,2048]{1,0:T(4,128)S(1)} %get-tuple-element.34), channel_id=1, source_target_pairs={{0,1},{1,2},{4,5},{5,6},{8,9},{9,10},{12,13},{13,14},{16,17},{17,1... | collective-permute-start | bytes 73736 | tf_op jit(solution)/shard_map/ppermute | solution.py:22
  75.9 2.3 %collective-permute-start.12 = (f32[2,352,128]{2,1,0:T(8,128)S(1)}, f32[2,352,128]{2,1,0:T(8,128)S(1)}, u32[]{:S(2)}, u32[]{:S(2)}) collective-permute-start(f32[2,352,128]{2,1,0:T(8,128)S(1)} %select_bitcast_fusion.2), channel_id=1, source_target_pairs={{0,4},{4,0},{8,12},{12,8},{1,5},{5,1},{9,13},{13,9},{2,6},{6,2},{1... | collective-permute-start | bytes 1081352 | tf_op jit(solution)/shard_map/ppermute | solution.py:27
  76.0 3.2 %collective-permute-start.8 = (f32[2,232,384]{2,1,0:T(8,128)S(1)}, f32[2,232,384]{2,1,0:T(8,128)S(1)}, u32[]{:S(2)}, u32[]{:S(2)}) collective-permute-start(f32[2,232,384]{2,1,0:T(8,128)S(1)} %select_bitcast_fusion), channel_id=1, source_target_pairs={{0,4},{4,0},{8,12},{12,8},{1,5},{5,1},{9,13},{13,9},{2,6},{6,2},{1... | collective-permute-start | bytes 2138120 | tf_op jit(solution)/shard_map/ppermute | solution.py:27
  76.6 9.2 %collective-permute-start.3 = (f32[1,128,512]{2,1,0:T(8,128)S(1)}, f32[1,128,512]{2,1,0:T(8,128)S(1)}, u32[]{:S(2)}, u32[]{:S(2)}) collective-permute-start(f32[1,128,512]{2,1,0:T(8,128)S(1)} %select_bitcast_fusion.4), channel_id=1, source_target_pairs={{0,8},{4,12},{8,0},{12,4},{1,9},{5,13},{9,1},{13,5},{2,10},{6,14},... | collective-permute-start | bytes 786440 | tf_op jit(solution)/shard_map/ppermute | solution.py:27
  78.3 11.5 %collective-permute-start.13 = (f32[1,352,128]{2,1,0:T(8,128)S(1)}, f32[1,352,128]{2,1,0:T(8,128)S(1)}, u32[]{:S(2)}, u32[]{:S(2)}) collective-permute-start(f32[1,352,128]{2,1,0:T(8,128)S(1)} %select_bitcast_fusion.5), channel_id=1, source_target_pairs={{0,8},{4,12},{8,0},{12,4},{1,9},{5,13},{9,1},{13,5},{2,10},{6,14},... | collective-permute-start | bytes 540680 | tf_op jit(solution)/shard_map/ppermute | solution.py:27
  79.5 17.0 %collective-permute-start.9 = (f32[1,232,384]{2,1,0:T(8,128)S(1)}, f32[1,232,384]{2,1,0:T(8,128)S(1)}, u32[]{:S(2)}, u32[]{:S(2)}) collective-permute-start(f32[1,232,384]{2,1,0:T(8,128)S(1)} %select_bitcast_fusion.3), channel_id=1, source_target_pairs={{0,8},{4,12},{8,0},{12,4},{1,9},{5,13},{9,1},{13,5},{2,10},{6,14},... | collective-permute-start | bytes 1069064 | tf_op jit(solution)/shard_map/ppermute | solution.py:27
  96.6 7.9 %collective-permute-start.15 = (f32[224,128]{1,0:T(8,128)S(1)}, f32[224,128]{1,0:T(8,128)S(1)}, u32[]{:S(2)}, u32[]{:S(2)}) collective-permute-start(f32[224,128]{1,0:T(8,128)S(1)} %fusion.6), channel_id=1, source_target_pairs={{1,0},{2,1},{3,2},{5,4},{6,5},{7,6},{9,8},{10,9},{11,10},{13,12},{... | collective-permute-start | bytes 344072 | tf_op jit(solution)/shard_map/ppermute | solution.py:17
  97.9 9.0 %collective-permute-start.14 = (f32[96,384]{1,0:T(8,128)S(1)}, f32[96,384]{1,0:T(8,128)S(1)}, u32[]{:S(2)}, u32[]{:S(2)}) collective-permute-start(f32[96,384]{1,0:T(8,128)S(1)} %fusion.5), channel_id=1, source_target_pairs={{1,0},{2,1},{3,2},{5,4},{6,5},{7,6},{9,8},{10,9},{11,10},{13,12},{... | collective-permute-start | bytes 442376 | tf_op jit(solution)/shard_map/ppermute | solution.py:17

commit v6 on v5

v6 whole, which is shorter than its diff:
```python
import functools

import jax
import jax.numpy as jnp
import numpy as np
from jax import lax
from jax.experimental import pallas as pl
from jax.experimental.pallas import tpu as pltpu
from jax.sharding import PartitionSpec as P

BAND = 3


EPSILON = 1e-05


def from_above(shard, axis):
    peers = lax.axis_size(axis)
    return lax.ppermute(shard, axis, [(i, i - 1) for i in range(1, peers)])


def from_below(shard, axis):
    peers = lax.axis_size(axis)
    return lax.ppermute(shard, axis, [(i, i + 1) for i in range(peers - 2)])


def swap(shard, axis, bit):
    peers = lax.axis_size(axis)
    return lax.ppermute(shard, axis, [(i, i ^ bit) for i in range(peers)])


def bits_of(peers):
    return [1 << k for k in range(peers.bit_length() - 1)]


def sum_all(value, axis):
    for bit in bits_of(lax.axis_size(axis)):
        value = value + swap(value, axis, bit)
    return value


def sum_rows(partial, axis, exact=None):
    place = lax.axis_index(axis)
    for bit in bits_of(lax.axis_size(axis)):
        pairs = partial.reshape(partial.shape[0] // 2, 2, *partial.shape[1:])
        high = (place & bit) != 0
        keep = jnp.where(high, pairs[:, 1], pairs[:, 0])
        give = jnp.where(high, pairs[:, 0], pairs[:, 1])
        if bit == 1 or exact is None:
            got = swap(give, axis, bit)
        else:
            rows = give.shape[1]
            near = lax.reduce_precision(give, 8, 7)
            left = (give[:, exact:] - near[:, exact:]).astype(jnp.bfloat16)
            got = jnp.concatenate([near.astype(jnp.bfloat16), left], axis=1)
            got = swap(got, axis, bit).astype(jnp.float32)
            left = got[:, rows:]
            got = got[:, :rows]
            if rows > exact:
                got = jnp.concatenate([got[:, :exact], got[:, exact:] + left], axis=1)
        partial = keep + got
    return partial[0]


GRANT = 20 << 20


def block_of(samples):
    return 512 if samples % 512 == 0 else samples


def in_hbm(array):
    return pltpu.with_memory_space_constraint(array, pltpu.HBM)


def like(shape, dtype):
    return jax.ShapeDtypeStruct(shape, dtype)


def mask_of(row):
    lanes = 128
    return jnp.transpose(jnp.broadcast_to(row.astype(jnp.float32), (lanes, row.shape[1]))) > 0.5


def head_kernel(kept, rows, dosage_ref, up_ref, down_ref, held, up_held, down_held, sems):
    samples, width = dosage_ref.shape
    edge = up_ref.shape[1]
    block = block_of(samples) // 2

    def move(source, target, kind, k):
        part = pl.ds(k * block, block)
        copy = pltpu.make_async_copy(source.at[part, :], target.at[part, :], sems.at[kind, k])
        copy.start()
        return copy

    arriving = [move(dosage_ref, held, 0, k) for k in range(samples // block)]
    leaving = []
    for k, copy in enumerate(arriving):
        part = pl.ds(k * block, block)
        copy.wait()
        values = held[part, :]
        owners = [values[:, low : low + kept] for low in range(0, width, rows)]
        up_held[part, :] = jnp.concatenate(owners, axis=1)
        leaving.append(move(up_held, up_ref, 1, k))
        down_held[part, :] = held[part, :edge]
        leaving.append(move(down_held, down_ref, 2, k))
    for copy in leaving:
        copy.wait()


def whole():
    return pl.BlockSpec(memory_space=pltpu.VMEM)


def head_pass(dosage, kept, rows):
    samples, width = dosage.shape
    edge = width // rows * kept
    half = jnp.bfloat16
    return pl.pallas_call(
        functools.partial(head_kernel, kept, rows),
        out_shape=(like((samples, edge), half),) * 2,
        in_specs=[pl.BlockSpec(memory_space=pl.ANY)],
        out_specs=(pl.BlockSpec(memory_space=pl.ANY),) * 2,
        scratch_shapes=[
            pltpu.VMEM((samples, width), half),
            pltpu.VMEM((samples, edge), half),
            pltpu.VMEM((samples, edge), half),
            pltpu.SemaphoreType.DMA((3, 2 * samples // block_of(samples))),
        ],
        compiler_params=pltpu.CompilerParams(vmem_limit_bytes=GRANT),
        name="head",
    )(in_hbm(dosage))


def moments_kernel(dosage_ref, observed_ref, chosen_ref, down_2, up_2, sums_ref):
    width = dosage_ref.shape[1]
    lanes = 128

    @pl.when(pl.program_id(0) == 0)
    def _():
        sums_ref[...] = jnp.zeros_like(sums_ref)

    present = mask_of(observed_ref[...])
    count = jnp.sum(jnp.where(present, 1.0, 0.0), axis=0, keepdims=True)
    for low in range(0, width, lanes):
        part = slice(low, low + lanes)
        kept = jnp.where(present, dosage_ref[:, part].astype(jnp.float32), 0.0)
        sums_ref[0:1, part] += jnp.sum(kept, axis=0, keepdims=True)
        sums_ref[1:2, part] += jnp.sum(kept * kept, axis=0, keepdims=True)
        sums_ref[2:3, part] += count
    down_2[...] = dosage_ref[:, width - down_2.shape[1] :]
    up = jnp.dot(dosage_ref[...], chosen_ref[...], preferred_element_type=jnp.float32)
    up_2[...] = up.astype(jnp.bfloat16)


def moments_pass(dosage, observed, chosen):
    samples, width = dosage.shape
    block, rest = block_of(samples), chosen.shape[1]
    return pl.pallas_call(
        moments_kernel,
        grid=(samples // block,),
        out_shape=(like((samples, rest), jnp.bfloat16),) * 2 + (like((8, width), jnp.float32),),
        in_specs=[
            pl.BlockSpec((block, width), lambda i: (i, 0)),
            pl.BlockSpec((1, block), lambda i: (0, i)),
            pl.BlockSpec((width, rest), lambda i: (0, 0)),
        ],
        out_specs=(pl.BlockSpec((block, rest), lambda i: (i, 0)),) * 2
        + (pl.BlockSpec((8, width), lambda i: (0, 0)),),
        compiler_params=pltpu.CompilerParams(vmem_limit_bytes=GRANT),
        cost_estimate=pl.CostEstimate(
            flops=2 * samples * width * rest,
            bytes_accessed=2 * samples * (width + 2 * rest),
            transcendentals=0,
        ),
        name="moments",
    )(in_hbm(dosage), observed, chosen)


def finish_moments(sums):
    centre = sums[0:1] / sums[2:3]
    spread_inverse = 1.0 / jnp.sqrt(sums[1:2] / sums[2:3] - centre * centre + EPSILON)
    return jnp.concatenate([centre, spread_inverse], axis=0)


def standardize(values, present, moments):
    spread = (values.astype(jnp.float32) - moments[0:1]) * moments[1:2]
    return jnp.where(present, spread, 0.0).astype(jnp.bfloat16)


def decode(values, facts_ref, present, first):
    parts = []
    for low in range(0, values.shape[1], present.shape[1]):
        part = slice(low, low + present.shape[1])
        place = slice(first + low, first + low + present.shape[1])
        spread = values[:, part].astype(jnp.float32) - facts_ref[0:1, place]
        spread = spread * facts_ref[1:2, place]
        parts.append(jnp.where(present, spread, 0.0).astype(jnp.bfloat16))
    return parts[0] if len(parts) == 1 else jnp.concatenate(parts, axis=1)


def cross(left, right):
    return lax.dot_general(
        left, right, (((0,), (0,)), ((), ())), preferred_element_type=jnp.float32
    )


def first_kernel(
    observed_ref,
    above_ref,
    below_ref,
    own_ref,
    above_f,
    below_f,
    out_ref,
    above_out,
    below_out,
    above_held,
    below_held,
    sems,
):
    peers, _, edge = out_ref.shape
    samples = own_ref.shape[0]
    rows = own_ref.shape[1] // peers
    kept = edge // peers
    block = block_of(samples)

    def move(source, target, kind, k):
        part = pl.ds(k * block, block)
        copy = pltpu.make_async_copy(source.at[part, :], target.at[part, :], sems.at[kind, k])
        copy.start()
        return copy

    arriving = []
    for k in range(samples // block):
        arriving.append(
            (move(above_ref, above_held, 0, k), move(below_ref, below_held, 1, k))
        )
    shares = [jnp.zeros((1, 128), jnp.float32)] * 2
    for k, copies in enumerate(arriving):
        part = slice(k * block, (k + 1) * block)
        own_present = mask_of(observed_ref[:, part])
        above_present = mask_of(above_f[2:3, part])
        below_present = mask_of(below_f[2:3, part])
        shares = [
            share
            + jnp.sum(jnp.where(other & above_present, 1.0, 0.0), axis=0, keepdims=True)
            for share, other in zip(shares, (own_present, below_present))
        ]
        copies[0].wait()
        above = decode(above_held[part, :], above_f, above_present, 0)
        above_out[part, :] = above
        near = cross(own_ref[part, :], above)
        copies[1].wait()
        below = decode(below_held[part, :], below_f, below_present, 0)
        below_out[part, :] = below
        far = cross(below, above)
        for owner in range(peers):
            into = out_ref.at[owner]
            add_to(into, slice(0, rows), near[owner * rows : (owner + 1) * rows], k)
            add_to(into, slice(rows, rows + kept), far[owner * kept : (owner + 1) * kept], k)
    for owner in range(peers):
        for low in range(0, edge, 128):
            out_ref[owner, rows + kept : rows + kept + 1, low : low + 128] = shares[0]
            out_ref[owner, rows + kept + 1 : rows + kept + 2, low : low + 128] = shares[1]
        out_ref[owner, rows + kept + 2 :, :] = jnp.zeros((6, edge), jnp.float32)


def add_to(ref, part, value, step):
    ref[part, :] = value if step == 0 else ref[part, :] + value


def first_pass(observed, above, below, own, above_f, below_f, peers):
    samples, width = own.shape
    edge = above.shape[1]
    half = jnp.bfloat16
    tall = (peers, width // peers + edge // peers + 8, edge)
    anywhere = pl.BlockSpec(memory_space=pl.ANY)
    return pl.pallas_call(
        first_kernel,
        out_shape=(like(tall, jnp.float32),) + (like((samples, edge), half),) * 2,
        in_specs=[whole(), anywhere, anywhere, whole(), whole(), whole()],
        out_specs=(whole(),) * 3,
        scratch_shapes=[
            pltpu.VMEM((samples, edge), half),
            pltpu.VMEM((samples, edge), half),
            pltpu.SemaphoreType.DMA((2, samples // block_of(samples))),
        ],
        compiler_params=pltpu.CompilerParams(vmem_limit_bytes=GRANT),
        cost_estimate=pl.CostEstimate(
            flops=2 * samples * edge * (width + edge),
            bytes_accessed=12 * samples * edge,
            transcendentals=0,
        ),
        name="first",
    )(observed, in_hbm(above), in_hbm(below), own, above_f, below_f)


def second_kernel(
    above_ref, below_ref, above_1, below_1, own_ref, above_f, below_f, out_ref
):
    peers, _, rest = out_ref.shape
    samples, width = own_ref.shape
    edge = above_1.shape[1]
    rows, kept, tail = width // peers, edge // peers, rest // peers
    block = block_of(samples)
    for k in range(samples // block):
        part = slice(k * block, (k + 1) * block)
        above = decode(above_ref[part, :], above_f, mask_of(above_f[2:3, part]), edge)
        below = decode(below_ref[part, :], below_f, mask_of(below_f[2:3, part]), edge)
        far = cross(below_1[part, :], above)
        last = cross(below, above_1[part, :])
        corner = cross(below, above)
        near = cross(own_ref[part, :], above)
        for owner in range(peers):
            into = out_ref.at[owner]
            add_to(into, slice(0, rows), near[owner * rows : (owner + 1) * rows], k)
            low = rows + kept
            add_to(into, slice(rows, low), far[owner * kept : (owner + 1) * kept], k)
            lines = slice(owner * tail, (owner + 1) * tail)
            for left in range(0, edge, rest):
                add_to(into, slice(low, low + tail), last[lines, left : left + rest], k)
                low += tail
            add_to(into, slice(low, low + tail), corner[lines], k)


def second_pass(above, below, above_1, below_1, own, above_f, below_f, peers):
    samples, width = own.shape
    edge, rest = above_1.shape[1], above.shape[1]
    tall = (peers, (width + edge + width) // peers, rest)
    return pl.pallas_call(
        second_kernel,
        out_shape=like(tall, jnp.float32),
        in_specs=[whole()] * 7,
        out_specs=whole(),
        compiler_params=pltpu.CompilerParams(vmem_limit_bytes=GRANT),
        cost_estimate=pl.CostEstimate(
            flops=2 * samples * rest * (2 * width + edge),
            bytes_accessed=2 * samples * (2 * width + edge),
            transcendentals=0,
        ),
        name="second",
    )(above, below, above_1, below_1, own, above_f, below_f)


def per_device(dosage, observed, band_reach):
    samples, width = dosage.shape
    peers = lax.axis_size("samp")
    rows = width // peers
    kept = 3 * rows // 4
    tail = rows - kept
    edge, rest = kept * peers, tail * peers
    owners = np.arange(peers)[:, None] * rows
    order = np.concatenate(
        [
            (owners + np.arange(0, kept)[None, :]).ravel(),
            (owners + np.arange(kept, rows)[None, :]).ravel(),
        ]
    )
    pieces = width // rest
    chosen = (np.arange(width)[:, None] == order[None, :]).astype(jnp.bfloat16)
    up_1, down_1 = head_pass(dosage, kept, rows)
    below_1 = from_below(up_1, "var")
    above_1 = from_above(down_1, "var")
    down_2, up_2, sums = moments_pass(dosage, observed, chosen[:, edge:])
    sums = sum_all(sums, "samp")
    moments = finish_moments(sums)
    cuts = [(k * rows, k * rows + kept) for k in range(peers)]
    cuts += [(k * rows + kept, (k + 1) * rows) for k in range(peers)]
    ordered = jnp.concatenate([moments[:, low:high] for low, high in cuts], axis=1)
    above_f, below_f = [
        jnp.concatenate(
            [jnp.pad(part, ((0, 0), (0, samples - width))), observed.astype(jnp.float32)]
        )
        for part in (moments, ordered)
    ]
    below_f = from_below(below_f, "var")
    above_f = from_above(above_f, "var")
    below_2 = from_below(up_2, "var")
    above_2 = from_above(down_2, "var")
    own = standardize(dosage, (observed[0] != 0)[:, None], moments)
    own = lax.optimization_barrier(own)
    same = sum_rows(cross(own, own).reshape(peers, rows, width), "samp")
    one, above_1, below_1 = first_pass(
        observed, above_1, below_1, own, above_f, below_f, peers
    )
    one = sum_rows(one, "samp", rows + kept)
    shares = jnp.maximum(one[rows + kept :], 1.0)
    near_1 = one[:rows] / shares[0:1]
    far_1 = one[rows : rows + kept] / shares[1:2]
    two = second_pass(
        above_2, below_2, above_1, below_1, own, above_f, below_f, peers
    )
    two = sum_rows(two, "samp", two.shape[1])
    far_2 = two[rows:] / shares[1:2, :rest]
    low = [far_2[kept + k * tail : kept + (k + 1) * tail] for k in range(pieces)]
    far = jnp.concatenate(
        [
            jnp.concatenate([far_1, far_2[:kept]], axis=1),
            jnp.concatenate(low, axis=1),
        ],
        axis=0,
    )
    far = from_above(far, "var")
    near = jnp.concatenate([near_1, two[:rows] / shares[0:1, :rest]], axis=1)
    result = jnp.stack([same / jnp.maximum(sums[2:3], 1.0), near, far], axis=1)
    keep = jnp.arange(BAND, dtype=jnp.int32) <= band_reach[0]
    return jnp.where(keep[None, :, None], result, jnp.float32(0.0))[None]


def solution(mesh):
    return jax.shard_map(
        per_device,
        mesh=mesh,
        in_specs=(P("samp", ("seg", "var")), P(("seg", "var"), "samp"), P(("seg", "var"))),
        out_specs=P(("seg", "var"), "samp", None, None),
        check_vma=False,
    )
```

time: 109 us -> 93.3 us (0.86)
  waiting for transfers between devices: 52.2 us -> 41.4 us
  Pallas kernels: 16.8 us -> 14 us
    ppermute x8, waiting for transfers between devices: 17.5 us -> 11.8 us  [swap(): return lax.ppermute(shard, axis, [(i, i ^ bit) for i in range(peers)])]
    ppermute x3, waiting for transfers between devices: 5.87 us -> 1.54 us  [from_below(): return lax.ppermute(shard, axis, [(i, i + 1) for i in range(peers - 2)])]
    pallas_call x3, Pallas kernels: 12.8 us -> 9.83 us  [the longest x1 4.62 us: first_pass(): pl.pallas_call(first_kernel, out_shape=(like(tall, jnp.float32),) + (like...]
    ppermute x3, starting transfers between devices: 13.7 us -> 15 us  [from_below(): return lax.ppermute(shard, axis, [(i, i + 1) for i in range(peers - 2)])]
    ppermute x5 -> x4, starting transfers between devices: 6.45 us -> 5.14 us  [from_above(): return lax.ppermute(shard, axis, [(i, i - 1) for i in range(1, peers)])]
    ppermute x5 -> x4, waiting for transfers between devices: 28.9 us -> 28.1 us  [from_above(): return lax.ppermute(shard, axis, [(i, i - 1) for i in range(1, peers)])]
    unnamed x10 -> x8, local copies, waits for them, and re-layouts: 3.35 us -> 2.57 us
  transfers between devices with their start and end apart: 16 -> 15, of which waited for: 8 -> 10; matrix products, arithmetic and copies ran while one was open for 6% -> 7% of each run, Pallas kernels for 9% -> 11%
where the time goes in v6:
time: 93.3 us; the launch traced here: 92.8 us
  waiting for transfers between devices  41.4 us (44%)
  starting transfers between devices  26 us (28%)
  Pallas kernels  14 us (15%)
  other arithmetic  6.42 us (7%)
  local copies, waits for them, and re-layouts  2.74 us (3%)
  matrix products  1.28 us (1%)
  between operations  0.98 us (1%)
    ppermute x4, waiting for transfers between devices, from_above(): return lax.ppermute(shard, axis, [(i, i - 1) for i in range(1, peers)])  28.1 us
    ppermute x3, starting transfers between devices, from_below(): return lax.ppermute(shard, axis, [(i, i + 1) for i in range(peers - 2)])  15 us
    ppermute x8, waiting for transfers between devices, swap(): return lax.ppermute(shard, axis, [(i, i ^ bit) for i in range(peers)])  11.8 us
    ppermute x8, starting transfers between devices, swap(): return lax.ppermute(shard, axis, [(i, i ^ bit) for i in range(peers)])  5.87 us
    ppermute x4, starting transfers between devices, from_above(): return lax.ppermute(shard, axis, [(i, i - 1) for i in range(1, peers)])  5.14 us
    pallas_call x1, Pallas kernels, first_pass(): pl.pallas_call(first_kernel, out_shape=(like(tall, jnp.float32),) + (like...  4.62 us
    pallas_call x1, Pallas kernels, moments_pass(): pl.pallas_call(moments_kernel, grid=(samples // block,), out_shape=(like(...  4.16 us
    pallas_call x1, Pallas kernels, head_pass(): pl.pallas_call(functools.partial(head_kernel, kept, rows), out_shape=(lik...  2.96 us
  transfers between devices with their start and end apart: 15, of which 10 were waited for; matrix products, arithmetic and copies ran while one was open for 7% of the time, Pallas kernels for 11%

profile of v6, /device:TPU:0, one launch (start us, length us, event | category | flops | bytes accessed | tf_op | source)
XLA Modules:
  0.0 92.8 jit_solution(10614049623437871299)
XLA Ops:
  0.0 0.7 copy-done
  0.7 0.9 copy-done.2
  1.6 4.2 %moments.1 = (bf16[2048,128]{1,0:T(8,128)(2,1)}, bf16[2048,128]{1,0:T(8,128)(2,1)}, f32[8,512]{1,0:T(8,128)S(1)}) custom-call(bf16[2048,512]{1,0:T(8,128)(2,1)} %dosage_ref.3, s32[1,2048]{1,0:T(1,128)S(1)} %copy-done, bf16[512,128]{1,0:T(8,128)(2,1)S(1)} %copy-done.2), custom_call_target="tpu_custom_call" | custom-call | flops 268435456 | bytes 3145728 | tf_op jit(solution)/shard_map/moments/pallas_call | solution.py:159
  5.8 1.3 %collective-permute-start.10 = (bf16[2048,128]{1,0:T(8,128)(2,1)}, bf16[2048,128]{1,0:T(8,128)(2,1)S(1)}, u32[]{:S(2)}, u32[]{:S(2)}) collective-permute-start(bf16[2048,128]{1,0:T(8,128)(2,1)} %get-tuple-element.17), channel_id=1, source_target_pairs={{1,0},{2,1},{3,2},{5,4},{6,5},{7,6},{9,8},{10,9},{11,10},{13,12},{... | collective-permute-start | bytes 1572872 | tf_op jit(solution)/shard_map/ppermute | solution.py:19
  7.0 5.6 %collective-permute-start.11 = (bf16[2048,128]{1,0:T(8,128)(2,1)}, bf16[2048,128]{1,0:T(8,128)(2,1)S(1)}, u32[]{:S(2)}, u32[]{:S(2)}) collective-permute-start(bf16[2048,128]{1,0:T(8,128)(2,1)} %get-tuple-element.18), channel_id=1, source_target_pairs={{0,1},{1,2},{4,5},{5,6},{8,9},{9,10},{12,13},{13,14},{16,17},{17,1... | collective-permute-start | bytes 1572872 | tf_op jit(solution)/shard_map/ppermute | solution.py:24
  12.7 3.0 %head.1 = (bf16[2048,384]{1,0:T(8,128)(2,1)}, bf16[2048,384]{1,0:T(8,128)(2,1)}) custom-call(bf16[2048,512]{1,0:T(8,128)(2,1)} %dosage_ref.3), custom_call_target="tpu_custom_call" | custom-call | tf_op jit(solution)/shard_map/head/pallas_call | solution.py:119
  15.6 1.3 %collective-permute-start.4 = (bf16[2048,384]{1,0:T(8,128)(2,1)}, bf16[2048,384]{1,0:T(8,128)(2,1)}, u32[]{:S(2)}, u32[]{:S(2)}) collective-permute-start(bf16[2048,384]{1,0:T(8,128)(2,1)} %get-tuple-element.14), channel_id=1, source_target_pairs={{1,0},{2,1},{3,2},{5,4},{6,5},{7,6},{9,8},{10,9},{11,10},{13,12},{... | collective-permute-start | bytes 4718600 | tf_op jit(solution)/shard_map/ppermute | solution.py:19
  16.9 5.7 %collective-permute-start.5 = (bf16[2048,384]{1,0:T(8,128)(2,1)}, bf16[2048,384]{1,0:T(8,128)(2,1)}, u32[]{:S(2)}, u32[]{:S(2)}) collective-permute-start(bf16[2048,384]{1,0:T(8,128)(2,1)} %get-tuple-element.15), channel_id=1, source_target_pairs={{0,1},{1,2},{4,5},{5,6},{8,9},{9,10},{12,13},{13,14},{16,17},{17,1... | collective-permute-start | bytes 4718600 | tf_op jit(solution)/shard_map/ppermute | solution.py:24
  23.9 1.9 %collective-permute-start.1 = (f32[8,512]{1,0:T(8,128)S(1)}, f32[8,512]{1,0:T(8,128)S(1)}, u32[]{:S(2)}, u32[]{:S(2)}) collective-permute-start(f32[8,512]{1,0:T(8,128)S(1)} %add.45), channel_id=1, source_target_pairs={{0,8},{4,12},{8,0},{12,4},{1,9},{5,13},{9,1},{13,5},{2,10},{6,14},... | collective-permute-start | bytes 49160 | tf_op jit(solution)/shard_map/ppermute | solution.py:29
  25.8 1.8 %collective-permute-done.1 = f32[8,512]{1,0:T(8,128)S(1)} collective-permute-done((f32[8,512]{1,0:T(8,128)S(1)}, f32[8,512]{1,0:T(8,128)S(1)}, u32[]{:S(2)}, u32[]{:S(2)}) %collective-permute-start.1) | collective-permute-done | bytes 16416 | tf_op jit(solution)/shard_map/ppermute | solution.py:29
  27.6 2.0 %select_convert_fusion.own_ref = bf16[2048,512]{1,0:T(8,128)(2,1)S(1)} fusion(bf16[2048,512]{1,0:T(8,128)(2,1)} %dosage_ref.3, f32[512]{0:T(512)S(1)} %bitcast.123, f32[512]{0:T(512)S(1)} %bitcast.124, pred[2048]{0:T(1024)(128)(4,1)S(1)} %compare_reduce_fusion), kind=kLoop, calls=%fused_computation | loop fusion | flops 5242880 | bytes 4200448 | tf_op jit(solution)/shard_map/convert_element_type | solution.py:188
  29.6 1.3 %fusion.21 = f32[512,512]{1,0:T(8,128)S(1)} fusion(bf16[2048,512]{1,0:T(8,128)(2,1)S(1)} %select_convert_fusion.own_ref), kind=kOutput, calls=%fused_computation.83 | convolution fusion | flops 1073741824 | bytes 3145728 | tf_op jit(solution)/shard_map/dot_general | solution.py:203
  30.9 1.0 %copy-done.3 = f32[512,512]{1,0:T(8,128)} copy-done((f32[512,512]{1,0:T(8,128)}, f32[512,512]{1,0:T(8,128)S(1)}, u32[]{:S(2)}) %copy-start.3) | copy-done | bytes 1048600
  31.9 0.9 %select_bitcast_fusion.1 = f32[2,128,512]{2,1,0:T(8,128)} fusion(f32[2,2,128,512]{3,2,1,0:T(8,128)S(1)} %bitcast.120, pred[]{:T(512)S(6)} %ne.24), kind=kLoop, calls=%fused_computation.11 | loop fusion | flops 131072 | bytes 1572865 | tf_op jit(solution)/shard_map/jit(_where)/select_n | solution.py:48
  33.0 2.0 %collective-permute-done.2 = f32[2,128,512]{2,1,0:T(8,128)} collective-permute-done((f32[2,128,512]{2,1,0:T(8,128)}, f32[2,128,512]{2,1,0:T(8,128)}, u32[]{:S(2)}, u32[]{:S(2)}) %collective-permute-start.2) | collective-permute-done | bytes 524320 | tf_op jit(solution)/shard_map/ppermute | solution.py:29
  35.0 1.3 %collective-permute-start.6 = (f32[3,2048]{1,0:T(4,128)S(1)}, f32[3,2048]{1,0:T(4,128)S(1)}, u32[]{:S(2)}, u32[]{:S(2)}) collective-permute-start(f32[3,2048]{1,0:T(4,128)S(1)} %get-tuple-element.37), channel_id=1, source_target_pairs={{1,0},{2,1},{3,2},{5,4},{6,5},{7,6},{9,8},{10,9},{11,10},{13,12},{... | collective-permute-start | bytes 73736 | tf_op jit(solution)/shard_map/ppermute | solution.py:19
  36.3 1.5 %fusion.1 = f32[1,2,128,512]{3,2,1,0:T(8,128)S(1)} fusion(f32[2,128,512]{2,1,0:T(8,128)} %collective-permute-done.2, f32[2,2,128,512]{3,2,1,0:T(8,128)} %bitcast.121, pred[]{:T(512)S(6)} %ne.24), kind=kLoop, calls=%fused_computation.10 | loop fusion | flops 262144 | bytes 2097153 | tf_op jit(solution)/shard_map/reshape | solution.py:45
  37.9 19.4 %collective-permute-done.6.above_f = f32[3,2048]{1,0:T(4,128)S(1)} collective-permute-done((f32[3,2048]{1,0:T(4,128)S(1)}, f32[3,2048]{1,0:T(4,128)S(1)}, u32[]{:S(2)}, u32[]{:S(2)}) %collective-permute-start.6) | collective-permute-done | bytes 24608 | tf_op jit(solution)/shard_map/ppermute | solution.py:19
  57.2 3.6 %collective-permute-start.7 = (f32[3,2048]{1,0:T(4,128)S(1)}, f32[3,2048]{1,0:T(4,128)S(1)}, u32[]{:S(2)}, u32[]{:S(2)}) collective-permute-start(f32[3,2048]{1,0:T(4,128)S(1)} %get-tuple-element.36), channel_id=1, source_target_pairs={{0,1},{1,2},{4,5},{5,6},{8,9},{9,10},{12,13},{13,14},{16,17},{17,1... | collective-permute-start | bytes 73736 | tf_op jit(solution)/shard_map/ppermute | solution.py:24
  60.9 1.5 %collective-permute-done.7.below_f = f32[3,2048]{1,0:T(4,128)S(1)} collective-permute-done((f32[3,2048]{1,0:T(4,128)S(1)}, f32[3,2048]{1,0:T(4,128)S(1)}, u32[]{:S(2)}, u32[]{:S(2)}) %collective-permute-start.7) | collective-permute-done | bytes 24608 | tf_op jit(solution)/shard_map/ppermute | solution.py:24
  62.5 1.5 %collective-permute-start.3 = (f32[1,128,512]{2,1,0:T(8,128)S(1)}, f32[1,128,512]{2,1,0:T(8,128)S(1)}, u32[]{:S(2)}, u32[]{:S(2)}) collective-permute-start(f32[1,128,512]{2,1,0:T(8,128)S(1)} %select_bitcast_fusion.4), channel_id=1, source_target_pairs={{0,8},{4,12},{8,0},{12,4},{1,9},{5,13},{9,1},{13,5},{2,10},{6,14},... | collective-permute-start | bytes 786440 | tf_op jit(solution)/shard_map/ppermute | solution.py:29
  64.0 4.6 %first.1 = (f32[4,232,384]{2,1,0:T(8,128)S(1)}, bf16[2048,384]{1,0:T(8,128)(2,1)S(1)}, bf16[2048,384]{1,0:T(8,128)(2,1)S(1)}) custom-call(s32[1,2048]{1,0:T(1,128)S(1)} %copy-done.1, bf16[2048,384]{1,0:T(8,128)(2,1)} %collective-permute-done.4.above_ref, bf16[2048,384]{1,0:T(8,128)(2,1)} %collective-permute-done.5.below_ref, ...), custom_call_target="tpu_custom_call" | custom-call | flops 1409286144 | bytes 9437184 | tf_op jit(solution)/shard_map/first/pallas_call | solution.py:279
  68.6 2.2 %second.1 = f32[4,352,128]{2,1,0:T(8,128)S(1)} custom-call(bf16[2048,128]{1,0:T(8,128)(2,1)S(1)} %collective-permute-done.10.above_ref, bf16[2048,128]{1,0:T(8,128)(2,1)S(1)} %collective-permute-done.11.below_ref, bf16[2048,384]{1,0:T(8,128)(2,1)S(1)} %get-tuple-element.19.above_1, bf16[2048,384]{1,0:T(8,128)(2,1)S(1)} %get-tuple-element.20.below_1, ...), custom_call_target="tpu_custom_call" | custom-call | flops 738197504 | bytes 5767168 | tf_op jit(solution)/shard_map/second/pallas_call | solution.py:331
  71.1 0.6 collective-permute-start.8
  71.7 1.0 %collective-permute-done.12 = f32[2,352,128]{2,1,0:T(8,128)S(1)} collective-permute-done((f32[2,352,128]{2,1,0:T(8,128)S(1)}, f32[2,352,128]{2,1,0:T(8,128)S(1)}, u32[]{:S(2)}, u32[]{:S(2)}) %collective-permute-start.12) | collective-permute-done | bytes 360480 | tf_op jit(solution)/shard_map/ppermute | solution.py:29
  72.7 0.6 collective-permute-start.13
  73.9 1.2 %collective-permute-start.9 = (bf16[1,240,384]{2,1,0:T(8,128)(2,1)S(1)}, bf16[1,240,384]{2,1,0:T(8,128)(2,1)S(1)}, u32[]{:S(2)}, u32[]{:S(2)}) collective-permute-start(bf16[1,240,384]{2,1,0:T(8,128)(2,1)S(1)} %pad_maximum_fusion), channel_id=1, source_target_pairs={{0,8},{4,12},{8,0},{12,4},{1,9},{5,13},{9,1},{13,5},{2,10},{6,14},... | collective-permute-start | bytes 552968 | tf_op jit(solution)/shard_map/ppermute | solution.py:29
  75.2 3.0 %collective-permute-done.13 = bf16[1,352,128]{2,1,0:T(8,128)(2,1)S(1)} collective-permute-done((bf16[1,352,128]{2,1,0:T(8,128)(2,1)S(1)}, bf16[1,352,128]{2,1,0:T(8,128)(2,1)S(1)}, u32[]{:S(2)}, u32[]{:S(2)}) %collective-permute-start.13) | collective-permute-done | bytes 90144 | tf_op jit(solution)/shard_map/ppermute | solution.py:29
  78.2 3.2 %collective-permute-done.9 = bf16[1,240,384]{2,1,0:T(8,128)(2,1)S(1)} collective-permute-done((bf16[1,240,384]{2,1,0:T(8,128)(2,1)S(1)}, bf16[1,240,384]{2,1,0:T(8,128)(2,1)S(1)}, u32[]{:S(2)}, u32[]{:S(2)}) %collective-permute-start.9) | collective-permute-done | bytes 184352 | tf_op jit(solution)/shard_map/ppermute | solution.py:29
  81.7 1.3 %collective-permute-start.14 = (f32[128,512]{1,0:T(8,128)S(1)}, f32[128,512]{1,0:T(8,128)S(1)}, u32[]{:S(2)}, u32[]{:S(2)}) collective-permute-start(f32[128,512]{1,0:T(8,128)S(1)} %maximum_maximum_fusion), channel_id=1, source_target_pairs={{1,0},{2,1},{3,2},{5,4},{6,5},{7,6},{9,8},{10,9},{11,10},{13,12},{... | collective-permute-start | bytes 786440 | tf_op jit(solution)/shard_map/ppermute | solution.py:19
  83.1 8.7 %collective-permute-done.14 = f32[128,512]{1,0:T(8,128)S(1)} collective-permute-done((f32[128,512]{1,0:T(8,128)S(1)}, f32[128,512]{1,0:T(8,128)S(1)}, u32[]{:S(2)}, u32[]{:S(2)}) %collective-permute-start.14) | collective-permute-done | bytes 262176 | tf_op jit(solution)/shard_map/ppermute | solution.py:19
  91.8 1.0 %maximum_select_fusion = f32[1,128,3,512]{3,1,2,0:T(8,128)} fusion(f32[1,128,1,512]{3,1,2,0:T(8,128)S(1)} %bitcast.122, f32[1,128,1,512]{3,1,2,0:T(8,128)S(1)} %maximum_bitcast_fusion, f32[1,128,1,512]{3,1,2,0:T(8,128)S(1)} %fusion.3, pred[3]{0:T(512)(128)(4,1)S(1)} %iota_compare_fusion.1), kind=kLoop, calls=%fused_computation.1 | loop fusion | flops 589824 | bytes 1572867 | tf_op jit(solution)/shard_map/jit(_where)/select_n | solution.py:408
  (53 shorter events, 2.1 us)
Async XLA Ops:
  0.0 0.7 copy-start
  0.7 0.9 copy-start.2
  1.6 21.1 %copy-start.1 = (s32[1,2048]{1,0:T(1,128)S(1)}, s32[1,2048]{1,0:T(1,128)}, u32[]{:S(2)}) copy-start(s32[1,2048]{1,0:T(1,128)} %observed_ref.3) | copy-start | bytes 24580
  5.8 62.8 %collective-permute-start.10 = (bf16[2048,128]{1,0:T(8,128)(2,1)}, bf16[2048,128]{1,0:T(8,128)(2,1)S(1)}, u32[]{:S(2)}, u32[]{:S(2)}) collective-permute-start(bf16[2048,128]{1,0:T(8,128)(2,1)} %get-tuple-element.17), channel_id=1, source_target_pairs={{1,0},{2,1},{3,2},{5,4},{6,5},{7,6},{9,8},{10,9},{11,10},{13,12},{... | collective-permute-start | bytes 1572872 | tf_op jit(solution)/shard_map/ppermute | solution.py:19
  7.0 61.5 %collective-permute-start.11 = (bf16[2048,128]{1,0:T(8,128)(2,1)}, bf16[2048,128]{1,0:T(8,128)(2,1)S(1)}, u32[]{:S(2)}, u32[]{:S(2)}) collective-permute-start(bf16[2048,128]{1,0:T(8,128)(2,1)} %get-tuple-element.18), channel_id=1, source_target_pairs={{0,1},{1,2},{4,5},{5,6},{8,9},{9,10},{12,13},{13,14},{16,17},{17,1... | collective-permute-start | bytes 1572872 | tf_op jit(solution)/shard_map/ppermute | solution.py:24
  15.6 48.3 %collective-permute-start.4 = (bf16[2048,384]{1,0:T(8,128)(2,1)}, bf16[2048,384]{1,0:T(8,128)(2,1)}, u32[]{:S(2)}, u32[]{:S(2)}) collective-permute-start(bf16[2048,384]{1,0:T(8,128)(2,1)} %get-tuple-element.14), channel_id=1, source_target_pairs={{1,0},{2,1},{3,2},{5,4},{6,5},{7,6},{9,8},{10,9},{11,10},{13,12},{... | collective-permute-start | bytes 4718600 | tf_op jit(solution)/shard_map/ppermute | solution.py:19
  16.9 47.0 %collective-permute-start.5 = (bf16[2048,384]{1,0:T(8,128)(2,1)}, bf16[2048,384]{1,0:T(8,128)(2,1)}, u32[]{:S(2)}, u32[]{:S(2)}) collective-permute-start(bf16[2048,384]{1,0:T(8,128)(2,1)} %get-tuple-element.15), channel_id=1, source_target_pairs={{0,1},{1,2},{4,5},{5,6},{8,9},{9,10},{12,13},{13,14},{16,17},{17,1... | collective-permute-start | bytes 4718600 | tf_op jit(solution)/shard_map/ppermute | solution.py:24
  22.7 1.2 %collective-permute-start = (f32[8,512]{1,0:T(8,128)S(1)}, f32[8,512]{1,0:T(8,128)S(1)}, u32[]{:S(2)}, u32[]{:S(2)}) collective-permute-start(f32[8,512]{1,0:T(8,128)S(1)} %get-tuple-element.13), channel_id=1, source_target_pairs={{0,4},{4,0},{8,12},{12,8},{1,5},{5,1},{9,13},{13,9},{2,6},{6,2},{1... | collective-permute-start | bytes 49160 | tf_op jit(solution)/shard_map/ppermute | solution.py:29
  23.9 3.7 %collective-permute-start.1 = (f32[8,512]{1,0:T(8,128)S(1)}, f32[8,512]{1,0:T(8,128)S(1)}, u32[]{:S(2)}, u32[]{:S(2)}) collective-permute-start(f32[8,512]{1,0:T(8,128)S(1)} %add.45), channel_id=1, source_target_pairs={{0,8},{4,12},{8,0},{12,4},{1,9},{5,13},{9,1},{13,5},{2,10},{6,14},... | collective-permute-start | bytes 49160 | tf_op jit(solution)/shard_map/ppermute | solution.py:29
  30.9 1.0 %copy-start.3 = (f32[512,512]{1,0:T(8,128)}, f32[512,512]{1,0:T(8,128)S(1)}, u32[]{:S(2)}) copy-start(f32[512,512]{1,0:T(8,128)S(1)} %fusion.21) | copy-start | bytes 3145732
  32.8 2.3 %collective-permute-start.2 = (f32[2,128,512]{2,1,0:T(8,128)}, f32[2,128,512]{2,1,0:T(8,128)}, u32[]{:S(2)}, u32[]{:S(2)}) collective-permute-start(f32[2,128,512]{2,1,0:T(8,128)} %select_bitcast_fusion.1), channel_id=1, source_target_pairs={{0,4},{4,0},{8,12},{12,8},{1,5},{5,1},{9,13},{13,9},{2,6},{6,2},{1... | collective-permute-start | bytes 1572872 | tf_op jit(solution)/shard_map/ppermute | solution.py:29
  35.0 22.2 %collective-permute-start.6 = (f32[3,2048]{1,0:T(4,128)S(1)}, f32[3,2048]{1,0:T(4,128)S(1)}, u32[]{:S(2)}, u32[]{:S(2)}) collective-permute-start(f32[3,2048]{1,0:T(4,128)S(1)} %get-tuple-element.37), channel_id=1, source_target_pairs={{1,0},{2,1},{3,2},{5,4},{6,5},{7,6},{9,8},{10,9},{11,10},{13,12},{... | collective-permute-start | bytes 73736 | tf_op jit(solution)/shard_map/ppermute | solution.py:19
  57.2 5.2 %collective-permute-start.7 = (f32[3,2048]{1,0:T(4,128)S(1)}, f32[3,2048]{1,0:T(4,128)S(1)}, u32[]{:S(2)}, u32[]{:S(2)}) collective-permute-start(f32[3,2048]{1,0:T(4,128)S(1)} %get-tuple-element.36), channel_id=1, source_target_pairs={{0,1},{1,2},{4,5},{5,6},{8,9},{9,10},{12,13},{13,14},{16,17},{17,1... | collective-permute-start | bytes 73736 | tf_op jit(solution)/shard_map/ppermute | solution.py:24
  62.5 9.2 %collective-permute-start.3 = (f32[1,128,512]{2,1,0:T(8,128)S(1)}, f32[1,128,512]{2,1,0:T(8,128)S(1)}, u32[]{:S(2)}, u32[]{:S(2)}) collective-permute-start(f32[1,128,512]{2,1,0:T(8,128)S(1)} %select_bitcast_fusion.4), channel_id=1, source_target_pairs={{0,8},{4,12},{8,0},{12,4},{1,9},{5,13},{9,1},{13,5},{2,10},{6,14},... | collective-permute-start | bytes 786440 | tf_op jit(solution)/shard_map/ppermute | solution.py:29
  70.9 1.7 %collective-permute-start.12 = (f32[2,352,128]{2,1,0:T(8,128)S(1)}, f32[2,352,128]{2,1,0:T(8,128)S(1)}, u32[]{:S(2)}, u32[]{:S(2)}) collective-permute-start(f32[2,352,128]{2,1,0:T(8,128)S(1)} %select_bitcast_fusion.2), channel_id=1, source_target_pairs={{0,4},{4,0},{8,12},{12,8},{1,5},{5,1},{9,13},{13,9},{2,6},{6,2},{1... | collective-permute-start | bytes 1081352 | tf_op jit(solution)/shard_map/ppermute | solution.py:29
  71.1 2.6 %collective-permute-start.8 = (f32[2,232,384]{2,1,0:T(8,128)S(1)}, f32[2,232,384]{2,1,0:T(8,128)S(1)}, u32[]{:S(2)}, u32[]{:S(2)}) collective-permute-start(f32[2,232,384]{2,1,0:T(8,128)S(1)} %select_bitcast_fusion), channel_id=1, source_target_pairs={{0,4},{4,0},{8,12},{12,8},{1,5},{5,1},{9,13},{13,9},{2,6},{6,2},{1... | collective-permute-start | bytes 2138120 | tf_op jit(solution)/shard_map/ppermute | solution.py:29
  72.7 5.5 %collective-permute-start.13 = (bf16[1,352,128]{2,1,0:T(8,128)(2,1)S(1)}, bf16[1,352,128]{2,1,0:T(8,128)(2,1)S(1)}, u32[]{:S(2)}, u32[]{:S(2)}) collective-permute-start(bf16[1,352,128]{2,1,0:T(8,128)(2,1)S(1)} %fusion.7), channel_id=1, source_target_pairs={{0,8},{4,12},{8,0},{12,4},{1,9},{5,13},{9,1},{13,5},{2,10},{6,14},... | collective-permute-start | bytes 270344 | tf_op jit(solution)/shard_map/ppermute | solution.py:29
  73.9 7.5 %collective-permute-start.9 = (bf16[1,240,384]{2,1,0:T(8,128)(2,1)S(1)}, bf16[1,240,384]{2,1,0:T(8,128)(2,1)S(1)}, u32[]{:S(2)}, u32[]{:S(2)}) collective-permute-start(bf16[1,240,384]{2,1,0:T(8,128)(2,1)S(1)} %pad_maximum_fusion), channel_id=1, source_target_pairs={{0,8},{4,12},{8,0},{12,4},{1,9},{5,13},{9,1},{13,5},{2,10},{6,14},... | collective-permute-start | bytes 552968 | tf_op jit(solution)/shard_map/ppermute | solution.py:29
  81.7 10.1 %collective-permute-start.14 = (f32[128,512]{1,0:T(8,128)S(1)}, f32[128,512]{1,0:T(8,128)S(1)}, u32[]{:S(2)}, u32[]{:S(2)}) collective-permute-start(f32[128,512]{1,0:T(8,128)S(1)} %maximum_maximum_fusion), channel_id=1, source_target_pairs={{1,0},{2,1},{3,2},{5,4},{6,5},{7,6},{9,8},{10,9},{11,10},{13,12},{... | collective-permute-start | bytes 786440 | tf_op jit(solution)/shard_map/ppermute | solution.py:19

commit v7 on v6

--- a/solution.py
+++ b/solution.py
@@ -2,7 +2,6 @@
 
 import jax
 import jax.numpy as jnp
-import numpy as np
 from jax import lax
 from jax.experimental import pallas as pl
 from jax.experimental.pallas import tpu as pltpu
@@ -14,14 +13,23 @@
 EPSILON = 1e-05
 
 
-def from_above(shard, axis):
+def trade(shard, axis, first):
     peers = lax.axis_size(axis)
-    return lax.ppermute(shard, axis, [(i, i - 1) for i in range(1, peers)])
-
-
-def from_below(shard, axis):
+    pairs = [(i, i + 1) for i in range(first, peers - 1, 2)]
+    return lax.ppermute(shard, axis, pairs + [(high, low) for low, high in pairs])
+
+
+def bring_back(shard, axis):
     peers = lax.axis_size(axis)
-    return lax.ppermute(shard, axis, [(i, i + 1) for i in range(peers - 2)])
+    return lax.ppermute(shard, axis, [(i, i - 1) for i in range(1, peers - 1)])
+
+
+def is_even():
+    return lax.axis_index("var") % 2 == 0
+
+
+def either(even, one, two):
+    return jnp.where(even, one, two), jnp.where(even, two, one)
 
 
 def swap(shard, axis, bit):
@@ -82,10 +90,11 @@
     return jnp.transpose(jnp.broadcast_to(row.astype(jnp.float32), (lanes, row.shape[1]))) > 0.5
 
 
-def head_kernel(kept, rows, dosage_ref, up_ref, down_ref, held, up_held, down_held, sems):
+def head_kernel(kept, rows, dosage_ref, a_ref, b_ref, held, a_held, b_held, sems):
     samples, width = dosage_ref.shape
-    edge = up_ref.shape[1]
+    edge = a_ref.shape[1]
     block = block_of(samples) // 2
+    even = is_even()
 
     def move(source, target, kind, k):
         part = pl.ds(k * block, block)
@@ -100,10 +109,10 @@
         copy.wait()
         values = held[part, :]
         owners = [values[:, low : low + kept] for low in range(0, width, rows)]
-        up_held[part, :] = jnp.concatenate(owners, axis=1)
-        leaving.append(move(up_held, up_ref, 1, k))
-        down_held[part, :] = held[part, :edge]
-        leaving.append(move(down_held, down_ref, 2, k))
+        up = jnp.concatenate(owners, axis=1)
+        a_held[part, :], b_held[part, :] = either(even, up, values[:, :edge])
+        leaving.append(move(a_held, a_ref, 1, k))
+        leaving.append(move(b_held, b_ref, 2, k))
     for copy in leaving:
         copy.wait()
 
@@ -132,7 +141,7 @@
     )(in_hbm(dosage))
 
 
-def moments_kernel(dosage_ref, observed_ref, chosen_ref, down_2, up_2, sums_ref):
+def moments_kernel(kept, rows, dosage_ref, observed_ref, a_ref, b_ref, sums_ref):
     width = dosage_ref.shape[1]
     lanes = 128
 
@@ -144,26 +153,26 @@
     count = jnp.sum(jnp.where(present, 1.0, 0.0), axis=0, keepdims=True)
     for low in range(0, width, lanes):
         part = slice(low, low + lanes)
-        kept = jnp.where(present, dosage_ref[:, part].astype(jnp.float32), 0.0)
-        sums_ref[0:1, part] += jnp.sum(kept, axis=0, keepdims=True)
-        sums_ref[1:2, part] += jnp.sum(kept * kept, axis=0, keepdims=True)
+        seen = jnp.where(present, dosage_ref[:, part].astype(jnp.float32), 0.0)
+        sums_ref[0:1, part] += jnp.sum(seen, axis=0, keepdims=True)
+        sums_ref[1:2, part] += jnp.sum(seen * seen, axis=0, keepdims=True)
         sums_ref[2:3, part] += count
-    down_2[...] = dosage_ref[:, width - down_2.shape[1] :]
-    up = jnp.dot(dosage_ref[...], chosen_ref[...], preferred_element_type=jnp.float32)
-    up_2[...] = up.astype(jnp.bfloat16)
-
-
-def moments_pass(dosage, observed, chosen):
+    values = dosage_ref[...]
+    up = jnp.concatenate([values[:, low + kept : low + rows] for low in range(0, width, rows)], 1)
+    down = values[:, width - a_ref.shape[1] :]
+    a_ref[...], b_ref[...] = either(is_even(), up, down)
+
+
+def moments_pass(dosage, observed, kept, rows):
     samples, width = dosage.shape
-    block, rest = block_of(samples), chosen.shape[1]
+    block, rest = block_of(samples), width // rows * (rows - kept)
     return pl.pallas_call(
-        moments_kernel,
+        functools.partial(moments_kernel, kept, rows),
         grid=(samples // block,),
         out_shape=(like((samples, rest), jnp.bfloat16),) * 2 + (like((8, width), jnp.float32),),
         in_specs=[
             pl.BlockSpec((block, width), lambda i: (i, 0)),
             pl.BlockSpec((1, block), lambda i: (0, i)),
-            pl.BlockSpec((width, rest), lambda i: (0, 0)),
         ],
         out_specs=(pl.BlockSpec((block, rest), lambda i: (i, 0)),) * 2
         + (pl.BlockSpec((8, width), lambda i: (0, 0)),),
@@ -174,13 +183,42 @@
             transcendentals=0,
         ),
         name="moments",
-    )(in_hbm(dosage), observed, chosen)
-
-
-def finish_moments(sums):
-    centre = sums[0:1] / sums[2:3]
-    spread_inverse = 1.0 / jnp.sqrt(sums[1:2] / sums[2:3] - centre * centre + EPSILON)
-    return jnp.concatenate([centre, spread_inverse], axis=0)
+    )(in_hbm(dosage), observed)
+
+
+def facts_kernel(kept, rows, sums_ref, observed_ref, moments_ref, a_ref, b_ref):
+    width = sums_ref.shape[1]
+    totals = sums_ref[2:3, :]
+    centre = sums_ref[0:1, :] / totals
+    inverse = 1.0 / jnp.sqrt(sums_ref[1:2, :] / totals - centre * centre + EPSILON)
+    moments_ref[0:1, :] = centre
+    moments_ref[1:2, :] = inverse
+    flags = observed_ref[...].astype(jnp.float32)
+    even = is_even()
+    cuts = [(low, low + kept) for low in range(0, width, rows)]
+    cuts += [(low + kept, low + rows) for low in range(0, width, rows)]
+    for line, natural in enumerate((centre, inverse)):
+        ordered = jnp.concatenate([natural[:, low:high] for low, high in cuts], axis=1)
+        one, two = either(even, ordered, natural)
+        a_ref[line : line + 1, :width] = one
+        b_ref[line : line + 1, :width] = two
+    for ref in (a_ref, b_ref):
+        ref[2:3, :] = flags
+        if width < ref.shape[1]:
+            ref[0:2, width:] = jnp.zeros((2, ref.shape[1] - width), jnp.float32)
+
+
+def facts_pass(sums, observed, kept, rows):
+    samples, width = observed.shape[1], sums.shape[1]
+    single = jnp.float32
+    return pl.pallas_call(
+        functools.partial(facts_kernel, kept, rows),
+        out_shape=(like((2, width), single),) + (like((3, samples), single),) * 2,
+        in_specs=[whole()] * 2,
+        out_specs=(whole(),) * 3,
+        compiler_params=pltpu.CompilerParams(vmem_limit_bytes=GRANT),
+        name="facts",
+    )(sums, observed)
 
 
 def standardize(values, present, moments):
@@ -188,13 +226,13 @@
     return jnp.where(present, spread, 0.0).astype(jnp.bfloat16)
 
 
-def decode(values, facts_ref, present, first):
+def decode(values, facts, present, first):
     parts = []
     for low in range(0, values.shape[1], present.shape[1]):
         part = slice(low, low + present.shape[1])
         place = slice(first + low, first + low + present.shape[1])
-        spread = values[:, part].astype(jnp.float32) - facts_ref[0:1, place]
-        spread = spread * facts_ref[1:2, place]
+        spread = values[:, part].astype(jnp.float32) - facts[0:1, place]
+        spread = spread * facts[1:2, place]
         parts.append(jnp.where(present, spread, 0.0).astype(jnp.bfloat16))
     return parts[0] if len(parts) == 1 else jnp.concatenate(parts, axis=1)
 
@@ -207,16 +245,16 @@
 
 def first_kernel(
     observed_ref,
-    above_ref,
-    below_ref,
+    a_ref,
+    b_ref,
     own_ref,
-    above_f,
-    below_f,
+    a_facts,
+    b_facts,
     out_ref,
     above_out,
     below_out,
-    above_held,
-    below_held,
+    a_held,
+    b_held,
     sems,
 ):
     peers, _, edge = out_ref.shape
@@ -234,8 +272,10 @@
     arriving = []
     for k in range(samples // block):
         arriving.append(
-            (move(above_ref, above_held, 0, k), move(below_ref, below_held, 1, k))
+            (move(a_ref, a_held, 0, k), move(b_ref, b_held, 1, k))
         )
+    even = is_even()
+    above_f, below_f = either(even, a_facts[...], b_facts[...])
     shares = [jnp.zeros((1, 128), jnp.float32)] * 2
     for k, copies in enumerate(arriving):
         part = slice(k * block, (k + 1) * block)
@@ -248,11 +288,12 @@
             for share, other in zip(shares, (own_present, below_present))
         ]
         copies[0].wait()
-        above = decode(above_held[part, :], above_f, above_present, 0)
+        copies[1].wait()
+        above, below = either(even, a_held[part, :], b_held[part, :])
+        above = decode(above, above_f, above_present, 0)
         above_out[part, :] = above
         near = cross(own_ref[part, :], above)
-        copies[1].wait()
-        below = decode(below_held[part, :], below_f, below_present, 0)
+        below = decode(below, below_f, below_present, 0)
         below_out[part, :] = below
         far = cross(below, above)
         for owner in range(peers):
@@ -296,18 +337,19 @@
     )(observed, in_hbm(above), in_hbm(below), own, above_f, below_f)
 
 
-def second_kernel(
-    above_ref, below_ref, above_1, below_1, own_ref, above_f, below_f, out_ref
-):
+def second_kernel(a_ref, b_ref, above_1, below_1, own_ref, a_facts, b_facts, out_ref):
     peers, _, rest = out_ref.shape
     samples, width = own_ref.shape
     edge = above_1.shape[1]
     rows, kept, tail = width // peers, edge // peers, rest // peers
     block = block_of(samples)
+    even = is_even()
+    above_f, below_f = either(even, a_facts[...], b_facts[...])
     for k in range(samples // block):
         part = slice(k * block, (k + 1) * block)
-        above = decode(above_ref[part, :], above_f, mask_of(above_f[2:3, part]), edge)
-        below = decode(below_ref[part, :], below_f, mask_of(below_f[2:3, part]), edge)
+        above, below = either(even, a_ref[part, :], b_ref[part, :])
+        above = decode(above, above_f, mask_of(above_f[2:3, part]), edge)
+        below = decode(below, below_f, mask_of(below_f[2:3, part]), edge)
         far = cross(below_1[part, :], above)
         last = cross(below, above_1[part, :])
         corner = cross(below, above)
@@ -344,55 +386,37 @@
 
 
 def per_device(dosage, observed, band_reach):
-    samples, width = dosage.shape
+    _, width = dosage.shape
     peers = lax.axis_size("samp")
     rows = width // peers
     kept = 3 * rows // 4
     tail = rows - kept
-    edge, rest = kept * peers, tail * peers
-    owners = np.arange(peers)[:, None] * rows
-    order = np.concatenate(
-        [
-            (owners + np.arange(0, kept)[None, :]).ravel(),
-            (owners + np.arange(kept, rows)[None, :]).ravel(),
-        ]
-    )
+    rest = tail * peers
     pieces = width // rest
-    chosen = (np.arange(width)[:, None] == order[None, :]).astype(jnp.bfloat16)
-    up_1, down_1 = head_pass(dosage, kept, rows)
-    below_1 = from_below(up_1, "var")
-    above_1 = from_above(down_1, "var")
-    down_2, up_2, sums = moments_pass(dosage, observed, chosen[:, edge:])
+    a_1, b_1 = head_pass(dosage, kept, rows)
+    a_1 = trade(a_1, "var", 0)
+    b_1 = trade(b_1, "var", 1)
+    a_2, b_2, sums = moments_pass(dosage, observed, kept, rows)
     sums = sum_all(sums, "samp")
-    moments = finish_moments(sums)
-    cuts = [(k * rows, k * rows + kept) for k in range(peers)]
-    cuts += [(k * rows + kept, (k + 1) * rows) for k in range(peers)]
-    ordered = jnp.concatenate([moments[:, low:high] for low, high in cuts], axis=1)
-    above_f, below_f = [
-        jnp.concatenate(
-            [jnp.pad(part, ((0, 0), (0, samples - width))), observed.astype(jnp.float32)]
-        )
-        for part in (moments, ordered)
-    ]
-    below_f = from_below(below_f, "var")
-    above_f = from_above(above_f, "var")
-    below_2 = from_below(up_2, "var")
-    above_2 = from_above(down_2, "var")
+    moments, a_f, b_f = facts_pass(sums, observed, kept, rows)
+    a_f = trade(a_f, "var", 0)
+    b_f = trade(b_f, "var", 1)
+    a_2 = trade(a_2, "var", 0)
+    b_2 = trade(b_2, "var", 1)
     own = standardize(dosage, (observed[0] != 0)[:, None], moments)
     own = lax.optimization_barrier(own)
     same = sum_rows(cross(own, own).reshape(peers, rows, width), "samp")
-    one, above_1, below_1 = first_pass(
-        observed, above_1, below_1, own, above_f, below_f, peers
-    )
+    one, above_1, below_1 = first_pass(observed, a_1, b_1, own, a_f, b_f, peers)
     one = sum_rows(one, "samp", rows + kept)
     shares = jnp.maximum(one[rows + kept :], 1.0)
     near_1 = one[:rows] / shares[0:1]
     far_1 = one[rows : rows + kept] / shares[1:2]
-    two = second_pass(
-        above_2, below_2, above_1, below_1, own, above_f, below_f, peers
-    )
+    far_1 = bring_back(far_1, "var")
+    two = second_pass(a_2, b_2, above_1, below_1, own, a_f, b_f, peers)
     two = sum_rows(two, "samp", two.shape[1])
     far_2 = two[rows:] / shares[1:2, :rest]
+    far_2 = bring_back(far_2, "var")
+    near = jnp.concatenate([near_1, two[:rows] / shares[0:1, :rest]], axis=1)
     low = [far_2[kept + k * tail : kept + (k + 1) * tail] for k in range(pieces)]
     far = jnp.concatenate(
         [
@@ -401,8 +425,6 @@
         ],
         axis=0,
     )
-    far = from_above(far, "var")
-    near = jnp.concatenate([near_1, two[:rows] / shares[0:1, :rest]], axis=1)
     result = jnp.stack([same / jnp.maximum(sums[2:3], 1.0), near, far], axis=1)
     keep = jnp.arange(BAND, dtype=jnp.int32) <= band_reach[0]
     return jnp.where(keep[None, :, None], result, jnp.float32(0.0))[None]

time: 93.3 us -> 93.6 us (level)
  waiting for transfers between devices: 41.4 us -> 51 us
  starting transfers between devices: 26 us -> 19.3 us
  local copies, waits for them, and re-layouts: 2.74 us -> 0.77 us
    ppermute x7 -> x8, waiting for transfers between devices: 29.6 us -> 41.1 us  [the longest x6 29.4 us: trade(): lax.ppermute(shard, axis, pairs + [(high, low) for low, high in pairs])]
    ppermute x7 -> x8, starting transfers between devices: 20.1 us -> 13.3 us  [the longest x6 10.7 us: trade(): lax.ppermute(shard, axis, pairs + [(high, low) for low, high in pairs])]
    ppermute x8, waiting for transfers between devices: 11.8 us -> 9.86 us  [swap(): return lax.ppermute(shard, axis, [(i, i ^ bit) for i in range(peers)])]
    unnamed x8 -> x6, local copies, waits for them, and re-layouts: 2.57 us -> 0.7 us
    pallas_call x1 -> x2, Pallas kernels: 4.16 us -> 4.41 us  [the longest x1 4.3 us: moments_pass(): pl.pallas_call(functools.partial(moments_kernel, kept, rows), grid=(sampl...]
  transfers between devices with their start and end apart: 15 -> 16, of which waited for: 10 -> 8; matrix products, arithmetic and copies ran while one was open for 7% -> 7% of each run, Pallas kernels for 11% -> 10%
where the time goes in v7:
time: 93.6 us; the launch traced here: 93.3 us
  waiting for transfers between devices  51 us (54%)
  starting transfers between devices  19.3 us (21%)
  Pallas kernels  13.6 us (15%)
  other arithmetic  6.38 us (7%)
  matrix products  1.28 us (1%)
  between operations  0.97 us (1%)
    ppermute x6, waiting for transfers between devices, trade(): lax.ppermute(shard, axis, pairs + [(high, low) for low, high in pairs])  29.4 us
    ppermute x2, waiting for transfers between devices, bring_back(): return lax.ppermute(shard, axis, [(i, i - 1) for i in range(1, peers - 1)])  11.7 us
    ppermute x6, starting transfers between devices, trade(): lax.ppermute(shard, axis, pairs + [(high, low) for low, high in pairs])  10.7 us
    ppermute x8, waiting for transfers between devices, swap(): return lax.ppermute(shard, axis, [(i, i ^ bit) for i in range(peers)])  9.86 us
    ppermute x8, starting transfers between devices, swap(): return lax.ppermute(shard, axis, [(i, i ^ bit) for i in range(peers)])  6.01 us
    pallas_call x1, Pallas kernels, moments_pass(): pl.pallas_call(functools.partial(moments_kernel, kept, rows), grid=(sampl...  4.3 us
    pallas_call x1, Pallas kernels, first_pass(): pl.pallas_call(first_kernel, out_shape=(like(tall, jnp.float32),) + (like...  3.92 us
    pallas_call x1, Pallas kernels, head_pass(): pl.pallas_call(functools.partial(head_kernel, kept, rows), out_shape=(lik...  2.99 us
  transfers between devices with their start and end apart: 16, of which 8 were waited for; matrix products, arithmetic and copies ran while one was open for 7% of the time, Pallas kernels for 10%

profile of v7, /device:TPU:0, one launch (start us, length us, event | category | flops | bytes accessed | tf_op | source)
XLA Modules:
  0.0 93.3 jit_solution(11320001804329981440)
XLA Ops:
  0.0 0.7 copy-done
  0.7 4.3 %moments.1 = (bf16[2048,128]{1,0:T(8,128)(2,1)}, bf16[2048,128]{1,0:T(8,128)(2,1)}, f32[8,512]{1,0:T(8,128)S(1)}) custom-call(bf16[2048,512]{1,0:T(8,128)(2,1)} %dosage_ref.3, s32[1,2048]{1,0:T(1,128)S(1)} %copy-done), custom_call_target="tpu_custom_call" | custom-call | flops 268435456 | bytes 3145728 | tf_op jit(solution)/shard_map/moments/pallas_call | solution.py:169
  5.0 0.5 collective-permute-start
  5.5 3.0 %head.1 = (bf16[2048,384]{1,0:T(8,128)(2,1)}, bf16[2048,384]{1,0:T(8,128)(2,1)}) custom-call(bf16[2048,512]{1,0:T(8,128)(2,1)} %dosage_ref.3), custom_call_target="tpu_custom_call" | custom-call | tf_op jit(solution)/shard_map/head/pallas_call | solution.py:128
  8.5 2.6 %collective-permute-start.4 = (bf16[2048,384]{1,0:T(8,128)(2,1)}, bf16[2048,384]{1,0:T(8,128)(2,1)}, u32[]{:S(2)}, u32[]{:S(2)}) collective-permute-start(bf16[2048,384]{1,0:T(8,128)(2,1)} %get-tuple-element.18), channel_id=1, source_target_pairs={{0,1},{2,3},{1,0},{3,2},{4,5},{6,7},{5,4},{7,6},{8,9},{10,11},{9,8... | collective-permute-start | bytes 4718600 | tf_op jit(solution)/shard_map/ppermute | solution.py:19
  11.1 1.9 %collective-permute-start.5 = (bf16[2048,384]{1,0:T(8,128)(2,1)}, bf16[2048,384]{1,0:T(8,128)(2,1)}, u32[]{:S(2)}, u32[]{:S(2)}) collective-permute-start(bf16[2048,384]{1,0:T(8,128)(2,1)} %get-tuple-element.19), channel_id=1, source_target_pairs={{1,2},{2,1},{5,6},{6,5},{9,10},{10,9},{13,14},{14,13},{17,18},{18,... | collective-permute-start | bytes 4718600 | tf_op jit(solution)/shard_map/ppermute | solution.py:19
  13.0 1.5 %collective-permute-start.1 = (f32[8,512]{1,0:T(8,128)S(1)}, f32[8,512]{1,0:T(8,128)S(1)}, u32[]{:S(2)}, u32[]{:S(2)}) collective-permute-start(f32[8,512]{1,0:T(8,128)S(1)} %add.35), channel_id=1, source_target_pairs={{0,8},{4,12},{8,0},{12,4},{1,9},{5,13},{9,1},{13,5},{2,10},{6,14},... | collective-permute-start | bytes 49160 | tf_op jit(solution)/shard_map/ppermute | solution.py:37
  14.5 2.2 %collective-permute-done.1 = f32[8,512]{1,0:T(8,128)S(1)} collective-permute-done((f32[8,512]{1,0:T(8,128)S(1)}, f32[8,512]{1,0:T(8,128)S(1)}, u32[]{:S(2)}, u32[]{:S(2)}) %collective-permute-start.1) | collective-permute-done | bytes 16416 | tf_op jit(solution)/shard_map/ppermute | solution.py:37
  16.9 1.9 %select_convert_fusion.own_ref = bf16[2048,512]{1,0:T(8,128)(2,1)S(1)} fusion(bf16[2048,512]{1,0:T(8,128)(2,1)} %dosage_ref.3, f32[512]{0:T(512)S(1)} %bitcast.125, f32[512]{0:T(512)S(1)} %bitcast.124, pred[2048]{0:T(1024)(128)(4,1)S(1)} %compare_reduce_fusion), kind=kLoop, calls=%fused_computation | loop fusion | flops 5242880 | bytes 4200448 | tf_op jit(solution)/shard_map/convert_element_type | solution.py:226
  18.8 1.3 %fusion.13 = f32[512,512]{1,0:T(8,128)S(1)} fusion(bf16[2048,512]{1,0:T(8,128)(2,1)S(1)} %select_convert_fusion.own_ref), kind=kOutput, calls=%fused_computation.52 | convolution fusion | flops 1073741824 | bytes 3145728 | tf_op jit(solution)/shard_map/dot_general | solution.py:241
  20.1 1.1 %select_bitcast_fusion.1 = f32[2,128,512]{2,1,0:T(8,128)} fusion(f32[2,2,128,512]{3,2,1,0:T(8,128)S(1)} %bitcast.121, pred[]{:T(512)S(6)} %ne.24), kind=kLoop, calls=%fused_computation.11 | loop fusion | flops 131072 | bytes 1572865 | tf_op jit(solution)/shard_map/jit(_where)/select_n | solution.py:56
  21.2 3.3 %collective-permute-start.10 = (bf16[2048,128]{1,0:T(8,128)(2,1)}, bf16[2048,128]{1,0:T(8,128)(2,1)S(1)}, u32[]{:S(2)}, u32[]{:S(2)}) collective-permute-start(bf16[2048,128]{1,0:T(8,128)(2,1)} %get-tuple-element.23), channel_id=1, source_target_pairs={{0,1},{2,3},{1,0},{3,2},{4,5},{6,7},{5,4},{7,6},{8,9},{10,11},{9,8... | collective-permute-start | bytes 1572872 | tf_op jit(solution)/shard_map/ppermute | solution.py:19
  24.4 0.7 collective-permute-start.11
  25.8 1.6 %collective-permute-start.6 = (f32[3,2048]{1,0:T(4,128)S(1)}, f32[3,2048]{1,0:T(4,128)S(1)}, u32[]{:S(2)}, u32[]{:S(2)}) collective-permute-start(f32[3,2048]{1,0:T(4,128)S(1)} %get-tuple-element.20), channel_id=1, source_target_pairs={{0,1},{2,3},{1,0},{3,2},{4,5},{6,7},{5,4},{7,6},{8,9},{10,11},{9,8... | collective-permute-start | bytes 73736 | tf_op jit(solution)/shard_map/ppermute | solution.py:19
  27.4 1.5 %fusion.1 = f32[1,2,128,512]{3,2,1,0:T(8,128)S(1)} fusion(f32[2,128,512]{2,1,0:T(8,128)} %collective-permute-done.2, f32[2,2,128,512]{3,2,1,0:T(8,128)} %bitcast.122, pred[]{:T(512)S(6)} %ne.24), kind=kLoop, calls=%fused_computation.10 | loop fusion | flops 262144 | bytes 2097153 | tf_op jit(solution)/shard_map/reshape | solution.py:53
  28.9 29.4 %collective-permute-done.6.a_facts = f32[3,2048]{1,0:T(4,128)S(1)} collective-permute-done((f32[3,2048]{1,0:T(4,128)S(1)}, f32[3,2048]{1,0:T(4,128)S(1)}, u32[]{:S(2)}, u32[]{:S(2)}) %collective-permute-start.6) | collective-permute-done | bytes 24608 | tf_op jit(solution)/shard_map/ppermute | solution.py:19
  58.3 0.7 collective-permute-start.7
  59.0 1.7 %collective-permute-start.3 = (f32[1,128,512]{2,1,0:T(8,128)S(1)}, f32[1,128,512]{2,1,0:T(8,128)S(1)}, u32[]{:S(2)}, u32[]{:S(2)}) collective-permute-start(f32[1,128,512]{2,1,0:T(8,128)S(1)} %select_bitcast_fusion.4), channel_id=1, source_target_pairs={{0,8},{4,12},{8,0},{12,4},{1,9},{5,13},{9,1},{13,5},{2,10},{6,14},... | collective-permute-start | bytes 786440 | tf_op jit(solution)/shard_map/ppermute | solution.py:37
  60.8 3.9 %first.1 = (f32[4,232,384]{2,1,0:T(8,128)S(1)}, bf16[2048,384]{1,0:T(8,128)(2,1)S(1)}, bf16[2048,384]{1,0:T(8,128)(2,1)S(1)}) custom-call(s32[1,2048]{1,0:T(1,128)S(1)} %copy-done.1, bf16[2048,384]{1,0:T(8,128)(2,1)} %collective-permute-done.4.a_ref, bf16[2048,384]{1,0:T(8,128)(2,1)} %collective-permute-done.5.b_ref, ...), custom_call_target="tpu_custom_call" | custom-call | flops 1409286144 | bytes 9437184 | tf_op jit(solution)/shard_map/first/pallas_call | solution.py:320
  64.7 2.3 %second.1 = f32[4,352,128]{2,1,0:T(8,128)S(1)} custom-call(bf16[2048,128]{1,0:T(8,128)(2,1)S(1)} %collective-permute-done.10.a_ref, bf16[2048,128]{1,0:T(8,128)(2,1)S(1)} %collective-permute-done.11.b_ref, bf16[2048,384]{1,0:T(8,128)(2,1)S(1)} %get-tuple-element.25.above_1, bf16[2048,384]{1,0:T(8,128)(2,1)S(1)} %get-tuple-element.26.below_1, ...), custom_call_target="tpu_custom_call" | custom-call | flops 738197504 | bytes 5767168 | tf_op jit(solution)/shard_map/second/pallas_call | solution.py:373
  67.2 0.6 collective-permute-start.8
  67.9 1.0 %collective-permute-done.12 = f32[2,352,128]{2,1,0:T(8,128)S(1)} collective-permute-done((f32[2,352,128]{2,1,0:T(8,128)S(1)}, f32[2,352,128]{2,1,0:T(8,128)S(1)}, u32[]{:S(2)}, u32[]{:S(2)}) %collective-permute-start.12) | collective-permute-done | bytes 360480 | tf_op jit(solution)/shard_map/ppermute | solution.py:37
  68.9 0.4 collective-permute-start.13
  69.3 0.5 collective-permute-done.8
  70.1 1.2 %collective-permute-start.9 = (bf16[1,240,384]{2,1,0:T(8,128)(2,1)S(1)}, bf16[1,240,384]{2,1,0:T(8,128)(2,1)S(1)}, u32[]{:S(2)}, u32[]{:S(2)}) collective-permute-start(bf16[1,240,384]{2,1,0:T(8,128)(2,1)S(1)} %pad_maximum_fusion), channel_id=1, source_target_pairs={{0,8},{4,12},{8,0},{12,4},{1,9},{5,13},{9,1},{13,5},{2,10},{6,14},... | collective-permute-start | bytes 552968 | tf_op jit(solution)/shard_map/ppermute | solution.py:37
  71.3 3.0 %collective-permute-done.13 = bf16[1,352,128]{2,1,0:T(8,128)(2,1)S(1)} collective-permute-done((bf16[1,352,128]{2,1,0:T(8,128)(2,1)S(1)}, bf16[1,352,128]{2,1,0:T(8,128)(2,1)S(1)}, u32[]{:S(2)}, u32[]{:S(2)}) %collective-permute-start.13) | collective-permute-done | bytes 90144 | tf_op jit(solution)/shard_map/ppermute | solution.py:37
  74.4 3.2 %collective-permute-done.9 = bf16[1,240,384]{2,1,0:T(8,128)(2,1)S(1)} collective-permute-done((bf16[1,240,384]{2,1,0:T(8,128)(2,1)S(1)}, bf16[1,240,384]{2,1,0:T(8,128)(2,1)S(1)}, u32[]{:S(2)}, u32[]{:S(2)}) %collective-permute-start.9) | collective-permute-done | bytes 184352 | tf_op jit(solution)/shard_map/ppermute | solution.py:37
  77.8 1.3 %collective-permute-start.15 = (f32[224,128]{1,0:T(8,128)S(1)}, f32[224,128]{1,0:T(8,128)S(1)}, u32[]{:S(2)}, u32[]{:S(2)}) collective-permute-start(f32[224,128]{1,0:T(8,128)S(1)} %fusion.6), channel_id=1, source_target_pairs={{1,0},{2,1},{5,4},{6,5},{9,8},{10,9},{13,12},{14,13},{17,16},{18,1... | collective-permute-start | bytes 344072 | tf_op jit(solution)/shard_map/ppermute | solution.py:24
  79.1 1.3 %collective-permute-start.14 = (f32[96,384]{1,0:T(8,128)S(1)}, f32[96,384]{1,0:T(8,128)S(1)}, u32[]{:S(2)}, u32[]{:S(2)}) collective-permute-start(f32[96,384]{1,0:T(8,128)S(1)} %fusion.5), channel_id=1, source_target_pairs={{1,0},{2,1},{5,4},{6,5},{9,8},{10,9},{13,12},{14,13},{17,16},{18,1... | collective-permute-start | bytes 442376 | tf_op jit(solution)/shard_map/ppermute | solution.py:24
  80.5 9.1 %collective-permute-done.15 = f32[224,128]{1,0:T(8,128)S(1)} collective-permute-done((f32[224,128]{1,0:T(8,128)S(1)}, f32[224,128]{1,0:T(8,128)S(1)}, u32[]{:S(2)}, u32[]{:S(2)}) %collective-permute-start.15) | collective-permute-done | bytes 114720 | tf_op jit(solution)/shard_map/ppermute | solution.py:24
  89.6 2.6 %collective-permute-done.14 = f32[96,384]{1,0:T(8,128)S(1)} collective-permute-done((f32[96,384]{1,0:T(8,128)S(1)}, f32[96,384]{1,0:T(8,128)S(1)}, u32[]{:S(2)}, u32[]{:S(2)}) %collective-permute-start.14) | collective-permute-done | bytes 147488 | tf_op jit(solution)/shard_map/ppermute | solution.py:24
  92.2 1.0 %maximum_select_fusion = f32[1,128,3,512]{3,1,2,0:T(8,128)} fusion(f32[1,128,1,512]{3,1,2,0:T(8,128)S(1)} %maximum_bitcast_fusion.1, f32[1,128,1,512]{3,1,2,0:T(8,128)S(1)} %maximum_bitcast_fusion, f32[1,128,1,512]{3,1,2,0:T(8,128)S(1)} %fusion.3, pred[3]{0:T(512)(128)(4,1)S(1)} %iota_compare_fusion), kind=kLoop, calls=%fused_computation.1 | loop fusion | flops 589824 | bytes 1572867 | tf_op jit(solution)/shard_map/jit(_where)/select_n | solution.py:430
  (49 shorter events, 1.1 us)
Async XLA Ops:
  0.0 0.7 copy-start
  0.7 13.8 %copy-start.1 = (s32[1,2048]{1,0:T(1,128)S(1)}, s32[1,2048]{1,0:T(1,128)}, u32[]{:S(2)}) copy-start(s32[1,2048]{1,0:T(1,128)} %observed_ref.5) | copy-start | bytes 24580
  5.0 8.0 %collective-permute-start = (f32[8,512]{1,0:T(8,128)S(1)}, f32[8,512]{1,0:T(8,128)S(1)}, u32[]{:S(2)}, u32[]{:S(2)}) collective-permute-start(f32[8,512]{1,0:T(8,128)S(1)} %get-tuple-element.16), channel_id=1, source_target_pairs={{0,4},{4,0},{8,12},{12,8},{1,5},{5,1},{9,13},{13,9},{2,6},{6,2},{1... | collective-permute-start | bytes 49160 | tf_op jit(solution)/shard_map/ppermute | solution.py:37
  8.5 52.3 %collective-permute-start.4 = (bf16[2048,384]{1,0:T(8,128)(2,1)}, bf16[2048,384]{1,0:T(8,128)(2,1)}, u32[]{:S(2)}, u32[]{:S(2)}) collective-permute-start(bf16[2048,384]{1,0:T(8,128)(2,1)} %get-tuple-element.18), channel_id=1, source_target_pairs={{0,1},{2,3},{1,0},{3,2},{4,5},{6,7},{5,4},{7,6},{8,9},{10,11},{9,8... | collective-permute-start | bytes 4718600 | tf_op jit(solution)/shard_map/ppermute | solution.py:19
  11.1 49.7 %collective-permute-start.5 = (bf16[2048,384]{1,0:T(8,128)(2,1)}, bf16[2048,384]{1,0:T(8,128)(2,1)}, u32[]{:S(2)}, u32[]{:S(2)}) collective-permute-start(bf16[2048,384]{1,0:T(8,128)(2,1)} %get-tuple-element.19), channel_id=1, source_target_pairs={{1,2},{2,1},{5,6},{6,5},{9,10},{10,9},{13,14},{14,13},{17,18},{18,... | collective-permute-start | bytes 4718600 | tf_op jit(solution)/shard_map/ppermute | solution.py:19
  13.0 3.7 %collective-permute-start.1 = (f32[8,512]{1,0:T(8,128)S(1)}, f32[8,512]{1,0:T(8,128)S(1)}, u32[]{:S(2)}, u32[]{:S(2)}) collective-permute-start(f32[8,512]{1,0:T(8,128)S(1)} %add.35), channel_id=1, source_target_pairs={{0,8},{4,12},{8,0},{12,4},{1,9},{5,13},{9,1},{13,5},{2,10},{6,14},... | collective-permute-start | bytes 49160 | tf_op jit(solution)/shard_map/ppermute | solution.py:37
  20.1 4.4 %copy-start.2 = (f32[512,512]{1,0:T(8,128)}, f32[512,512]{1,0:T(8,128)S(1)}, u32[]{:S(2)}) copy-start(f32[512,512]{1,0:T(8,128)S(1)} %fusion.13) | copy-start | bytes 3145732
  21.2 4.7 %collective-permute-start.2 = (f32[2,128,512]{2,1,0:T(8,128)}, f32[2,128,512]{2,1,0:T(8,128)}, u32[]{:S(2)}, u32[]{:S(2)}) collective-permute-start(f32[2,128,512]{2,1,0:T(8,128)} %select_bitcast_fusion.1), channel_id=1, source_target_pairs={{0,4},{4,0},{8,12},{12,8},{1,5},{5,1},{9,13},{13,9},{2,6},{6,2},{1... | collective-permute-start | bytes 1572872 | tf_op jit(solution)/shard_map/ppermute | solution.py:37
  21.2 43.5 %collective-permute-start.10 = (bf16[2048,128]{1,0:T(8,128)(2,1)}, bf16[2048,128]{1,0:T(8,128)(2,1)S(1)}, u32[]{:S(2)}, u32[]{:S(2)}) collective-permute-start(bf16[2048,128]{1,0:T(8,128)(2,1)} %get-tuple-element.23), channel_id=1, source_target_pairs={{0,1},{2,3},{1,0},{3,2},{4,5},{6,7},{5,4},{7,6},{8,9},{10,11},{9,8... | collective-permute-start | bytes 1572872 | tf_op jit(solution)/shard_map/ppermute | solution.py:19
  24.4 40.3 %collective-permute-start.11 = (bf16[2048,128]{1,0:T(8,128)(2,1)}, bf16[2048,128]{1,0:T(8,128)(2,1)S(1)}, u32[]{:S(2)}, u32[]{:S(2)}) collective-permute-start(bf16[2048,128]{1,0:T(8,128)(2,1)} %get-tuple-element.24), channel_id=1, source_target_pairs={{1,2},{2,1},{5,6},{6,5},{9,10},{10,9},{13,14},{14,13},{17,18},{18,... | collective-permute-start | bytes 1572872 | tf_op jit(solution)/shard_map/ppermute | solution.py:19
  25.8 32.5 %collective-permute-start.6 = (f32[3,2048]{1,0:T(4,128)S(1)}, f32[3,2048]{1,0:T(4,128)S(1)}, u32[]{:S(2)}, u32[]{:S(2)}) collective-permute-start(f32[3,2048]{1,0:T(4,128)S(1)} %get-tuple-element.20), channel_id=1, source_target_pairs={{0,1},{2,3},{1,0},{3,2},{4,5},{6,7},{5,4},{7,6},{8,9},{10,11},{9,8... | collective-permute-start | bytes 73736 | tf_op jit(solution)/shard_map/ppermute | solution.py:19
  58.3 0.7 collective-permute-start.7
  59.0 8.7 %collective-permute-start.3 = (f32[1,128,512]{2,1,0:T(8,128)S(1)}, f32[1,128,512]{2,1,0:T(8,128)S(1)}, u32[]{:S(2)}, u32[]{:S(2)}) collective-permute-start(f32[1,128,512]{2,1,0:T(8,128)S(1)} %select_bitcast_fusion.4), channel_id=1, source_target_pairs={{0,8},{4,12},{8,0},{12,4},{1,9},{5,13},{9,1},{13,5},{2,10},{6,14},... | collective-permute-start | bytes 786440 | tf_op jit(solution)/shard_map/ppermute | solution.py:37
  67.1 1.7 %collective-permute-start.12 = (f32[2,352,128]{2,1,0:T(8,128)S(1)}, f32[2,352,128]{2,1,0:T(8,128)S(1)}, u32[]{:S(2)}, u32[]{:S(2)}) collective-permute-start(f32[2,352,128]{2,1,0:T(8,128)S(1)} %select_bitcast_fusion.2), channel_id=1, source_target_pairs={{0,4},{4,0},{8,12},{12,8},{1,5},{5,1},{9,13},{13,9},{2,6},{6,2},{1... | collective-permute-start | bytes 1081352 | tf_op jit(solution)/shard_map/ppermute | solution.py:37
  67.2 2.6 %collective-permute-start.8 = (f32[2,232,384]{2,1,0:T(8,128)S(1)}, f32[2,232,384]{2,1,0:T(8,128)S(1)}, u32[]{:S(2)}, u32[]{:S(2)}) collective-permute-start(f32[2,232,384]{2,1,0:T(8,128)S(1)} %select_bitcast_fusion), channel_id=1, source_target_pairs={{0,4},{4,0},{8,12},{12,8},{1,5},{5,1},{9,13},{13,9},{2,6},{6,2},{1... | collective-permute-start | bytes 2138120 | tf_op jit(solution)/shard_map/ppermute | solution.py:37
  68.9 5.5 %collective-permute-start.13 = (bf16[1,352,128]{2,1,0:T(8,128)(2,1)S(1)}, bf16[1,352,128]{2,1,0:T(8,128)(2,1)S(1)}, u32[]{:S(2)}, u32[]{:S(2)}) collective-permute-start(bf16[1,352,128]{2,1,0:T(8,128)(2,1)S(1)} %fusion.7), channel_id=1, source_target_pairs={{0,8},{4,12},{8,0},{12,4},{1,9},{5,13},{9,1},{13,5},{2,10},{6,14},... | collective-permute-start | bytes 270344 | tf_op jit(solution)/shard_map/ppermute | solution.py:37
  70.1 7.5 %collective-permute-start.9 = (bf16[1,240,384]{2,1,0:T(8,128)(2,1)S(1)}, bf16[1,240,384]{2,1,0:T(8,128)(2,1)S(1)}, u32[]{:S(2)}, u32[]{:S(2)}) collective-permute-start(bf16[1,240,384]{2,1,0:T(8,128)(2,1)S(1)} %pad_maximum_fusion), channel_id=1, source_target_pairs={{0,8},{4,12},{8,0},{12,4},{1,9},{5,13},{9,1},{13,5},{2,10},{6,14},... | collective-permute-start | bytes 552968 | tf_op jit(solution)/shard_map/ppermute | solution.py:37
  77.8 11.8 %collective-permute-start.15 = (f32[224,128]{1,0:T(8,128)S(1)}, f32[224,128]{1,0:T(8,128)S(1)}, u32[]{:S(2)}, u32[]{:S(2)}) collective-permute-start(f32[224,128]{1,0:T(8,128)S(1)} %fusion.6), channel_id=1, source_target_pairs={{1,0},{2,1},{5,4},{6,5},{9,8},{10,9},{13,12},{14,13},{17,16},{18,1... | collective-permute-start | bytes 344072 | tf_op jit(solution)/shard_map/ppermute | solution.py:24
  79.1 13.1 %collective-permute-start.14 = (f32[96,384]{1,0:T(8,128)S(1)}, f32[96,384]{1,0:T(8,128)S(1)}, u32[]{:S(2)}, u32[]{:S(2)}) collective-permute-start(f32[96,384]{1,0:T(8,128)S(1)} %fusion.5), channel_id=1, source_target_pairs={{1,0},{2,1},{5,4},{6,5},{9,8},{10,9},{13,12},{14,13},{17,16},{18,1... | collective-permute-start | bytes 442376 | tf_op jit(solution)/shard_map/ppermute | solution.py:24

commit v8 on v7

--- a/solution.py
+++ b/solution.py
@@ -337,11 +337,10 @@
     )(observed, in_hbm(above), in_hbm(below), own, above_f, below_f)
 
 
-def second_kernel(a_ref, b_ref, above_1, below_1, own_ref, a_facts, b_facts, out_ref):
+def second_kernel(a_ref, b_ref, above_1, below_1, a_facts, b_facts, out_ref, above_out):
     peers, _, rest = out_ref.shape
-    samples, width = own_ref.shape
-    edge = above_1.shape[1]
-    rows, kept, tail = width // peers, edge // peers, rest // peers
+    samples, edge = above_1.shape
+    kept, tail = edge // peers, rest // peers
     block = block_of(samples)
     even = is_even()
     above_f, below_f = either(even, a_facts[...], b_facts[...])
@@ -350,15 +349,14 @@
         above, below = either(even, a_ref[part, :], b_ref[part, :])
         above = decode(above, above_f, mask_of(above_f[2:3, part]), edge)
         below = decode(below, below_f, mask_of(below_f[2:3, part]), edge)
+        above_out[part, :] = above
         far = cross(below_1[part, :], above)
         last = cross(below, above_1[part, :])
         corner = cross(below, above)
-        near = cross(own_ref[part, :], above)
         for owner in range(peers):
             into = out_ref.at[owner]
-            add_to(into, slice(0, rows), near[owner * rows : (owner + 1) * rows], k)
-            low = rows + kept
-            add_to(into, slice(rows, low), far[owner * kept : (owner + 1) * kept], k)
+            low = kept
+            add_to(into, slice(0, low), far[owner * kept : (owner + 1) * kept], k)
             lines = slice(owner * tail, (owner + 1) * tail)
             for left in range(0, edge, rest):
                 add_to(into, slice(low, low + tail), last[lines, left : left + rest], k)
@@ -366,23 +364,23 @@
             add_to(into, slice(low, low + tail), corner[lines], k)
 
 
-def second_pass(above, below, above_1, below_1, own, above_f, below_f, peers):
-    samples, width = own.shape
-    edge, rest = above_1.shape[1], above.shape[1]
-    tall = (peers, (width + edge + width) // peers, rest)
+def second_pass(a_2, b_2, above_1, below_1, a_facts, b_facts, peers):
+    samples, edge = above_1.shape
+    rest = a_2.shape[1]
+    tall = (peers, (edge + edge + rest) // peers, rest)
     return pl.pallas_call(
         second_kernel,
-        out_shape=like(tall, jnp.float32),
-        in_specs=[whole()] * 7,
-        out_specs=whole(),
+        out_shape=(like(tall, jnp.float32), like((samples, rest), jnp.bfloat16)),
+        in_specs=[whole()] * 6,
+        out_specs=(whole(),) * 2,
         compiler_params=pltpu.CompilerParams(vmem_limit_bytes=GRANT),
         cost_estimate=pl.CostEstimate(
-            flops=2 * samples * rest * (2 * width + edge),
-            bytes_accessed=2 * samples * (2 * width + edge),
+            flops=2 * samples * rest * (2 * edge + rest),
+            bytes_accessed=4 * samples * (edge + rest),
             transcendentals=0,
         ),
         name="second",
-    )(above, below, above_1, below_1, own, above_f, below_f)
+    )(a_2, b_2, above_1, below_1, a_facts, b_facts)
 
 
 def per_device(dosage, observed, band_reach):
@@ -412,11 +410,13 @@
     near_1 = one[:rows] / shares[0:1]
     far_1 = one[rows : rows + kept] / shares[1:2]
     far_1 = bring_back(far_1, "var")
-    two = second_pass(a_2, b_2, above_1, below_1, own, a_f, b_f, peers)
-    two = sum_rows(two, "samp", two.shape[1])
-    far_2 = two[rows:] / shares[1:2, :rest]
+    two, above_2 = second_pass(a_2, b_2, above_1, below_1, a_f, b_f, peers)
+    far_2 = sum_rows(two, "samp", two.shape[1]) / shares[1:2, :rest]
     far_2 = bring_back(far_2, "var")
-    near = jnp.concatenate([near_1, two[:rows] / shares[0:1, :rest]], axis=1)
+    near_2 = cross(own, above_2).reshape(peers, rows, rest)
+    near_2 = sum_rows(near_2, "samp", rows) / shares[0:1, :rest]
+    near = jnp.concatenate([near_1, near_2], axis=1)
+    same = same / jnp.maximum(sums[2:3], 1.0)
     low = [far_2[kept + k * tail : kept + (k + 1) * tail] for k in range(pieces)]
     far = jnp.concatenate(
         [
@@ -425,9 +425,14 @@
         ],
         axis=0,
     )
-    result = jnp.stack([same / jnp.maximum(sums[2:3], 1.0), near, far], axis=1)
-    keep = jnp.arange(BAND, dtype=jnp.int32) <= band_reach[0]
-    return jnp.where(keep[None, :, None], result, jnp.float32(0.0))[None]
+    planes = [same, near] + [jnp.zeros_like(same)] * (BAND - 2)
+    planes = [
+        jnp.where(k <= band_reach[0], plane, 0.0) for k, plane in enumerate(planes)
+    ]
+    result = lax.optimization_barrier(jnp.stack(planes, axis=0))
+    far = jnp.where(BAND - 1 <= band_reach[0], far, 0.0)
+    result = lax.dynamic_update_index_in_dim(result, far, BAND - 1, 0)
+    return jnp.transpose(result, (1, 0, 2))[None]
 
 
 def solution(mesh):

time: 93.6 us -> 101 us (1.079)
  waiting for transfers between devices: 51 us -> 58.1 us
  local copies, waits for them, and re-layouts: 0.77 us -> 2.63 us
  Pallas kernels: 13.6 us -> 11.9 us
  other arithmetic: 6.38 us -> 5.24 us
    ppermute x2, waiting for transfers between devices: 11.7 us -> 20.7 us  [bring_back(): return lax.ppermute(shard, axis, [(i, i - 1) for i in range(1, peers - 1)])]
    ppermute x6, waiting for transfers between devices: 29.4 us -> 27 us  [trade(): lax.ppermute(shard, axis, pairs + [(high, low) for low, high in pairs])]
    ppermute x8 -> x10, starting transfers between devices: 6.01 us -> 8.19 us  [swap(): return lax.ppermute(shard, axis, [(i, i ^ bit) for i in range(peers)])]
    unnamed x6 -> x8, local copies, waits for them, and re-layouts: 0.7 us -> 2.54 us
    ppermute x6, starting transfers between devices: 10.7 us -> 9.2 us  [trade(): lax.ppermute(shard, axis, pairs + [(high, low) for low, high in pairs])]
    dot_general x1 -> x2, matrix products: 1.28 us -> 2.03 us  [cross(): lax.dot_general(left, right, (((0,), (0,)), ((), ())), preferred_element_...]
    ppermute x8 -> x10, waiting for transfers between devices: 9.86 us -> 10.5 us  [swap(): return lax.ppermute(shard, axis, [(i, i ^ bit) for i in range(peers)])]
  transfers between devices with their start and end apart: 16 -> 18, of which waited for: 8 -> 6; matrix products, arithmetic and copies ran while one was open for 7% -> 7% of each run, Pallas kernels for 10% -> 8%
where the time goes in v8:
time: 101 us
  waiting for transfers between devices  58.1 us (58%)
  starting transfers between devices  20 us (20%)
  Pallas kernels  11.9 us (12%)
  other arithmetic  5.24 us (5%)
  local copies, waits for them, and re-layouts  2.63 us (3%)
  matrix products  2.03 us (2%)
  between operations  1.08 us (1%)
    ppermute x6, waiting for transfers between devices, trade(): lax.ppermute(shard, axis, pairs + [(high, low) for low, high in pairs])  27 us
    ppermute x2, waiting for transfers between devices, bring_back(): return lax.ppermute(shard, axis, [(i, i - 1) for i in range(1, peers - 1)])  20.7 us
    ppermute x10, waiting for transfers between devices, swap(): return lax.ppermute(shard, axis, [(i, i ^ bit) for i in range(peers)])  10.5 us
    ppermute x6, starting transfers between devices, trade(): lax.ppermute(shard, axis, pairs + [(high, low) for low, high in pairs])  9.2 us
    ppermute x10, starting transfers between devices, swap(): return lax.ppermute(shard, axis, [(i, i ^ bit) for i in range(peers)])  8.19 us
    pallas_call x1, Pallas kernels, first_pass(): pl.pallas_call(first_kernel, out_shape=(like(tall, jnp.float32),) + (like...  3.92 us
    pallas_call x1, Pallas kernels, moments_pass(): pl.pallas_call(functools.partial(moments_kernel, kept, rows), grid=(sampl...  3.36 us
    pallas_call x1, Pallas kernels, head_pass(): pl.pallas_call(functools.partial(head_kernel, kept, rows), out_shape=(lik...  2.99 us
  transfers between devices with their start and end apart: 18, of which 6 were waited for; matrix products, arithmetic and copies ran while one was open for 7% of the time, Pallas kernels for 8%

profile of v8, /device:TPU:0, one launch (start us, length us, event | category | flops | bytes accessed | tf_op | source)
XLA Modules:
  0.0 101.0 jit_solution(11193292789895177034)
XLA Ops:
  0.0 0.7 copy-done
  0.7 3.4 %moments.1 = (bf16[2048,128]{1,0:T(8,128)(2,1)S(1)}, bf16[2048,128]{1,0:T(8,128)(2,1)S(1)}, f32[8,512]{1,0:T(8,128)S(1)}) custom-call(bf16[2048,512]{1,0:T(8,128)(2,1)} %dosage_ref.3, s32[1,2048]{1,0:T(1,128)S(1)} %copy-done), custom_call_target="tpu_custom_call" | custom-call | flops 268435456 | bytes 3145728 | tf_op jit(solution)/shard_map/moments/pallas_call | solution.py:169
  4.1 0.6 collective-permute-start
  4.6 3.0 %head.1 = (bf16[2048,384]{1,0:T(8,128)(2,1)}, bf16[2048,384]{1,0:T(8,128)(2,1)}) custom-call(bf16[2048,512]{1,0:T(8,128)(2,1)} %dosage_ref.3), custom_call_target="tpu_custom_call" | custom-call | tf_op jit(solution)/shard_map/head/pallas_call | solution.py:128
  7.6 2.6 %collective-permute-start.4 = (bf16[2048,384]{1,0:T(8,128)(2,1)}, bf16[2048,384]{1,0:T(8,128)(2,1)}, u32[]{:S(2)}, u32[]{:S(2)}) collective-permute-start(bf16[2048,384]{1,0:T(8,128)(2,1)} %get-tuple-element.20), channel_id=1, source_target_pairs={{0,1},{2,3},{1,0},{3,2},{4,5},{6,7},{5,4},{7,6},{8,9},{10,11},{9,8... | collective-permute-start | bytes 4718600 | tf_op jit(solution)/shard_map/ppermute | solution.py:19
  10.3 1.8 %collective-permute-start.5 = (bf16[2048,384]{1,0:T(8,128)(2,1)}, bf16[2048,384]{1,0:T(8,128)(2,1)}, u32[]{:S(2)}, u32[]{:S(2)}) collective-permute-start(bf16[2048,384]{1,0:T(8,128)(2,1)} %get-tuple-element.21), channel_id=1, source_target_pairs={{1,2},{2,1},{5,6},{6,5},{9,10},{10,9},{13,14},{14,13},{17,18},{18,... | collective-permute-start | bytes 4718600 | tf_op jit(solution)/shard_map/ppermute | solution.py:19
  12.1 1.5 %collective-permute-start.1 = (f32[8,512]{1,0:T(8,128)S(1)}, f32[8,512]{1,0:T(8,128)S(1)}, u32[]{:S(2)}, u32[]{:S(2)}) collective-permute-start(f32[8,512]{1,0:T(8,128)S(1)} %add.43), channel_id=1, source_target_pairs={{0,8},{4,12},{8,0},{12,4},{1,9},{5,13},{9,1},{13,5},{2,10},{6,14},... | collective-permute-start | bytes 49160 | tf_op jit(solution)/shard_map/ppermute | solution.py:37
  13.6 2.2 %collective-permute-done.1 = f32[8,512]{1,0:T(8,128)S(1)} collective-permute-done((f32[8,512]{1,0:T(8,128)S(1)}, f32[8,512]{1,0:T(8,128)S(1)}, u32[]{:S(2)}, u32[]{:S(2)}) %collective-permute-start.1) | collective-permute-done | bytes 16416 | tf_op jit(solution)/shard_map/ppermute | solution.py:37
  16.0 2.0 %select_convert_fusion.own_ref = bf16[2048,512]{1,0:T(8,128)(2,1)S(1)} fusion(bf16[2048,512]{1,0:T(8,128)(2,1)} %dosage_ref.3, f32[512]{0:T(512)S(1)} %bitcast.148, f32[512]{0:T(512)S(1)} %bitcast.147, pred[2048]{0:T(1024)(128)(4,1)S(1)} %compare_reduce_fusion), kind=kLoop, calls=%fused_computation | loop fusion | flops 5242880 | bytes 4200448 | tf_op jit(solution)/shard_map/convert_element_type | solution.py:226
  17.9 1.3 %fusion.15 = f32[512,512]{1,0:T(8,128)S(1)} fusion(bf16[2048,512]{1,0:T(8,128)(2,1)S(1)} %select_convert_fusion.own_ref), kind=kOutput, calls=%fused_computation.59 | convolution fusion | flops 1073741824 | bytes 3145728 | tf_op jit(solution)/shard_map/dot_general | solution.py:241
  19.2 1.0 copy-done.2
  20.2 0.9 select_bitcast_fusion.1
  21.1 2.2 %collective-permute-done.2 = f32[2,128,512]{2,1,0:T(8,128)} collective-permute-done((f32[2,128,512]{2,1,0:T(8,128)}, f32[2,128,512]{2,1,0:T(8,128)}, u32[]{:S(2)}, u32[]{:S(2)}) %collective-permute-start.2) | collective-permute-done | bytes 524320 | tf_op jit(solution)/shard_map/ppermute | solution.py:37
  23.3 1.5 %fusion.1 = f32[1,2,128,512]{3,2,1,0:T(8,128)S(1)} fusion(f32[2,128,512]{2,1,0:T(8,128)} %collective-permute-done.2, f32[2,2,128,512]{3,2,1,0:T(8,128)} %bitcast.143, pred[]{:T(512)S(6)} %ne.26), kind=kLoop, calls=%fused_computation.10 | loop fusion | flops 262144 | bytes 2097153 | tf_op jit(solution)/shard_map/reshape | solution.py:53
  24.9 1.6 %collective-permute-start.3 = (f32[1,128,512]{2,1,0:T(8,128)S(1)}, f32[1,128,512]{2,1,0:T(8,128)S(1)}, u32[]{:S(2)}, u32[]{:S(2)}) collective-permute-start(f32[1,128,512]{2,1,0:T(8,128)S(1)} %select_bitcast_fusion.3), channel_id=1, source_target_pairs={{0,8},{4,12},{8,0},{12,4},{1,9},{5,13},{9,1},{13,5},{2,10},{6,14},... | collective-permute-start | bytes 786440 | tf_op jit(solution)/shard_map/ppermute | solution.py:37
  26.4 3.3 %collective-permute-start.10 = (bf16[2048,128]{1,0:T(8,128)(2,1)S(1)}, bf16[2048,128]{1,0:T(8,128)(2,1)S(1)}, u32[]{:S(2)}, u32[]{:S(2)}) collective-permute-start(bf16[2048,128]{1,0:T(8,128)(2,1)S(1)} %get-tuple-element.25), channel_id=1, source_target_pairs={{0,1},{2,3},{1,0},{3,2},{4,5},{6,7},{5,4},{7,6},{8,9},{10,11},{9,8... | collective-permute-start | bytes 1572872 | tf_op jit(solution)/shard_map/ppermute | solution.py:19
  30.5 27.0 %collective-permute-done.6.a_facts = f32[3,2048]{1,0:T(4,128)S(1)} collective-permute-done((f32[3,2048]{1,0:T(4,128)S(1)}, f32[3,2048]{1,0:T(4,128)S(1)}, u32[]{:S(2)}, u32[]{:S(2)}) %collective-permute-start.6) | collective-permute-done | bytes 24608 | tf_op jit(solution)/shard_map/ppermute | solution.py:19
  57.5 0.7 collective-permute-start.11
  58.2 0.7 collective-permute-start.7
  58.9 3.9 %first.1 = (f32[4,232,384]{2,1,0:T(8,128)S(1)}, bf16[2048,384]{1,0:T(8,128)(2,1)S(1)}, bf16[2048,384]{1,0:T(8,128)(2,1)S(1)}) custom-call(s32[1,2048]{1,0:T(1,128)S(1)} %copy-done.1, bf16[2048,384]{1,0:T(8,128)(2,1)} %collective-permute-done.4.a_ref, bf16[2048,384]{1,0:T(8,128)(2,1)} %collective-permute-done.5.b_ref, ...), custom_call_target="tpu_custom_call" | custom-call | flops 1409286144 | bytes 9437184 | tf_op jit(solution)/shard_map/first/pallas_call | solution.py:320
  63.1 1.6 %second.1 = (f32[4,224,128]{2,1,0:T(8,128)S(1)}, bf16[2048,128]{1,0:T(8,128)(2,1)S(1)}) custom-call(bf16[2048,128]{1,0:T(8,128)(2,1)S(1)} %collective-permute-done.10.a_ref, bf16[2048,128]{1,0:T(8,128)(2,1)S(1)} %collective-permute-done.11.b_ref, bf16[2048,384]{1,0:T(8,128)(2,1)S(1)} %get-tuple-element.27.above_1, ...), custom_call_target="tpu_custom_call" | custom-call | flops 469762048 | bytes 4194304 | tf_op jit(solution)/shard_map/second/pallas_call | solution.py:371
  64.6 0.7 fusion.16
  65.4 0.5 collective-permute-start.12
  66.1 0.9 collective-permute-done.12
  67.0 1.7 %collective-permute-start.13 = (bf16[1,128,128]{2,1,0:T(8,128)(2,1)S(1)}, bf16[1,128,128]{2,1,0:T(8,128)(2,1)S(1)}, u32[]{:S(2)}, u32[]{:S(2)}) collective-permute-start(bf16[1,128,128]{2,1,0:T(8,128)(2,1)S(1)} %fusion.10), channel_id=1, source_target_pairs={{0,8},{4,12},{8,0},{12,4},{1,9},{5,13},{9,1},{13,5},{2,10},{6,14},... | collective-permute-start | bytes 98312 | tf_op jit(solution)/shard_map/ppermute | solution.py:37
  69.0 0.5 collective-permute-start.9
  69.6 1.6 %collective-permute-start.16 = (bf16[1,224,128]{2,1,0:T(8,128)(2,1)S(1)}, bf16[1,224,128]{2,1,0:T(8,128)(2,1)S(1)}, u32[]{:S(2)}, u32[]{:S(2)}) collective-permute-start(bf16[1,224,128]{2,1,0:T(8,128)(2,1)S(1)} %fusion.9), channel_id=1, source_target_pairs={{0,8},{4,12},{8,0},{12,4},{1,9},{5,13},{9,1},{13,5},{2,10},{6,14},... | collective-permute-start | bytes 172040 | tf_op jit(solution)/shard_map/ppermute | solution.py:37
  71.2 5.1 %collective-permute-done.9 = bf16[1,240,384]{2,1,0:T(8,128)(2,1)S(1)} collective-permute-done((bf16[1,240,384]{2,1,0:T(8,128)(2,1)S(1)}, bf16[1,240,384]{2,1,0:T(8,128)(2,1)S(1)}, u32[]{:S(2)}, u32[]{:S(2)}) %collective-permute-start.9) | collective-permute-done | bytes 184352 | tf_op jit(solution)/shard_map/ppermute | solution.py:37
  76.5 1.3 %collective-permute-start.14 = (f32[96,384]{1,0:T(8,128)S(1)}, f32[96,384]{1,0:T(8,128)S(1)}, u32[]{:S(2)}, u32[]{:S(2)}) collective-permute-start(f32[96,384]{1,0:T(8,128)S(1)} %fusion.6), channel_id=1, source_target_pairs={{1,0},{2,1},{5,4},{6,5},{9,8},{10,9},{13,12},{14,13},{17,16},{18,1... | collective-permute-start | bytes 442376 | tf_op jit(solution)/shard_map/ppermute | solution.py:24
  77.9 1.3 %collective-permute-start.17 = (f32[224,128]{1,0:T(8,128)S(1)}, f32[224,128]{1,0:T(8,128)S(1)}, u32[]{:S(2)}, u32[]{:S(2)}) collective-permute-start(f32[224,128]{1,0:T(8,128)S(1)} %bitcast_divide_fusion), channel_id=1, source_target_pairs={{1,0},{2,1},{5,4},{6,5},{9,8},{10,9},{13,12},{14,13},{17,16},{18,1... | collective-permute-start | bytes 344072 | tf_op jit(solution)/shard_map/ppermute | solution.py:24
  79.4 20.7 %collective-permute-done.17 = f32[224,128]{1,0:T(8,128)S(1)} collective-permute-done((f32[224,128]{1,0:T(8,128)S(1)}, f32[224,128]{1,0:T(8,128)S(1)}, u32[]{:S(2)}, u32[]{:S(2)}) %collective-permute-start.17) | collective-permute-done | bytes 114720 | tf_op jit(solution)/shard_map/ppermute | solution.py:24
  100.2 0.9 copy-done.3
  (60 shorter events, 1.4 us)
Async XLA Ops:
  0.0 0.7 copy-start
  0.7 12.9 %copy-start.1 = (s32[1,2048]{1,0:T(1,128)S(1)}, s32[1,2048]{1,0:T(1,128)}, u32[]{:S(2)}) copy-start(s32[1,2048]{1,0:T(1,128)} %observed_ref.5) | copy-start | bytes 24580
  4.1 8.0 %collective-permute-start = (f32[8,512]{1,0:T(8,128)S(1)}, f32[8,512]{1,0:T(8,128)S(1)}, u32[]{:S(2)}, u32[]{:S(2)}) collective-permute-start(f32[8,512]{1,0:T(8,128)S(1)} %get-tuple-element.18), channel_id=1, source_target_pairs={{0,4},{4,0},{8,12},{12,8},{1,5},{5,1},{9,13},{13,9},{2,6},{6,2},{1... | collective-permute-start | bytes 49160 | tf_op jit(solution)/shard_map/ppermute | solution.py:37
  7.6 51.3 %collective-permute-start.4 = (bf16[2048,384]{1,0:T(8,128)(2,1)}, bf16[2048,384]{1,0:T(8,128)(2,1)}, u32[]{:S(2)}, u32[]{:S(2)}) collective-permute-start(bf16[2048,384]{1,0:T(8,128)(2,1)} %get-tuple-element.20), channel_id=1, source_target_pairs={{0,1},{2,3},{1,0},{3,2},{4,5},{6,7},{5,4},{7,6},{8,9},{10,11},{9,8... | collective-permute-start | bytes 4718600 | tf_op jit(solution)/shard_map/ppermute | solution.py:19
  10.3 48.7 %collective-permute-start.5 = (bf16[2048,384]{1,0:T(8,128)(2,1)}, bf16[2048,384]{1,0:T(8,128)(2,1)}, u32[]{:S(2)}, u32[]{:S(2)}) collective-permute-start(bf16[2048,384]{1,0:T(8,128)(2,1)} %get-tuple-element.21), channel_id=1, source_target_pairs={{1,2},{2,1},{5,6},{6,5},{9,10},{10,9},{13,14},{14,13},{17,18},{18,... | collective-permute-start | bytes 4718600 | tf_op jit(solution)/shard_map/ppermute | solution.py:19
  12.1 3.7 %collective-permute-start.1 = (f32[8,512]{1,0:T(8,128)S(1)}, f32[8,512]{1,0:T(8,128)S(1)}, u32[]{:S(2)}, u32[]{:S(2)}) collective-permute-start(f32[8,512]{1,0:T(8,128)S(1)} %add.43), channel_id=1, source_target_pairs={{0,8},{4,12},{8,0},{12,4},{1,9},{5,13},{9,1},{13,5},{2,10},{6,14},... | collective-permute-start | bytes 49160 | tf_op jit(solution)/shard_map/ppermute | solution.py:37
  19.2 1.0 copy-start.2
  21.1 2.3 %collective-permute-start.2 = (f32[2,128,512]{2,1,0:T(8,128)}, f32[2,128,512]{2,1,0:T(8,128)}, u32[]{:S(2)}, u32[]{:S(2)}) collective-permute-start(f32[2,128,512]{2,1,0:T(8,128)} %select_bitcast_fusion.1), channel_id=1, source_target_pairs={{0,4},{4,0},{8,12},{12,8},{1,5},{5,1},{9,13},{13,9},{2,6},{6,2},{1... | collective-permute-start | bytes 1572872 | tf_op jit(solution)/shard_map/ppermute | solution.py:37
  24.9 33.3 %collective-permute-start.3 = (f32[1,128,512]{2,1,0:T(8,128)S(1)}, f32[1,128,512]{2,1,0:T(8,128)S(1)}, u32[]{:S(2)}, u32[]{:S(2)}) collective-permute-start(f32[1,128,512]{2,1,0:T(8,128)S(1)} %select_bitcast_fusion.3), channel_id=1, source_target_pairs={{0,8},{4,12},{8,0},{12,4},{1,9},{5,13},{9,1},{13,5},{2,10},{6,14},... | collective-permute-start | bytes 786440 | tf_op jit(solution)/shard_map/ppermute | solution.py:37
  26.4 36.6 %collective-permute-start.10 = (bf16[2048,128]{1,0:T(8,128)(2,1)S(1)}, bf16[2048,128]{1,0:T(8,128)(2,1)S(1)}, u32[]{:S(2)}, u32[]{:S(2)}) collective-permute-start(bf16[2048,128]{1,0:T(8,128)(2,1)S(1)} %get-tuple-element.25), channel_id=1, source_target_pairs={{0,1},{2,3},{1,0},{3,2},{4,5},{6,7},{5,4},{7,6},{8,9},{10,11},{9,8... | collective-permute-start | bytes 1572872 | tf_op jit(solution)/shard_map/ppermute | solution.py:19
  30.4 27.1 %collective-permute-start.6 = (f32[3,2048]{1,0:T(4,128)S(1)}, f32[3,2048]{1,0:T(4,128)S(1)}, u32[]{:S(2)}, u32[]{:S(2)}) collective-permute-start(f32[3,2048]{1,0:T(4,128)S(1)} %get-tuple-element.22), channel_id=1, source_target_pairs={{0,1},{2,3},{1,0},{3,2},{4,5},{6,7},{5,4},{7,6},{8,9},{10,11},{9,8... | collective-permute-start | bytes 73736 | tf_op jit(solution)/shard_map/ppermute | solution.py:19
  57.5 5.6 %collective-permute-start.11 = (bf16[2048,128]{1,0:T(8,128)(2,1)S(1)}, bf16[2048,128]{1,0:T(8,128)(2,1)S(1)}, u32[]{:S(2)}, u32[]{:S(2)}) collective-permute-start(bf16[2048,128]{1,0:T(8,128)(2,1)S(1)} %get-tuple-element.26), channel_id=1, source_target_pairs={{1,2},{2,1},{5,6},{6,5},{9,10},{10,9},{13,14},{14,13},{17,18},{18,... | collective-permute-start | bytes 1572872 | tf_op jit(solution)/shard_map/ppermute | solution.py:19
  58.2 0.8 collective-permute-start.7
  63.0 5.8 %collective-permute-start.8 = (f32[2,232,384]{2,1,0:T(8,128)S(1)}, f32[2,232,384]{2,1,0:T(8,128)S(1)}, u32[]{:S(2)}, u32[]{:S(2)}) collective-permute-start(f32[2,232,384]{2,1,0:T(8,128)S(1)} %select_bitcast_fusion), channel_id=1, source_target_pairs={{0,4},{4,0},{8,12},{12,8},{1,5},{5,1},{9,13},{13,9},{2,6},{6,2},{1... | collective-permute-start | bytes 2138120 | tf_op jit(solution)/shard_map/ppermute | solution.py:37
  65.4 1.5 %collective-permute-start.12 = (f32[2,128,128]{2,1,0:T(8,128)S(1)}, f32[2,128,128]{2,1,0:T(8,128)S(1)}, u32[]{:S(2)}, u32[]{:S(2)}) collective-permute-start(f32[2,128,128]{2,1,0:T(8,128)S(1)} %select_bitcast_fusion.5), channel_id=1, source_target_pairs={{0,4},{4,0},{8,12},{12,8},{1,5},{5,1},{9,13},{13,9},{2,6},{6,2},{1... | collective-permute-start | bytes 393224 | tf_op jit(solution)/shard_map/ppermute | solution.py:37
  66.0 2.7 %collective-permute-start.15 = (f32[2,224,128]{2,1,0:T(8,128)S(1)}, f32[2,224,128]{2,1,0:T(8,128)S(1)}, u32[]{:S(2)}, u32[]{:S(2)}) collective-permute-start(f32[2,224,128]{2,1,0:T(8,128)S(1)} %select_bitcast_fusion.4), channel_id=1, source_target_pairs={{0,4},{4,0},{8,12},{12,8},{1,5},{5,1},{9,13},{13,9},{2,6},{6,2},{1... | collective-permute-start | bytes 688136 | tf_op jit(solution)/shard_map/ppermute | solution.py:37
  67.0 12.2 %collective-permute-start.13 = (bf16[1,128,128]{2,1,0:T(8,128)(2,1)S(1)}, bf16[1,128,128]{2,1,0:T(8,128)(2,1)S(1)}, u32[]{:S(2)}, u32[]{:S(2)}) collective-permute-start(bf16[1,128,128]{2,1,0:T(8,128)(2,1)S(1)} %fusion.10), channel_id=1, source_target_pairs={{0,8},{4,12},{8,0},{12,4},{1,9},{5,13},{9,1},{13,5},{2,10},{6,14},... | collective-permute-start | bytes 98312 | tf_op jit(solution)/shard_map/ppermute | solution.py:37
  69.0 7.3 %collective-permute-start.9 = (bf16[1,240,384]{2,1,0:T(8,128)(2,1)S(1)}, bf16[1,240,384]{2,1,0:T(8,128)(2,1)S(1)}, u32[]{:S(2)}, u32[]{:S(2)}) collective-permute-start(bf16[1,240,384]{2,1,0:T(8,128)(2,1)S(1)} %pad_maximum_fusion.1), channel_id=1, source_target_pairs={{0,8},{4,12},{8,0},{12,4},{1,9},{5,13},{9,1},{13,5},{2,10},{6,14},... | collective-permute-start | bytes 552968 | tf_op jit(solution)/shard_map/ppermute | solution.py:37
  69.6 8.3 %collective-permute-start.16 = (bf16[1,224,128]{2,1,0:T(8,128)(2,1)S(1)}, bf16[1,224,128]{2,1,0:T(8,128)(2,1)S(1)}, u32[]{:S(2)}, u32[]{:S(2)}) collective-permute-start(bf16[1,224,128]{2,1,0:T(8,128)(2,1)S(1)} %fusion.9), channel_id=1, source_target_pairs={{0,8},{4,12},{8,0},{12,4},{1,9},{5,13},{9,1},{13,5},{2,10},{6,14},... | collective-permute-start | bytes 172040 | tf_op jit(solution)/shard_map/ppermute | solution.py:37
  76.5 23.6 %collective-permute-start.14 = (f32[96,384]{1,0:T(8,128)S(1)}, f32[96,384]{1,0:T(8,128)S(1)}, u32[]{:S(2)}, u32[]{:S(2)}) collective-permute-start(f32[96,384]{1,0:T(8,128)S(1)} %fusion.6), channel_id=1, source_target_pairs={{1,0},{2,1},{5,4},{6,5},{9,8},{10,9},{13,12},{14,13},{17,16},{18,1... | collective-permute-start | bytes 442376 | tf_op jit(solution)/shard_map/ppermute | solution.py:24
  77.9 22.2 %collective-permute-start.17 = (f32[224,128]{1,0:T(8,128)S(1)}, f32[224,128]{1,0:T(8,128)S(1)}, u32[]{:S(2)}, u32[]{:S(2)}) collective-permute-start(f32[224,128]{1,0:T(8,128)S(1)} %bitcast_divide_fusion), channel_id=1, source_target_pairs={{1,0},{2,1},{5,4},{6,5},{9,8},{10,9},{13,12},{14,13},{17,16},{18,1... | collective-permute-start | bytes 344072 | tf_op jit(solution)/shard_map/ppermute | solution.py:24
  100.2 0.9 copy-start.3

commit v9 on v8

v9 whole, which is shorter than its diff:
```python
import functools

import jax
import jax.numpy as jnp
from jax import lax
from jax.experimental import pallas as pl
from jax.experimental.pallas import tpu as pltpu
from jax.sharding import PartitionSpec as P

BAND = 3


EPSILON = 1e-05


def trade(shard, axis, first):
    peers = lax.axis_size(axis)
    pairs = [(i, i + 1) for i in range(first, peers - 1, 2)]
    return lax.ppermute(shard, axis, pairs + [(high, low) for low, high in pairs])


def bring_back(shard, axis):
    peers = lax.axis_size(axis)
    return lax.ppermute(shard, axis, [(i, i - 1) for i in range(1, peers - 1)])


def is_even():
    return lax.axis_index("var") % 2 == 0


def either(even, one, two):
    return jnp.where(even, one, two), jnp.where(even, two, one)


def swap(shard, axis, bit):
    peers = lax.axis_size(axis)
    return lax.ppermute(shard, axis, [(i, i ^ bit) for i in range(peers)])


def bits_of(peers):
    return [1 << k for k in range(peers.bit_length() - 1)]


def sum_all(value, axis):
    for bit in bits_of(lax.axis_size(axis)):
        value = value + swap(value, axis, bit)
    return value


def sum_rows(partial, axis, roles, exact=None):
    for bit in bits_of(lax.axis_size(axis)):
        pairs = partial.reshape(partial.shape[0] // 2, 2, *partial.shape[1:])
        keep = jnp.where(roles[bit], pairs[:, 1], pairs[:, 0])
        give = jnp.where(roles[bit], pairs[:, 0], pairs[:, 1])
        if bit == 1 or exact is None:
            got = swap(give, axis, bit)
        else:
            rows = give.shape[1]
            near = lax.reduce_precision(give, 8, 7)
            left = (give[:, exact:] - near[:, exact:]).astype(jnp.bfloat16)
            got = jnp.concatenate([near.astype(jnp.bfloat16), left], axis=1)
            got = swap(got, axis, bit).astype(jnp.float32)
            left = got[:, rows:]
            got = got[:, :rows]
            if rows > exact:
                got = jnp.concatenate([got[:, :exact], got[:, exact:] + left], axis=1)
        partial = keep + got
    return partial[0]


GRANT = 20 << 20


def block_of(samples):
    return 512 if samples % 512 == 0 else samples


def in_hbm(array):
    return pltpu.with_memory_space_constraint(array, pltpu.HBM)


def like(shape, dtype):
    return jax.ShapeDtypeStruct(shape, dtype)


def mask_of(row):
    lanes = 128
    return jnp.transpose(jnp.broadcast_to(row.astype(jnp.float32), (lanes, row.shape[1]))) > 0.5


def head_kernel(kept, rows, dosage_ref, a_ref, b_ref, held, sems):
    samples, width = dosage_ref.shape
    edge = a_ref.shape[1]
    block = block_of(samples) // 2
    even = is_even()
    copies = []
    for k in range(samples // block):
        part = pl.ds(k * block, block)
        copy = pltpu.make_async_copy(dosage_ref.at[part, :], held.at[part, :], sems.at[k])
        copy.start()
        copies.append(copy)
    for k, copy in enumerate(copies):
        part = pl.ds(k * block, block)
        copy.wait()
        values = held[part, :]
        owners = [values[:, low : low + kept] for low in range(0, width, rows)]
        up = jnp.concatenate(owners, axis=1)
        a_ref[part, :], b_ref[part, :] = either(even, up, values[:, :edge])


def whole():
    return pl.BlockSpec(memory_space=pltpu.VMEM)


def head_pass(dosage, kept, rows):
    samples, width = dosage.shape
    edge = width // rows * kept
    half = jnp.bfloat16
    return pl.pallas_call(
        functools.partial(head_kernel, kept, rows),
        out_shape=(like((samples, edge), half),) * 2,
        in_specs=[pl.BlockSpec(memory_space=pl.ANY)],
        out_specs=(whole(),) * 2,
        scratch_shapes=[
            pltpu.VMEM((samples, width), half),
            pltpu.SemaphoreType.DMA((2 * samples // block_of(samples),)),
        ],
        compiler_params=pltpu.CompilerParams(vmem_limit_bytes=GRANT),
        name="head",
    )(in_hbm(dosage))


def moments_kernel(cuts, rows, dosage_ref, observed_ref, *refs):
    width = dosage_ref.shape[1]
    lanes = 128
    peers = width // rows
    sums_ref = refs[-1]

    @pl.when(pl.program_id(0) == 0)
    def _():
        sums_ref[...] = jnp.zeros_like(sums_ref)

    present = mask_of(observed_ref[...])
    count = jnp.sum(jnp.where(present, 1.0, 0.0), axis=0, keepdims=True)
    for low in range(0, width, lanes):
        part = slice(low, low + lanes)
        seen = jnp.where(present, dosage_ref[:, part].astype(jnp.float32), 0.0)
        sums_ref[0:1, part] += jnp.sum(seen, axis=0, keepdims=True)
        sums_ref[1:2, part] += jnp.sum(seen * seen, axis=0, keepdims=True)
        sums_ref[2:3, part] += count
    values = dosage_ref[...]
    for k, (low, high) in enumerate(cuts):
        owners = [values[:, first + low : first + high] for first in range(0, width, rows)]
        up = jnp.concatenate(owners, axis=1)
        down = values[:, low * peers : high * peers]
        refs[2 * k][...], refs[2 * k + 1][...] = either(is_even(), up, down)


def moments_pass(dosage, observed, cuts, rows):
    samples, width = dosage.shape
    block = block_of(samples)
    sizes = [(high - low) * width // rows for low, high in cuts for _ in range(2)]
    return pl.pallas_call(
        functools.partial(moments_kernel, cuts, rows),
        grid=(samples // block,),
        out_shape=tuple(like((samples, size), jnp.bfloat16) for size in sizes)
        + (like((8, width), jnp.float32),),
        in_specs=[
            pl.BlockSpec((block, width), lambda i: (i, 0)),
            pl.BlockSpec((1, block), lambda i: (0, i)),
        ],
        out_specs=tuple(pl.BlockSpec((block, size), lambda i: (i, 0)) for size in sizes)
        + (pl.BlockSpec((8, width), lambda i: (0, 0)),),
        compiler_params=pltpu.CompilerParams(vmem_limit_bytes=GRANT),
        cost_estimate=pl.CostEstimate(
            flops=8 * samples * width, bytes_accessed=4 * samples * width, transcendentals=0
        ),
        name="moments",
    )(in_hbm(dosage), observed)


def facts_kernel(cuts, rows, sums_ref, observed_ref, moments_ref, a_ref, b_ref):
    width = sums_ref.shape[1]
    totals = sums_ref[2:3, :]
    centre = sums_ref[0:1, :] / totals
    inverse = 1.0 / jnp.sqrt(sums_ref[1:2, :] / totals - centre * centre + EPSILON)
    moments_ref[0:1, :] = centre
    moments_ref[1:2, :] = inverse
    flags = observed_ref[...].astype(jnp.float32)
    even = is_even()
    cuts = [(first + low, first + high) for low, high in cuts for first in range(0, width, rows)]
    for line, natural in enumerate((centre, inverse)):
        ordered = jnp.concatenate([natural[:, low:high] for low, high in cuts], axis=1)
        one, two = either(even, ordered, natural)
        a_ref[line : line + 1, :width] = one
        b_ref[line : line + 1, :width] = two
    for ref in (a_ref, b_ref):
        ref[2:3, :] = flags
        if width < ref.shape[1]:
            ref[0:2, width:] = jnp.zeros((2, ref.shape[1] - width), jnp.float32)


def facts_pass(sums, observed, cuts, rows):
    samples, width = observed.shape[1], sums.shape[1]
    single = jnp.float32
    return pl.pallas_call(
        functools.partial(facts_kernel, cuts, rows),
        out_shape=(like((2, width), single),) + (like((3, samples), single),) * 2,
        in_specs=[whole()] * 2,
        out_specs=(whole(),) * 3,
        compiler_params=pltpu.CompilerParams(vmem_limit_bytes=GRANT),
        name="facts",
    )(sums, observed)


def standardize(values, present, moments):
    spread = (values.astype(jnp.float32) - moments[0:1]) * moments[1:2]
    return jnp.where(present, spread, 0.0).astype(jnp.bfloat16)


def decode(values, facts, present, first):
    parts = []
    for low in range(0, values.shape[1], present.shape[1]):
        part = slice(low, low + present.shape[1])
        place = slice(first + low, first + low + present.shape[1])
        spread = values[:, part].astype(jnp.float32) - facts[0:1, place]
        spread = spread * facts[1:2, place]
        parts.append(jnp.where(present, spread, 0.0).astype(jnp.bfloat16))
    return parts[0] if len(parts) == 1 else jnp.concatenate(parts, axis=1)


def cross(left, right):
    return lax.dot_general(
        left, right, (((0,), (0,)), ((), ())), preferred_element_type=jnp.float32
    )


def chunk_kernel(step, marks, last, observed_ref, a_ref, b_ref, a_facts, b_facts, *refs):
    lanes = 128
    olds = refs[: 2 * min(step, 1)]
    out_ref, *fresh_refs = refs[len(olds) :]
    peers = out_ref.shape[0]
    samples, _ = a_ref.shape
    old = olds[0].shape[1] if olds else 0
    block = block_of(samples)
    even = is_even()
    above_f, below_f = either(even, a_facts[...], b_facts[...])
    shares = [jnp.zeros((1, lanes), jnp.float32)] * 2
    for k in range(samples // block):
        part = slice(k * block, (k + 1) * block)
        above_present = mask_of(above_f[2:3, part])
        below_present = mask_of(below_f[2:3, part])
        if step == 0:
            own_present = mask_of(observed_ref[:, part])
            shares = [
                share
                + jnp.sum(jnp.where(other & above_present, 1.0, 0.0), axis=0, keepdims=True)
                for share, other in zip(shares, (own_present, below_present))
            ]
        above, below = either(even, a_ref[part, :], b_ref[part, :])
        above = decode(above, above_f, above_present, old)
        below = decode(below, below_f, below_present, old)
        if last:
            fresh_refs[0][part, :] = above
        else:
            for ref, value, earlier in zip(fresh_refs, (above, below), olds or (None, None)):
                if old:
                    ref[part, :old] = earlier[part, :]
                ref[part, old:] = value
        products = []
        if old:
            product = cross(olds[1][part, :], above)
            for low, high in zip(marks[:step], marks[1 : step + 1]):
                products.append(product[low * peers : high * peers])
            products.append(cross(below, olds[0][part, :]))
        products.append(cross(below, above))
        for owner in range(peers):
            into = out_ref.at[owner]
            low = 0
            for product in products:
                tall = product.shape[0] // peers
                for left in range(0, product.shape[1], lanes):
                    value = product[owner * tall : (owner + 1) * tall, left : left + lanes]
                    add_to(into, slice(low, low + tall), value, k)
                    low += tall
    if step == 0:
        low = out_ref.shape[1] - 8
        for owner in range(peers):
            out_ref[owner, low : low + 1, :] = shares[0]
            out_ref[owner, low + 1 : low + 2, :] = shares[1]
            out_ref[owner, low + 2 :, :] = jnp.zeros((6, lanes), jnp.float32)


def add_to(ref, part, value, step):
    ref[part, :] = value if step == 0 else ref[part, :] + value


def chunk_pass(step, marks, peers, observed, a, b, a_facts, b_facts, olds):
    samples, fresh = a.shape
    last = step == len(marks) - 2
    lanes = 128
    old = olds[0].shape[1] if olds else 0
    lines = (2 * old * fresh + fresh * fresh) // (peers * lanes) + (8 if step == 0 else 0)
    stored = like((samples, fresh if last else old + fresh), jnp.bfloat16)
    results = (like((peers, lines, lanes), jnp.float32),) + (stored,) * (1 if last else 2)
    return pl.pallas_call(
        functools.partial(chunk_kernel, step, marks, last),
        out_shape=results,
        in_specs=[whole()] * (5 + len(olds)),
        out_specs=(whole(),) * len(results),
        compiler_params=pltpu.CompilerParams(vmem_limit_bytes=GRANT),
        cost_estimate=pl.CostEstimate(
            flops=2 * samples * lines * peers * lanes,
            bytes_accessed=8 * samples * fresh,
            transcendentals=0,
        ),
    )(observed, a, b, a_facts, b_facts, *olds)


def unpack(lines, shapes):
    blocks, low = [], 0
    for tall, wide in shapes:
        pieces = []
        for _ in range(wide // lines.shape[1]):
            pieces.append(lines[low : low + tall])
            low += tall
        blocks.append(jnp.concatenate(pieces, axis=1) if len(pieces) > 1 else pieces[0])
    return blocks


def per_device(dosage, observed, band_reach):
    _, width = dosage.shape
    peers = lax.axis_size("samp")
    rows = width // peers
    marks = (0, rows // 2, 3 * rows // 4, rows)
    cuts = tuple(zip(marks[:-1], marks[1:]))
    heights = [high - low for low, high in cuts]
    wides = [height * peers for height in heights]
    a_1, b_1 = head_pass(dosage, heights[0], rows)
    a_1 = trade(a_1, "var", 0)
    b_1 = trade(b_1, "var", 1)
    place = lax.axis_index("samp")
    roles = {bit: (place & bit) != 0 for bit in bits_of(peers)}
    a_2, b_2, a_3, b_3, sums = moments_pass(dosage, observed, cuts[1:], rows)
    sums = sum_all(sums, "samp")
    moments, a_f, b_f = facts_pass(sums, observed, cuts, rows)
    a_f = trade(a_f, "var", 0)
    b_f = trade(b_f, "var", 1)
    a_2 = trade(a_2, "var", 0)
    b_2 = trade(b_2, "var", 1)
    a_3 = trade(a_3, "var", 0)
    b_3 = trade(b_3, "var", 1)
    own = standardize(dosage, (observed[0] != 0)[:, None], moments)
    own = lax.optimization_barrier(own)
    same = sum_rows(cross(own, own).reshape(peers, rows, width), "samp", roles)
    chunks = [(a_1, b_1), (a_2, b_2), (a_3, b_3)]
    products, olds, aboves = [], [], []
    for step, (a, b) in enumerate(chunks):
        product, *olds = chunk_pass(step, marks, peers, observed, a, b, a_f, b_f, olds)
        products.append(product)
        aboves.append(olds[0])
    shapes = [
        [(heights[j], wides[step]) for j in range(step)]
        + [(heights[step], wides[j]) for j in range(step + 1)]
        for step in range(3)
    ]
    lines = products[1].shape[1] + products[0].shape[1] - 8
    one = jnp.concatenate([products[1], products[0]], axis=1)
    one = sum_rows(one, "samp", roles, lines)
    shares = jnp.maximum(one[lines:], 1.0)
    far_1 = one[:lines] / shares[1:2]
    far_1 = bring_back(far_1, "var")
    near_1 = cross(own, aboves[1]).reshape(peers, rows, -1)
    near_1 = sum_rows(near_1, "samp", roles, rows)
    near_1 = near_1 / jnp.concatenate([shares[0:1]] * (near_1.shape[1] // 128), axis=1)
    far_2 = sum_rows(products[2], "samp", roles, products[2].shape[1]) / shares[1:2]
    far_2 = bring_back(far_2, "var")
    near_2 = cross(own, aboves[2]).reshape(peers, rows, -1)
    near_2 = sum_rows(near_2, "samp", roles, rows) / shares[0:1]
    early = unpack(far_1, shapes[1] + shapes[0])
    near = jnp.concatenate([near_1, near_2], axis=1)
    same = same / jnp.maximum(sums[2:3], 1.0)
    late = unpack(far_2, shapes[2])
    far = jnp.concatenate(
        [
            jnp.concatenate([early[3], early[0], late[0]], axis=1),
            jnp.concatenate([early[1], early[2], late[1]], axis=1),
            jnp.concatenate(late[2:], axis=1),
        ],
        axis=0,
    )
    planes = [same, near] + [jnp.zeros_like(same)] * (BAND - 2)
    planes = [
        jnp.where(k <= band_reach[0], plane, 0.0) for k, plane in enumerate(planes)
    ]
    result = lax.optimization_barrier(jnp.stack(planes, axis=0))
    far = jnp.where(BAND - 1 <= band_reach[0], far, 0.0)
    result = lax.dynamic_update_index_in_dim(result, far, BAND - 1, 0)
    return jnp.transpose(result, (1, 0, 2))[None]


def solution(mesh):
    return jax.shard_map(
        per_device,
        mesh=mesh,
        in_specs=(P("samp", ("seg", "var")), P(("seg", "var"), "samp"), P(("seg", "var"))),
        out_specs=P(("seg", "var"), "samp", None, None),
        check_vma=False,
    )
```

time: 101 us -> 98.2 us (0.972)
  waiting for transfers between devices: 58.1 us -> 34.9 us
  starting transfers between devices: 20 us -> 37.8 us
  local copies, waits for them, and re-layouts: 2.63 us -> 5.17 us
  matrix products: 2.03 us -> 3.29 us
  other arithmetic: 5.24 us -> 4.13 us
    ppermute x2, waiting for transfers between devices: 20.7 us -> 3.18 us  [bring_back(): return lax.ppermute(shard, axis, [(i, i - 1) for i in range(1, peers - 1)])]
    ppermute x6 -> x8, starting transfers between devices: 9.2 us -> 24.9 us  [trade(): lax.ppermute(shard, axis, pairs + [(high, low) for low, high in pairs])]
    ppermute x6 -> x8, waiting for transfers between devices: 27 us -> 21.8 us  [trade(): lax.ppermute(shard, axis, pairs + [(high, low) for low, high in pairs])]
    unnamed x8 -> x30, local copies, waits for them, and re-layouts: 2.54 us -> 5.1 us
    ppermute x10 -> x12, starting transfers between devices: 8.19 us -> 10.2 us  [swap(): return lax.ppermute(shard, axis, [(i, i ^ bit) for i in range(peers)])]
    dot_general x2 -> x3, matrix products: 2.03 us -> 3.29 us  [cross(): lax.dot_general(left, right, (((0,), (0,)), ((), ())), preferred_element_...]
    convert_element_type x1, other arithmetic: 1.95 us -> 0.73 us  [standardize(): return jnp.where(present, spread, 0.0).astype(jnp.bfloat16)]
    pallas_call x4 -> x5, Pallas kernels: 8.95 us -> 8.44 us  [the longest x3 4.51 us: chunk_pass(): pl.pallas_call(functools.partial(chunk_kernel, step, marks, last), out_sh...]
  transfers between devices with their start and end apart: 18 -> 22, of which waited for: 6 -> 8; matrix products, arithmetic and copies ran while one was open for 7% -> 5% of each run, Pallas kernels for 8% -> 8%
where the time goes in v9:
time: 98.2 us; the launch traced here: 97.8 us
  starting transfers between devices  37.8 us (38%)
  waiting for transfers between devices  34.9 us (36%)
  Pallas kernels  11.3 us (12%)
  local copies, waits for them, and re-layouts  5.17 us (5%)
  other arithmetic  4.13 us (4%)
  matrix products  3.29 us (3%)
  between operations  1.21 us (1%)
    ppermute x8, starting transfers between devices, trade(): lax.ppermute(shard, axis, pairs + [(high, low) for low, high in pairs])  24.9 us
    ppermute x8, waiting for transfers between devices, trade(): lax.ppermute(shard, axis, pairs + [(high, low) for low, high in pairs])  21.8 us
    ppermute x12, starting transfers between devices, swap(): return lax.ppermute(shard, axis, [(i, i ^ bit) for i in range(peers)])  10.2 us
    ppermute x12, waiting for transfers between devices, swap(): return lax.ppermute(shard, axis, [(i, i ^ bit) for i in range(peers)])  10 us
    unnamed x30, local copies, waits for them, and re-layouts  5.1 us
    pallas_call x3, Pallas kernels, chunk_pass(): pl.pallas_call(functools.partial(chunk_kernel, step, marks, last), out_sh...  4.51 us
    pallas_call x1, Pallas kernels, moments_pass(): pl.pallas_call(functools.partial(moments_kernel, cuts, rows), grid=(sampl...  3.83 us
    dot_general x3, matrix products, cross(): lax.dot_general(left, right, (((0,), (0,)), ((), ())), preferred_element_...  3.29 us
  transfers between devices with their start and end apart: 22, of which 8 were waited for; matrix products, arithmetic and copies ran while one was open for 5% of the time, Pallas kernels for 8%

profile of v9, /device:TPU:0, one launch (start us, length us, event | category | flops | bytes accessed | tf_op | source)
XLA Modules:
  0.0 97.8 jit_solution(17264225806665333040)
XLA Ops:
  0.7 3.8 %moments.1 = (bf16[2048,128]{1,0:T(8,128)(2,1)S(1)}, bf16[2048,128]{1,0:T(8,128)(2,1)S(1)}, bf16[2048,128]{1,0:T(8,128)(2,1)S(1)}, bf16[2048,128]{1,0:T(8,128)(2,1)S(1)}, f32[8,512]{1,0:T(8,128)S(1)}) custom-call(bf16[2048,512]{1,0:T(8,128)(2,1)} %dosage_ref.3, s32[1,2048]{1,0:T(1,128)S(1)} %copy-done), custom_call_target="tpu_custom_call" | custom-call | flops 8388608 | bytes 4194304 | tf_op jit(solution)/shard_map/moments/pallas_call | solution.py:163
  4.5 0.8 copy-done.2
  5.3 0.8 copy-done.4
  6.1 0.8 copy-done.6
  7.0 0.8 copy-done.8
  8.3 0.8 collective-permute-done
  9.1 2.8 %collective-permute-start.1 = (f32[8,512]{1,0:T(8,128)S(1)}, f32[8,512]{1,0:T(8,128)S(1)}, u32[]{:S(2)}, u32[]{:S(2)}) collective-permute-start(f32[8,512]{1,0:T(8,128)S(1)} %add.49), channel_id=1, source_target_pairs={{0,8},{4,12},{8,0},{12,4},{1,9},{5,13},{9,1},{13,5},{2,10},{6,14},... | collective-permute-start | bytes 49160 | tf_op jit(solution)/shard_map/ppermute | solution.py:37
  12.0 1.7 %collective-permute-done.1 = f32[8,512]{1,0:T(8,128)S(1)} collective-permute-done((f32[8,512]{1,0:T(8,128)S(1)}, f32[8,512]{1,0:T(8,128)S(1)}, u32[]{:S(2)}, u32[]{:S(2)}) %collective-permute-start.1) | collective-permute-done | bytes 16416 | tf_op jit(solution)/shard_map/ppermute | solution.py:37
  14.5 1.3 %fusion.19 = f32[512,512]{1,0:T(8,128)S(1)} fusion(bf16[2048,512]{1,0:T(8,128)(2,1)S(1)} %select_convert_fusion), kind=kOutput, calls=%fused_computation.70 | convolution fusion | flops 1073741824 | bytes 3145728 | tf_op jit(solution)/shard_map/dot_general | solution.py:233
  15.9 1.0 select_bitcast_fusion
  17.1 2.9 %head.1 = (bf16[2048,256]{1,0:T(8,128)(2,1)}, bf16[2048,256]{1,0:T(8,128)(2,1)S(1)}) custom-call(bf16[2048,512]{1,0:T(8,128)(2,1)} %dosage_ref.3), custom_call_target="tpu_custom_call" | custom-call | tf_op jit(solution)/shard_map/head/pallas_call | solution.py:119
  19.9 2.2 %collective-permute-start.8 = (bf16[2048,256]{1,0:T(8,128)(2,1)}, bf16[2048,256]{1,0:T(8,128)(2,1)S(1)}, u32[]{:S(2)}, u32[]{:S(2)}) collective-permute-start(bf16[2048,256]{1,0:T(8,128)(2,1)} %get-tuple-element.29), channel_id=1, source_target_pairs={{0,1},{2,3},{1,0},{3,2},{4,5},{6,7},{5,4},{7,6},{8,9},{10,11},{9,8... | collective-permute-start | bytes 3145736 | tf_op jit(solution)/shard_map/ppermute | solution.py:19
  22.9 4.4 %collective-permute-start.6 = (f32[3,2048]{1,0:T(4,128)S(1)}, f32[3,2048]{1,0:T(4,128)S(1)}, u32[]{:S(2)}, u32[]{:S(2)}) collective-permute-start(f32[3,2048]{1,0:T(4,128)S(1)} %get-tuple-element.27), channel_id=1, source_target_pairs={{0,1},{2,3},{1,0},{3,2},{4,5},{6,7},{5,4},{7,6},{8,9},{10,11},{9,8... | collective-permute-start | bytes 73736 | tf_op jit(solution)/shard_map/ppermute | solution.py:19
  27.3 1.5 %fusion = f32[1,2,128,512]{3,2,1,0:T(8,128)S(1)} fusion(f32[2,128,512]{2,1,0:T(8,128)} %collective-permute-done.2, f32[2,2,128,512]{3,2,1,0:T(8,128)} %bitcast.176, pred[]{:T(512)S(6)} %ne.20), kind=kLoop, calls=%fused_computation.6 | loop fusion | flops 262144 | bytes 2097153 | tf_op jit(solution)/shard_map/reshape | solution.py:52
  28.8 1.6 %collective-permute-start.3 = (f32[1,128,512]{2,1,0:T(8,128)S(1)}, f32[1,128,512]{2,1,0:T(8,128)S(1)}, u32[]{:S(2)}, u32[]{:S(2)}) collective-permute-start(f32[1,128,512]{2,1,0:T(8,128)S(1)} %select_bitcast_fusion.3), channel_id=1, source_target_pairs={{0,8},{4,12},{8,0},{12,4},{1,9},{5,13},{9,1},{13,5},{2,10},{6,14},... | collective-permute-start | bytes 786440 | tf_op jit(solution)/shard_map/ppermute | solution.py:37
  30.6 16.5 %collective-permute-done.6.a_facts = f32[3,2048]{1,0:T(4,128)S(1)} collective-permute-done((f32[3,2048]{1,0:T(4,128)S(1)}, f32[3,2048]{1,0:T(4,128)S(1)}, u32[]{:S(2)}, u32[]{:S(2)}) %collective-permute-start.6) | collective-permute-done | bytes 24608 | tf_op jit(solution)/shard_map/ppermute | solution.py:19
  49.2 15.5 %collective-permute-start.14 = (bf16[2048,128]{1,0:T(8,128)(2,1)S(1)}, bf16[2048,128]{1,0:T(8,128)(2,1)S(1)}, u32[]{:S(2)}, u32[]{:S(2)}) collective-permute-start(bf16[2048,128]{1,0:T(8,128)(2,1)S(1)} %copy-done.5), channel_id=1, source_target_pairs={{0,1},{2,3},{1,0},{3,2},{4,5},{6,7},{5,4},{7,6},{8,9},{10,11},{9,8... | collective-permute-start | bytes 1572872 | tf_op jit(solution)/shard_map/ppermute | solution.py:19
  65.4 1.5 %shard_map.37 = (f32[4,136,128]{2,1,0:T(8,128)S(1)}, bf16[2048,256]{1,0:T(8,128)(2,1)S(1)}, bf16[2048,256]{1,0:T(8,128)(2,1)S(1)}) custom-call(s32[1,2048]{1,0:T(1,128)S(1)} %copy-done.1, bf16[2048,256]{1,0:T(8,128)(2,1)S(1)} %collective-permute-done.8.a_ref, bf16[2048,256]{1,0:T(8,128)(2,1)S(1)} %collective-permute-done.9.b_ref, ...), custom_call_target="tpu_custom_call" | custom-call | flops 285212672 | bytes 4194304 | tf_op jit(solution)/shard_map/pallas_call | solution.py:306
  66.9 1.5 %shard_map.38 = (f32[4,160,128]{2,1,0:T(8,128)S(1)}, bf16[2048,384]{1,0:T(8,128)(2,1)S(1)}, bf16[2048,384]{1,0:T(8,128)(2,1)S(1)}) custom-call(s32[1,2048]{1,0:T(1,128)S(1)} %copy-done.1, bf16[2048,128]{1,0:T(8,128)(2,1)S(1)} %collective-permute-done.4.a_ref, bf16[2048,128]{1,0:T(8,128)(2,1)S(1)} %collective-permute-done.5.b_ref, ...), custom_call_target="tpu_custom_call" | custom-call | flops 335544320 | bytes 2097152 | tf_op jit(solution)/shard_map/pallas_call | solution.py:306
  68.6 1.3 %fusion.20 = f32[512,384]{1,0:T(8,128)S(1)} fusion(bf16[2048,512]{1,0:T(8,128)(2,1)S(1)} %copy-done.12, bf16[2048,384]{1,0:T(8,128)(2,1)S(1)} %get-tuple-element.33.refs_0_), kind=kOutput, calls=%fused_computation.71 | convolution fusion | flops 805306368 | bytes 4456448 | tf_op jit(solution)/shard_map/dot_general | solution.py:233
  69.8 5.2 %collective-permute-done.14.a_ref = bf16[2048,128]{1,0:T(8,128)(2,1)S(1)} collective-permute-done((bf16[2048,128]{1,0:T(8,128)(2,1)S(1)}, bf16[2048,128]{1,0:T(8,128)(2,1)S(1)}, u32[]{:S(2)}, u32[]{:S(2)}) %collective-permute-start.14) | collective-permute-done | bytes 524320 | tf_op jit(solution)/shard_map/ppermute | solution.py:19
  75.1 1.5 %shard_map.39 = (f32[4,224,128]{2,1,0:T(8,128)S(1)}, bf16[2048,128]{1,0:T(8,128)(2,1)S(1)}) custom-call(s32[1,2048]{1,0:T(1,128)S(1)} %copy-done.1, bf16[2048,128]{1,0:T(8,128)(2,1)S(1)} %collective-permute-done.14.a_ref, bf16[2048,128]{1,0:T(8,128)(2,1)S(1)} %collective-permute-done.15.b_ref, f32[3,2048]{1,0:T(4,128)S(1)} %collective-permute-done.6.a_facts, ...), custom_call_target="tpu_custom_call" | custom-call | flops 469762048 | bytes 2097152 | tf_op jit(solution)/shard_map/pallas_call | solution.py:306
  78.2 0.9 collective-permute-done.16
  79.1 1.6 %collective-permute-start.17 = (bf16[1,128,128]{2,1,0:T(8,128)(2,1)S(1)}, bf16[1,128,128]{2,1,0:T(8,128)(2,1)S(1)}, u32[]{:S(2)}, u32[]{:S(2)}) collective-permute-start(bf16[1,128,128]{2,1,0:T(8,128)(2,1)S(1)} %fusion.13), channel_id=1, source_target_pairs={{0,8},{4,12},{8,0},{12,4},{1,9},{5,13},{9,1},{13,5},{2,10},{6,14},... | collective-permute-start | bytes 98312 | tf_op jit(solution)/shard_map/ppermute | solution.py:37
  81.5 1.6 %collective-permute-start.20 = (bf16[1,224,128]{2,1,0:T(8,128)(2,1)S(1)}, bf16[1,224,128]{2,1,0:T(8,128)(2,1)S(1)}, u32[]{:S(2)}, u32[]{:S(2)}) collective-permute-start(bf16[1,224,128]{2,1,0:T(8,128)(2,1)S(1)} %fusion.12), channel_id=1, source_target_pairs={{0,8},{4,12},{8,0},{12,4},{1,9},{5,13},{9,1},{13,5},{2,10},{6,14},... | collective-permute-start | bytes 172040 | tf_op jit(solution)/shard_map/ppermute | solution.py:37
  83.1 2.8 %collective-permute-done.13 = bf16[1,304,128]{2,1,0:T(8,128)(2,1)S(1)} collective-permute-done((bf16[1,304,128]{2,1,0:T(8,128)(2,1)S(1)}, bf16[1,304,128]{2,1,0:T(8,128)(2,1)S(1)}, u32[]{:S(2)}, u32[]{:S(2)}) %collective-permute-start.13) | collective-permute-done | bytes 77856 | tf_op jit(solution)/shard_map/ppermute | solution.py:37
  86.0 1.3 %collective-permute-start.18 = (f32[288,128]{1,0:T(8,128)S(1)}, f32[288,128]{1,0:T(8,128)S(1)}, u32[]{:S(2)}, u32[]{:S(2)}) collective-permute-start(f32[288,128]{1,0:T(8,128)S(1)} %fusion.8), channel_id=1, source_target_pairs={{1,0},{2,1},{5,4},{6,5},{9,8},{10,9},{13,12},{14,13},{17,16},{18,1... | collective-permute-start | bytes 442376 | tf_op jit(solution)/shard_map/ppermute | solution.py:24
  87.4 1.3 %collective-permute-start.21 = (f32[224,128]{1,0:T(8,128)S(1)}, f32[224,128]{1,0:T(8,128)S(1)}, u32[]{:S(2)}, u32[]{:S(2)}) collective-permute-start(f32[224,128]{1,0:T(8,128)S(1)} %bitcast_divide_fusion), channel_id=1, source_target_pairs={{1,0},{2,1},{5,4},{6,5},{9,8},{10,9},{13,12},{14,13},{17,16},{18,1... | collective-permute-start | bytes 344072 | tf_op jit(solution)/shard_map/ppermute | solution.py:24
  88.8 0.9 collective-permute-start.11
  89.7 3.8 %collective-permute-done.11 = bf16[1,128,384]{2,1,0:T(8,128)(2,1)S(1)} collective-permute-done((bf16[1,128,384]{2,1,0:T(8,128)(2,1)S(1)}, bf16[1,128,384]{2,1,0:T(8,128)(2,1)S(1)}, u32[]{:S(2)}, u32[]{:S(2)}) %collective-permute-start.11) | collective-permute-done | bytes 98336 | tf_op jit(solution)/shard_map/ppermute | solution.py:37
  93.6 3.2 %collective-permute-done.21 = f32[224,128]{1,0:T(8,128)S(1)} collective-permute-done((f32[224,128]{1,0:T(8,128)S(1)}, f32[224,128]{1,0:T(8,128)S(1)}, u32[]{:S(2)}, u32[]{:S(2)}) %collective-permute-start.21) | collective-permute-done | bytes 114720 | tf_op jit(solution)/shard_map/ppermute | solution.py:24
  97.0 0.9 copy-done.14
  (98 shorter events, 8.4 us)
Async XLA Ops:
  0.7 13.0 %copy-start.1 = (s32[1,2048]{1,0:T(1,128)S(1)}, s32[1,2048]{1,0:T(1,128)}, u32[]{:S(2)}) copy-start(s32[1,2048]{1,0:T(1,128)} %observed_ref.9) | copy-start | bytes 24580
  0.7 13.1 %copy-start.10 = (bf16[2048,512]{1,0:T(8,128)(2,1)S(1)}, bf16[2048,512]{1,0:T(8,128)(2,1)}, u32[]{:S(2)}) copy-start(bf16[2048,512]{1,0:T(8,128)(2,1)} %dosage_ref.3) | copy-start | bytes 6291460
  7.8 1.3 %collective-permute-start = (f32[8,512]{1,0:T(8,128)S(1)}, f32[8,512]{1,0:T(8,128)S(1)}, u32[]{:S(2)}, u32[]{:S(2)}) collective-permute-start(f32[8,512]{1,0:T(8,128)S(1)} %get-tuple-element.23), channel_id=1, source_target_pairs={{0,4},{4,0},{8,12},{12,8},{1,5},{5,1},{9,13},{13,9},{2,6},{6,2},{1... | collective-permute-start | bytes 49160 | tf_op jit(solution)/shard_map/ppermute | solution.py:37
  9.1 4.5 %collective-permute-start.1 = (f32[8,512]{1,0:T(8,128)S(1)}, f32[8,512]{1,0:T(8,128)S(1)}, u32[]{:S(2)}, u32[]{:S(2)}) collective-permute-start(f32[8,512]{1,0:T(8,128)S(1)} %add.49), channel_id=1, source_target_pairs={{0,8},{4,12},{8,0},{12,4},{1,9},{5,13},{9,1},{13,5},{2,10},{6,14},... | collective-permute-start | bytes 49160 | tf_op jit(solution)/shard_map/ppermute | solution.py:37
  14.5 1.4 %copy-start.11 = (bf16[2048,512]{1,0:T(8,128)(2,1)}, bf16[2048,512]{1,0:T(8,128)(2,1)S(1)}, u32[]{:S(2)}) copy-start(bf16[2048,512]{1,0:T(8,128)(2,1)S(1)} %select_convert_fusion) | copy-start | bytes 6291460
  15.9 1.2 %copy-start.13 = (f32[512,512]{1,0:T(8,128)}, f32[512,512]{1,0:T(8,128)S(1)}, u32[]{:S(2)}) copy-start(f32[512,512]{1,0:T(8,128)S(1)} %fusion.19) | copy-start | bytes 3145732
  17.1 10.2 %collective-permute-start.2 = (f32[2,128,512]{2,1,0:T(8,128)}, f32[2,128,512]{2,1,0:T(8,128)}, u32[]{:S(2)}, u32[]{:S(2)}) collective-permute-start(f32[2,128,512]{2,1,0:T(8,128)} %select_bitcast_fusion), channel_id=1, source_target_pairs={{0,4},{4,0},{8,12},{12,8},{1,5},{5,1},{9,13},{13,9},{2,6},{6,2},{1... | collective-permute-start | bytes 1572872 | tf_op jit(solution)/shard_map/ppermute | solution.py:37
  19.9 44.7 %collective-permute-start.8 = (bf16[2048,256]{1,0:T(8,128)(2,1)}, bf16[2048,256]{1,0:T(8,128)(2,1)S(1)}, u32[]{:S(2)}, u32[]{:S(2)}) collective-permute-start(bf16[2048,256]{1,0:T(8,128)(2,1)} %get-tuple-element.29), channel_id=1, source_target_pairs={{0,1},{2,3},{1,0},{3,2},{4,5},{6,7},{5,4},{7,6},{8,9},{10,11},{9,8... | collective-permute-start | bytes 3145736 | tf_op jit(solution)/shard_map/ppermute | solution.py:19
  22.1 43.3 %collective-permute-start.9 = (bf16[2048,256]{1,0:T(8,128)(2,1)S(1)}, bf16[2048,256]{1,0:T(8,128)(2,1)S(1)}, u32[]{:S(2)}, u32[]{:S(2)}) collective-permute-start(bf16[2048,256]{1,0:T(8,128)(2,1)S(1)} %get-tuple-element.30), channel_id=1, source_target_pairs={{1,2},{2,1},{5,6},{6,5},{9,10},{10,9},{13,14},{14,13},{17,18},{18,... | collective-permute-start | bytes 3145736 | tf_op jit(solution)/shard_map/ppermute | solution.py:19
  22.9 7.6 %copy-start.9 = (bf16[2048,128]{1,0:T(8,128)(2,1)S(1)}, bf16[2048,128]{1,0:T(8,128)(2,1)}, u32[]{:S(2)}) copy-start(bf16[2048,128]{1,0:T(8,128)(2,1)} %copy-done.8) | copy-start | bytes 1572868
  22.9 24.2 %copy-start.7 = (bf16[2048,128]{1,0:T(8,128)(2,1)S(1)}, bf16[2048,128]{1,0:T(8,128)(2,1)}, u32[]{:S(2)}) copy-start(bf16[2048,128]{1,0:T(8,128)(2,1)} %copy-done.6) | copy-start | bytes 1572868
  22.9 26.3 %copy-start.5 = (bf16[2048,128]{1,0:T(8,128)(2,1)S(1)}, bf16[2048,128]{1,0:T(8,128)(2,1)}, u32[]{:S(2)}) copy-start(bf16[2048,128]{1,0:T(8,128)(2,1)} %copy-done.4) | copy-start | bytes 1572868
  22.9 41.8 %copy-start.3 = (bf16[2048,128]{1,0:T(8,128)(2,1)S(1)}, bf16[2048,128]{1,0:T(8,128)(2,1)}, u32[]{:S(2)}) copy-start(bf16[2048,128]{1,0:T(8,128)(2,1)} %copy-done.2) | copy-start | bytes 1572868
  22.9 24.2 %collective-permute-start.6 = (f32[3,2048]{1,0:T(4,128)S(1)}, f32[3,2048]{1,0:T(4,128)S(1)}, u32[]{:S(2)}, u32[]{:S(2)}) collective-permute-start(f32[3,2048]{1,0:T(4,128)S(1)} %get-tuple-element.27), channel_id=1, source_target_pairs={{0,1},{2,3},{1,0},{3,2},{4,5},{6,7},{5,4},{7,6},{8,9},{10,11},{9,8... | collective-permute-start | bytes 73736 | tf_op jit(solution)/shard_map/ppermute | solution.py:19
  28.8 19.6 %collective-permute-start.3 = (f32[1,128,512]{2,1,0:T(8,128)S(1)}, f32[1,128,512]{2,1,0:T(8,128)S(1)}, u32[]{:S(2)}, u32[]{:S(2)}) collective-permute-start(f32[1,128,512]{2,1,0:T(8,128)S(1)} %select_bitcast_fusion.3), channel_id=1, source_target_pairs={{0,8},{4,12},{8,0},{12,4},{1,9},{5,13},{9,1},{13,5},{2,10},{6,14},... | collective-permute-start | bytes 786440 | tf_op jit(solution)/shard_map/ppermute | solution.py:37
  30.4 36.4 %collective-permute-start.4 = (bf16[2048,128]{1,0:T(8,128)(2,1)S(1)}, bf16[2048,128]{1,0:T(8,128)(2,1)S(1)}, u32[]{:S(2)}, u32[]{:S(2)}) collective-permute-start(bf16[2048,128]{1,0:T(8,128)(2,1)S(1)} %copy-done.9), channel_id=1, source_target_pairs={{0,1},{2,3},{1,0},{3,2},{4,5},{6,7},{5,4},{7,6},{8,9},{10,11},{9,8... | collective-permute-start | bytes 1572872 | tf_op jit(solution)/shard_map/ppermute | solution.py:19
  47.0 19.8 %collective-permute-start.5 = (bf16[2048,128]{1,0:T(8,128)(2,1)S(1)}, bf16[2048,128]{1,0:T(8,128)(2,1)S(1)}, u32[]{:S(2)}, u32[]{:S(2)}) collective-permute-start(bf16[2048,128]{1,0:T(8,128)(2,1)S(1)} %copy-done.7), channel_id=1, source_target_pairs={{1,2},{2,1},{5,6},{6,5},{9,10},{10,9},{13,14},{14,13},{17,18},{18,... | collective-permute-start | bytes 1572872 | tf_op jit(solution)/shard_map/ppermute | solution.py:19
  48.4 0.8 collective-permute-start.7
  49.2 25.9 %collective-permute-start.14 = (bf16[2048,128]{1,0:T(8,128)(2,1)S(1)}, bf16[2048,128]{1,0:T(8,128)(2,1)S(1)}, u32[]{:S(2)}, u32[]{:S(2)}) collective-permute-start(bf16[2048,128]{1,0:T(8,128)(2,1)S(1)} %copy-done.5), channel_id=1, source_target_pairs={{0,1},{2,3},{1,0},{3,2},{4,5},{6,7},{5,4},{7,6},{8,9},{10,11},{9,8... | collective-permute-start | bytes 1572872 | tf_op jit(solution)/shard_map/ppermute | solution.py:19
  64.7 10.4 %collective-permute-start.15 = (bf16[2048,128]{1,0:T(8,128)(2,1)S(1)}, bf16[2048,128]{1,0:T(8,128)(2,1)S(1)}, u32[]{:S(2)}, u32[]{:S(2)}) collective-permute-start(bf16[2048,128]{1,0:T(8,128)(2,1)S(1)} %copy-done.3), channel_id=1, source_target_pairs={{1,2},{2,1},{5,6},{6,5},{9,10},{10,9},{13,14},{14,13},{17,18},{18,... | collective-permute-start | bytes 1572872 | tf_op jit(solution)/shard_map/ppermute | solution.py:19
  66.9 1.7 %copy-start.12 = (bf16[2048,512]{1,0:T(8,128)(2,1)S(1)}, bf16[2048,512]{1,0:T(8,128)(2,1)}, u32[]{:S(2)}) copy-start(bf16[2048,512]{1,0:T(8,128)(2,1)} %copy-done.11) | copy-start | bytes 6291460
  68.5 12.2 %collective-permute-start.12 = (f32[2,296,128]{2,1,0:T(8,128)S(1)}, f32[2,296,128]{2,1,0:T(8,128)S(1)}, u32[]{:S(2)}, u32[]{:S(2)}) collective-permute-start(f32[2,296,128]{2,1,0:T(8,128)S(1)} %select_bitcast_fusion.2), channel_id=1, source_target_pairs={{0,4},{4,0},{8,12},{12,8},{1,5},{5,1},{9,13},{13,9},{2,6},{6,2},{1... | collective-permute-start | bytes 909320 | tf_op jit(solution)/shard_map/ppermute | solution.py:37
  76.7 4.0 %collective-permute-start.19 = (f32[2,224,128]{2,1,0:T(8,128)S(1)}, f32[2,224,128]{2,1,0:T(8,128)S(1)}, u32[]{:S(2)}, u32[]{:S(2)}) collective-permute-start(f32[2,224,128]{2,1,0:T(8,128)S(1)} %select_bitcast_fusion.4), channel_id=1, source_target_pairs={{0,4},{4,0},{8,12},{12,8},{1,5},{5,1},{9,13},{13,9},{2,6},{6,2},{1... | collective-permute-start | bytes 688136 | tf_op jit(solution)/shard_map/ppermute | solution.py:37
  77.5 1.5 %collective-permute-start.16 = (f32[2,128,128]{2,1,0:T(8,128)S(1)}, f32[2,128,128]{2,1,0:T(8,128)S(1)}, u32[]{:S(2)}, u32[]{:S(2)}) collective-permute-start(f32[2,128,128]{2,1,0:T(8,128)S(1)} %select_bitcast_fusion.6), channel_id=1, source_target_pairs={{0,4},{4,0},{8,12},{12,8},{1,5},{5,1},{9,13},{13,9},{2,6},{6,2},{1... | collective-permute-start | bytes 393224 | tf_op jit(solution)/shard_map/ppermute | solution.py:37
  78.1 10.5 %collective-permute-start.10 = (f32[2,128,384]{2,1,0:T(8,128)S(1)}, f32[2,128,384]{2,1,0:T(8,128)S(1)}, u32[]{:S(2)}, u32[]{:S(2)}) collective-permute-start(f32[2,128,384]{2,1,0:T(8,128)S(1)} %select_bitcast_fusion.1), channel_id=1, source_target_pairs={{0,4},{4,0},{8,12},{12,8},{1,5},{5,1},{9,13},{13,9},{2,6},{6,2},{1... | collective-permute-start | bytes 1179656 | tf_op jit(solution)/shard_map/ppermute | solution.py:37
  79.1 10.5 %collective-permute-start.17 = (bf16[1,128,128]{2,1,0:T(8,128)(2,1)S(1)}, bf16[1,128,128]{2,1,0:T(8,128)(2,1)S(1)}, u32[]{:S(2)}, u32[]{:S(2)}) collective-permute-start(bf16[1,128,128]{2,1,0:T(8,128)(2,1)S(1)} %fusion.13), channel_id=1, source_target_pairs={{0,8},{4,12},{8,0},{12,4},{1,9},{5,13},{9,1},{13,5},{2,10},{6,14},... | collective-permute-start | bytes 98312 | tf_op jit(solution)/shard_map/ppermute | solution.py:37
  80.9 5.0 %collective-permute-start.13 = (bf16[1,304,128]{2,1,0:T(8,128)(2,1)S(1)}, bf16[1,304,128]{2,1,0:T(8,128)(2,1)S(1)}, u32[]{:S(2)}, u32[]{:S(2)}) collective-permute-start(bf16[1,304,128]{2,1,0:T(8,128)(2,1)S(1)} %pad_maximum_fusion.2), channel_id=1, source_target_pairs={{0,8},{4,12},{8,0},{12,4},{1,9},{5,13},{9,1},{13,5},{2,10},{6,14},... | collective-permute-start | bytes 233480 | tf_op jit(solution)/shard_map/ppermute | solution.py:37
  81.5 5.8 %collective-permute-start.20 = (bf16[1,224,128]{2,1,0:T(8,128)(2,1)S(1)}, bf16[1,224,128]{2,1,0:T(8,128)(2,1)S(1)}, u32[]{:S(2)}, u32[]{:S(2)}) collective-permute-start(bf16[1,224,128]{2,1,0:T(8,128)(2,1)S(1)} %fusion.12), channel_id=1, source_target_pairs={{0,8},{4,12},{8,0},{12,4},{1,9},{5,13},{9,1},{13,5},{2,10},{6,14},... | collective-permute-start | bytes 172040 | tf_op jit(solution)/shard_map/ppermute | solution.py:37
  86.0 10.8 %collective-permute-start.18 = (f32[288,128]{1,0:T(8,128)S(1)}, f32[288,128]{1,0:T(8,128)S(1)}, u32[]{:S(2)}, u32[]{:S(2)}) collective-permute-start(f32[288,128]{1,0:T(8,128)S(1)} %fusion.8), channel_id=1, source_target_pairs={{1,0},{2,1},{5,4},{6,5},{9,8},{10,9},{13,12},{14,13},{17,16},{18,1... | collective-permute-start | bytes 442376 | tf_op jit(solution)/shard_map/ppermute | solution.py:24
  87.4 9.4 %collective-permute-start.21 = (f32[224,128]{1,0:T(8,128)S(1)}, f32[224,128]{1,0:T(8,128)S(1)}, u32[]{:S(2)}, u32[]{:S(2)}) collective-permute-start(f32[224,128]{1,0:T(8,128)S(1)} %bitcast_divide_fusion), channel_id=1, source_target_pairs={{1,0},{2,1},{5,4},{6,5},{9,8},{10,9},{13,12},{14,13},{17,16},{18,1... | collective-permute-start | bytes 344072 | tf_op jit(solution)/shard_map/ppermute | solution.py:24
  88.8 4.7 %collective-permute-start.11 = (bf16[1,128,384]{2,1,0:T(8,128)(2,1)S(1)}, bf16[1,128,384]{2,1,0:T(8,128)(2,1)S(1)}, u32[]{:S(2)}, u32[]{:S(2)}) collective-permute-start(bf16[1,128,384]{2,1,0:T(8,128)(2,1)S(1)} %fusion.10), channel_id=1, source_target_pairs={{0,8},{4,12},{8,0},{12,4},{1,9},{5,13},{9,1},{13,5},{2,10},{6,14},... | collective-permute-start | bytes 294920 | tf_op jit(solution)/shard_map/ppermute | solution.py:37
  96.9 0.9 copy-start.14
  (5 other events, 3.9 us)

commit v10 on v9

--- a/solution.py
+++ b/solution.py
@@ -389,14 +389,9 @@
         ],
         axis=0,
     )
-    planes = [same, near] + [jnp.zeros_like(same)] * (BAND - 2)
-    planes = [
-        jnp.where(k <= band_reach[0], plane, 0.0) for k, plane in enumerate(planes)
-    ]
-    result = lax.optimization_barrier(jnp.stack(planes, axis=0))
-    far = jnp.where(BAND - 1 <= band_reach[0], far, 0.0)
-    result = lax.dynamic_update_index_in_dim(result, far, BAND - 1, 0)
-    return jnp.transpose(result, (1, 0, 2))[None]
+    result = jnp.stack([same, near, far], axis=1)
+    keep = jnp.arange(BAND, dtype=jnp.int32) <= band_reach[0]
+    return jnp.where(keep[None, :, None], result, jnp.float32(0.0))[None]
 
 
 def solution(mesh):

time: 98.2 us -> 107 us (1.090)
  waiting for transfers between devices: 34.9 us -> 50.8 us
  starting transfers between devices: 37.8 us -> 30 us
  local copies, waits for them, and re-layouts: 5.17 us -> 3.49 us
    ppermute x8, waiting for transfers between devices: 21.8 us -> 31.1 us  [trade(): lax.ppermute(shard, axis, pairs + [(high, low) for low, high in pairs])]
    ppermute x8, starting transfers between devices: 24.9 us -> 17.1 us  [trade(): lax.ppermute(shard, axis, pairs + [(high, low) for low, high in pairs])]
    ppermute x12, waiting for transfers between devices: 10 us -> 16.5 us  [swap(): return lax.ppermute(shard, axis, [(i, i ^ bit) for i in range(peers)])]
    unnamed x30 -> x20, local copies, waits for them, and re-layouts: 5.1 us -> 3.45 us
  transfers between devices with their start and end apart: 22 -> 22, of which waited for: 8 -> 9; matrix products, arithmetic and copies ran while one was open for 5% -> 4% of each run, Pallas kernels for 8% -> 7%
where the time goes in v10:
time: 107 us; the launch traced here: 106 us
  waiting for transfers between devices  50.8 us (47%)
  starting transfers between devices  30 us (28%)
  Pallas kernels  12.3 us (11%)
  other arithmetic  5.01 us (5%)
  local copies, waits for them, and re-layouts  3.49 us (3%)
  matrix products  3.3 us (3%)
  between operations  1.23 us (1%)
    ppermute x8, waiting for transfers between devices, trade(): lax.ppermute(shard, axis, pairs + [(high, low) for low, high in pairs])  31.1 us
    ppermute x8, starting transfers between devices, trade(): lax.ppermute(shard, axis, pairs + [(high, low) for low, high in pairs])  17.1 us
    ppermute x12, waiting for transfers between devices, swap(): return lax.ppermute(shard, axis, [(i, i ^ bit) for i in range(peers)])  16.5 us
    ppermute x12, starting transfers between devices, swap(): return lax.ppermute(shard, axis, [(i, i ^ bit) for i in range(peers)])  10.3 us
    pallas_call x3, Pallas kernels, chunk_pass(): pl.pallas_call(functools.partial(chunk_kernel, step, marks, last), out_sh...  4.53 us
    pallas_call x1, Pallas kernels, moments_pass(): pl.pallas_call(functools.partial(moments_kernel, cuts, rows), grid=(sampl...  4.45 us
    unnamed x20, local copies, waits for them, and re-layouts  3.45 us
    dot_general x3, matrix products, cross(): lax.dot_general(left, right, (((0,), (0,)), ((), ())), preferred_element_...  3.3 us
  transfers between devices with their start and end apart: 22, of which 9 were waited for; matrix products, arithmetic and copies ran while one was open for 4% of the time, Pallas kernels for 7%

profile of v10, /device:TPU:0, one launch (start us, length us, event | category | flops | bytes accessed | tf_op | source)
XLA Modules:
  0.0 106.2 jit_solution(6639996579428932223)
XLA Ops:
  0.7 4.4 %moments.1 = (bf16[2048,128]{1,0:T(8,128)(2,1)}, bf16[2048,128]{1,0:T(8,128)(2,1)}, bf16[2048,128]{1,0:T(8,128)(2,1)S(1)}, bf16[2048,128]{1,0:T(8,128)(2,1)S(1)}, f32[8,512]{1,0:T(8,128)S(1)}) custom-call(bf16[2048,512]{1,0:T(8,128)(2,1)} %dosage_ref.3, s32[1,2048]{1,0:T(1,128)S(1)} %copy-done), custom_call_target="tpu_custom_call" | custom-call | flops 8388608 | bytes 4194304 | tf_op jit(solution)/shard_map/moments/pallas_call | solution.py:163
  5.2 0.8 copy-done.2
  7.3 0.8 collective-permute-done
  8.1 2.8 %collective-permute-start.1 = (f32[8,512]{1,0:T(8,128)S(1)}, f32[8,512]{1,0:T(8,128)S(1)}, u32[]{:S(2)}, u32[]{:S(2)}) collective-permute-start(f32[8,512]{1,0:T(8,128)S(1)} %add.47), channel_id=1, source_target_pairs={{0,8},{4,12},{8,0},{12,4},{1,9},{5,13},{9,1},{13,5},{2,10},{6,14},... | collective-permute-start | bytes 49160 | tf_op jit(solution)/shard_map/ppermute | solution.py:37
  11.0 1.7 %collective-permute-done.1 = f32[8,512]{1,0:T(8,128)S(1)} collective-permute-done((f32[8,512]{1,0:T(8,128)S(1)}, f32[8,512]{1,0:T(8,128)S(1)}, u32[]{:S(2)}, u32[]{:S(2)}) %collective-permute-start.1) | collective-permute-done | bytes 16416 | tf_op jit(solution)/shard_map/ppermute | solution.py:37
  13.5 1.3 %fusion.15 = f32[512,512]{1,0:T(8,128)S(1)} fusion(bf16[2048,512]{1,0:T(8,128)(2,1)S(1)} %select_convert_fusion), kind=kOutput, calls=%fused_computation.67 | convolution fusion | flops 1073741824 | bytes 3145728 | tf_op jit(solution)/shard_map/dot_general | solution.py:233
  14.9 1.0 copy-done.9
  15.9 0.9 select_bitcast_fusion
  16.8 3.2 %head.1 = (bf16[2048,256]{1,0:T(8,128)(2,1)}, bf16[2048,256]{1,0:T(8,128)(2,1)}) custom-call(bf16[2048,512]{1,0:T(8,128)(2,1)} %dosage_ref.3), custom_call_target="tpu_custom_call" | custom-call | tf_op jit(solution)/shard_map/head/pallas_call | solution.py:119
  20.1 2.2 %collective-permute-start.8 = (bf16[2048,256]{1,0:T(8,128)(2,1)}, bf16[2048,256]{1,0:T(8,128)(2,1)S(1)}, u32[]{:S(2)}, u32[]{:S(2)}) collective-permute-start(bf16[2048,256]{1,0:T(8,128)(2,1)} %get-tuple-element.29), channel_id=1, source_target_pairs={{0,1},{2,3},{1,0},{3,2},{4,5},{6,7},{5,4},{7,6},{8,9},{10,11},{9,8... | collective-permute-start | bytes 3145736 | tf_op jit(solution)/shard_map/ppermute | solution.py:19
  23.0 4.4 %collective-permute-start.4 = (bf16[2048,128]{1,0:T(8,128)(2,1)}, bf16[2048,128]{1,0:T(8,128)(2,1)S(1)}, u32[]{:S(2)}, u32[]{:S(2)}) collective-permute-start(bf16[2048,128]{1,0:T(8,128)(2,1)} %get-tuple-element.25), channel_id=1, source_target_pairs={{0,1},{2,3},{1,0},{3,2},{4,5},{6,7},{5,4},{7,6},{8,9},{10,11},{9,8... | collective-permute-start | bytes 1572872 | tf_op jit(solution)/shard_map/ppermute | solution.py:19
  28.8 1.3 %collective-permute-start.6 = (f32[3,2048]{1,0:T(4,128)S(1)}, f32[3,2048]{1,0:T(4,128)S(1)}, u32[]{:S(2)}, u32[]{:S(2)}) collective-permute-start(f32[3,2048]{1,0:T(4,128)S(1)} %get-tuple-element.27), channel_id=1, source_target_pairs={{0,1},{2,3},{1,0},{3,2},{4,5},{6,7},{5,4},{7,6},{8,9},{10,11},{9,8... | collective-permute-start | bytes 73736 | tf_op jit(solution)/shard_map/ppermute | solution.py:19
  30.2 1.5 %fusion = f32[1,2,128,512]{3,2,1,0:T(8,128)S(1)} fusion(f32[2,128,512]{2,1,0:T(8,128)} %collective-permute-done.2, f32[2,2,128,512]{3,2,1,0:T(8,128)} %bitcast.178, pred[]{:T(512)S(6)} %ne.20), kind=kLoop, calls=%fused_computation.6 | loop fusion | flops 262144 | bytes 2097153 | tf_op jit(solution)/shard_map/reshape | solution.py:52
  31.7 26.5 %collective-permute-done.6.a_facts = f32[3,2048]{1,0:T(4,128)S(1)} collective-permute-done((f32[3,2048]{1,0:T(4,128)S(1)}, f32[3,2048]{1,0:T(4,128)S(1)}, u32[]{:S(2)}, u32[]{:S(2)}) %collective-permute-start.6) | collective-permute-done | bytes 24608 | tf_op jit(solution)/shard_map/ppermute | solution.py:19
  58.2 1.7 %collective-permute-start.3 = (f32[1,128,512]{2,1,0:T(8,128)S(1)}, f32[1,128,512]{2,1,0:T(8,128)S(1)}, u32[]{:S(2)}, u32[]{:S(2)}) collective-permute-start(f32[1,128,512]{2,1,0:T(8,128)S(1)} %select_bitcast_fusion.3), channel_id=1, source_target_pairs={{0,8},{4,12},{8,0},{12,4},{1,9},{5,13},{9,1},{13,5},{2,10},{6,14},... | collective-permute-start | bytes 786440 | tf_op jit(solution)/shard_map/ppermute | solution.py:37
  59.9 6.5 %collective-permute-done.3 = f32[1,128,512]{2,1,0:T(8,128)S(1)} collective-permute-done((f32[1,128,512]{2,1,0:T(8,128)S(1)}, f32[1,128,512]{2,1,0:T(8,128)S(1)}, u32[]{:S(2)}, u32[]{:S(2)}) %collective-permute-start.3) | collective-permute-done | bytes 262176 | tf_op jit(solution)/shard_map/ppermute | solution.py:37
  67.1 6.5 %collective-permute-start.14 = (bf16[2048,128]{1,0:T(8,128)(2,1)S(1)}, bf16[2048,128]{1,0:T(8,128)(2,1)S(1)}, u32[]{:S(2)}, u32[]{:S(2)}) collective-permute-start(bf16[2048,128]{1,0:T(8,128)(2,1)S(1)} %copy-done.5), channel_id=1, source_target_pairs={{0,1},{2,3},{1,0},{3,2},{4,5},{6,7},{5,4},{7,6},{8,9},{10,11},{9,8... | collective-permute-start | bytes 1572872 | tf_op jit(solution)/shard_map/ppermute | solution.py:19
  74.3 1.5 %shard_map.37 = (f32[4,136,128]{2,1,0:T(8,128)S(1)}, bf16[2048,256]{1,0:T(8,128)(2,1)S(1)}, bf16[2048,256]{1,0:T(8,128)(2,1)S(1)}) custom-call(s32[1,2048]{1,0:T(1,128)S(1)} %copy-done.1, bf16[2048,256]{1,0:T(8,128)(2,1)S(1)} %collective-permute-done.8.a_ref, bf16[2048,256]{1,0:T(8,128)(2,1)S(1)} %collective-permute-done.9.b_ref, ...), custom_call_target="tpu_custom_call" | custom-call | flops 285212672 | bytes 4194304 | tf_op jit(solution)/shard_map/pallas_call | solution.py:306
  75.8 1.5 %shard_map.38 = (f32[4,160,128]{2,1,0:T(8,128)S(1)}, bf16[2048,384]{1,0:T(8,128)(2,1)S(1)}, bf16[2048,384]{1,0:T(8,128)(2,1)S(1)}) custom-call(s32[1,2048]{1,0:T(1,128)S(1)} %copy-done.1, bf16[2048,128]{1,0:T(8,128)(2,1)S(1)} %collective-permute-done.4.a_ref, bf16[2048,128]{1,0:T(8,128)(2,1)S(1)} %collective-permute-done.5.b_ref, ...), custom_call_target="tpu_custom_call" | custom-call | flops 335544320 | bytes 2097152 | tf_op jit(solution)/shard_map/pallas_call | solution.py:306
  77.6 1.3 %fusion.16 = f32[512,384]{1,0:T(8,128)S(1)} fusion(bf16[2048,512]{1,0:T(8,128)(2,1)S(1)} %copy-done.8, bf16[2048,384]{1,0:T(8,128)(2,1)S(1)} %get-tuple-element.33.refs_0_), kind=kOutput, calls=%fused_computation.68 | convolution fusion | flops 805306368 | bytes 4456448 | tf_op jit(solution)/shard_map/dot_general | solution.py:233
  78.8 4.5 %collective-permute-done.14.a_ref = bf16[2048,128]{1,0:T(8,128)(2,1)S(1)} collective-permute-done((bf16[2048,128]{1,0:T(8,128)(2,1)S(1)}, bf16[2048,128]{1,0:T(8,128)(2,1)S(1)}, u32[]{:S(2)}, u32[]{:S(2)}) %collective-permute-start.14) | collective-permute-done | bytes 524320 | tf_op jit(solution)/shard_map/ppermute | solution.py:19
  83.4 1.5 %shard_map.39 = (f32[4,224,128]{2,1,0:T(8,128)S(1)}, bf16[2048,128]{1,0:T(8,128)(2,1)S(1)}) custom-call(s32[1,2048]{1,0:T(1,128)S(1)} %copy-done.1, bf16[2048,128]{1,0:T(8,128)(2,1)S(1)} %collective-permute-done.14.a_ref, bf16[2048,128]{1,0:T(8,128)(2,1)S(1)} %collective-permute-done.15.b_ref, f32[3,2048]{1,0:T(4,128)S(1)} %collective-permute-done.6.a_facts, ...), custom_call_target="tpu_custom_call" | custom-call | flops 469762048 | bytes 2097152 | tf_op jit(solution)/shard_map/pallas_call | solution.py:306
  86.5 0.9 collective-permute-done.16
  87.4 1.6 %collective-permute-start.17 = (bf16[1,128,128]{2,1,0:T(8,128)(2,1)S(1)}, bf16[1,128,128]{2,1,0:T(8,128)(2,1)S(1)}, u32[]{:S(2)}, u32[]{:S(2)}) collective-permute-start(bf16[1,128,128]{2,1,0:T(8,128)(2,1)S(1)} %fusion.9), channel_id=1, source_target_pairs={{0,8},{4,12},{8,0},{12,4},{1,9},{5,13},{9,1},{13,5},{2,10},{6,14},... | collective-permute-start | bytes 98312 | tf_op jit(solution)/shard_map/ppermute | solution.py:37
  89.8 1.6 %collective-permute-start.20 = (bf16[1,224,128]{2,1,0:T(8,128)(2,1)S(1)}, bf16[1,224,128]{2,1,0:T(8,128)(2,1)S(1)}, u32[]{:S(2)}, u32[]{:S(2)}) collective-permute-start(bf16[1,224,128]{2,1,0:T(8,128)(2,1)S(1)} %fusion.8), channel_id=1, source_target_pairs={{0,8},{4,12},{8,0},{12,4},{1,9},{5,13},{9,1},{13,5},{2,10},{6,14},... | collective-permute-start | bytes 172040 | tf_op jit(solution)/shard_map/ppermute | solution.py:37
  91.3 2.8 %collective-permute-done.13 = bf16[1,304,128]{2,1,0:T(8,128)(2,1)S(1)} collective-permute-done((bf16[1,304,128]{2,1,0:T(8,128)(2,1)S(1)}, bf16[1,304,128]{2,1,0:T(8,128)(2,1)S(1)}, u32[]{:S(2)}, u32[]{:S(2)}) %collective-permute-start.13) | collective-permute-done | bytes 77856 | tf_op jit(solution)/shard_map/ppermute | solution.py:37
  94.3 1.3 %collective-permute-start.18 = (f32[288,128]{1,0:T(8,128)S(1)}, f32[288,128]{1,0:T(8,128)S(1)}, u32[]{:S(2)}, u32[]{:S(2)}) collective-permute-start(f32[288,128]{1,0:T(8,128)S(1)} %fusion.5), channel_id=1, source_target_pairs={{1,0},{2,1},{5,4},{6,5},{9,8},{10,9},{13,12},{14,13},{17,16},{18,1... | collective-permute-start | bytes 442376 | tf_op jit(solution)/shard_map/ppermute | solution.py:24
  95.6 1.3 %collective-permute-start.21 = (f32[224,128]{1,0:T(8,128)S(1)}, f32[224,128]{1,0:T(8,128)S(1)}, u32[]{:S(2)}, u32[]{:S(2)}) collective-permute-start(f32[224,128]{1,0:T(8,128)S(1)} %bitcast_divide_fusion.2), channel_id=1, source_target_pairs={{1,0},{2,1},{5,4},{6,5},{9,8},{10,9},{13,12},{14,13},{17,16},{18,1... | collective-permute-start | bytes 344072 | tf_op jit(solution)/shard_map/ppermute | solution.py:24
  97.1 0.9 collective-permute-start.11
  98.0 3.8 %collective-permute-done.11 = bf16[1,128,384]{2,1,0:T(8,128)(2,1)S(1)} collective-permute-done((bf16[1,128,384]{2,1,0:T(8,128)(2,1)S(1)}, bf16[1,128,384]{2,1,0:T(8,128)(2,1)S(1)}, u32[]{:S(2)}, u32[]{:S(2)}) %collective-permute-start.11) | collective-permute-done | bytes 98336 | tf_op jit(solution)/shard_map/ppermute | solution.py:37
  101.8 3.3 %collective-permute-done.21 = f32[224,128]{1,0:T(8,128)S(1)} collective-permute-done((f32[224,128]{1,0:T(8,128)S(1)}, f32[224,128]{1,0:T(8,128)S(1)}, u32[]{:S(2)}, u32[]{:S(2)}) %collective-permute-start.21) | collective-permute-done | bytes 114720 | tf_op jit(solution)/shard_map/ppermute | solution.py:24
  105.2 1.0 maximum_select_fusion
  (86 shorter events, 8.7 us)
Async XLA Ops:
  0.0 0.7 copy-start
  0.7 12.0 %copy-start.1 = (s32[1,2048]{1,0:T(1,128)S(1)}, s32[1,2048]{1,0:T(1,128)}, u32[]{:S(2)}) copy-start(s32[1,2048]{1,0:T(1,128)} %observed_ref.9) | copy-start | bytes 24580
  0.7 12.1 %copy-start.6 = (bf16[2048,512]{1,0:T(8,128)(2,1)S(1)}, bf16[2048,512]{1,0:T(8,128)(2,1)}, u32[]{:S(2)}) copy-start(bf16[2048,512]{1,0:T(8,128)(2,1)} %dosage_ref.3) | copy-start | bytes 6291460
  5.2 0.8 copy-start.2
  6.0 0.8 copy-start.4
  6.8 1.3 %collective-permute-start = (f32[8,512]{1,0:T(8,128)S(1)}, f32[8,512]{1,0:T(8,128)S(1)}, u32[]{:S(2)}, u32[]{:S(2)}) collective-permute-start(f32[8,512]{1,0:T(8,128)S(1)} %get-tuple-element.23), channel_id=1, source_target_pairs={{0,4},{4,0},{8,12},{12,8},{1,5},{5,1},{9,13},{13,9},{2,6},{6,2},{1... | collective-permute-start | bytes 49160 | tf_op jit(solution)/shard_map/ppermute | solution.py:37
  8.1 4.5 %collective-permute-start.1 = (f32[8,512]{1,0:T(8,128)S(1)}, f32[8,512]{1,0:T(8,128)S(1)}, u32[]{:S(2)}, u32[]{:S(2)}) collective-permute-start(f32[8,512]{1,0:T(8,128)S(1)} %add.47), channel_id=1, source_target_pairs={{0,8},{4,12},{8,0},{12,4},{1,9},{5,13},{9,1},{13,5},{2,10},{6,14},... | collective-permute-start | bytes 49160 | tf_op jit(solution)/shard_map/ppermute | solution.py:37
  13.5 1.4 %copy-start.7 = (bf16[2048,512]{1,0:T(8,128)(2,1)}, bf16[2048,512]{1,0:T(8,128)(2,1)S(1)}, u32[]{:S(2)}) copy-start(bf16[2048,512]{1,0:T(8,128)(2,1)S(1)} %select_convert_fusion) | copy-start | bytes 6291460
  14.9 1.0 copy-start.9
  16.8 12.0 %collective-permute-start.2 = (f32[2,128,512]{2,1,0:T(8,128)}, f32[2,128,512]{2,1,0:T(8,128)}, u32[]{:S(2)}, u32[]{:S(2)}) collective-permute-start(f32[2,128,512]{2,1,0:T(8,128)} %select_bitcast_fusion), channel_id=1, source_target_pairs={{0,4},{4,0},{8,12},{12,8},{1,5},{5,1},{9,13},{13,9},{2,6},{6,2},{1... | collective-permute-start | bytes 1572872 | tf_op jit(solution)/shard_map/ppermute | solution.py:37
  20.1 53.6 %collective-permute-start.8 = (bf16[2048,256]{1,0:T(8,128)(2,1)}, bf16[2048,256]{1,0:T(8,128)(2,1)S(1)}, u32[]{:S(2)}, u32[]{:S(2)}) collective-permute-start(bf16[2048,256]{1,0:T(8,128)(2,1)} %get-tuple-element.29), channel_id=1, source_target_pairs={{0,1},{2,3},{1,0},{3,2},{4,5},{6,7},{5,4},{7,6},{8,9},{10,11},{9,8... | collective-permute-start | bytes 3145736 | tf_op jit(solution)/shard_map/ppermute | solution.py:19
  22.3 52.1 %collective-permute-start.9 = (bf16[2048,256]{1,0:T(8,128)(2,1)}, bf16[2048,256]{1,0:T(8,128)(2,1)S(1)}, u32[]{:S(2)}, u32[]{:S(2)}) collective-permute-start(bf16[2048,256]{1,0:T(8,128)(2,1)} %get-tuple-element.30), channel_id=1, source_target_pairs={{1,2},{2,1},{5,6},{6,5},{9,10},{10,9},{13,14},{14,13},{17,18},{18,... | collective-permute-start | bytes 3145736 | tf_op jit(solution)/shard_map/ppermute | solution.py:19
  23.0 52.8 %collective-permute-start.4 = (bf16[2048,128]{1,0:T(8,128)(2,1)}, bf16[2048,128]{1,0:T(8,128)(2,1)S(1)}, u32[]{:S(2)}, u32[]{:S(2)}) collective-permute-start(bf16[2048,128]{1,0:T(8,128)(2,1)} %get-tuple-element.25), channel_id=1, source_target_pairs={{0,1},{2,3},{1,0},{3,2},{4,5},{6,7},{5,4},{7,6},{8,9},{10,11},{9,8... | collective-permute-start | bytes 1572872 | tf_op jit(solution)/shard_map/ppermute | solution.py:19
  27.4 48.4 %collective-permute-start.5 = (bf16[2048,128]{1,0:T(8,128)(2,1)}, bf16[2048,128]{1,0:T(8,128)(2,1)S(1)}, u32[]{:S(2)}, u32[]{:S(2)}) collective-permute-start(bf16[2048,128]{1,0:T(8,128)(2,1)} %get-tuple-element.26), channel_id=1, source_target_pairs={{1,2},{2,1},{5,6},{6,5},{9,10},{10,9},{13,14},{14,13},{17,18},{18,... | collective-permute-start | bytes 1572872 | tf_op jit(solution)/shard_map/ppermute | solution.py:19
  28.1 39.0 %copy-start.5 = (bf16[2048,128]{1,0:T(8,128)(2,1)S(1)}, bf16[2048,128]{1,0:T(8,128)(2,1)}, u32[]{:S(2)}) copy-start(bf16[2048,128]{1,0:T(8,128)(2,1)} %copy-done.4) | copy-start | bytes 1572868
  28.1 45.6 %copy-start.3 = (bf16[2048,128]{1,0:T(8,128)(2,1)S(1)}, bf16[2048,128]{1,0:T(8,128)(2,1)}, u32[]{:S(2)}) copy-start(bf16[2048,128]{1,0:T(8,128)(2,1)} %copy-done.2) | copy-start | bytes 1572868
  28.8 29.4 %collective-permute-start.6 = (f32[3,2048]{1,0:T(4,128)S(1)}, f32[3,2048]{1,0:T(4,128)S(1)}, u32[]{:S(2)}, u32[]{:S(2)}) collective-permute-start(f32[3,2048]{1,0:T(4,128)S(1)} %get-tuple-element.27), channel_id=1, source_target_pairs={{0,1},{2,3},{1,0},{3,2},{4,5},{6,7},{5,4},{7,6},{8,9},{10,11},{9,8... | collective-permute-start | bytes 73736 | tf_op jit(solution)/shard_map/ppermute | solution.py:19
  58.2 8.1 %collective-permute-start.3 = (f32[1,128,512]{2,1,0:T(8,128)S(1)}, f32[1,128,512]{2,1,0:T(8,128)S(1)}, u32[]{:S(2)}, u32[]{:S(2)}) collective-permute-start(f32[1,128,512]{2,1,0:T(8,128)S(1)} %select_bitcast_fusion.3), channel_id=1, source_target_pairs={{0,8},{4,12},{8,0},{12,4},{1,9},{5,13},{9,1},{13,5},{2,10},{6,14},... | collective-permute-start | bytes 786440 | tf_op jit(solution)/shard_map/ppermute | solution.py:37
  66.4 0.7 collective-permute-start.7
  67.1 16.2 %collective-permute-start.14 = (bf16[2048,128]{1,0:T(8,128)(2,1)S(1)}, bf16[2048,128]{1,0:T(8,128)(2,1)S(1)}, u32[]{:S(2)}, u32[]{:S(2)}) collective-permute-start(bf16[2048,128]{1,0:T(8,128)(2,1)S(1)} %copy-done.5), channel_id=1, source_target_pairs={{0,1},{2,3},{1,0},{3,2},{4,5},{6,7},{5,4},{7,6},{8,9},{10,11},{9,8... | collective-permute-start | bytes 1572872 | tf_op jit(solution)/shard_map/ppermute | solution.py:19
  73.6 9.7 %collective-permute-start.15 = (bf16[2048,128]{1,0:T(8,128)(2,1)S(1)}, bf16[2048,128]{1,0:T(8,128)(2,1)S(1)}, u32[]{:S(2)}, u32[]{:S(2)}) collective-permute-start(bf16[2048,128]{1,0:T(8,128)(2,1)S(1)} %copy-done.3), channel_id=1, source_target_pairs={{1,2},{2,1},{5,6},{6,5},{9,10},{10,9},{13,14},{14,13},{17,18},{18,... | collective-permute-start | bytes 1572872 | tf_op jit(solution)/shard_map/ppermute | solution.py:19
  75.8 1.7 %copy-start.8 = (bf16[2048,512]{1,0:T(8,128)(2,1)S(1)}, bf16[2048,512]{1,0:T(8,128)(2,1)}, u32[]{:S(2)}) copy-start(bf16[2048,512]{1,0:T(8,128)(2,1)} %copy-done.7) | copy-start | bytes 6291460
  77.5 11.5 %collective-permute-start.12 = (f32[2,296,128]{2,1,0:T(8,128)S(1)}, f32[2,296,128]{2,1,0:T(8,128)S(1)}, u32[]{:S(2)}, u32[]{:S(2)}) collective-permute-start(f32[2,296,128]{2,1,0:T(8,128)S(1)} %select_bitcast_fusion.2), channel_id=1, source_target_pairs={{0,4},{4,0},{8,12},{12,8},{1,5},{5,1},{9,13},{13,9},{2,6},{6,2},{1... | collective-permute-start | bytes 909320 | tf_op jit(solution)/shard_map/ppermute | solution.py:37
  84.9 4.0 %collective-permute-start.19 = (f32[2,224,128]{2,1,0:T(8,128)S(1)}, f32[2,224,128]{2,1,0:T(8,128)S(1)}, u32[]{:S(2)}, u32[]{:S(2)}) collective-permute-start(f32[2,224,128]{2,1,0:T(8,128)S(1)} %select_bitcast_fusion.4), channel_id=1, source_target_pairs={{0,4},{4,0},{8,12},{12,8},{1,5},{5,1},{9,13},{13,9},{2,6},{6,2},{1... | collective-permute-start | bytes 688136 | tf_op jit(solution)/shard_map/ppermute | solution.py:37
  85.8 1.5 %collective-permute-start.16 = (f32[2,128,128]{2,1,0:T(8,128)S(1)}, f32[2,128,128]{2,1,0:T(8,128)S(1)}, u32[]{:S(2)}, u32[]{:S(2)}) collective-permute-start(f32[2,128,128]{2,1,0:T(8,128)S(1)} %select_bitcast_fusion.6), channel_id=1, source_target_pairs={{0,4},{4,0},{8,12},{12,8},{1,5},{5,1},{9,13},{13,9},{2,6},{6,2},{1... | collective-permute-start | bytes 393224 | tf_op jit(solution)/shard_map/ppermute | solution.py:37
  86.4 10.5 %collective-permute-start.10 = (f32[2,128,384]{2,1,0:T(8,128)S(1)}, f32[2,128,384]{2,1,0:T(8,128)S(1)}, u32[]{:S(2)}, u32[]{:S(2)}) collective-permute-start(f32[2,128,384]{2,1,0:T(8,128)S(1)} %select_bitcast_fusion.1), channel_id=1, source_target_pairs={{0,4},{4,0},{8,12},{12,8},{1,5},{5,1},{9,13},{13,9},{2,6},{6,2},{1... | collective-permute-start | bytes 1179656 | tf_op jit(solution)/shard_map/ppermute | solution.py:37
  87.4 10.5 %collective-permute-start.17 = (bf16[1,128,128]{2,1,0:T(8,128)(2,1)S(1)}, bf16[1,128,128]{2,1,0:T(8,128)(2,1)S(1)}, u32[]{:S(2)}, u32[]{:S(2)}) collective-permute-start(bf16[1,128,128]{2,1,0:T(8,128)(2,1)S(1)} %fusion.9), channel_id=1, source_target_pairs={{0,8},{4,12},{8,0},{12,4},{1,9},{5,13},{9,1},{13,5},{2,10},{6,14},... | collective-permute-start | bytes 98312 | tf_op jit(solution)/shard_map/ppermute | solution.py:37
  89.1 5.0 %collective-permute-start.13 = (bf16[1,304,128]{2,1,0:T(8,128)(2,1)S(1)}, bf16[1,304,128]{2,1,0:T(8,128)(2,1)S(1)}, u32[]{:S(2)}, u32[]{:S(2)}) collective-permute-start(bf16[1,304,128]{2,1,0:T(8,128)(2,1)S(1)} %pad_maximum_fusion.1), channel_id=1, source_target_pairs={{0,8},{4,12},{8,0},{12,4},{1,9},{5,13},{9,1},{13,5},{2,10},{6,14},... | collective-permute-start | bytes 233480 | tf_op jit(solution)/shard_map/ppermute | solution.py:37
  89.8 5.8 %collective-permute-start.20 = (bf16[1,224,128]{2,1,0:T(8,128)(2,1)S(1)}, bf16[1,224,128]{2,1,0:T(8,128)(2,1)S(1)}, u32[]{:S(2)}, u32[]{:S(2)}) collective-permute-start(bf16[1,224,128]{2,1,0:T(8,128)(2,1)S(1)} %fusion.8), channel_id=1, source_target_pairs={{0,8},{4,12},{8,0},{12,4},{1,9},{5,13},{9,1},{13,5},{2,10},{6,14},... | collective-permute-start | bytes 172040 | tf_op jit(solution)/shard_map/ppermute | solution.py:37
  94.3 10.8 %collective-permute-start.18 = (f32[288,128]{1,0:T(8,128)S(1)}, f32[288,128]{1,0:T(8,128)S(1)}, u32[]{:S(2)}, u32[]{:S(2)}) collective-permute-start(f32[288,128]{1,0:T(8,128)S(1)} %fusion.5), channel_id=1, source_target_pairs={{1,0},{2,1},{5,4},{6,5},{9,8},{10,9},{13,12},{14,13},{17,16},{18,1... | collective-permute-start | bytes 442376 | tf_op jit(solution)/shard_map/ppermute | solution.py:24
  95.6 9.4 %collective-permute-start.21 = (f32[224,128]{1,0:T(8,128)S(1)}, f32[224,128]{1,0:T(8,128)S(1)}, u32[]{:S(2)}, u32[]{:S(2)}) collective-permute-start(f32[224,128]{1,0:T(8,128)S(1)} %bitcast_divide_fusion.2), channel_id=1, source_target_pairs={{1,0},{2,1},{5,4},{6,5},{9,8},{10,9},{13,12},{14,13},{17,16},{18,1... | collective-permute-start | bytes 344072 | tf_op jit(solution)/shard_map/ppermute | solution.py:24
  97.1 4.7 %collective-permute-start.11 = (bf16[1,128,384]{2,1,0:T(8,128)(2,1)S(1)}, bf16[1,128,384]{2,1,0:T(8,128)(2,1)S(1)}, u32[]{:S(2)}, u32[]{:S(2)}) collective-permute-start(bf16[1,128,384]{2,1,0:T(8,128)(2,1)S(1)} %fusion.7), channel_id=1, source_target_pairs={{0,8},{4,12},{8,0},{12,4},{1,9},{5,13},{9,1},{13,5},{2,10},{6,14},... | collective-permute-start | bytes 294920 | tf_op jit(solution)/shard_map/ppermute | solution.py:37

commit v11 on v10

--- a/solution.py
+++ b/solution.py
@@ -192,12 +192,11 @@
     for line, natural in enumerate((centre, inverse)):
         ordered = jnp.concatenate([natural[:, low:high] for low, high in cuts], axis=1)
         one, two = either(even, ordered, natural)
-        a_ref[line : line + 1, :width] = one
-        b_ref[line : line + 1, :width] = two
+        a_ref[line : line + 1, :] = one
+        b_ref[line : line + 1, :] = two
     for ref in (a_ref, b_ref):
-        ref[2:3, :] = flags
-        if width < ref.shape[1]:
-            ref[0:2, width:] = jnp.zeros((2, ref.shape[1] - width), jnp.float32)
+        for line in range(flags.shape[1] // width):
+            ref[2 + line : 3 + line, :] = flags[:, line * width : (line + 1) * width]
 
 
 def facts_pass(sums, observed, cuts, rows):
@@ -205,7 +204,7 @@
     single = jnp.float32
     return pl.pallas_call(
         functools.partial(facts_kernel, cuts, rows),
-        out_shape=(like((2, width), single),) + (like((3, samples), single),) * 2,
+        out_shape=(like((2, width), single),) + (like((2 + samples // width, width), single),) * 2,
         in_specs=[whole()] * 2,
         out_specs=(whole(),) * 3,
         compiler_params=pltpu.CompilerParams(vmem_limit_bytes=GRANT),
@@ -216,6 +215,11 @@
 def standardize(values, present, moments):
     spread = (values.astype(jnp.float32) - moments[0:1]) * moments[1:2]
     return jnp.where(present, spread, 0.0).astype(jnp.bfloat16)
+
+
+def flags_in(facts, k, block):
+    lines = block // facts.shape[1]
+    return jnp.concatenate([facts[2 + k * lines + j : 3 + k * lines + j] for j in range(lines)], 1)
 
 
 def decode(values, facts, present, first):
@@ -248,8 +252,8 @@
     shares = [jnp.zeros((1, lanes), jnp.float32)] * 2
     for k in range(samples // block):
         part = slice(k * block, (k + 1) * block)
-        above_present = mask_of(above_f[2:3, part])
-        below_present = mask_of(below_f[2:3, part])
+        above_present = mask_of(flags_in(above_f, k, block))
+        below_present = mask_of(flags_in(below_f, k, block))
         if step == 0:
             own_present = mask_of(observed_ref[:, part])
             shares = [
@@ -364,13 +368,14 @@
         + [(heights[step], wides[j]) for j in range(step + 1)]
         for step in range(3)
     ]
-    lines = products[1].shape[1] + products[0].shape[1] - 8
-    one = jnp.concatenate([products[1], products[0]], axis=1)
-    one = sum_rows(one, "samp", roles, lines)
-    shares = jnp.maximum(one[lines:], 1.0)
-    far_1 = one[:lines] / shares[1:2]
+    shares = jnp.maximum(sum_all(products[0][0, -8:], "samp"), 1.0)
+    near_0 = cross(own, aboves[0]).reshape(peers, rows, -1)
+    one = jnp.concatenate([products[1], products[0][:, :-8]], axis=1)
+    one = sum_rows(one, "samp", roles, one.shape[1])
+    far_1 = one / shares[1:2]
     far_1 = bring_back(far_1, "var")
-    near_1 = cross(own, aboves[1]).reshape(peers, rows, -1)
+    near_1 = cross(own, aboves[1][:, wides[0] :]).reshape(peers, rows, -1)
+    near_1 = jnp.concatenate([near_0, near_1], axis=2)
     near_1 = sum_rows(near_1, "samp", roles, rows)
     near_1 = near_1 / jnp.concatenate([shares[0:1]] * (near_1.shape[1] // 128), axis=1)
     far_2 = sum_rows(products[2], "samp", roles, products[2].shape[1]) / shares[1:2]

time: 107 us -> 113 us (1.056)
  starting transfers between devices: 30 us -> 40.2 us
  waiting for transfers between devices: 50.8 us -> 47.6 us
    ppermute x8, starting transfers between devices: 17.1 us -> 25.4 us  [trade(): lax.ppermute(shard, axis, pairs + [(high, low) for low, high in pairs])]
    ppermute x12 -> x14, waiting for transfers between devices: 16.5 us -> 9.28 us  [swap(): return lax.ppermute(shard, axis, [(i, i ^ bit) for i in range(peers)])]
    ppermute x2, waiting for transfers between devices: 3.28 us -> 6.21 us  [bring_back(): return lax.ppermute(shard, axis, [(i, i - 1) for i in range(1, peers - 1)])]
    ppermute x12 -> x14, starting transfers between devices: 10.3 us -> 12.2 us  [swap(): return lax.ppermute(shard, axis, [(i, i ^ bit) for i in range(peers)])]
    dot_general x3 -> x4, matrix products: 3.3 us -> 3.51 us  [cross(): lax.dot_general(left, right, (((0,), (0,)), ((), ())), preferred_element_...]
  transfers between devices with their start and end apart: 22 -> 24, of which waited for: 9 -> 10; matrix products, arithmetic and copies ran while one was open for 4% -> 4% of each run, Pallas kernels for 7% -> 7%
where the time goes in v11:
time: 113 us
  waiting for transfers between devices  47.6 us (42%)
  starting transfers between devices  40.2 us (36%)
  Pallas kernels  12.3 us (11%)
  other arithmetic  4.9 us (4%)
  matrix products  3.51 us (3%)
  local copies, waits for them, and re-layouts  3.46 us (3%)
  between operations  1.17 us (1%)
    ppermute x8, waiting for transfers between devices, trade(): lax.ppermute(shard, axis, pairs + [(high, low) for low, high in pairs])  32.1 us
    ppermute x8, starting transfers between devices, trade(): lax.ppermute(shard, axis, pairs + [(high, low) for low, high in pairs])  25.4 us
    ppermute x14, starting transfers between devices, swap(): return lax.ppermute(shard, axis, [(i, i ^ bit) for i in range(peers)])  12.2 us
    ppermute x14, waiting for transfers between devices, swap(): return lax.ppermute(shard, axis, [(i, i ^ bit) for i in range(peers)])  9.28 us
    ppermute x2, waiting for transfers between devices, bring_back(): return lax.ppermute(shard, axis, [(i, i - 1) for i in range(1, peers - 1)])  6.21 us
    pallas_call x3, Pallas kernels, chunk_pass(): pl.pallas_call(functools.partial(chunk_kernel, step, marks, last), out_sh...  4.53 us
    pallas_call x1, Pallas kernels, moments_pass(): pl.pallas_call(functools.partial(moments_kernel, cuts, rows), grid=(sampl...  4.42 us
    dot_general x4, matrix products, cross(): lax.dot_general(left, right, (((0,), (0,)), ((), ())), preferred_element_...  3.51 us
  transfers between devices with their start and end apart: 24, of which 10 were waited for; matrix products, arithmetic and copies ran while one was open for 4% of the time, Pallas kernels for 7%

profile of v11, /device:TPU:0, one launch (start us, length us, event | category | flops | bytes accessed | tf_op | source)
XLA Modules:
  0.0 113.1 jit_solution(6399355716442305365)
XLA Ops:
  0.7 4.4 %moments.1 = (bf16[2048,128]{1,0:T(8,128)(2,1)}, bf16[2048,128]{1,0:T(8,128)(2,1)S(1)}, bf16[2048,128]{1,0:T(8,128)(2,1)S(1)}, bf16[2048,128]{1,0:T(8,128)(2,1)S(1)}, f32[8,512]{1,0:T(8,128)S(1)}) custom-call(bf16[2048,512]{1,0:T(8,128)(2,1)} %dosage_ref.3, s32[1,2048]{1,0:T(1,128)S(1)} %copy-done), custom_call_target="tpu_custom_call" | custom-call | flops 8388608 | bytes 4194304 | tf_op jit(solution)/shard_map/moments/pallas_call | solution.py:163
  5.1 0.8 copy-done.2
  5.9 0.8 copy-done.4
  7.2 0.8 collective-permute-done
  8.1 2.8 %collective-permute-start.1 = (f32[8,512]{1,0:T(8,128)S(1)}, f32[8,512]{1,0:T(8,128)S(1)}, u32[]{:S(2)}, u32[]{:S(2)}) collective-permute-start(f32[8,512]{1,0:T(8,128)S(1)} %add.42), channel_id=1, source_target_pairs={{0,8},{4,12},{8,0},{12,4},{1,9},{5,13},{9,1},{13,5},{2,10},{6,14},... | collective-permute-start | bytes 49160 | tf_op jit(solution)/shard_map/ppermute | solution.py:37
  10.9 1.7 %collective-permute-done.1 = f32[8,512]{1,0:T(8,128)S(1)} collective-permute-done((f32[8,512]{1,0:T(8,128)S(1)}, f32[8,512]{1,0:T(8,128)S(1)}, u32[]{:S(2)}, u32[]{:S(2)}) %collective-permute-start.1) | collective-permute-done | bytes 16416 | tf_op jit(solution)/shard_map/ppermute | solution.py:37
  13.5 1.3 %fusion.21 = f32[512,512]{1,0:T(8,128)S(1)} fusion(bf16[2048,512]{1,0:T(8,128)(2,1)S(1)} %select_convert_fusion), kind=kOutput, calls=%fused_computation.70 | convolution fusion | flops 1073741824 | bytes 3145728 | tf_op jit(solution)/shard_map/dot_general | solution.py:237
  14.8 1.0 copy-done.9
  15.9 0.9 select_bitcast_fusion
  16.7 3.2 %head.1 = (bf16[2048,256]{1,0:T(8,128)(2,1)}, bf16[2048,256]{1,0:T(8,128)(2,1)}) custom-call(bf16[2048,512]{1,0:T(8,128)(2,1)} %dosage_ref.3), custom_call_target="tpu_custom_call" | custom-call | tf_op jit(solution)/shard_map/head/pallas_call | solution.py:119
  19.9 2.2 %collective-permute-start.4 = (bf16[2048,256]{1,0:T(8,128)(2,1)}, bf16[2048,256]{1,0:T(8,128)(2,1)S(1)}, u32[]{:S(2)}, u32[]{:S(2)}) collective-permute-start(bf16[2048,256]{1,0:T(8,128)(2,1)} %get-tuple-element.25), channel_id=1, source_target_pairs={{0,1},{2,3},{1,0},{3,2},{4,5},{6,7},{5,4},{7,6},{8,9},{10,11},{9,8... | collective-permute-start | bytes 3145736 | tf_op jit(solution)/shard_map/ppermute | solution.py:19
  22.8 4.4 %collective-permute-start.8 = (bf16[2048,128]{1,0:T(8,128)(2,1)}, bf16[2048,128]{1,0:T(8,128)(2,1)S(1)}, u32[]{:S(2)}, u32[]{:S(2)}) collective-permute-start(bf16[2048,128]{1,0:T(8,128)(2,1)} %get-tuple-element.30), channel_id=1, source_target_pairs={{0,1},{2,3},{1,0},{3,2},{4,5},{6,7},{5,4},{7,6},{8,9},{10,11},{9,8... | collective-permute-start | bytes 1572872 | tf_op jit(solution)/shard_map/ppermute | solution.py:19
  28.1 1.5 %fusion = f32[1,2,128,512]{3,2,1,0:T(8,128)S(1)} fusion(f32[2,128,512]{2,1,0:T(8,128)} %collective-permute-done.2, f32[2,2,128,512]{3,2,1,0:T(8,128)} %bitcast.181, pred[]{:T(512)S(6)} %ne.20), kind=kLoop, calls=%fused_computation.8 | loop fusion | flops 262144 | bytes 2097153 | tf_op jit(solution)/shard_map/reshape | solution.py:52
  29.6 1.6 %collective-permute-start.3 = (f32[1,128,512]{2,1,0:T(8,128)S(1)}, f32[1,128,512]{2,1,0:T(8,128)S(1)}, u32[]{:S(2)}, u32[]{:S(2)}) collective-permute-start(f32[1,128,512]{2,1,0:T(8,128)S(1)} %select_bitcast_fusion.3), channel_id=1, source_target_pairs={{0,8},{4,12},{8,0},{12,4},{1,9},{5,13},{9,1},{13,5},{2,10},{6,14},... | collective-permute-start | bytes 786440 | tf_op jit(solution)/shard_map/ppermute | solution.py:37
  31.2 26.5 %collective-permute-done.6.a_facts = f32[6,512]{1,0:T(8,128)S(1)} collective-permute-done((f32[6,512]{1,0:T(8,128)S(1)}, f32[6,512]{1,0:T(8,128)S(1)}, u32[]{:S(2)}, u32[]{:S(2)}) %collective-permute-start.6) | collective-permute-done | bytes 12320 | tf_op jit(solution)/shard_map/ppermute | solution.py:19
  59.2 16.0 %collective-permute-start.14 = (bf16[2048,128]{1,0:T(8,128)(2,1)S(1)}, bf16[2048,128]{1,0:T(8,128)(2,1)S(1)}, u32[]{:S(2)}, u32[]{:S(2)}) collective-permute-start(bf16[2048,128]{1,0:T(8,128)(2,1)S(1)} %copy-done.3), channel_id=1, source_target_pairs={{0,1},{2,3},{1,0},{3,2},{4,5},{6,7},{5,4},{7,6},{8,9},{10,11},{9,8... | collective-permute-start | bytes 1572872 | tf_op jit(solution)/shard_map/ppermute | solution.py:19
  75.9 1.5 %shard_map.37 = (f32[4,136,128]{2,1,0:T(8,128)S(1)}, bf16[2048,256]{1,0:T(8,128)(2,1)S(1)}, bf16[2048,256]{1,0:T(8,128)(2,1)S(1)}) custom-call(s32[1,2048]{1,0:T(1,128)S(1)} %copy-done.1, bf16[2048,256]{1,0:T(8,128)(2,1)S(1)} %collective-permute-done.4.a_ref, bf16[2048,256]{1,0:T(8,128)(2,1)S(1)} %collective-permute-done.5.b_ref, ...), custom_call_target="tpu_custom_call" | custom-call | flops 285212672 | bytes 4194304 | tf_op jit(solution)/shard_map/pallas_call | solution.py:310
  77.5 1.5 %shard_map.38 = (f32[4,160,128]{2,1,0:T(8,128)S(1)}, bf16[2048,384]{1,0:T(8,128)(2,1)S(1)}, bf16[2048,384]{1,0:T(8,128)(2,1)S(1)}) custom-call(s32[1,2048]{1,0:T(1,128)S(1)} %copy-done.1, bf16[2048,128]{1,0:T(8,128)(2,1)S(1)} %collective-permute-done.8.a_ref, bf16[2048,128]{1,0:T(8,128)(2,1)S(1)} %collective-permute-done.9.b_ref, ...), custom_call_target="tpu_custom_call" | custom-call | flops 335544320 | bytes 2097152 | tf_op jit(solution)/shard_map/pallas_call | solution.py:310
  80.6 5.5 %collective-permute-done.14.a_ref = bf16[2048,128]{1,0:T(8,128)(2,1)S(1)} collective-permute-done((bf16[2048,128]{1,0:T(8,128)(2,1)S(1)}, bf16[2048,128]{1,0:T(8,128)(2,1)S(1)}, u32[]{:S(2)}, u32[]{:S(2)}) %collective-permute-start.14) | collective-permute-done | bytes 524320 | tf_op jit(solution)/shard_map/ppermute | solution.py:19
  86.1 1.5 %shard_map.39 = (f32[4,224,128]{2,1,0:T(8,128)S(1)}, bf16[2048,128]{1,0:T(8,128)(2,1)S(1)}) custom-call(s32[1,2048]{1,0:T(1,128)S(1)} %copy-done.1, bf16[2048,128]{1,0:T(8,128)(2,1)S(1)} %collective-permute-done.14.a_ref, bf16[2048,128]{1,0:T(8,128)(2,1)S(1)} %collective-permute-done.15.b_ref, f32[6,512]{1,0:T(8,128)S(1)} %collective-permute-done.6.a_facts, ...), custom_call_target="tpu_custom_call" | custom-call | flops 469762048 | bytes 2097152 | tf_op jit(solution)/shard_map/pallas_call | solution.py:310
  89.3 1.6 %collective-permute-start.13 = (f32[8,128]{1,0:T(8,128)S(1)}, f32[8,128]{1,0:T(8,128)S(1)}, u32[]{:S(2)}, u32[]{:S(2)}) collective-permute-start(f32[8,128]{1,0:T(8,128)S(1)} %fusion.15), channel_id=1, source_target_pairs={{0,8},{4,12},{8,0},{12,4},{1,9},{5,13},{9,1},{13,5},{2,10},{6,14},... | collective-permute-start | bytes 12296 | tf_op jit(solution)/shard_map/ppermute | solution.py:37
  91.1 1.8 %collective-permute-done.13 = f32[8,128]{1,0:T(8,128)S(1)} collective-permute-done((f32[8,128]{1,0:T(8,128)S(1)}, f32[8,128]{1,0:T(8,128)S(1)}, u32[]{:S(2)}, u32[]{:S(2)}) %collective-permute-start.13) | collective-permute-done | bytes 4128 | tf_op jit(solution)/shard_map/ppermute | solution.py:37
  93.0 1.6 %collective-permute-start.17 = (bf16[1,128,128]{2,1,0:T(8,128)(2,1)S(1)}, bf16[1,128,128]{2,1,0:T(8,128)(2,1)S(1)}, u32[]{:S(2)}, u32[]{:S(2)}) collective-permute-start(bf16[1,128,128]{2,1,0:T(8,128)(2,1)S(1)} %fusion.14), channel_id=1, source_target_pairs={{0,8},{4,12},{8,0},{12,4},{1,9},{5,13},{9,1},{13,5},{2,10},{6,14},... | collective-permute-start | bytes 98312 | tf_op jit(solution)/shard_map/ppermute | solution.py:37
  94.6 2.4 %collective-permute-done.17 = bf16[1,128,128]{2,1,0:T(8,128)(2,1)S(1)} collective-permute-done((bf16[1,128,128]{2,1,0:T(8,128)(2,1)S(1)}, bf16[1,128,128]{2,1,0:T(8,128)(2,1)S(1)}, u32[]{:S(2)}, u32[]{:S(2)}) %collective-permute-start.17) | collective-permute-done | bytes 32800 | tf_op jit(solution)/shard_map/ppermute | solution.py:37
  97.1 1.6 %collective-permute-start.22 = (bf16[1,224,128]{2,1,0:T(8,128)(2,1)S(1)}, bf16[1,224,128]{2,1,0:T(8,128)(2,1)S(1)}, u32[]{:S(2)}, u32[]{:S(2)}) collective-permute-start(bf16[1,224,128]{2,1,0:T(8,128)(2,1)S(1)} %fusion.13), channel_id=1, source_target_pairs={{0,8},{4,12},{8,0},{12,4},{1,9},{5,13},{9,1},{13,5},{2,10},{6,14},... | collective-permute-start | bytes 172040 | tf_op jit(solution)/shard_map/ppermute | solution.py:37
  99.3 2.0 %collective-permute-done.22 = bf16[1,224,128]{2,1,0:T(8,128)(2,1)S(1)} collective-permute-done((bf16[1,224,128]{2,1,0:T(8,128)(2,1)S(1)}, bf16[1,224,128]{2,1,0:T(8,128)(2,1)S(1)}, u32[]{:S(2)}, u32[]{:S(2)}) %collective-permute-start.22) | collective-permute-done | bytes 57376 | tf_op jit(solution)/shard_map/ppermute | solution.py:37
  101.3 1.3 %collective-permute-start.23 = (f32[224,128]{1,0:T(8,128)S(1)}, f32[224,128]{1,0:T(8,128)S(1)}, u32[]{:S(2)}, u32[]{:S(2)}) collective-permute-start(f32[224,128]{1,0:T(8,128)S(1)} %bitcast_divide_fusion.3), channel_id=1, source_target_pairs={{1,0},{2,1},{5,4},{6,5},{9,8},{10,9},{13,12},{14,13},{17,16},{18,1... | collective-permute-start | bytes 344072 | tf_op jit(solution)/shard_map/ppermute | solution.py:24
  103.2 1.3 %collective-permute-start.20 = (f32[288,128]{1,0:T(8,128)S(1)}, f32[288,128]{1,0:T(8,128)S(1)}, u32[]{:S(2)}, u32[]{:S(2)}) collective-permute-start(f32[288,128]{1,0:T(8,128)S(1)} %bitcast_divide_fusion.2), channel_id=1, source_target_pairs={{1,0},{2,1},{5,4},{6,5},{9,8},{10,9},{13,12},{14,13},{17,16},{18,1... | collective-permute-start | bytes 442376 | tf_op jit(solution)/shard_map/ppermute | solution.py:24
  104.6 1.1 collective-permute-start.11
  105.7 4.0 %collective-permute-done.23 = f32[224,128]{1,0:T(8,128)S(1)} collective-permute-done((f32[224,128]{1,0:T(8,128)S(1)}, f32[224,128]{1,0:T(8,128)S(1)}, u32[]{:S(2)}, u32[]{:S(2)}) %collective-permute-start.23) | collective-permute-done | bytes 114720 | tf_op jit(solution)/shard_map/ppermute | solution.py:24
  109.7 2.2 %collective-permute-done.20 = f32[288,128]{1,0:T(8,128)S(1)} collective-permute-done((f32[288,128]{1,0:T(8,128)S(1)}, f32[288,128]{1,0:T(8,128)S(1)}, u32[]{:S(2)}, u32[]{:S(2)}) %collective-permute-start.20) | collective-permute-done | bytes 147488 | tf_op jit(solution)/shard_map/ppermute | solution.py:24
  112.0 1.0 maximum_select_fusion
  (87 shorter events, 10.1 us)
Async XLA Ops:
  0.7 11.9 %copy-start.1 = (s32[1,2048]{1,0:T(1,128)S(1)}, s32[1,2048]{1,0:T(1,128)}, u32[]{:S(2)}) copy-start(s32[1,2048]{1,0:T(1,128)} %observed_ref.9) | copy-start | bytes 24580
  0.7 12.0 %copy-start.8 = (bf16[2048,512]{1,0:T(8,128)(2,1)S(1)}, bf16[2048,512]{1,0:T(8,128)(2,1)}, u32[]{:S(2)}) copy-start(bf16[2048,512]{1,0:T(8,128)(2,1)} %dosage_ref.3) | copy-start | bytes 6291460
  5.9 0.8 copy-start.4
  6.7 1.3 %collective-permute-start = (f32[8,512]{1,0:T(8,128)S(1)}, f32[8,512]{1,0:T(8,128)S(1)}, u32[]{:S(2)}, u32[]{:S(2)}) collective-permute-start(f32[8,512]{1,0:T(8,128)S(1)} %get-tuple-element.23), channel_id=1, source_target_pairs={{0,4},{4,0},{8,12},{12,8},{1,5},{5,1},{9,13},{13,9},{2,6},{6,2},{1... | collective-permute-start | bytes 49160 | tf_op jit(solution)/shard_map/ppermute | solution.py:37
  8.1 4.5 %collective-permute-start.1 = (f32[8,512]{1,0:T(8,128)S(1)}, f32[8,512]{1,0:T(8,128)S(1)}, u32[]{:S(2)}, u32[]{:S(2)}) collective-permute-start(f32[8,512]{1,0:T(8,128)S(1)} %add.42), channel_id=1, source_target_pairs={{0,8},{4,12},{8,0},{12,4},{1,9},{5,13},{9,1},{13,5},{2,10},{6,14},... | collective-permute-start | bytes 49160 | tf_op jit(solution)/shard_map/ppermute | solution.py:37
  13.5 1.4 %copy-start.6 = (bf16[2048,512]{1,0:T(8,128)(2,1)}, bf16[2048,512]{1,0:T(8,128)(2,1)S(1)}, u32[]{:S(2)}) copy-start(bf16[2048,512]{1,0:T(8,128)(2,1)S(1)} %select_convert_fusion) | copy-start | bytes 6291460
  14.8 1.0 copy-start.9
  16.7 11.4 %collective-permute-start.2 = (f32[2,128,512]{2,1,0:T(8,128)}, f32[2,128,512]{2,1,0:T(8,128)}, u32[]{:S(2)}, u32[]{:S(2)}) collective-permute-start(f32[2,128,512]{2,1,0:T(8,128)} %select_bitcast_fusion), channel_id=1, source_target_pairs={{0,4},{4,0},{8,12},{12,8},{1,5},{5,1},{9,13},{13,9},{2,6},{6,2},{1... | collective-permute-start | bytes 1572872 | tf_op jit(solution)/shard_map/ppermute | solution.py:37
  19.9 55.3 %collective-permute-start.4 = (bf16[2048,256]{1,0:T(8,128)(2,1)}, bf16[2048,256]{1,0:T(8,128)(2,1)S(1)}, u32[]{:S(2)}, u32[]{:S(2)}) collective-permute-start(bf16[2048,256]{1,0:T(8,128)(2,1)} %get-tuple-element.25), channel_id=1, source_target_pairs={{0,1},{2,3},{1,0},{3,2},{4,5},{6,7},{5,4},{7,6},{8,9},{10,11},{9,8... | collective-permute-start | bytes 3145736 | tf_op jit(solution)/shard_map/ppermute | solution.py:19
  22.1 53.8 %collective-permute-start.5 = (bf16[2048,256]{1,0:T(8,128)(2,1)}, bf16[2048,256]{1,0:T(8,128)(2,1)S(1)}, u32[]{:S(2)}, u32[]{:S(2)}) collective-permute-start(bf16[2048,256]{1,0:T(8,128)(2,1)} %get-tuple-element.26), channel_id=1, source_target_pairs={{1,2},{2,1},{5,6},{6,5},{9,10},{10,9},{13,14},{14,13},{17,18},{18,... | collective-permute-start | bytes 3145736 | tf_op jit(solution)/shard_map/ppermute | solution.py:19
  22.8 54.7 %collective-permute-start.8 = (bf16[2048,128]{1,0:T(8,128)(2,1)}, bf16[2048,128]{1,0:T(8,128)(2,1)S(1)}, u32[]{:S(2)}, u32[]{:S(2)}) collective-permute-start(bf16[2048,128]{1,0:T(8,128)(2,1)} %get-tuple-element.30), channel_id=1, source_target_pairs={{0,1},{2,3},{1,0},{3,2},{4,5},{6,7},{5,4},{7,6},{8,9},{10,11},{9,8... | collective-permute-start | bytes 1572872 | tf_op jit(solution)/shard_map/ppermute | solution.py:19
  27.2 30.5 %copy-start.5 = (bf16[2048,128]{1,0:T(8,128)(2,1)S(1)}, bf16[2048,128]{1,0:T(8,128)(2,1)}, u32[]{:S(2)}) copy-start(bf16[2048,128]{1,0:T(8,128)(2,1)} %copy-done.4) | copy-start | bytes 1572868
  27.2 32.0 %copy-start.3 = (bf16[2048,128]{1,0:T(8,128)(2,1)S(1)}, bf16[2048,128]{1,0:T(8,128)(2,1)}, u32[]{:S(2)}) copy-start(bf16[2048,128]{1,0:T(8,128)(2,1)} %copy-done.2) | copy-start | bytes 1572868
  28.0 29.8 %collective-permute-start.6 = (f32[6,512]{1,0:T(8,128)S(1)}, f32[6,512]{1,0:T(8,128)S(1)}, u32[]{:S(2)}, u32[]{:S(2)}) collective-permute-start(f32[6,512]{1,0:T(8,128)S(1)} %get-tuple-element.27), channel_id=1, source_target_pairs={{0,1},{2,3},{1,0},{3,2},{4,5},{6,7},{5,4},{7,6},{8,9},{10,11},{9,8... | collective-permute-start | bytes 36872 | tf_op jit(solution)/shard_map/ppermute | solution.py:19
  29.6 28.8 %collective-permute-start.3 = (f32[1,128,512]{2,1,0:T(8,128)S(1)}, f32[1,128,512]{2,1,0:T(8,128)S(1)}, u32[]{:S(2)}, u32[]{:S(2)}) collective-permute-start(f32[1,128,512]{2,1,0:T(8,128)S(1)} %select_bitcast_fusion.3), channel_id=1, source_target_pairs={{0,8},{4,12},{8,0},{12,4},{1,9},{5,13},{9,1},{13,5},{2,10},{6,14},... | collective-permute-start | bytes 786440 | tf_op jit(solution)/shard_map/ppermute | solution.py:37
  57.8 19.8 %collective-permute-start.9 = (bf16[2048,128]{1,0:T(8,128)(2,1)S(1)}, bf16[2048,128]{1,0:T(8,128)(2,1)S(1)}, u32[]{:S(2)}, u32[]{:S(2)}) collective-permute-start(bf16[2048,128]{1,0:T(8,128)(2,1)S(1)} %copy-done.5), channel_id=1, source_target_pairs={{1,2},{2,1},{5,6},{6,5},{9,10},{10,9},{13,14},{14,13},{17,18},{18,... | collective-permute-start | bytes 1572872 | tf_op jit(solution)/shard_map/ppermute | solution.py:19
  58.5 0.7 collective-permute-start.7
  59.2 26.9 %collective-permute-start.14 = (bf16[2048,128]{1,0:T(8,128)(2,1)S(1)}, bf16[2048,128]{1,0:T(8,128)(2,1)S(1)}, u32[]{:S(2)}, u32[]{:S(2)}) collective-permute-start(bf16[2048,128]{1,0:T(8,128)(2,1)S(1)} %copy-done.3), channel_id=1, source_target_pairs={{0,1},{2,3},{1,0},{3,2},{4,5},{6,7},{5,4},{7,6},{8,9},{10,11},{9,8... | collective-permute-start | bytes 1572872 | tf_op jit(solution)/shard_map/ppermute | solution.py:19
  75.2 10.9 %collective-permute-start.15 = (bf16[2048,128]{1,0:T(8,128)(2,1)S(1)}, bf16[2048,128]{1,0:T(8,128)(2,1)S(1)}, u32[]{:S(2)}, u32[]{:S(2)}) collective-permute-start(bf16[2048,128]{1,0:T(8,128)(2,1)S(1)} %get-tuple-element.36), channel_id=1, source_target_pairs={{1,2},{2,1},{5,6},{6,5},{9,10},{10,9},{13,14},{14,13},{17,18},{18,... | collective-permute-start | bytes 1572872 | tf_op jit(solution)/shard_map/ppermute | solution.py:19
  77.4 1.7 %copy-start.7 = (bf16[2048,512]{1,0:T(8,128)(2,1)S(1)}, bf16[2048,512]{1,0:T(8,128)(2,1)}, u32[]{:S(2)}) copy-start(bf16[2048,512]{1,0:T(8,128)(2,1)} %copy-done.6) | copy-start | bytes 6291460
  77.4 11.8 %collective-permute-start.12 = (f32[8,128]{1,0:T(8,128)S(1)}, f32[8,128]{1,0:T(8,128)S(1)}, u32[]{:S(2)}, u32[]{:S(2)}) collective-permute-start(f32[8,128]{1,0:T(8,128)S(1)} %slice_bitcast_fusion.8), channel_id=1, source_target_pairs={{0,4},{4,0},{8,12},{12,8},{1,5},{5,1},{9,13},{13,9},{2,6},{6,2},{1... | collective-permute-start | bytes 12296 | tf_op jit(solution)/shard_map/ppermute | solution.py:37
  87.7 9.3 %collective-permute-start.21 = (f32[2,224,128]{2,1,0:T(8,128)S(1)}, f32[2,224,128]{2,1,0:T(8,128)S(1)}, u32[]{:S(2)}, u32[]{:S(2)}) collective-permute-start(f32[2,224,128]{2,1,0:T(8,128)S(1)} %select_bitcast_fusion.4), channel_id=1, source_target_pairs={{0,4},{4,0},{8,12},{12,8},{1,5},{5,1},{9,13},{13,9},{2,6},{6,2},{1... | collective-permute-start | bytes 688136 | tf_op jit(solution)/shard_map/ppermute | solution.py:37
  87.8 10.8 %collective-permute-start.18 = (f32[2,288,128]{2,1,0:T(8,128)S(1)}, f32[2,288,128]{2,1,0:T(8,128)S(1)}, u32[]{:S(2)}, u32[]{:S(2)}) collective-permute-start(f32[2,288,128]{2,1,0:T(8,128)S(1)} %select_bitcast_fusion.2), channel_id=1, source_target_pairs={{0,4},{4,0},{8,12},{12,8},{1,5},{5,1},{9,13},{13,9},{2,6},{6,2},{1... | collective-permute-start | bytes 884744 | tf_op jit(solution)/shard_map/ppermute | solution.py:37
  89.2 3.8 %collective-permute-start.16 = (f32[2,128,128]{2,1,0:T(8,128)S(1)}, f32[2,128,128]{2,1,0:T(8,128)S(1)}, u32[]{:S(2)}, u32[]{:S(2)}) collective-permute-start(f32[2,128,128]{2,1,0:T(8,128)S(1)} %select_bitcast_fusion.5), channel_id=1, source_target_pairs={{0,4},{4,0},{8,12},{12,8},{1,5},{5,1},{9,13},{13,9},{2,6},{6,2},{1... | collective-permute-start | bytes 393224 | tf_op jit(solution)/shard_map/ppermute | solution.py:37
  89.3 3.7 %collective-permute-start.13 = (f32[8,128]{1,0:T(8,128)S(1)}, f32[8,128]{1,0:T(8,128)S(1)}, u32[]{:S(2)}, u32[]{:S(2)}) collective-permute-start(f32[8,128]{1,0:T(8,128)S(1)} %fusion.15), channel_id=1, source_target_pairs={{0,8},{4,12},{8,0},{12,4},{1,9},{5,13},{9,1},{13,5},{2,10},{6,14},... | collective-permute-start | bytes 12296 | tf_op jit(solution)/shard_map/ppermute | solution.py:37
  90.9 13.6 %collective-permute-start.10 = (f32[2,128,384]{2,1,0:T(8,128)S(1)}, f32[2,128,384]{2,1,0:T(8,128)S(1)}, u32[]{:S(2)}, u32[]{:S(2)}) collective-permute-start(f32[2,128,384]{2,1,0:T(8,128)S(1)} %select_bitcast_fusion.1), channel_id=1, source_target_pairs={{0,4},{4,0},{8,12},{12,8},{1,5},{5,1},{9,13},{13,9},{2,6},{6,2},{1... | collective-permute-start | bytes 1179656 | tf_op jit(solution)/shard_map/ppermute | solution.py:37
  93.0 4.0 %collective-permute-start.17 = (bf16[1,128,128]{2,1,0:T(8,128)(2,1)S(1)}, bf16[1,128,128]{2,1,0:T(8,128)(2,1)S(1)}, u32[]{:S(2)}, u32[]{:S(2)}) collective-permute-start(bf16[1,128,128]{2,1,0:T(8,128)(2,1)S(1)} %fusion.14), channel_id=1, source_target_pairs={{0,8},{4,12},{8,0},{12,4},{1,9},{5,13},{9,1},{13,5},{2,10},{6,14},... | collective-permute-start | bytes 98312 | tf_op jit(solution)/shard_map/ppermute | solution.py:37
  97.1 4.2 %collective-permute-start.22 = (bf16[1,224,128]{2,1,0:T(8,128)(2,1)S(1)}, bf16[1,224,128]{2,1,0:T(8,128)(2,1)S(1)}, u32[]{:S(2)}, u32[]{:S(2)}) collective-permute-start(bf16[1,224,128]{2,1,0:T(8,128)(2,1)S(1)} %fusion.13), channel_id=1, source_target_pairs={{0,8},{4,12},{8,0},{12,4},{1,9},{5,13},{9,1},{13,5},{2,10},{6,14},... | collective-permute-start | bytes 172040 | tf_op jit(solution)/shard_map/ppermute | solution.py:37
  98.7 4.4 %collective-permute-start.19 = (bf16[1,288,128]{2,1,0:T(8,128)(2,1)S(1)}, bf16[1,288,128]{2,1,0:T(8,128)(2,1)S(1)}, u32[]{:S(2)}, u32[]{:S(2)}) collective-permute-start(bf16[1,288,128]{2,1,0:T(8,128)(2,1)S(1)} %fusion.12), channel_id=1, source_target_pairs={{0,8},{4,12},{8,0},{12,4},{1,9},{5,13},{9,1},{13,5},{2,10},{6,14},... | collective-permute-start | bytes 221192 | tf_op jit(solution)/shard_map/ppermute | solution.py:37
  101.3 8.3 %collective-permute-start.23 = (f32[224,128]{1,0:T(8,128)S(1)}, f32[224,128]{1,0:T(8,128)S(1)}, u32[]{:S(2)}, u32[]{:S(2)}) collective-permute-start(f32[224,128]{1,0:T(8,128)S(1)} %bitcast_divide_fusion.3), channel_id=1, source_target_pairs={{1,0},{2,1},{5,4},{6,5},{9,8},{10,9},{13,12},{14,13},{17,16},{18,1... | collective-permute-start | bytes 344072 | tf_op jit(solution)/shard_map/ppermute | solution.py:24
  103.2 8.8 %collective-permute-start.20 = (f32[288,128]{1,0:T(8,128)S(1)}, f32[288,128]{1,0:T(8,128)S(1)}, u32[]{:S(2)}, u32[]{:S(2)}) collective-permute-start(f32[288,128]{1,0:T(8,128)S(1)} %bitcast_divide_fusion.2), channel_id=1, source_target_pairs={{1,0},{2,1},{5,4},{6,5},{9,8},{10,9},{13,12},{14,13},{17,16},{18,1... | collective-permute-start | bytes 442376 | tf_op jit(solution)/shard_map/ppermute | solution.py:24
  104.6 5.1 %collective-permute-start.11 = (bf16[1,128,384]{2,1,0:T(8,128)(2,1)S(1)}, bf16[1,128,384]{2,1,0:T(8,128)(2,1)S(1)}, u32[]{:S(2)}, u32[]{:S(2)}) collective-permute-start(bf16[1,128,384]{2,1,0:T(8,128)(2,1)S(1)} %fusion.11), channel_id=1, source_target_pairs={{0,8},{4,12},{8,0},{12,4},{1,9},{5,13},{9,1},{13,5},{2,10},{6,14},... | collective-permute-start | bytes 294920 | tf_op jit(solution)/shard_map/ppermute | solution.py:37
  (2 other events, 1.5 us)

commit v12 on v11

--- a/solution.py
+++ b/solution.py
@@ -276,8 +276,10 @@
             product = cross(olds[1][part, :], above)
             for low, high in zip(marks[:step], marks[1 : step + 1]):
                 products.append(product[low * peers : high * peers])
-            products.append(cross(below, olds[0][part, :]))
-        products.append(cross(below, above))
+            product = cross(below, jnp.concatenate([olds[0][part, :], above], axis=1))
+            products.append(product)
+        else:
+            products.append(cross(below, above))
         for owner in range(peers):
             into = out_ref.at[owner]
             low = 0
@@ -368,14 +370,13 @@
         + [(heights[step], wides[j]) for j in range(step + 1)]
         for step in range(3)
     ]
-    shares = jnp.maximum(sum_all(products[0][0, -8:], "samp"), 1.0)
-    near_0 = cross(own, aboves[0]).reshape(peers, rows, -1)
-    one = jnp.concatenate([products[1], products[0][:, :-8]], axis=1)
-    one = sum_rows(one, "samp", roles, one.shape[1])
-    far_1 = one / shares[1:2]
+    lines = products[1].shape[1] + products[0].shape[1] - 8
+    one = jnp.concatenate([products[1], products[0]], axis=1)
+    one = sum_rows(one, "samp", roles, lines)
+    shares = jnp.maximum(one[lines:], 1.0)
+    far_1 = one[:lines] / shares[1:2]
     far_1 = bring_back(far_1, "var")
-    near_1 = cross(own, aboves[1][:, wides[0] :]).reshape(peers, rows, -1)
-    near_1 = jnp.concatenate([near_0, near_1], axis=2)
+    near_1 = cross(own, aboves[1]).reshape(peers, rows, -1)
     near_1 = sum_rows(near_1, "samp", roles, rows)
     near_1 = near_1 / jnp.concatenate([shares[0:1]] * (near_1.shape[1] // 128), axis=1)
     far_2 = sum_rows(products[2], "samp", roles, products[2].shape[1]) / shares[1:2]

time: 113 us -> 106 us (0.938)
  starting transfers between devices: 40.2 us -> 29.9 us
  waiting for transfers between devices: 47.6 us -> 50.5 us
    ppermute x8, starting transfers between devices: 25.4 us -> 16.9 us  [trade(): lax.ppermute(shard, axis, pairs + [(high, low) for low, high in pairs])]
    ppermute x14 -> x12, waiting for transfers between devices: 9.28 us -> 16.5 us  [swap(): return lax.ppermute(shard, axis, [(i, i ^ bit) for i in range(peers)])]
    ppermute x2, waiting for transfers between devices: 6.21 us -> 3.28 us  [bring_back(): return lax.ppermute(shard, axis, [(i, i - 1) for i in range(1, peers - 1)])]
    ppermute x14 -> x12, starting transfers between devices: 12.2 us -> 10.3 us  [swap(): return lax.ppermute(shard, axis, [(i, i ^ bit) for i in range(peers)])]
    ppermute x8, waiting for transfers between devices: 32.1 us -> 30.7 us  [trade(): lax.ppermute(shard, axis, pairs + [(high, low) for low, high in pairs])]
    dot_general x4 -> x3, matrix products: 3.51 us -> 3.3 us  [cross(): lax.dot_general(left, right, (((0,), (0,)), ((), ())), preferred_element_...]
  transfers between devices with their start and end apart: 24 -> 22, of which waited for: 10 -> 9; matrix products, arithmetic and copies ran while one was open for 4% -> 4% of each run, Pallas kernels for 7% -> 7%
where the time goes in v12:
time: 106 us
  waiting for transfers between devices  50.5 us (48%)
  starting transfers between devices  29.9 us (28%)
  Pallas kernels  12.3 us (12%)
  other arithmetic  5.02 us (5%)
  local copies, waits for them, and re-layouts  3.49 us (3%)
  matrix products  3.3 us (3%)
  between operations  1.22 us (1%)
    ppermute x8, waiting for transfers between devices, trade(): lax.ppermute(shard, axis, pairs + [(high, low) for low, high in pairs])  30.7 us
    ppermute x8, starting transfers between devices, trade(): lax.ppermute(shard, axis, pairs + [(high, low) for low, high in pairs])  16.9 us
    ppermute x12, waiting for transfers between devices, swap(): return lax.ppermute(shard, axis, [(i, i ^ bit) for i in range(peers)])  16.5 us
    ppermute x12, starting transfers between devices, swap(): return lax.ppermute(shard, axis, [(i, i ^ bit) for i in range(peers)])  10.3 us
    pallas_call x3, Pallas kernels, chunk_pass(): pl.pallas_call(functools.partial(chunk_kernel, step, marks, last), out_sh...  4.55 us
    pallas_call x1, Pallas kernels, moments_pass(): pl.pallas_call(functools.partial(moments_kernel, cuts, rows), grid=(sampl...  4.45 us
    unnamed x20, local copies, waits for them, and re-layouts  3.45 us
    dot_general x3, matrix products, cross(): lax.dot_general(left, right, (((0,), (0,)), ((), ())), preferred_element_...  3.3 us
  transfers between devices with their start and end apart: 22, of which 9 were waited for; matrix products, arithmetic and copies ran while one was open for 4% of the time, Pallas kernels for 7%

profile of v12, /device:TPU:0, one launch (start us, length us, event | category | flops | bytes accessed | tf_op | source)
XLA Modules:
  0.0 105.7 jit_solution(1491769547856152720)
XLA Ops:
  0.7 4.4 %moments.1 = (bf16[2048,128]{1,0:T(8,128)(2,1)}, bf16[2048,128]{1,0:T(8,128)(2,1)}, bf16[2048,128]{1,0:T(8,128)(2,1)S(1)}, bf16[2048,128]{1,0:T(8,128)(2,1)S(1)}, f32[8,512]{1,0:T(8,128)S(1)}) custom-call(bf16[2048,512]{1,0:T(8,128)(2,1)} %dosage_ref.3, s32[1,2048]{1,0:T(1,128)S(1)} %copy-done), custom_call_target="tpu_custom_call" | custom-call | flops 8388608 | bytes 4194304 | tf_op jit(solution)/shard_map/moments/pallas_call | solution.py:163
  5.2 0.8 copy-done.2
  7.3 0.8 collective-permute-done
  8.1 2.8 %collective-permute-start.1 = (f32[8,512]{1,0:T(8,128)S(1)}, f32[8,512]{1,0:T(8,128)S(1)}, u32[]{:S(2)}, u32[]{:S(2)}) collective-permute-start(f32[8,512]{1,0:T(8,128)S(1)} %add.47), channel_id=1, source_target_pairs={{0,8},{4,12},{8,0},{12,4},{1,9},{5,13},{9,1},{13,5},{2,10},{6,14},... | collective-permute-start | bytes 49160 | tf_op jit(solution)/shard_map/ppermute | solution.py:37
  11.0 1.7 %collective-permute-done.1 = f32[8,512]{1,0:T(8,128)S(1)} collective-permute-done((f32[8,512]{1,0:T(8,128)S(1)}, f32[8,512]{1,0:T(8,128)S(1)}, u32[]{:S(2)}, u32[]{:S(2)}) %collective-permute-start.1) | collective-permute-done | bytes 16416 | tf_op jit(solution)/shard_map/ppermute | solution.py:37
  13.5 1.3 %fusion.15 = f32[512,512]{1,0:T(8,128)S(1)} fusion(bf16[2048,512]{1,0:T(8,128)(2,1)S(1)} %select_convert_fusion), kind=kOutput, calls=%fused_computation.67 | convolution fusion | flops 1073741824 | bytes 3145728 | tf_op jit(solution)/shard_map/dot_general | solution.py:237
  14.9 1.0 copy-done.9
  15.9 0.9 select_bitcast_fusion
  16.8 3.2 %head.1 = (bf16[2048,256]{1,0:T(8,128)(2,1)}, bf16[2048,256]{1,0:T(8,128)(2,1)}) custom-call(bf16[2048,512]{1,0:T(8,128)(2,1)} %dosage_ref.3), custom_call_target="tpu_custom_call" | custom-call | tf_op jit(solution)/shard_map/head/pallas_call | solution.py:119
  20.1 2.2 %collective-permute-start.8 = (bf16[2048,256]{1,0:T(8,128)(2,1)}, bf16[2048,256]{1,0:T(8,128)(2,1)S(1)}, u32[]{:S(2)}, u32[]{:S(2)}) collective-permute-start(bf16[2048,256]{1,0:T(8,128)(2,1)} %get-tuple-element.29), channel_id=1, source_target_pairs={{0,1},{2,3},{1,0},{3,2},{4,5},{6,7},{5,4},{7,6},{8,9},{10,11},{9,8... | collective-permute-start | bytes 3145736 | tf_op jit(solution)/shard_map/ppermute | solution.py:19
  23.0 4.4 %collective-permute-start.4 = (bf16[2048,128]{1,0:T(8,128)(2,1)}, bf16[2048,128]{1,0:T(8,128)(2,1)S(1)}, u32[]{:S(2)}, u32[]{:S(2)}) collective-permute-start(bf16[2048,128]{1,0:T(8,128)(2,1)} %get-tuple-element.25), channel_id=1, source_target_pairs={{0,1},{2,3},{1,0},{3,2},{4,5},{6,7},{5,4},{7,6},{8,9},{10,11},{9,8... | collective-permute-start | bytes 1572872 | tf_op jit(solution)/shard_map/ppermute | solution.py:19
  28.8 1.3 %collective-permute-start.6 = (f32[6,512]{1,0:T(8,128)S(1)}, f32[6,512]{1,0:T(8,128)S(1)}, u32[]{:S(2)}, u32[]{:S(2)}) collective-permute-start(f32[6,512]{1,0:T(8,128)S(1)} %get-tuple-element.27), channel_id=1, source_target_pairs={{0,1},{2,3},{1,0},{3,2},{4,5},{6,7},{5,4},{7,6},{8,9},{10,11},{9,8... | collective-permute-start | bytes 36872 | tf_op jit(solution)/shard_map/ppermute | solution.py:19
  30.2 1.5 %fusion = f32[1,2,128,512]{3,2,1,0:T(8,128)S(1)} fusion(f32[2,128,512]{2,1,0:T(8,128)} %collective-permute-done.2, f32[2,2,128,512]{3,2,1,0:T(8,128)} %bitcast.178, pred[]{:T(512)S(6)} %ne.20), kind=kLoop, calls=%fused_computation.6 | loop fusion | flops 262144 | bytes 2097153 | tf_op jit(solution)/shard_map/reshape | solution.py:52
  31.7 26.2 %collective-permute-done.6.a_facts = f32[6,512]{1,0:T(8,128)S(1)} collective-permute-done((f32[6,512]{1,0:T(8,128)S(1)}, f32[6,512]{1,0:T(8,128)S(1)}, u32[]{:S(2)}, u32[]{:S(2)}) %collective-permute-start.6) | collective-permute-done | bytes 12320 | tf_op jit(solution)/shard_map/ppermute | solution.py:19
  57.9 1.7 %collective-permute-start.3 = (f32[1,128,512]{2,1,0:T(8,128)S(1)}, f32[1,128,512]{2,1,0:T(8,128)S(1)}, u32[]{:S(2)}, u32[]{:S(2)}) collective-permute-start(f32[1,128,512]{2,1,0:T(8,128)S(1)} %select_bitcast_fusion.3), channel_id=1, source_target_pairs={{0,8},{4,12},{8,0},{12,4},{1,9},{5,13},{9,1},{13,5},{2,10},{6,14},... | collective-permute-start | bytes 786440 | tf_op jit(solution)/shard_map/ppermute | solution.py:37
  59.5 6.5 %collective-permute-done.3 = f32[1,128,512]{2,1,0:T(8,128)S(1)} collective-permute-done((f32[1,128,512]{2,1,0:T(8,128)S(1)}, f32[1,128,512]{2,1,0:T(8,128)S(1)}, u32[]{:S(2)}, u32[]{:S(2)}) %collective-permute-start.3) | collective-permute-done | bytes 262176 | tf_op jit(solution)/shard_map/ppermute | solution.py:37
  66.8 6.3 %collective-permute-start.14 = (bf16[2048,128]{1,0:T(8,128)(2,1)S(1)}, bf16[2048,128]{1,0:T(8,128)(2,1)S(1)}, u32[]{:S(2)}, u32[]{:S(2)}) collective-permute-start(bf16[2048,128]{1,0:T(8,128)(2,1)S(1)} %copy-done.5), channel_id=1, source_target_pairs={{0,1},{2,3},{1,0},{3,2},{4,5},{6,7},{5,4},{7,6},{8,9},{10,11},{9,8... | collective-permute-start | bytes 1572872 | tf_op jit(solution)/shard_map/ppermute | solution.py:19
  73.8 1.5 %shard_map.37 = (f32[4,136,128]{2,1,0:T(8,128)S(1)}, bf16[2048,256]{1,0:T(8,128)(2,1)S(1)}, bf16[2048,256]{1,0:T(8,128)(2,1)S(1)}) custom-call(s32[1,2048]{1,0:T(1,128)S(1)} %copy-done.1, bf16[2048,256]{1,0:T(8,128)(2,1)S(1)} %collective-permute-done.8.a_ref, bf16[2048,256]{1,0:T(8,128)(2,1)S(1)} %collective-permute-done.9.b_ref, ...), custom_call_target="tpu_custom_call" | custom-call | flops 285212672 | bytes 4194304 | tf_op jit(solution)/shard_map/pallas_call | solution.py:312
  75.3 1.5 %shard_map.38 = (f32[4,160,128]{2,1,0:T(8,128)S(1)}, bf16[2048,384]{1,0:T(8,128)(2,1)S(1)}, bf16[2048,384]{1,0:T(8,128)(2,1)S(1)}) custom-call(s32[1,2048]{1,0:T(1,128)S(1)} %copy-done.1, bf16[2048,128]{1,0:T(8,128)(2,1)S(1)} %collective-permute-done.4.a_ref, bf16[2048,128]{1,0:T(8,128)(2,1)S(1)} %collective-permute-done.5.b_ref, ...), custom_call_target="tpu_custom_call" | custom-call | flops 335544320 | bytes 2097152 | tf_op jit(solution)/shard_map/pallas_call | solution.py:312
  77.0 1.3 %fusion.16 = f32[512,384]{1,0:T(8,128)S(1)} fusion(bf16[2048,512]{1,0:T(8,128)(2,1)S(1)} %copy-done.8, bf16[2048,384]{1,0:T(8,128)(2,1)S(1)} %get-tuple-element.33.refs_0_), kind=kOutput, calls=%fused_computation.68 | convolution fusion | flops 805306368 | bytes 4456448 | tf_op jit(solution)/shard_map/dot_general | solution.py:237
  78.3 4.5 %collective-permute-done.14.a_ref = bf16[2048,128]{1,0:T(8,128)(2,1)S(1)} collective-permute-done((bf16[2048,128]{1,0:T(8,128)(2,1)S(1)}, bf16[2048,128]{1,0:T(8,128)(2,1)S(1)}, u32[]{:S(2)}, u32[]{:S(2)}) %collective-permute-start.14) | collective-permute-done | bytes 524320 | tf_op jit(solution)/shard_map/ppermute | solution.py:19
  82.8 1.5 %shard_map.39 = (f32[4,224,128]{2,1,0:T(8,128)S(1)}, bf16[2048,128]{1,0:T(8,128)(2,1)S(1)}) custom-call(s32[1,2048]{1,0:T(1,128)S(1)} %copy-done.1, bf16[2048,128]{1,0:T(8,128)(2,1)S(1)} %collective-permute-done.14.a_ref, bf16[2048,128]{1,0:T(8,128)(2,1)S(1)} %collective-permute-done.15.b_ref, f32[6,512]{1,0:T(8,128)S(1)} %collective-permute-done.6.a_facts, ...), custom_call_target="tpu_custom_call" | custom-call | flops 469762048 | bytes 2097152 | tf_op jit(solution)/shard_map/pallas_call | solution.py:312
  86.0 0.9 collective-permute-done.16
  86.9 1.6 %collective-permute-start.17 = (bf16[1,128,128]{2,1,0:T(8,128)(2,1)S(1)}, bf16[1,128,128]{2,1,0:T(8,128)(2,1)S(1)}, u32[]{:S(2)}, u32[]{:S(2)}) collective-permute-start(bf16[1,128,128]{2,1,0:T(8,128)(2,1)S(1)} %fusion.9), channel_id=1, source_target_pairs={{0,8},{4,12},{8,0},{12,4},{1,9},{5,13},{9,1},{13,5},{2,10},{6,14},... | collective-permute-start | bytes 98312 | tf_op jit(solution)/shard_map/ppermute | solution.py:37
  89.2 1.6 %collective-permute-start.20 = (bf16[1,224,128]{2,1,0:T(8,128)(2,1)S(1)}, bf16[1,224,128]{2,1,0:T(8,128)(2,1)S(1)}, u32[]{:S(2)}, u32[]{:S(2)}) collective-permute-start(bf16[1,224,128]{2,1,0:T(8,128)(2,1)S(1)} %fusion.8), channel_id=1, source_target_pairs={{0,8},{4,12},{8,0},{12,4},{1,9},{5,13},{9,1},{13,5},{2,10},{6,14},... | collective-permute-start | bytes 172040 | tf_op jit(solution)/shard_map/ppermute | solution.py:37
  90.8 2.8 %collective-permute-done.13 = bf16[1,304,128]{2,1,0:T(8,128)(2,1)S(1)} collective-permute-done((bf16[1,304,128]{2,1,0:T(8,128)(2,1)S(1)}, bf16[1,304,128]{2,1,0:T(8,128)(2,1)S(1)}, u32[]{:S(2)}, u32[]{:S(2)}) %collective-permute-start.13) | collective-permute-done | bytes 77856 | tf_op jit(solution)/shard_map/ppermute | solution.py:37
  93.8 1.3 %collective-permute-start.18 = (f32[288,128]{1,0:T(8,128)S(1)}, f32[288,128]{1,0:T(8,128)S(1)}, u32[]{:S(2)}, u32[]{:S(2)}) collective-permute-start(f32[288,128]{1,0:T(8,128)S(1)} %fusion.5), channel_id=1, source_target_pairs={{1,0},{2,1},{5,4},{6,5},{9,8},{10,9},{13,12},{14,13},{17,16},{18,1... | collective-permute-start | bytes 442376 | tf_op jit(solution)/shard_map/ppermute | solution.py:24
  95.1 1.3 %collective-permute-start.21 = (f32[224,128]{1,0:T(8,128)S(1)}, f32[224,128]{1,0:T(8,128)S(1)}, u32[]{:S(2)}, u32[]{:S(2)}) collective-permute-start(f32[224,128]{1,0:T(8,128)S(1)} %bitcast_divide_fusion.2), channel_id=1, source_target_pairs={{1,0},{2,1},{5,4},{6,5},{9,8},{10,9},{13,12},{14,13},{17,16},{18,1... | collective-permute-start | bytes 344072 | tf_op jit(solution)/shard_map/ppermute | solution.py:24
  96.5 0.9 collective-permute-start.11
  97.4 3.8 %collective-permute-done.11 = bf16[1,128,384]{2,1,0:T(8,128)(2,1)S(1)} collective-permute-done((bf16[1,128,384]{2,1,0:T(8,128)(2,1)S(1)}, bf16[1,128,384]{2,1,0:T(8,128)(2,1)S(1)}, u32[]{:S(2)}, u32[]{:S(2)}) %collective-permute-start.11) | collective-permute-done | bytes 98336 | tf_op jit(solution)/shard_map/ppermute | solution.py:37
  101.3 3.3 %collective-permute-done.21 = f32[224,128]{1,0:T(8,128)S(1)} collective-permute-done((f32[224,128]{1,0:T(8,128)S(1)}, f32[224,128]{1,0:T(8,128)S(1)}, u32[]{:S(2)}, u32[]{:S(2)}) %collective-permute-start.21) | collective-permute-done | bytes 114720 | tf_op jit(solution)/shard_map/ppermute | solution.py:24
  104.6 1.0 maximum_select_fusion
  (86 shorter events, 8.7 us)
Async XLA Ops:
  0.0 0.7 copy-start
  0.7 12.0 %copy-start.1 = (s32[1,2048]{1,0:T(1,128)S(1)}, s32[1,2048]{1,0:T(1,128)}, u32[]{:S(2)}) copy-start(s32[1,2048]{1,0:T(1,128)} %observed_ref.9) | copy-start | bytes 24580
  0.7 12.1 %copy-start.6 = (bf16[2048,512]{1,0:T(8,128)(2,1)S(1)}, bf16[2048,512]{1,0:T(8,128)(2,1)}, u32[]{:S(2)}) copy-start(bf16[2048,512]{1,0:T(8,128)(2,1)} %dosage_ref.3) | copy-start | bytes 6291460
  5.2 0.8 copy-start.2
  6.0 0.8 copy-start.4
  6.8 1.3 %collective-permute-start = (f32[8,512]{1,0:T(8,128)S(1)}, f32[8,512]{1,0:T(8,128)S(1)}, u32[]{:S(2)}, u32[]{:S(2)}) collective-permute-start(f32[8,512]{1,0:T(8,128)S(1)} %get-tuple-element.23), channel_id=1, source_target_pairs={{0,4},{4,0},{8,12},{12,8},{1,5},{5,1},{9,13},{13,9},{2,6},{6,2},{1... | collective-permute-start | bytes 49160 | tf_op jit(solution)/shard_map/ppermute | solution.py:37
  8.1 4.5 %collective-permute-start.1 = (f32[8,512]{1,0:T(8,128)S(1)}, f32[8,512]{1,0:T(8,128)S(1)}, u32[]{:S(2)}, u32[]{:S(2)}) collective-permute-start(f32[8,512]{1,0:T(8,128)S(1)} %add.47), channel_id=1, source_target_pairs={{0,8},{4,12},{8,0},{12,4},{1,9},{5,13},{9,1},{13,5},{2,10},{6,14},... | collective-permute-start | bytes 49160 | tf_op jit(solution)/shard_map/ppermute | solution.py:37
  13.5 1.4 %copy-start.7 = (bf16[2048,512]{1,0:T(8,128)(2,1)}, bf16[2048,512]{1,0:T(8,128)(2,1)S(1)}, u32[]{:S(2)}) copy-start(bf16[2048,512]{1,0:T(8,128)(2,1)S(1)} %select_convert_fusion) | copy-start | bytes 6291460
  14.9 1.0 copy-start.9
  16.8 12.0 %collective-permute-start.2 = (f32[2,128,512]{2,1,0:T(8,128)}, f32[2,128,512]{2,1,0:T(8,128)}, u32[]{:S(2)}, u32[]{:S(2)}) collective-permute-start(f32[2,128,512]{2,1,0:T(8,128)} %select_bitcast_fusion), channel_id=1, source_target_pairs={{0,4},{4,0},{8,12},{12,8},{1,5},{5,1},{9,13},{13,9},{2,6},{6,2},{1... | collective-permute-start | bytes 1572872 | tf_op jit(solution)/shard_map/ppermute | solution.py:37
  20.1 53.0 %collective-permute-start.8 = (bf16[2048,256]{1,0:T(8,128)(2,1)}, bf16[2048,256]{1,0:T(8,128)(2,1)S(1)}, u32[]{:S(2)}, u32[]{:S(2)}) collective-permute-start(bf16[2048,256]{1,0:T(8,128)(2,1)} %get-tuple-element.29), channel_id=1, source_target_pairs={{0,1},{2,3},{1,0},{3,2},{4,5},{6,7},{5,4},{7,6},{8,9},{10,11},{9,8... | collective-permute-start | bytes 3145736 | tf_op jit(solution)/shard_map/ppermute | solution.py:19
  22.3 51.6 %collective-permute-start.9 = (bf16[2048,256]{1,0:T(8,128)(2,1)}, bf16[2048,256]{1,0:T(8,128)(2,1)S(1)}, u32[]{:S(2)}, u32[]{:S(2)}) collective-permute-start(bf16[2048,256]{1,0:T(8,128)(2,1)} %get-tuple-element.30), channel_id=1, source_target_pairs={{1,2},{2,1},{5,6},{6,5},{9,10},{10,9},{13,14},{14,13},{17,18},{18,... | collective-permute-start | bytes 3145736 | tf_op jit(solution)/shard_map/ppermute | solution.py:19
  23.0 52.3 %collective-permute-start.4 = (bf16[2048,128]{1,0:T(8,128)(2,1)}, bf16[2048,128]{1,0:T(8,128)(2,1)S(1)}, u32[]{:S(2)}, u32[]{:S(2)}) collective-permute-start(bf16[2048,128]{1,0:T(8,128)(2,1)} %get-tuple-element.25), channel_id=1, source_target_pairs={{0,1},{2,3},{1,0},{3,2},{4,5},{6,7},{5,4},{7,6},{8,9},{10,11},{9,8... | collective-permute-start | bytes 1572872 | tf_op jit(solution)/shard_map/ppermute | solution.py:19
  27.4 47.9 %collective-permute-start.5 = (bf16[2048,128]{1,0:T(8,128)(2,1)}, bf16[2048,128]{1,0:T(8,128)(2,1)S(1)}, u32[]{:S(2)}, u32[]{:S(2)}) collective-permute-start(bf16[2048,128]{1,0:T(8,128)(2,1)} %get-tuple-element.26), channel_id=1, source_target_pairs={{1,2},{2,1},{5,6},{6,5},{9,10},{10,9},{13,14},{14,13},{17,18},{18,... | collective-permute-start | bytes 1572872 | tf_op jit(solution)/shard_map/ppermute | solution.py:19
  28.1 38.7 %copy-start.5 = (bf16[2048,128]{1,0:T(8,128)(2,1)S(1)}, bf16[2048,128]{1,0:T(8,128)(2,1)}, u32[]{:S(2)}) copy-start(bf16[2048,128]{1,0:T(8,128)(2,1)} %copy-done.4) | copy-start | bytes 1572868
  28.1 45.0 %copy-start.3 = (bf16[2048,128]{1,0:T(8,128)(2,1)S(1)}, bf16[2048,128]{1,0:T(8,128)(2,1)}, u32[]{:S(2)}) copy-start(bf16[2048,128]{1,0:T(8,128)(2,1)} %copy-done.2) | copy-start | bytes 1572868
  28.8 29.0 %collective-permute-start.6 = (f32[6,512]{1,0:T(8,128)S(1)}, f32[6,512]{1,0:T(8,128)S(1)}, u32[]{:S(2)}, u32[]{:S(2)}) collective-permute-start(f32[6,512]{1,0:T(8,128)S(1)} %get-tuple-element.27), channel_id=1, source_target_pairs={{0,1},{2,3},{1,0},{3,2},{4,5},{6,7},{5,4},{7,6},{8,9},{10,11},{9,8... | collective-permute-start | bytes 36872 | tf_op jit(solution)/shard_map/ppermute | solution.py:19
  57.9 8.1 %collective-permute-start.3 = (f32[1,128,512]{2,1,0:T(8,128)S(1)}, f32[1,128,512]{2,1,0:T(8,128)S(1)}, u32[]{:S(2)}, u32[]{:S(2)}) collective-permute-start(f32[1,128,512]{2,1,0:T(8,128)S(1)} %select_bitcast_fusion.3), channel_id=1, source_target_pairs={{0,8},{4,12},{8,0},{12,4},{1,9},{5,13},{9,1},{13,5},{2,10},{6,14},... | collective-permute-start | bytes 786440 | tf_op jit(solution)/shard_map/ppermute | solution.py:37
  66.0 0.7 collective-permute-start.7
  66.8 16.1 %collective-permute-start.14 = (bf16[2048,128]{1,0:T(8,128)(2,1)S(1)}, bf16[2048,128]{1,0:T(8,128)(2,1)S(1)}, u32[]{:S(2)}, u32[]{:S(2)}) collective-permute-start(bf16[2048,128]{1,0:T(8,128)(2,1)S(1)} %copy-done.5), channel_id=1, source_target_pairs={{0,1},{2,3},{1,0},{3,2},{4,5},{6,7},{5,4},{7,6},{8,9},{10,11},{9,8... | collective-permute-start | bytes 1572872 | tf_op jit(solution)/shard_map/ppermute | solution.py:19
  73.1 9.7 %collective-permute-start.15 = (bf16[2048,128]{1,0:T(8,128)(2,1)S(1)}, bf16[2048,128]{1,0:T(8,128)(2,1)S(1)}, u32[]{:S(2)}, u32[]{:S(2)}) collective-permute-start(bf16[2048,128]{1,0:T(8,128)(2,1)S(1)} %copy-done.3), channel_id=1, source_target_pairs={{1,2},{2,1},{5,6},{6,5},{9,10},{10,9},{13,14},{14,13},{17,18},{18,... | collective-permute-start | bytes 1572872 | tf_op jit(solution)/shard_map/ppermute | solution.py:19
  75.3 1.7 %copy-start.8 = (bf16[2048,512]{1,0:T(8,128)(2,1)S(1)}, bf16[2048,512]{1,0:T(8,128)(2,1)}, u32[]{:S(2)}) copy-start(bf16[2048,512]{1,0:T(8,128)(2,1)} %copy-done.7) | copy-start | bytes 6291460
  77.0 11.5 %collective-permute-start.12 = (f32[2,296,128]{2,1,0:T(8,128)S(1)}, f32[2,296,128]{2,1,0:T(8,128)S(1)}, u32[]{:S(2)}, u32[]{:S(2)}) collective-permute-start(f32[2,296,128]{2,1,0:T(8,128)S(1)} %select_bitcast_fusion.2), channel_id=1, source_target_pairs={{0,4},{4,0},{8,12},{12,8},{1,5},{5,1},{9,13},{13,9},{2,6},{6,2},{1... | collective-permute-start | bytes 909320 | tf_op jit(solution)/shard_map/ppermute | solution.py:37
  84.4 4.0 %collective-permute-start.19 = (f32[2,224,128]{2,1,0:T(8,128)S(1)}, f32[2,224,128]{2,1,0:T(8,128)S(1)}, u32[]{:S(2)}, u32[]{:S(2)}) collective-permute-start(f32[2,224,128]{2,1,0:T(8,128)S(1)} %select_bitcast_fusion.4), channel_id=1, source_target_pairs={{0,4},{4,0},{8,12},{12,8},{1,5},{5,1},{9,13},{13,9},{2,6},{6,2},{1... | collective-permute-start | bytes 688136 | tf_op jit(solution)/shard_map/ppermute | solution.py:37
  85.3 1.5 %collective-permute-start.16 = (f32[2,128,128]{2,1,0:T(8,128)S(1)}, f32[2,128,128]{2,1,0:T(8,128)S(1)}, u32[]{:S(2)}, u32[]{:S(2)}) collective-permute-start(f32[2,128,128]{2,1,0:T(8,128)S(1)} %select_bitcast_fusion.6), channel_id=1, source_target_pairs={{0,4},{4,0},{8,12},{12,8},{1,5},{5,1},{9,13},{13,9},{2,6},{6,2},{1... | collective-permute-start | bytes 393224 | tf_op jit(solution)/shard_map/ppermute | solution.py:37
  85.9 10.5 %collective-permute-start.10 = (f32[2,128,384]{2,1,0:T(8,128)S(1)}, f32[2,128,384]{2,1,0:T(8,128)S(1)}, u32[]{:S(2)}, u32[]{:S(2)}) collective-permute-start(f32[2,128,384]{2,1,0:T(8,128)S(1)} %select_bitcast_fusion.1), channel_id=1, source_target_pairs={{0,4},{4,0},{8,12},{12,8},{1,5},{5,1},{9,13},{13,9},{2,6},{6,2},{1... | collective-permute-start | bytes 1179656 | tf_op jit(solution)/shard_map/ppermute | solution.py:37
  86.9 10.5 %collective-permute-start.17 = (bf16[1,128,128]{2,1,0:T(8,128)(2,1)S(1)}, bf16[1,128,128]{2,1,0:T(8,128)(2,1)S(1)}, u32[]{:S(2)}, u32[]{:S(2)}) collective-permute-start(bf16[1,128,128]{2,1,0:T(8,128)(2,1)S(1)} %fusion.9), channel_id=1, source_target_pairs={{0,8},{4,12},{8,0},{12,4},{1,9},{5,13},{9,1},{13,5},{2,10},{6,14},... | collective-permute-start | bytes 98312 | tf_op jit(solution)/shard_map/ppermute | solution.py:37
  88.6 5.0 %collective-permute-start.13 = (bf16[1,304,128]{2,1,0:T(8,128)(2,1)S(1)}, bf16[1,304,128]{2,1,0:T(8,128)(2,1)S(1)}, u32[]{:S(2)}, u32[]{:S(2)}) collective-permute-start(bf16[1,304,128]{2,1,0:T(8,128)(2,1)S(1)} %pad_maximum_fusion.1), channel_id=1, source_target_pairs={{0,8},{4,12},{8,0},{12,4},{1,9},{5,13},{9,1},{13,5},{2,10},{6,14},... | collective-permute-start | bytes 233480 | tf_op jit(solution)/shard_map/ppermute | solution.py:37
  89.2 5.8 %collective-permute-start.20 = (bf16[1,224,128]{2,1,0:T(8,128)(2,1)S(1)}, bf16[1,224,128]{2,1,0:T(8,128)(2,1)S(1)}, u32[]{:S(2)}, u32[]{:S(2)}) collective-permute-start(bf16[1,224,128]{2,1,0:T(8,128)(2,1)S(1)} %fusion.8), channel_id=1, source_target_pairs={{0,8},{4,12},{8,0},{12,4},{1,9},{5,13},{9,1},{13,5},{2,10},{6,14},... | collective-permute-start | bytes 172040 | tf_op jit(solution)/shard_map/ppermute | solution.py:37
  93.8 10.8 %collective-permute-start.18 = (f32[288,128]{1,0:T(8,128)S(1)}, f32[288,128]{1,0:T(8,128)S(1)}, u32[]{:S(2)}, u32[]{:S(2)}) collective-permute-start(f32[288,128]{1,0:T(8,128)S(1)} %fusion.5), channel_id=1, source_target_pairs={{1,0},{2,1},{5,4},{6,5},{9,8},{10,9},{13,12},{14,13},{17,16},{18,1... | collective-permute-start | bytes 442376 | tf_op jit(solution)/shard_map/ppermute | solution.py:24
  95.1 9.4 %collective-permute-start.21 = (f32[224,128]{1,0:T(8,128)S(1)}, f32[224,128]{1,0:T(8,128)S(1)}, u32[]{:S(2)}, u32[]{:S(2)}) collective-permute-start(f32[224,128]{1,0:T(8,128)S(1)} %bitcast_divide_fusion.2), channel_id=1, source_target_pairs={{1,0},{2,1},{5,4},{6,5},{9,8},{10,9},{13,12},{14,13},{17,16},{18,1... | collective-permute-start | bytes 344072 | tf_op jit(solution)/shard_map/ppermute | solution.py:24
  96.5 4.7 %collective-permute-start.11 = (bf16[1,128,384]{2,1,0:T(8,128)(2,1)S(1)}, bf16[1,128,384]{2,1,0:T(8,128)(2,1)S(1)}, u32[]{:S(2)}, u32[]{:S(2)}) collective-permute-start(bf16[1,128,384]{2,1,0:T(8,128)(2,1)S(1)} %fusion.7), channel_id=1, source_target_pairs={{0,8},{4,12},{8,0},{12,4},{1,9},{5,13},{9,1},{13,5},{2,10},{6,14},... | collective-permute-start | bytes 294920 | tf_op jit(solution)/shard_map/ppermute | solution.py:37
